TPU v7x, 32 devices: a whole 2x2x4 slice. The times are simulated.
32 devices in a mesh: chan: 8 (over z, x), tm: 4 (over y, core).
Axes of the slice: x: 2, y: 2, z: 4, core: 2. Of those that a mesh axis runs over, the one named last changes fastest.
Arguments:
- records: bfloat16 [1280, 16, 7680], P('chan', 'tm'), may hold values from -6 to 6
- valid_mask: int32 [8, 16], P('chan', 'tm'), may hold values 0 or 1
- band_limits: int32 [8, 2], P('chan'), may hold values from 0 to 321, as said below
Outputs:
- correlations: float32 [1280, 32, 128], P('chan', 'tm')
Inputs may be any that keep to these rules, and one draw needn't show every extreme that they name: band_limits[b, 0] <= 289 and 1 <= band_limits[b, 1] - band_limits[b, 0] <= 32.
All inputs are finite; a program needn't handle non-finite values. No bound on the sum of `valid_mask` on one device may be relied on, other than what follows from the above.
Results may differ from a plain program's by a relative error of at most 0.013.
Values may be sent and summed in bfloat16 or wider, within the bound.
No kernel may reach another device: no remote copies, remote signals or barrier semaphores. Data moves between devices by JAX's collectives and lax.ppermute only.
A program may use at most 256 MiB of HBM per device.

v0:
```python
import math

import jax
import jax.numpy as jnp
from jax import lax
from jax.sharding import PartitionSpec as P

BINS = 512
LAGS = 128
PAIRS = 32
REACH = 2


def passed_along(block, axis, distance):
    devices = range(lax.axis_size(axis))
    route = [(i - distance, i) for i in devices if i - distance in devices]
    return lax.ppermute(block, axis, route)


def dft_table_of(samples, bins):
    times = jnp.arange(samples, dtype=jnp.int32)[:, None]
    freqs = 32 + jnp.arange(bins, dtype=jnp.int32)[None, :]
    phase = (times * freqs % samples).astype(jnp.float32) * (2.0 * math.pi / samples)
    return jnp.concatenate([jnp.cos(phase), -jnp.sin(phase)], axis=1).astype(jnp.bfloat16)


def lag_table_of(samples, bins, lags):
    freqs = 32 + jnp.arange(bins, dtype=jnp.int32)[:, None]
    shifts = (jnp.arange(lags, dtype=jnp.int32) - lags // 2 + samples) % samples
    phase = (freqs * shifts[None, :] % samples).astype(jnp.float32) * (2.0 * math.pi / samples)
    factor = 1.0 / math.sqrt(bins)
    return (jnp.concatenate([jnp.cos(phase), -jnp.sin(phase)], axis=0) * factor).astype(
        jnp.bfloat16
    )


def whiten(spectra, bins):
    real_part = spectra[:, :bins]
    imag_part = spectra[:, bins:]
    power_sum = real_part * real_part + imag_part * imag_part
    water_level = jnp.mean(power_sum, axis=1, keepdims=True)
    inverse_amp = 1.0 / jnp.sqrt(power_sum + 0.1 * water_level + 1e-06)
    return jnp.concatenate([real_part * inverse_amp, imag_part * inverse_amp], axis=1).astype(
        jnp.bfloat16
    )


def cross_stack(
    extended, ext_weight, lowest, first_pair, pair_total, group_size, lag_table, block_size
):
    seg_total = extended.shape[1]
    bins = extended.shape[2] // 2
    own_panel = extended[:block_size]
    own_weight = ext_weight[:block_size]

    def one_block(block_index):
        offsets = lowest + first_pair + block_index * 4 + jnp.arange(4, dtype=jnp.int32)
        partner = jax.vmap(
            lambda offset: lax.dynamic_slice_in_dim(extended, offset, block_size, 0)
        )(offsets)
        partner_weight = jax.vmap(
            lambda offset: lax.dynamic_slice_in_dim(ext_weight, offset, block_size, 0)
        )(offsets)
        mine = own_panel.astype(jnp.float32)[None]
        theirs = partner.astype(jnp.float32)
        weight = own_weight.astype(jnp.float32)[None] * partner_weight.astype(jnp.float32)
        real_mix = (
            mine[..., :bins] * theirs[..., :bins] + mine[..., bins:] * theirs[..., bins:]
        ) * weight[..., None]
        imag_mix = (
            mine[..., bins:] * theirs[..., :bins] - mine[..., :bins] * theirs[..., bins:]
        ) * weight[..., None]
        cross_sum = jnp.concatenate([real_mix, imag_mix], axis=-1)
        cross_sum = cross_sum.reshape(
            4, block_size, seg_total // group_size, group_size, 2 * bins
        ).sum(axis=3)
        cross_sum = cross_sum.astype(jnp.bfloat16)
        correlation = jnp.einsum(
            "qcgf,fl->qcl", cross_sum, lag_table, preferred_element_type=jnp.float32
        )
        pair_count = jnp.sum(weight, axis=-1)
        return (correlation, pair_count)

    correlation, pair_count = lax.map(one_block, jnp.arange(pair_total // 4, dtype=jnp.int32))
    lags = correlation.shape[-1]
    correlation = jnp.transpose(correlation, (2, 0, 1, 3)).reshape(block_size, pair_total, lags)
    pair_count = jnp.transpose(pair_count, (2, 0, 1)).reshape(block_size, pair_total)
    return (correlation, pair_count)


def shards(records, valid_mask, band_limits):
    block_size, seg_local, samples = records.shape
    dft_table = dft_table_of(samples, BINS)
    spectra = jnp.dot(
        records.reshape(block_size * seg_local, samples),
        dft_table,
        preferred_element_type=jnp.float32,
    )
    white = whiten(spectra, BINS).reshape(block_size, seg_local, 2 * BINS)
    marks = valid_mask.astype(jnp.bfloat16)
    panels = [white]
    flags = [marks]
    for hop_count in range(1, REACH + 1):
        got_panel, got_flags = passed_along((white, marks), "chan", -hop_count)
        panels.append(got_panel)
        flags.append(got_flags)
    extended = jnp.concatenate(panels, axis=0)
    ext_flags = jnp.concatenate(flags, axis=0)
    lowest = band_limits[0, 0]
    highest = band_limits[0, 1]
    lag_table = lag_table_of(samples, BINS, LAGS)
    partial_corr, partial_count = cross_stack(
        extended,
        jnp.repeat(ext_flags, block_size, axis=0),
        lowest,
        0,
        PAIRS,
        seg_local,
        lag_table,
        block_size,
    )
    summed, pair_count = (
        lax.psum_scatter(
            partial_corr.astype(jnp.bfloat16), "tm", scatter_dimension=1, tiled=True
        ).astype(jnp.float32),
        lax.psum_scatter(
            partial_count.astype(jnp.bfloat16), "tm", scatter_dimension=1, tiled=True
        ).astype(jnp.float32),
    )
    pair_share = summed.shape[1]
    pair_index = lax.axis_index("tm") * pair_share + jnp.arange(pair_share, dtype=jnp.int32)
    inside = lowest + pair_index < highest
    result = summed / jnp.maximum(pair_count, 1.0)[..., None]
    return jnp.where(inside[None, :, None], result, jnp.zeros_like(result))


def solution(mesh):
    placed = (P("chan", "tm", None), P("chan", "tm"), P("chan", None))
    return jax.shard_map(
        shards, mesh=mesh, in_specs=placed, out_specs=P("chan", "tm", None), check_vma=False
    )
```

profile of v0, /device:TPU:0, one launch (start us, length us, event | category | flops | bytes accessed | tf_op | source)
XLA Modules:
  0.0 597.8 jit_solution(6376396024425547947)
XLA Ops:
  6.5 13.2 %reshape.89 = bf16[640,7680]{1,0:T(8,128)(2,1)} reshape(bf16[160,4,7680]{2,1,0:T(4,128)(2,1)} %param.5) | data formatting | bytes 19660800 | tf_op jit(solution)/shard_map/reshape | solution.py:95
  19.8 66.9 %cosine_convert_fusion = (bf16[7680,512]{1,0:T(8,128)(2,1)}, bf16[7680,512]{1,0:T(8,128)(2,1)}) fusion(s32[512]{0:T(512)S(1)} %iota_add_fusion), kind=kLoop, calls=%fused_computation.29 | loop fusion | flops 47185920 | bytes 15730688 | tf_op jit(solution)/shard_map/convert.5
  86.7 16.5 %fusion.23 = f32[640,1024]{1,0:T(8,128)S(1)} fusion(bf16[640,7680]{1,0:T(8,128)(2,1)} %reshape.89, bf16[7680,512]{1,0:T(8,128)(2,1)} %get-tuple-element.168, bf16[7680,512]{1,0:T(8,128)(2,1)} %get-tuple-element.167), kind=kOutput, calls=%fused_computation.35 | convolution fusion | flops 10097786880 | bytes 28180480 | tf_op jit(solution)/shard_map/dot_general | solution.py:94
  114.4 54.4 %collective-permute-done.3 = bf16[1,4]{0,1:T(4,128)(2,1)S(1)} collective-permute-done((bf16[1,4]{0,1:T(4,128)(2,1)S(1)}, bf16[1,4]{0,1:T(4,128)(2,1)S(1)}, u32[]{:S(2)}, u32[]{:S(2)}) %collective-permute-start.3) | collective-permute-done | bytes 40 | tf_op jit(solution)/shard_map/ppermute | solution.py:17
  174.2 364.7 %while.21 = (s32[]{:T(128)}, bf16[8,4,160,128]{3,2,1,0:T(8,128)(2,1)}, bf16[8,4,160]{2,1,0:T(4,128)(2,1)S(1)}, bf16[160,4,1024]{2,1,0:T(4,128)(2,1)S(1)}, s32[8]...) while((s32[]{:T(128)}, ...), condition=%wide.region_4.5_spmd.clone, body=%wide.region_1.4_spmd.clone.sunk | while | flops 186129312 | bytes 75368728 | solution.py:84
  183.5 11.6 %while.22 = (s32[]{:T(128)}, bf16[480,4,1024]{2,1,0:T(4,128)(2,1)}, s32[4,3]{1,0:T(4,128)S(1)}, bf16[4,160,4,1024]{3,2,1,0:T(4,128)(2,1)}, s32[]{:T(128)}) while((s32[]{:T(128)}, bf16[480,4,1024]{2,1,0:T(4,128)(2,1)}, s32[4,3]{1,0:T(4,128)S(1)}, bf16[4,160,4,1024]{3,2,1,0:T(4,128)(2,1)}, s32[]{:T(128)}) %tuple.71), condition=%wide.while_cond, body=%wide.while_body.sunk | while | flops 2 | bytes 2621545 | solution.py:59
  195.1 9.6 %convert_element_type.135 = f32[4,160,4,1024]{3,2,1,0:T(4,128)} convert(bf16[4,160,4,1024]{3,2,1,0:T(4,128)(2,1)} %get-tuple-element.298) | non-fusion elementwise | flops 2621440 | bytes 15728640 | tf_op jit(solution)/shard_map/while/body/eval_jaxpr/convert_element_type | solution.py:65
  211.1 7.6 %maximum_reduce_fusion.2 = bf16[4,160,1024]{2,1,0:T(8,128)(2,1)S(1)} fusion(f32[4,160,4,512]{3,2,1,0:T(4,128)S(1)} %get-tuple-element.303, f32[4,160,4,512]{3,2,1,0:T(4,128)S(1)} %get-tuple-element.304), kind=kLoop, calls=%fused_computation.6.clone.1 | loop fusion | flops 4587520 | bytes 11796480 | tf_op jit(solution)/shard_map/while/body/eval_jaxpr/reduce_sum | solution.py:76
  229.1 11.6 %while.22 = (s32[]{:T(128)}, bf16[480,4,1024]{2,1,0:T(4,128)(2,1)}, s32[4,3]{1,0:T(4,128)S(1)}, bf16[4,160,4,1024]{3,2,1,0:T(4,128)(2,1)}, s32[]{:T(128)}) while((s32[]{:T(128)}, bf16[480,4,1024]{2,1,0:T(4,128)(2,1)}, s32[4,3]{1,0:T(4,128)S(1)}, bf16[4,160,4,1024]{3,2,1,0:T(4,128)(2,1)}, s32[]{:T(128)}) %tuple.71), condition=%wide.while_cond, body=%wide.while_body.sunk | while | flops 2 | bytes 2621545 | solution.py:59
  240.7 9.6 %convert_element_type.135 = f32[4,160,4,1024]{3,2,1,0:T(4,128)} convert(bf16[4,160,4,1024]{3,2,1,0:T(4,128)(2,1)} %get-tuple-element.298) | non-fusion elementwise | flops 2621440 | bytes 15728640 | tf_op jit(solution)/shard_map/while/body/eval_jaxpr/convert_element_type | solution.py:65
  256.6 7.6 %maximum_reduce_fusion.2 = bf16[4,160,1024]{2,1,0:T(8,128)(2,1)S(1)} fusion(f32[4,160,4,512]{3,2,1,0:T(4,128)S(1)} %get-tuple-element.303, f32[4,160,4,512]{3,2,1,0:T(4,128)S(1)} %get-tuple-element.304), kind=kLoop, calls=%fused_computation.6.clone.1 | loop fusion | flops 4587520 | bytes 11796480 | tf_op jit(solution)/shard_map/while/body/eval_jaxpr/reduce_sum | solution.py:76
  274.7 11.6 %while.22 = (s32[]{:T(128)}, bf16[480,4,1024]{2,1,0:T(4,128)(2,1)}, s32[4,3]{1,0:T(4,128)S(1)}, bf16[4,160,4,1024]{3,2,1,0:T(4,128)(2,1)}, s32[]{:T(128)}) while((s32[]{:T(128)}, bf16[480,4,1024]{2,1,0:T(4,128)(2,1)}, s32[4,3]{1,0:T(4,128)S(1)}, bf16[4,160,4,1024]{3,2,1,0:T(4,128)(2,1)}, s32[]{:T(128)}) %tuple.71), condition=%wide.while_cond, body=%wide.while_body.sunk | while | flops 2 | bytes 2621545 | solution.py:59
  286.3 9.6 %convert_element_type.135 = f32[4,160,4,1024]{3,2,1,0:T(4,128)} convert(bf16[4,160,4,1024]{3,2,1,0:T(4,128)(2,1)} %get-tuple-element.298) | non-fusion elementwise | flops 2621440 | bytes 15728640 | tf_op jit(solution)/shard_map/while/body/eval_jaxpr/convert_element_type | solution.py:65
  302.2 7.6 %maximum_reduce_fusion.2 = bf16[4,160,1024]{2,1,0:T(8,128)(2,1)S(1)} fusion(f32[4,160,4,512]{3,2,1,0:T(4,128)S(1)} %get-tuple-element.303, f32[4,160,4,512]{3,2,1,0:T(4,128)S(1)} %get-tuple-element.304), kind=kLoop, calls=%fused_computation.6.clone.1 | loop fusion | flops 4587520 | bytes 11796480 | tf_op jit(solution)/shard_map/while/body/eval_jaxpr/reduce_sum | solution.py:76
  320.3 11.6 %while.22 = (s32[]{:T(128)}, bf16[480,4,1024]{2,1,0:T(4,128)(2,1)}, s32[4,3]{1,0:T(4,128)S(1)}, bf16[4,160,4,1024]{3,2,1,0:T(4,128)(2,1)}, s32[]{:T(128)}) while((s32[]{:T(128)}, bf16[480,4,1024]{2,1,0:T(4,128)(2,1)}, s32[4,3]{1,0:T(4,128)S(1)}, bf16[4,160,4,1024]{3,2,1,0:T(4,128)(2,1)}, s32[]{:T(128)}) %tuple.71), condition=%wide.while_cond, body=%wide.while_body.sunk | while | flops 2 | bytes 2621545 | solution.py:59
  331.9 9.6 %convert_element_type.135 = f32[4,160,4,1024]{3,2,1,0:T(4,128)} convert(bf16[4,160,4,1024]{3,2,1,0:T(4,128)(2,1)} %get-tuple-element.298) | non-fusion elementwise | flops 2621440 | bytes 15728640 | tf_op jit(solution)/shard_map/while/body/eval_jaxpr/convert_element_type | solution.py:65
  341.5 6.3 %add_multiply_fusion.2 = (f32[4,160,4,512]{3,2,1,0:T(4,128)S(1)}, f32[4,160,4,512]{3,2,1,0:T(4,128)S(1)}) fusion(f32[4,160,4,1024]{3,2,1,0:T(4,128)} %convert_element_type.135, f32[4,160,4]{2,1,0:T(8,128)S(1)} %copy.39, f32[160,4,512]{2,1,0:T(4,128)S(1)} %get-tuple-element.301, f32[160,4,512]{2,1,0:T(4,128)S(1)} %get-tuple-element.302), kind=kLoop, calls=%fused_computation.8.clone.1 | loop fusion | flops 10485760 | bytes 23603200 | tf_op jit(solution)/shard_map/while/body/eval_jaxpr/mul | solution.py:67
  347.8 7.6 %maximum_reduce_fusion.2 = bf16[4,160,1024]{2,1,0:T(8,128)(2,1)S(1)} fusion(f32[4,160,4,512]{3,2,1,0:T(4,128)S(1)} %get-tuple-element.303, f32[4,160,4,512]{3,2,1,0:T(4,128)S(1)} %get-tuple-element.304), kind=kLoop, calls=%fused_computation.6.clone.1 | loop fusion | flops 4587520 | bytes 11796480 | tf_op jit(solution)/shard_map/while/body/eval_jaxpr/reduce_sum | solution.py:76
  365.9 11.6 %while.22 = (s32[]{:T(128)}, bf16[480,4,1024]{2,1,0:T(4,128)(2,1)}, s32[4,3]{1,0:T(4,128)S(1)}, bf16[4,160,4,1024]{3,2,1,0:T(4,128)(2,1)}, s32[]{:T(128)}) while((s32[]{:T(128)}, bf16[480,4,1024]{2,1,0:T(4,128)(2,1)}, s32[4,3]{1,0:T(4,128)S(1)}, bf16[4,160,4,1024]{3,2,1,0:T(4,128)(2,1)}, s32[]{:T(128)}) %tuple.71), condition=%wide.while_cond, body=%wide.while_body.sunk | while | flops 2 | bytes 2621545 | solution.py:59
  377.5 9.6 %convert_element_type.135 = f32[4,160,4,1024]{3,2,1,0:T(4,128)} convert(bf16[4,160,4,1024]{3,2,1,0:T(4,128)(2,1)} %get-tuple-element.298) | non-fusion elementwise | flops 2621440 | bytes 15728640 | tf_op jit(solution)/shard_map/while/body/eval_jaxpr/convert_element_type | solution.py:65
  393.4 7.6 %maximum_reduce_fusion.2 = bf16[4,160,1024]{2,1,0:T(8,128)(2,1)S(1)} fusion(f32[4,160,4,512]{3,2,1,0:T(4,128)S(1)} %get-tuple-element.303, f32[4,160,4,512]{3,2,1,0:T(4,128)S(1)} %get-tuple-element.304), kind=kLoop, calls=%fused_computation.6.clone.1 | loop fusion | flops 4587520 | bytes 11796480 | tf_op jit(solution)/shard_map/while/body/eval_jaxpr/reduce_sum | solution.py:76
  411.5 11.6 %while.22 = (s32[]{:T(128)}, bf16[480,4,1024]{2,1,0:T(4,128)(2,1)}, s32[4,3]{1,0:T(4,128)S(1)}, bf16[4,160,4,1024]{3,2,1,0:T(4,128)(2,1)}, s32[]{:T(128)}) while((s32[]{:T(128)}, bf16[480,4,1024]{2,1,0:T(4,128)(2,1)}, s32[4,3]{1,0:T(4,128)S(1)}, bf16[4,160,4,1024]{3,2,1,0:T(4,128)(2,1)}, s32[]{:T(128)}) %tuple.71), condition=%wide.while_cond, body=%wide.while_body.sunk | while | flops 2 | bytes 2621545 | solution.py:59
  423.1 9.6 %convert_element_type.135 = f32[4,160,4,1024]{3,2,1,0:T(4,128)} convert(bf16[4,160,4,1024]{3,2,1,0:T(4,128)(2,1)} %get-tuple-element.298) | non-fusion elementwise | flops 2621440 | bytes 15728640 | tf_op jit(solution)/shard_map/while/body/eval_jaxpr/convert_element_type | solution.py:65
  439.0 7.6 %maximum_reduce_fusion.2 = bf16[4,160,1024]{2,1,0:T(8,128)(2,1)S(1)} fusion(f32[4,160,4,512]{3,2,1,0:T(4,128)S(1)} %get-tuple-element.303, f32[4,160,4,512]{3,2,1,0:T(4,128)S(1)} %get-tuple-element.304), kind=kLoop, calls=%fused_computation.6.clone.1 | loop fusion | flops 4587520 | bytes 11796480 | tf_op jit(solution)/shard_map/while/body/eval_jaxpr/reduce_sum | solution.py:76
  457.1 11.6 %while.22 = (s32[]{:T(128)}, bf16[480,4,1024]{2,1,0:T(4,128)(2,1)}, s32[4,3]{1,0:T(4,128)S(1)}, bf16[4,160,4,1024]{3,2,1,0:T(4,128)(2,1)}, s32[]{:T(128)}) while((s32[]{:T(128)}, bf16[480,4,1024]{2,1,0:T(4,128)(2,1)}, s32[4,3]{1,0:T(4,128)S(1)}, bf16[4,160,4,1024]{3,2,1,0:T(4,128)(2,1)}, s32[]{:T(128)}) %tuple.71), condition=%wide.while_cond, body=%wide.while_body.sunk | while | flops 2 | bytes 2621545 | solution.py:59
  468.7 9.6 %convert_element_type.135 = f32[4,160,4,1024]{3,2,1,0:T(4,128)} convert(bf16[4,160,4,1024]{3,2,1,0:T(4,128)(2,1)} %get-tuple-element.298) | non-fusion elementwise | flops 2621440 | bytes 15728640 | tf_op jit(solution)/shard_map/while/body/eval_jaxpr/convert_element_type | solution.py:65
  484.6 7.6 %maximum_reduce_fusion.2 = bf16[4,160,1024]{2,1,0:T(8,128)(2,1)S(1)} fusion(f32[4,160,4,512]{3,2,1,0:T(4,128)S(1)} %get-tuple-element.303, f32[4,160,4,512]{3,2,1,0:T(4,128)S(1)} %get-tuple-element.304), kind=kLoop, calls=%fused_computation.6.clone.1 | loop fusion | flops 4587520 | bytes 11796480 | tf_op jit(solution)/shard_map/while/body/eval_jaxpr/reduce_sum | solution.py:76
  502.7 11.6 %while.22 = (s32[]{:T(128)}, bf16[480,4,1024]{2,1,0:T(4,128)(2,1)}, s32[4,3]{1,0:T(4,128)S(1)}, bf16[4,160,4,1024]{3,2,1,0:T(4,128)(2,1)}, s32[]{:T(128)}) while((s32[]{:T(128)}, bf16[480,4,1024]{2,1,0:T(4,128)(2,1)}, s32[4,3]{1,0:T(4,128)S(1)}, bf16[4,160,4,1024]{3,2,1,0:T(4,128)(2,1)}, s32[]{:T(128)}) %tuple.71), condition=%wide.while_cond, body=%wide.while_body.sunk | while | flops 2 | bytes 2621545 | solution.py:59
  514.2 9.6 %convert_element_type.135 = f32[4,160,4,1024]{3,2,1,0:T(4,128)} convert(bf16[4,160,4,1024]{3,2,1,0:T(4,128)(2,1)} %get-tuple-element.298) | non-fusion elementwise | flops 2621440 | bytes 15728640 | tf_op jit(solution)/shard_map/while/body/eval_jaxpr/convert_element_type | solution.py:65
  530.2 7.6 %maximum_reduce_fusion.2 = bf16[4,160,1024]{2,1,0:T(8,128)(2,1)S(1)} fusion(f32[4,160,4,512]{3,2,1,0:T(4,128)S(1)} %get-tuple-element.303, f32[4,160,4,512]{3,2,1,0:T(4,128)S(1)} %get-tuple-element.304), kind=kLoop, calls=%fused_computation.6.clone.1 | loop fusion | flops 4587520 | bytes 11796480 | tf_op jit(solution)/shard_map/while/body/eval_jaxpr/reduce_sum | solution.py:76
  545.0 14.5 %reduce-scatter.9.cloned.1.call-done = bf16[8,160]{1,0:T(8,128)(2,1)} async-done(((bf16[32,160]{1,0:T(8,128)(2,1)}), bf16[8,160]{1,0:T(8,128)(2,1)}) %reduce-scatter.9.cloned.1.call-update) | async-done | bytes 2576
  560.4 28.5 %reduce-scatter.7.cloned.1.call-done = bf16[8,20480]{1,0:T(8,128)(2,1)} async-done(((bf16[32,20480]{1,0:T(8,128)(2,1)}), bf16[8,20480]{1,0:T(8,128)(2,1)}) %reduce-scatter.7.cloned.1.call-update) | async-done | bytes 327696
  (378 shorter events, 277.9 us)
Async XLA Ops:
  6.5 553.0 %reduce-scatter.9.cloned.1.call-start = ((), (), s32[]{:S(2)}) async-start(), calls=%async_computation.3 | async-start | bytes 20480
  103.4 6.1 %copy-start.3 = (s32[1,4]{1,0:T(1,128)S(1)}, s32[1,4]{1,0:T(1,128)}, u32[]{:S(2)}) copy-start(s32[1,4]{1,0:T(1,128)} %param.6) | copy-start | bytes 52
  103.4 9.2 %copy-start.2 = (s32[1,2]{1,0:T(1,128)S(1)}, s32[1,2]{1,0:T(1,128)}, u32[]{:S(2)}) copy-start(s32[1,2]{1,0:T(1,128)} %param.7) | copy-start | bytes 28
  107.0 61.9 %collective-permute-start.1 = (bf16[160,4,1024]{2,1,0:T(4,128)(2,1)S(1)}, bf16[160,4,1024]{2,1,0:T(4,128)(2,1)S(1)}, u32[]{:S(2)}, u32[]{:S(2)}) collective-permute-start(bf16[160,4,1024]{2,1,0:T(4,128)(2,1)S(1)} %constant_dynamic-update-slice_fusion), channel_id=1, source_target_pairs={{8,0},{12,4},{16,8},{20,12},{24,16},{28,20},{9,1},{13,5},{17,9},{2... | collective-permute-start | bytes 3932168 | tf_op jit(solution)/shard_map/ppermute | solution.py:17
  108.3 60.6 %collective-permute-start = (bf16[160,4,1024]{2,1,0:T(4,128)(2,1)S(1)}, bf16[160,4,1024]{2,1,0:T(4,128)(2,1)}, u32[]{:S(2)}, u32[]{:S(2)}) collective-permute-start(bf16[160,4,1024]{2,1,0:T(4,128)(2,1)S(1)} %constant_dynamic-update-slice_fusion), channel_id=1, source_target_pairs={{4,0},{8,4},{12,8},{16,12},{20,16},{24,20},{28,24},{5,1},{9,5},{13... | collective-permute-start | bytes 3932168 | tf_op jit(solution)/shard_map/ppermute | solution.py:17
  109.8 59.0 %collective-permute-start.3 = (bf16[1,4]{0,1:T(4,128)(2,1)S(1)}, bf16[1,4]{0,1:T(4,128)(2,1)S(1)}, u32[]{:S(2)}, u32[]{:S(2)}) collective-permute-start(bf16[1,4]{0,1:T(4,128)(2,1)S(1)} %get-tuple-element.156), channel_id=1, source_target_pairs={{8,0},{12,4},{16,8},{20,12},{24,16},{28,20},{9,1},{13,5},{17,9},{2... | collective-permute-start | bytes 32 | tf_op jit(solution)/shard_map/ppermute | solution.py:17
  111.1 57.7 %collective-permute-start.2 = (bf16[1,4]{0,1:T(4,128)(2,1)S(1)}, bf16[1,4]{0,1:T(4,128)(2,1)S(1)}, u32[]{:S(2)}, u32[]{:S(2)}) collective-permute-start(bf16[1,4]{0,1:T(4,128)(2,1)S(1)} %get-tuple-element.156), channel_id=1, source_target_pairs={{4,0},{8,4},{12,8},{16,12},{20,16},{24,20},{28,24},{5,1},{9,5},{13... | collective-permute-start | bytes 32 | tf_op jit(solution)/shard_map/ppermute | solution.py:17
  174.2 8.0 %copy-start = (bf16[160,4,1024]{2,1,0:T(4,128)(2,1)}, bf16[160,4,1024]{2,1,0:T(4,128)(2,1)S(1)}, u32[]{:S(2)}) copy-start(bf16[160,4,1024]{2,1,0:T(4,128)(2,1)S(1)} %get-tuple-element.378) | copy-start | bytes 3932164 | tf_op jit(solution)/shard_map/while
  211.0 8.8 %copy-start.1 = (bf16[160,4,1024]{2,1,0:T(4,128)(2,1)S(1)}, bf16[160,4,1024]{2,1,0:T(4,128)(2,1)}, u32[]{:S(2)}) copy-start(bf16[160,4,1024]{2,1,0:T(4,128)(2,1)} %copy-done) | copy-start | bytes 3932164 | tf_op jit(solution)/shard_map/while
  219.8 8.0 %copy-start = (bf16[160,4,1024]{2,1,0:T(4,128)(2,1)}, bf16[160,4,1024]{2,1,0:T(4,128)(2,1)S(1)}, u32[]{:S(2)}) copy-start(bf16[160,4,1024]{2,1,0:T(4,128)(2,1)S(1)} %get-tuple-element.378) | copy-start | bytes 3932164 | tf_op jit(solution)/shard_map/while
  256.6 8.8 %copy-start.1 = (bf16[160,4,1024]{2,1,0:T(4,128)(2,1)S(1)}, bf16[160,4,1024]{2,1,0:T(4,128)(2,1)}, u32[]{:S(2)}) copy-start(bf16[160,4,1024]{2,1,0:T(4,128)(2,1)} %copy-done) | copy-start | bytes 3932164 | tf_op jit(solution)/shard_map/while
  265.4 8.0 %copy-start = (bf16[160,4,1024]{2,1,0:T(4,128)(2,1)}, bf16[160,4,1024]{2,1,0:T(4,128)(2,1)S(1)}, u32[]{:S(2)}) copy-start(bf16[160,4,1024]{2,1,0:T(4,128)(2,1)S(1)} %get-tuple-element.378) | copy-start | bytes 3932164 | tf_op jit(solution)/shard_map/while
  302.2 8.8 %copy-start.1 = (bf16[160,4,1024]{2,1,0:T(4,128)(2,1)S(1)}, bf16[160,4,1024]{2,1,0:T(4,128)(2,1)}, u32[]{:S(2)}) copy-start(bf16[160,4,1024]{2,1,0:T(4,128)(2,1)} %copy-done) | copy-start | bytes 3932164 | tf_op jit(solution)/shard_map/while
  311.0 8.0 %copy-start = (bf16[160,4,1024]{2,1,0:T(4,128)(2,1)}, bf16[160,4,1024]{2,1,0:T(4,128)(2,1)S(1)}, u32[]{:S(2)}) copy-start(bf16[160,4,1024]{2,1,0:T(4,128)(2,1)S(1)} %get-tuple-element.378) | copy-start | bytes 3932164 | tf_op jit(solution)/shard_map/while
  347.8 8.8 %copy-start.1 = (bf16[160,4,1024]{2,1,0:T(4,128)(2,1)S(1)}, bf16[160,4,1024]{2,1,0:T(4,128)(2,1)}, u32[]{:S(2)}) copy-start(bf16[160,4,1024]{2,1,0:T(4,128)(2,1)} %copy-done) | copy-start | bytes 3932164 | tf_op jit(solution)/shard_map/while
  356.6 8.0 %copy-start = (bf16[160,4,1024]{2,1,0:T(4,128)(2,1)}, bf16[160,4,1024]{2,1,0:T(4,128)(2,1)S(1)}, u32[]{:S(2)}) copy-start(bf16[160,4,1024]{2,1,0:T(4,128)(2,1)S(1)} %get-tuple-element.378) | copy-start | bytes 3932164 | tf_op jit(solution)/shard_map/while
  393.4 8.8 %copy-start.1 = (bf16[160,4,1024]{2,1,0:T(4,128)(2,1)S(1)}, bf16[160,4,1024]{2,1,0:T(4,128)(2,1)}, u32[]{:S(2)}) copy-start(bf16[160,4,1024]{2,1,0:T(4,128)(2,1)} %copy-done) | copy-start | bytes 3932164 | tf_op jit(solution)/shard_map/while
  402.2 8.0 %copy-start = (bf16[160,4,1024]{2,1,0:T(4,128)(2,1)}, bf16[160,4,1024]{2,1,0:T(4,128)(2,1)S(1)}, u32[]{:S(2)}) copy-start(bf16[160,4,1024]{2,1,0:T(4,128)(2,1)S(1)} %get-tuple-element.378) | copy-start | bytes 3932164 | tf_op jit(solution)/shard_map/while
  439.0 8.8 %copy-start.1 = (bf16[160,4,1024]{2,1,0:T(4,128)(2,1)S(1)}, bf16[160,4,1024]{2,1,0:T(4,128)(2,1)}, u32[]{:S(2)}) copy-start(bf16[160,4,1024]{2,1,0:T(4,128)(2,1)} %copy-done) | copy-start | bytes 3932164 | tf_op jit(solution)/shard_map/while
  447.8 8.0 %copy-start = (bf16[160,4,1024]{2,1,0:T(4,128)(2,1)}, bf16[160,4,1024]{2,1,0:T(4,128)(2,1)S(1)}, u32[]{:S(2)}) copy-start(bf16[160,4,1024]{2,1,0:T(4,128)(2,1)S(1)} %get-tuple-element.378) | copy-start | bytes 3932164 | tf_op jit(solution)/shard_map/while
  484.6 8.8 %copy-start.1 = (bf16[160,4,1024]{2,1,0:T(4,128)(2,1)S(1)}, bf16[160,4,1024]{2,1,0:T(4,128)(2,1)}, u32[]{:S(2)}) copy-start(bf16[160,4,1024]{2,1,0:T(4,128)(2,1)} %copy-done) | copy-start | bytes 3932164 | tf_op jit(solution)/shard_map/while
  493.4 8.0 %copy-start = (bf16[160,4,1024]{2,1,0:T(4,128)(2,1)}, bf16[160,4,1024]{2,1,0:T(4,128)(2,1)S(1)}, u32[]{:S(2)}) copy-start(bf16[160,4,1024]{2,1,0:T(4,128)(2,1)S(1)} %get-tuple-element.378) | copy-start | bytes 3932164 | tf_op jit(solution)/shard_map/while
  530.2 8.8 %copy-start.1 = (bf16[160,4,1024]{2,1,0:T(4,128)(2,1)S(1)}, bf16[160,4,1024]{2,1,0:T(4,128)(2,1)}, u32[]{:S(2)}) copy-start(bf16[160,4,1024]{2,1,0:T(4,128)(2,1)} %copy-done) | copy-start | bytes 3932164 | tf_op jit(solution)/shard_map/while
  539.6 49.2 %reduce-scatter.7.cloned.1.call-start = ((), (), s32[]{:S(2)}) async-start(), calls=%async_computation.2 | async-start | bytes 1638400
Sparse Core Ops, SparseCore 0:
  539.7 19.7 reduce-scatter.8
  562.2 26.5 reduce-scatter.6
where the time goes:
time: 600 us; the launch traced here: 598 us
  other arithmetic  272 us (45%)
  local copies, waits for them, and re-layouts  172 us (29%)
  waiting for transfers between devices  97.4 us (16%)
  matrix products  25.9 us (4%)
  between operations  13.6 us (2%)
  loops' own time  11.4 us (2%)
    gather x160, local copies, waits for them, and re-layouts  136 us
    convert_element_type x8, other arithmetic, one_block(): theirs = partner.astype(jnp.float32)  77.1 us
    another operation x2, other arithmetic  68.2 us
    reduce_sum x8, other arithmetic, one_block(): cross_sum = cross_sum.reshape(4, block_size, seg_total // group_size, gro...  60.7 us
    ppermute x4, waiting for transfers between devices, passed_along(): return lax.ppermute(block, axis, route)  54.4 us
    mul x8, other arithmetic, one_block(): (mine[..., :bins] * theirs[..., :bins] + mine[..., bins:] * theirs[..., b...  50.2 us
    unnamed x4, waiting for transfers between devices  43 us
    dot_general x1, matrix products, shards(): jnp.dot(records.reshape(block_size * seg_local, samples), dft_table, pref...  16.5 us
  transfers between devices with their start and end apart: 6, of which 3 were waited for; matrix products, arithmetic and copies ran while one was open for 1% of the time, Pallas kernels for 0%

commit v1 on v0

v1 whole, which is shorter than its diff:
```python
import functools
import math

import jax
import jax.numpy as jnp
import numpy as np
from jax import lax
from jax.experimental import pallas as pl
from jax.experimental.pallas import tpu as pltpu
from jax.sharding import PartitionSpec as P

BINS = 512
LAGS = 128
PAIRS = 32
REACH = 2
STEPS = 5


def bin_order(bins):
    return np.concatenate([np.arange(0, bins, 2), np.arange(1, bins, 2)])


def dft_table_of(samples, bins):
    times = np.arange(samples // 2, dtype=np.int64)[:, None]
    freqs = 32 + bin_order(bins)[None, :]
    phase = (times * freqs % samples) * (2.0 * math.pi / samples)
    half = bins // 2
    real, imag = np.cos(phase), -np.sin(phase)
    parts = [real[:, :half], imag[:, :half], real[:, half:], imag[:, half:]]
    return np.concatenate(parts, axis=1).astype(jnp.bfloat16)


def lag_table_of(samples, bins, lags):
    freqs = 32 + bin_order(bins)[:, None]
    shifts = (np.arange(lags) - lags // 2 + samples) % samples
    phase = (freqs * shifts[None, :] % samples) * (2.0 * math.pi / samples)
    factor = 1.0 / math.sqrt(bins)
    return (np.concatenate([np.cos(phase), -np.sin(phase)], axis=0) * factor).astype(jnp.bfloat16)


def spectra_kernel(valid_ref, first_ref, second_ref, table_ref, white_ref, acc):
    step = pl.program_id(0)
    channels, segs, width = first_ref.shape
    lane_tiles = acc.shape[0]
    bins = table_ref.shape[1] // 2
    first = first_ref[...].astype(jnp.float32)
    second = second_ref[...].astype(jnp.float32)
    even = (first + second).reshape(channels * segs, width).astype(jnp.bfloat16)
    odd = (first - second).reshape(channels * segs, width).astype(jnp.bfloat16)
    even_part = jnp.dot(even, table_ref[:, :bins], preferred_element_type=jnp.float32)
    odd_part = jnp.dot(odd, table_ref[:, bins:], preferred_element_type=jnp.float32)
    half_tiles = lane_tiles // 2

    def part_of(tile):
        part = even_part if tile < half_tiles else odd_part
        at = tile % half_tiles * 128
        return part[:, at : at + 128]

    @pl.when(step == 0)
    def _():
        for tile in range(lane_tiles):
            acc[tile] = part_of(tile)

    @pl.when(step > 0)
    def _():
        for tile in range(lane_tiles):
            acc[tile] += part_of(tile)

    @pl.when(step == pl.num_programs(0) - 1)
    def _():
        quarter = lane_tiles // 4
        reals = [*range(quarter), *range(2 * quarter, 3 * quarter)]
        for seg in range(segs):
            rows = pl.ds(seg, channels, stride=segs)
            power_sum = None
            for tile in reals:
                real, imag = acc[tile, rows, :], acc[tile + quarter, rows, :]
                power = real * real + imag * imag
                power_sum = power if power_sum is None else power_sum + power
            water = jnp.sum(power_sum, axis=1, keepdims=True) * (1.0 / bins)
            usable = valid_ref[0, seg].astype(jnp.float32)
            for place, tile in enumerate(reals):
                real, imag = acc[tile, rows, :], acc[tile + quarter, rows, :]
                power = real * real + imag * imag
                scale = lax.rsqrt(power + 0.1 * water + 1e-06) * usable
                at = place * 128
                white_ref[seg, :, at : at + 128] = (real * scale).astype(jnp.bfloat16)
                white_ref[seg, :, bins + at : bins + at + 128] = (imag * scale).astype(
                    jnp.bfloat16
                )


def whitened(records, valid_mask, table):
    channels, segs, samples = records.shape
    width = samples // 2 // STEPS
    return pl.pallas_call(
        spectra_kernel,
        name="spectra",
        grid_spec=pltpu.PrefetchScalarGridSpec(
            num_scalar_prefetch=1,
            grid=(STEPS,),
            in_specs=[
                pl.BlockSpec((channels, segs, width), lambda k, valid: (0, 0, k)),
                pl.BlockSpec((channels, segs, width), lambda k, valid: (0, 0, k + STEPS)),
                pl.BlockSpec((width, 2 * BINS), lambda k, valid: (k, 0)),
            ],
            out_specs=pl.BlockSpec((segs, channels, 2 * BINS), lambda k, valid: (0, 0, 0)),
            scratch_shapes=[
                pltpu.VMEM((2 * BINS // 128, channels * segs, 128), jnp.float32),
            ],
        ),
        out_shape=jax.ShapeDtypeStruct((segs, channels, 2 * BINS), jnp.bfloat16),
        compiler_params=pltpu.CompilerParams(vmem_limit_bytes=56 << 20),
        cost_estimate=pl.CostEstimate(
            flops=2 * channels * segs * samples * BINS,
            bytes_accessed=2 * channels * segs * samples + 2 * samples * BINS,
            transcendentals=channels * segs * BINS,
        ),
    )(valid_mask, records, records, table)


CH_TILE = 16


def cross_kernel(lowest_ref, own_ref, next_ref, far_ref, lag_ref, out_ref, wide, mixed):
    segs, channels, columns = own_ref.shape
    bins = columns // 2
    lane_tiles = bins // 128
    lowest = lowest_ref[0]
    tile = pl.program_id(0)

    @pl.when(tile == 0)
    def _():
        for hop, ref in enumerate((own_ref, next_ref, far_ref)):
            for seg in range(segs):
                for lane in range(2 * lane_tiles):
                    block = ref[seg, :, lane * 128 : lane * 128 + 128]
                    wide[seg * 2 * lane_tiles + lane, pl.ds(hop * channels, channels), :] = (
                        block.astype(jnp.float32)
                    )

    def one_channel(index, carry):
        channel = tile * CH_TILE + index
        for lane in range(lane_tiles):
            mine = []
            for seg in range(segs):
                for part in range(2):
                    slab = seg * 2 * lane_tiles + part * lane_tiles + lane
                    row = wide[slab, pl.ds(channel, 1), :]
                    mine.append(jnp.broadcast_to(row, (8, 128)))
            for pair in range(0, PAIRS, 16):
                reals, imags = [], []
                for half in range(2):
                    start = channel + lowest + pair + 8 * half
                    real = imag = None
                    for seg in range(segs):
                        slab = seg * 2 * lane_tiles + lane
                        their_real = wide[slab, pl.ds(start, 8), :]
                        their_imag = wide[slab + lane_tiles, pl.ds(start, 8), :]
                        my_real, my_imag = mine[2 * seg], mine[2 * seg + 1]
                        re = my_real * their_real + my_imag * their_imag
                        im = my_imag * their_real - my_real * their_imag
                        real = re if real is None else real + re
                        imag = im if imag is None else imag + im
                    reals.append(real)
                    imags.append(imag)
                rows = pl.ds(pl.multiple_of(index * PAIRS + pair, 16), 16)
                mixed[rows, lane * 128 : lane * 128 + 128] = jnp.concatenate(reals, axis=0).astype(
                    jnp.bfloat16
                )
                mixed[rows, bins + lane * 128 : bins + lane * 128 + 128] = jnp.concatenate(
                    imags, axis=0
                ).astype(jnp.bfloat16)
        return carry

    lax.fori_loop(0, CH_TILE, one_channel, 0)
    lagged = jnp.dot(mixed[...], lag_ref[...], preferred_element_type=jnp.float32)
    out_ref[...] = lagged.reshape(CH_TILE, PAIRS, LAGS).astype(out_ref.dtype)


def correlated(lowest, own, following, far, lag_table):
    segs, channels, columns = own.shape
    whole = pl.BlockSpec((segs, channels, columns), lambda i, low: (0, 0, 0))
    return pl.pallas_call(
        cross_kernel,
        name="cross",
        grid_spec=pltpu.PrefetchScalarGridSpec(
            num_scalar_prefetch=1,
            grid=(channels // CH_TILE,),
            in_specs=[
                whole,
                whole,
                whole,
                pl.BlockSpec(lag_table.shape, lambda i, low: (0, 0)),
            ],
            out_specs=pl.BlockSpec((CH_TILE, PAIRS, LAGS), lambda i, low: (i, 0, 0)),
            scratch_shapes=[
                pltpu.VMEM((segs * columns // 128, (REACH + 1) * channels, 128), jnp.float32),
                pltpu.VMEM((CH_TILE * PAIRS, columns), jnp.bfloat16),
            ],
        ),
        out_shape=jax.ShapeDtypeStruct((channels, PAIRS, LAGS), jnp.bfloat16),
        compiler_params=pltpu.CompilerParams(vmem_limit_bytes=56 << 20),
        cost_estimate=pl.CostEstimate(
            flops=2 * channels * PAIRS * columns * LAGS,
            bytes_accessed=6 * segs * channels * columns,
            transcendentals=0,
        ),
    )(lowest, own, following, far, lag_table)


def shards(records, valid_mask, band_limits):
    channels, segs, samples = records.shape
    blocks = lax.axis_size("chan")
    block = lax.axis_index("chan")
    white = whitened(records, valid_mask, jnp.asarray(dft_table_of(samples, BINS)))
    far = lax.ppermute(white, "chan", [(i + 2, i) for i in range(blocks - 2)])
    from_odd = lax.ppermute(white, "chan", [(i + 1, i) for i in range(0, blocks - 1, 2)])
    from_even = lax.ppermute(far, "chan", [(i - 1, i) for i in range(1, blocks, 2)])
    following = jnp.where(block % 2 == 0, from_odd, from_even)
    lowest = band_limits[0, 0]
    highest = band_limits[0, 1]
    partial = correlated(
        lowest[None], white, following, far, jnp.asarray(lag_table_of(samples, BINS, LAGS))
    )
    summed = lax.psum_scatter(partial, "tm", scatter_dimension=1, tiled=True).astype(jnp.float32)
    marks = lax.all_gather(valid_mask, ("chan", "tm"), axis=0, tiled=True)
    marks = marks.reshape(blocks, -1)
    marks = jnp.concatenate([marks, jnp.zeros((REACH, marks.shape[1]), jnp.int32)], axis=0)
    near = lax.dynamic_slice_in_dim(marks, block, REACH + 1, 0)
    counts = jnp.sum(near[:1] * near, axis=1)
    share = summed.shape[1]
    pair = lax.axis_index("tm") * share + jnp.arange(share, dtype=jnp.int32)
    partner = jnp.arange(channels, dtype=jnp.int32)[:, None] + lowest + pair[None, :]
    hop = partner // channels
    count = jnp.where(hop == 0, counts[0], jnp.where(hop == 1, counts[1], counts[2]))
    scale = 1.0 / jnp.maximum(count, 1).astype(jnp.float32)
    scale = jnp.where((lowest + pair < highest)[None, :], scale, 0.0)
    return summed * scale[..., None]


def solution(mesh):
    placed = (P("chan", "tm", None), P("chan", "tm"), P("chan", None))
    return jax.shard_map(
        shards, mesh=mesh, in_specs=placed, out_specs=P("chan", "tm", None), check_vma=False
    )
```

time: 600 us -> 167 us (0.28)
  other arithmetic: 272 us -> 7.09 us
  local copies, waits for them, and re-layouts: 172 us -> 7.01 us
  blocking collectives: 0 us -> 40.4 us
  waiting for transfers between devices: 97.4 us -> 58.2 us
  Pallas kernels: 0 us -> 34 us
  matrix products: 25.9 us -> 0 us
  loops' own time: 11.4 us -> 0 us
    gather x160 -> x0, local copies, waits for them, and re-layouts: 136 us -> none
    convert_element_type x26 -> x0, other arithmetic: 83.4 us -> none  [the longest x8 77.1 us: one_block(): theirs = partner.astype(jnp.float32)]
    another operation x2 -> x0, other arithmetic: 68.2 us -> none
    reduce_sum x17 -> x1, other arithmetic: 61.7 us -> 0.12 us  [shards(): counts = jnp.sum(near[:1] * near, axis=1)]
    mul x9 -> x1, other arithmetic: 50.2 us -> 1.07 us  [shards(): return summed * scale[..., None]]
    unnamed x4 -> x2, waiting for transfers between devices: 43 us -> 0.04 us
    all_gather x0 -> x1, blocking collectives: none -> 40.4 us  [shards(): marks = lax.all_gather(valid_mask, ('chan', 'tm'), axis=0, tiled=True)]
    pallas_call x0 -> x2, Pallas kernels: none -> 34 us  [the longest x1 20.9 us: correlated(): pl.pallas_call(cross_kernel, name='cross', grid_spec=pltpu.PrefetchScalar...]
  transfers between devices with their start and end apart: 6 -> 4, of which waited for: 3 -> 2; matrix products, arithmetic and copies ran while one was open for 1% -> 4% of each run, Pallas kernels for 0% -> 0%
where the time goes in v1:
time: 167 us; the launch traced here: 166 us
  waiting for transfers between devices  58.2 us (35%)
  blocking collectives  40.4 us (24%)
  Pallas kernels  34 us (20%)
  between operations  13.5 us (8%)
  other arithmetic  7.09 us (4%)
  local copies, waits for them, and re-layouts  7.01 us (4%)
  starting transfers between devices  6.21 us (4%)
    all_gather x1, blocking collectives, shards(): marks = lax.all_gather(valid_mask, ('chan', 'tm'), axis=0, tiled=True)  40.4 us
    ppermute x1, waiting for transfers between devices, shards(): far = lax.ppermute(white, 'chan', [(i + 2, i) for i in range(blocks - 2)])  31.4 us
    ppermute x1, waiting for transfers between devices, shards(): lax.ppermute(far, 'chan', [(i - 1, i) for i in range(1, blocks, 2)])  26.8 us
    pallas_call x1, Pallas kernels, correlated(): pl.pallas_call(cross_kernel, name='cross', grid_spec=pltpu.PrefetchScalar...  20.9 us
    pallas_call x1, Pallas kernels, whitened(): pl.pallas_call(spectra_kernel, name='spectra', grid_spec=pltpu.PrefetchSc...  13.1 us
    unnamed x7, local copies, waits for them, and re-layouts  5.05 us
    ppermute x1, starting transfers between devices, shards(): lax.ppermute(far, 'chan', [(i - 1, i) for i in range(1, blocks, 2)])  3.63 us
  transfers between devices with their start and end apart: 4, of which 2 were waited for; matrix products, arithmetic and copies ran while one was open for 4% of the time, Pallas kernels for 0%

profile of v1, /device:TPU:0, one launch (start us, length us, event | category | flops | bytes accessed | tf_op | source)
XLA Modules:
  0.0 166.4 jit_solution(1349954829926576563)
XLA Ops:
  6.5 0.0 copy-start
  6.5 0.0 reduce-scatter.4.cloned.1.call-start
  6.5 13.1 %spectra.1.own_ref = bf16[4,160,1024]{2,1,0:T(8,128)(2,1)} custom-call(s32[1,4]{1,0:T(1,128)} %valid_ref.1, bf16[160,4,7680]{2,1,0:T(4,128)(2,1)} %second_ref.1, bf16[160,4,7680]{2,1,0:T(4,128)(2,1)} %second_ref.1, bf16[3840,1024]{1,0:T(8,128)(2,1)} %constant.47.clone.table_ref), custom_call_target="tpu_custom_call" | custom-call | flops 5033164800 | bytes 17694720 | tf_op jit(solution)/shard_map/spectra/pallas_call | solution.py:96
  19.6 1.3 collective-permute-start.1
  20.9 1.3 collective-permute-start
  22.2 31.4 %collective-permute-done.1.far_ref = bf16[4,160,1024]{2,1,0:T(8,128)(2,1)} collective-permute-done((bf16[4,160,1024]{2,1,0:T(8,128)(2,1)}, bf16[4,160,1024]{2,1,0:T(8,128)(2,1)}, u32[]{:S(2)}, u32[]{:S(2)}) %collective-permute-start.1) | collective-permute-done | bytes 1310752 | tf_op jit(solution)/shard_map/ppermute | solution.py:217
  53.6 3.6 %collective-permute-start.2 = (bf16[4,160,1024]{2,1,0:T(8,128)(2,1)}, bf16[4,160,1024]{2,1,0:T(8,128)(2,1)S(1)}, u32[]{:S(2)}, u32[]{:S(2)}) collective-permute-start(bf16[4,160,1024]{2,1,0:T(8,128)(2,1)} %collective-permute-done.1.far_ref), channel_id=1, source_target_pairs={{0,4},{8,12},{16,20},{24,28},{1,5},{9,13},{17,21},{25,29},{2,6},{1... | collective-permute-start | bytes 3932168 | tf_op jit(solution)/shard_map/ppermute | solution.py:219
  57.3 0.0 copy-done
  57.3 0.6 fusion.3
  57.9 0.0 collective-permute-done
  57.9 26.8 %collective-permute-done.2 = bf16[4,160,1024]{2,1,0:T(8,128)(2,1)S(1)} collective-permute-done((bf16[4,160,1024]{2,1,0:T(8,128)(2,1)}, bf16[4,160,1024]{2,1,0:T(8,128)(2,1)S(1)}, u32[]{:S(2)}, u32[]{:S(2)}) %collective-permute-start.2) | collective-permute-done | bytes 1310752 | tf_op jit(solution)/shard_map/ppermute | solution.py:219
  84.7 1.2 broadcast_select_fusion.next_ref
  85.9 20.9 %cross.1 = bf16[160,32,128]{2,1,0:T(8,128)(2,1)} custom-call(s32[1]{0:T(128)} %bitcast.2.lowest_ref, bf16[4,160,1024]{2,1,0:T(8,128)(2,1)} %spectra.1.own_ref, bf16[4,160,1024]{2,1,0:T(8,128)(2,1)} %broadcast_select_fusion.next_ref, bf16[4,160,1024]{2,1,0:T(8,128)(2,1)} %collective-permute-done.1.far_ref, bf16[1024,128]{1,0:T(8,128)(2,1)} %constant.48.clone.lag_ref), custom_call_target="tpu_custom_call" | custom-call | flops 1342177280 | bytes 3932160 | tf_op jit(solution)/shard_map/cross/pallas_call | solution.py:184
  106.8 1.8 %copy.7 = bf16[160,32,128]{2,0,1:T(8,128)(2,1)S(1)} copy(bf16[160,32,128]{2,1,0:T(8,128)(2,1)} %cross.1) | data formatting | bytes 2621440
  108.6 1.6 copy.14
  110.2 0.0 copy-start.1
  110.2 0.0 reduce-scatter.4.cloned.1.call-update
  110.2 0.6 copy-done.1
  110.8 40.4 %all-gather = s32[32,1,4]{2,1,0:T(1,128)S(1)} all-gather(s32[1,1,4]{2,1,0:T(1,128)S(1)} %bitcast.25), channel_id=1, replica_groups=mesh['chan'=8,'tm'=4] {'chan','tm'}, dimensions={0}, use_global_device_ids=true | all-gather | bytes 528 | tf_op jit(solution)/shard_map/all_gather | solution.py:227
  151.2 0.5 broadcast.109
  151.7 0.7 reduce.3
  152.4 0.1 reshape.71
  152.5 1.3 add_compare_fusion
  153.8 0.7 iota_add_fusion
  154.6 0.1 multiply_reduce_fusion
  154.7 0.7 fusion.4
  155.3 2.0 %divide_select_fusion = f32[160,8]{0,1:T(8,128)S(1)} fusion(s32[]{:T(128)} %bitcast.9, s32[]{:T(128)} %bitcast.8, s32[]{:T(128)} %bitcast.7, s32[8]{0:T(128)S(1)} %iota_add_fusion.1, s32[160]{0:T(256)S(1)} %iota_add_fusion, pred[8]{0:T(512)(128)(4,1)S(1)} %add_compare_fusion), kind=kLoop, calls=%fused_computation.10 | loop fusion | flops 21760 | bytes 5812 | tf_op jit(solution)/shard_map/jit(_where)/select_n | solution.py:238
  157.3 0.1 copy.6
  157.4 0.0 reduce-scatter.4.cloned.1.call-done
  157.5 1.0 copy.15
  158.5 1.1 convert_multiply_fusion
  (3 shorter events, 0.0 us)
Async XLA Ops:
  6.5 50.7 %copy-start = (s32[1,2]{1,0:T(1,128)S(1)}, s32[1,2]{1,0:T(1,128)}, u32[]{:S(2)}) copy-start(s32[1,2]{1,0:T(1,128)} %param.7) | copy-start | bytes 28
  6.5 150.9 %reduce-scatter.4.cloned.1.call-start = ((), (), s32[]{:S(2)}) async-start(), calls=%async_computation.1 | async-start | bytes 1638400
  19.6 34.0 %collective-permute-start.1 = (bf16[4,160,1024]{2,1,0:T(8,128)(2,1)}, bf16[4,160,1024]{2,1,0:T(8,128)(2,1)}, u32[]{:S(2)}, u32[]{:S(2)}) collective-permute-start(bf16[4,160,1024]{2,1,0:T(8,128)(2,1)} %spectra.1.own_ref), channel_id=1, source_target_pairs={{8,0},{12,4},{16,8},{20,12},{24,16},{28,20},{9,1},{13,5},{17,9},{2... | collective-permute-start | bytes 3932168 | tf_op jit(solution)/shard_map/ppermute | solution.py:217
  20.9 37.0 %collective-permute-start = (bf16[4,160,1024]{2,1,0:T(8,128)(2,1)}, bf16[4,160,1024]{2,1,0:T(8,128)(2,1)S(1)}, u32[]{:S(2)}, u32[]{:S(2)}) collective-permute-start(bf16[4,160,1024]{2,1,0:T(8,128)(2,1)} %spectra.1.own_ref), channel_id=1, source_target_pairs={{4,0},{12,8},{20,16},{28,24},{5,1},{13,9},{21,17},{29,25},{6,2},{1... | collective-permute-start | bytes 3932168 | tf_op jit(solution)/shard_map/ppermute | solution.py:218
  53.6 31.0 %collective-permute-start.2 = (bf16[4,160,1024]{2,1,0:T(8,128)(2,1)}, bf16[4,160,1024]{2,1,0:T(8,128)(2,1)S(1)}, u32[]{:S(2)}, u32[]{:S(2)}) collective-permute-start(bf16[4,160,1024]{2,1,0:T(8,128)(2,1)} %collective-permute-done.1.far_ref), channel_id=1, source_target_pairs={{0,4},{8,12},{16,20},{24,28},{1,5},{9,13},{17,21},{25,29},{2,6},{1... | collective-permute-start | bytes 3932168 | tf_op jit(solution)/shard_map/ppermute | solution.py:219
  110.2 0.7 copy-start.1
Sparse Core Ops, SparseCore 0:
  110.3 28.7 reduce-scatter.3

commit v2 on v1

v2 whole, which is shorter than its diff:
```python
import functools
import math

import jax
import jax.numpy as jnp
import numpy as np
from jax import lax
from jax.experimental import pallas as pl
from jax.experimental.pallas import tpu as pltpu
from jax.sharding import PartitionSpec as P

BINS = 512
LAGS = 128
PAIRS = 32
REACH = 2
STEPS = 3
CHUNKS = 2


def bin_order(bins):
    return np.concatenate([np.arange(0, bins, 2), np.arange(1, bins, 2)])


def dft_table_of(samples, bins):
    times = np.arange(samples // 2, dtype=np.int64)[:, None]
    freqs = 32 + bin_order(bins)[None, :]
    phase = (times * freqs % samples) * (2.0 * math.pi / samples)
    half = bins // 2
    real, imag = np.cos(phase), -np.sin(phase)
    parts = [real[:, :half], imag[:, :half], real[:, half:], imag[:, half:]]
    return np.concatenate(parts, axis=1).astype(jnp.bfloat16)


def lag_table_of(samples, bins, lags):
    freqs = 32 + bin_order(bins)[:, None]
    shifts = (np.arange(lags) - lags // 2 + samples) % samples
    phase = (freqs * shifts[None, :] % samples) * (2.0 * math.pi / samples)
    factor = 1.0 / math.sqrt(bins)
    return (np.concatenate([np.cos(phase), -np.sin(phase)], axis=0) * factor).astype(jnp.bfloat16)


def spectra_kernel(valid_ref, first_ref, second_ref, table_ref, *rest):
    *white_refs, acc = rest
    step = pl.program_id(0)
    channels, segs, width = first_ref.shape
    lane_tiles = acc.shape[0]
    bins = table_ref.shape[1] // 2
    first = first_ref[...].astype(jnp.float32)
    second = second_ref[...].astype(jnp.float32)
    even = (first + second).reshape(channels * segs, width).astype(jnp.bfloat16)
    odd = (first - second).reshape(channels * segs, width).astype(jnp.bfloat16)
    even_part = jnp.dot(even, table_ref[:, :bins], preferred_element_type=jnp.float32)
    odd_part = jnp.dot(odd, table_ref[:, bins:], preferred_element_type=jnp.float32)
    half_tiles = lane_tiles // 2

    def part_of(tile):
        part = even_part if tile < half_tiles else odd_part
        at = tile % half_tiles * 128
        return part[:, at : at + 128]

    @pl.when(step == 0)
    def _():
        for tile in range(lane_tiles):
            acc[tile] = part_of(tile)

    @pl.when(step > 0)
    def _():
        for tile in range(lane_tiles):
            acc[tile] += part_of(tile)

    @pl.when(step == pl.num_programs(0) - 1)
    def _():
        quarter = lane_tiles // 4
        reals = [*range(quarter), *range(2 * quarter, 3 * quarter)]
        for seg in range(segs):
            rows = pl.ds(seg, channels, stride=segs)
            power_sum = None
            for tile in reals:
                real, imag = acc[tile, rows, :], acc[tile + quarter, rows, :]
                power = real * real + imag * imag
                power_sum = power if power_sum is None else power_sum + power
            water = jnp.sum(power_sum, axis=1, keepdims=True) * (1.0 / bins)
            usable = valid_ref[0, seg].astype(jnp.float32)
            for place, tile in enumerate(reals):
                real, imag = acc[tile, rows, :], acc[tile + quarter, rows, :]
                power = real * real + imag * imag
                scale = lax.rsqrt(power + 0.1 * water + 1e-06) * usable
                at = place * 128
                group = segs // len(white_refs)
                white_ref = white_refs[seg // group].at[seg % group]
                white_ref[:, at : at + 128] = (real * scale).astype(jnp.bfloat16)
                white_ref[:, bins + at : bins + at + 128] = (imag * scale).astype(jnp.bfloat16)


def whitened(records, valid_mask, table):
    channels, segs, samples = records.shape
    width = samples // 2 // STEPS
    return pl.pallas_call(
        spectra_kernel,
        name="spectra",
        grid_spec=pltpu.PrefetchScalarGridSpec(
            num_scalar_prefetch=1,
            grid=(STEPS,),
            in_specs=[
                pl.BlockSpec((channels, segs, width), lambda k, valid: (0, 0, k)),
                pl.BlockSpec((channels, segs, width), lambda k, valid: (0, 0, k + STEPS)),
                pl.BlockSpec((width, 2 * BINS), lambda k, valid: (k, 0)),
            ],
            out_specs=[
                pl.BlockSpec((segs // CHUNKS, channels, 2 * BINS), lambda k, valid: (0, 0, 0))
            ]
            * CHUNKS,
            scratch_shapes=[
                pltpu.VMEM((2 * BINS // 128, channels * segs, 128), jnp.float32),
            ],
        ),
        out_shape=[jax.ShapeDtypeStruct((segs // CHUNKS, channels, 2 * BINS), jnp.bfloat16)]
        * CHUNKS,
        compiler_params=pltpu.CompilerParams(vmem_limit_bytes=56 << 20),
        cost_estimate=pl.CostEstimate(
            flops=2 * channels * segs * samples * BINS,
            bytes_accessed=2 * channels * segs * samples + 2 * samples * BINS,
            transcendentals=channels * segs * BINS,
        ),
    )(valid_mask, records, records, table)


CH_TILE = 16
TILES = 2


def cross_kernel(place_ref, scale_ref, own_ref, next_ref, far_ref, lag_ref, *rest, first, last):
    if not first:
        before_ref, *rest = rest
    if last:
        keep_ref, other_ref, send_ref, wide, mixed, turned = rest
    else:
        out_ref, wide, mixed = rest
    segs, channels, columns = own_ref.shape
    bins = columns // 2
    lane_tiles = bins // 128
    lowest = place_ref[0]
    step = pl.program_id(0)

    @pl.when(step == 0)
    def _():
        for hop, ref in enumerate((own_ref, next_ref, far_ref)):
            for seg in range(segs):
                for lane in range(2 * lane_tiles):
                    block = ref[seg, :, lane * 128 : lane * 128 + 128]
                    wide[seg * 2 * lane_tiles + lane, pl.ds(hop * channels, channels), :] = (
                        block.astype(jnp.float32)
                    )

    for tile in range(TILES):
        base = pl.multiple_of((step * TILES + tile) * CH_TILE, CH_TILE)
        for lane in range(lane_tiles):
            mine = {}
            for half in range(2):
                for seg in range(segs):
                    for part in range(2):
                        slab = (seg * 2 + part) * lane_tiles + lane
                        mine[half, seg, part] = wide[slab, pl.ds(base + 8 * half, 8), :]
            for pair in range(PAIRS):
                start = base + lowest + place_ref[1 + pair // 8] + pair % 8
                reals, imags = [], []
                for half in range(2):
                    real = imag = None
                    for seg in range(segs):
                        slab = seg * 2 * lane_tiles + lane
                        rows = pl.ds(start + 8 * half, 8)
                        their_real = wide[slab, rows, :]
                        their_imag = wide[slab + lane_tiles, rows, :]
                        my_real, my_imag = mine[half, seg, 0], mine[half, seg, 1]
                        re = my_real * their_real + my_imag * their_imag
                        im = my_imag * their_real - my_real * their_imag
                        real = re if real is None else real + re
                        imag = im if imag is None else imag + im
                    reals.append(real)
                    imags.append(imag)
                rows = slice(pair * CH_TILE, pair * CH_TILE + CH_TILE)
                at = lane * 128
                mixed[tile, rows, at : at + 128] = jnp.concatenate(reals, axis=0).astype(
                    jnp.bfloat16
                )
                mixed[tile, rows, bins + at : bins + at + 128] = jnp.concatenate(
                    imags, axis=0
                ).astype(jnp.bfloat16)
        lagged = jnp.dot(mixed[tile], lag_ref[...], preferred_element_type=jnp.float32)
        if not first:
            lagged += before_ref[tile]
        if not last:
            out_ref[tile] = lagged
            continue
        near = lax.broadcasted_iota(jnp.int32, (CH_TILE, LAGS), 0)
        for pair in range(PAIRS):
            offset = lowest + place_ref[1 + pair // 8] + pair % 8
            partner = near + (base + offset)
            scale = jnp.where(
                partner < channels,
                scale_ref[0],
                jnp.where(partner < 2 * channels, scale_ref[1], scale_ref[2]),
            )
            inside = jnp.where(offset < place_ref[5], 1.0, 0.0)
            rows = slice(pair * CH_TILE, pair * CH_TILE + CH_TILE)
            turned[pair // 8, pl.ds(pair % 8, CH_TILE, stride=8), :] = (
                lagged[rows] * (scale * inside)
            )
        shape = (CH_TILE, 8, LAGS)
        rows = slice(tile * CH_TILE, tile * CH_TILE + CH_TILE)
        keep_ref[rows] = turned[0].reshape(shape)
        other_ref[rows] = turned[1].reshape(shape)
        for side in range(2):
            send_ref[side, rows] = turned[2 + side].reshape(shape).astype(jnp.bfloat16)


def correlated(places, scales, own, following, far, lag_table, before=None, last=False):
    segs, channels, columns = own.shape
    whole = pl.BlockSpec((segs, channels, columns), lambda i, *_: (0, 0, 0))
    rows = TILES * CH_TILE
    raw = pl.BlockSpec((TILES, PAIRS * CH_TILE, LAGS), lambda i, *_: (i, 0, 0))
    raw_shape = jax.ShapeDtypeStruct((channels // CH_TILE, PAIRS * CH_TILE, LAGS), jnp.float32)
    scratch = [
        pltpu.VMEM((segs * columns // 128, (REACH + 1) * channels, 128), jnp.float32),
        pltpu.VMEM((TILES, CH_TILE * PAIRS, columns), jnp.bfloat16),
    ]
    out_specs, out_shape = raw, raw_shape
    if last:
        kept = pl.BlockSpec((rows, 8, LAGS), lambda i, *_: (i, 0, 0))
        sent = pl.BlockSpec((2, rows, 8, LAGS), lambda i, *_: (0, i, 0, 0))
        out_specs = [kept, kept, sent]
        kept_shape = jax.ShapeDtypeStruct((channels, 8, LAGS), jnp.float32)
        sent_shape = jax.ShapeDtypeStruct((2, channels, 8, LAGS), jnp.bfloat16)
        out_shape = [kept_shape, kept_shape, sent_shape]
        scratch.append(pltpu.VMEM((4, CH_TILE * 8, LAGS), jnp.float32))
    return pl.pallas_call(
        functools.partial(cross_kernel, first=before is None, last=last),
        name="cross",
        grid_spec=pltpu.PrefetchScalarGridSpec(
            num_scalar_prefetch=2,
            grid=(channels // rows,),
            in_specs=[
                whole,
                whole,
                whole,
                pl.BlockSpec(lag_table.shape, lambda i, *_: (0, 0)),
                *([] if before is None else [raw]),
            ],
            out_specs=out_specs,
            scratch_shapes=scratch,
        ),
        out_shape=out_shape,
        compiler_params=pltpu.CompilerParams(vmem_limit_bytes=56 << 20),
        cost_estimate=pl.CostEstimate(
            flops=2 * channels * PAIRS * columns * LAGS,
            bytes_accessed=6 * segs * channels * columns,
            transcendentals=0,
        ),
    )(places, scales, own, following, far, lag_table, *([] if before is None else [before]))


def shards(records, valid_mask, band_limits):
    channels, segs, samples = records.shape
    blocks = lax.axis_size("chan")
    block = lax.axis_index("chan")
    rank = lax.axis_index("tm")
    lowest = band_limits[0, 0]
    highest = band_limits[0, 1]

    hop_far = [(i + 2, i) for i in range(blocks - 2)]
    hop_near = [(i + 1, i) for i in range(blocks - 1)]
    to_even = [(i + 1, i) for i in range(0, blocks - 1, 2)]
    to_odd = [(i - 1, i) for i in range(1, blocks, 2)]
    core_swap = [(i, i ^ 1) for i in range(4)]
    side_swap = [(i, i ^ 2) for i in range(4)]

    marks = jnp.stack(
        [
            valid_mask,
            lax.ppermute(valid_mask, "chan", hop_near),
            lax.ppermute(valid_mask, "chan", hop_far),
        ]
    )
    counts = jnp.sum(marks * valid_mask[None], axis=(1, 2))
    counts += lax.ppermute(counts, "tm", core_swap)
    counts += lax.ppermute(counts, "tm", side_swap)
    scales = 1.0 / jnp.maximum(counts, 1).astype(jnp.float32)
    places = jnp.stack(
        [
            lowest,
            8 * rank,
            8 * (rank ^ 2),
            8 * (rank ^ 1),
            8 * (rank ^ 3),
            highest,
        ]
    )

    lag_table = jnp.asarray(lag_table_of(samples, BINS, LAGS))
    whites = whitened(records, valid_mask, jnp.asarray(dft_table_of(samples, BINS)))
    fars = [lax.ppermute(white, "chan", hop_far) for white in whites]
    before = None
    for at, (white, far) in enumerate(zip(whites, fars)):
        from_odd = lax.ppermute(white, "chan", to_even)
        from_even = lax.ppermute(far, "chan", to_odd)
        following = jnp.where(block % 2 == 0, from_odd, from_even)
        before = correlated(
            places, scales, white, following, far, lag_table, before, last=at == CHUNKS - 1
        )
    keep, other, send = before
    got = lax.ppermute(send, "tm", core_swap)
    passing = (other + got[1].astype(jnp.float32)).astype(jnp.bfloat16)
    passed = lax.ppermute(passing, "tm", side_swap)
    return keep + got[0].astype(jnp.float32) + passed.astype(jnp.float32)


def solution(mesh):
    placed = (P("chan", "tm", None), P("chan", "tm"), P("chan", None))
    return jax.shard_map(
        shards, mesh=mesh, in_specs=placed, out_specs=P("chan", "tm", None), check_vma=False
    )
```

time: 167 us -> 107 us (0.64)
  blocking collectives: 40.4 us -> 0 us
  waiting for transfers between devices: 58.2 us -> 41.5 us
  between operations: 13.5 us -> 0.11 us
  starting transfers between devices: 6.21 us -> 18.3 us
  Pallas kernels: 34 us -> 38.8 us
  local copies, waits for them, and re-layouts: 7.01 us -> 2.62 us
    all_gather x1 -> x0, blocking collectives: 40.4 us -> none  [shards(): marks = lax.all_gather(valid_mask, ('chan', 'tm'), axis=0, tiled=True)]
    ppermute x3 -> x12, waiting for transfers between devices: 58.2 us -> 41.5 us  [the longest x2 23.6 us: shards(): fars = [lax.ppermute(white, 'chan', hop_far) for white in whites]]
    ppermute x3 -> x12, starting transfers between devices: 6.21 us -> 18.3 us  [the longest x2 7.49 us: shards(): from_even = lax.ppermute(far, 'chan', to_odd)]
    pallas_call x1 -> x2, Pallas kernels: 20.9 us -> 26.4 us  [correlated(): pl.pallas_call(functools.partial(cross_kernel, first=before is None, last...]
    unnamed x7 -> x6, local copies, waits for them, and re-layouts: 5.05 us -> 0.01 us
    select_n x1 -> x0, other arithmetic: 1.98 us -> none  [shards(): scale = jnp.where((lowest + pair < highest)[None, :], scale, 0.0)]
    another operation x0 -> x1, local copies, waits for them, and re-layouts: none -> 1.96 us  [shards(): jnp.stack([lowest, 8 * rank, 8 * (rank ^ 2), 8 * (rank ^ 1), 8 * (rank ^...]
  transfers between devices with their start and end apart: 4 -> 12, of which waited for: 2 -> 7; matrix products, arithmetic and copies ran while one was open for 4% -> 4% of each run, Pallas kernels for 0% -> 0%
where the time goes in v2:
time: 107 us
  waiting for transfers between devices  41.5 us (39%)
  Pallas kernels  38.8 us (36%)
  starting transfers between devices  18.3 us (17%)
  other arithmetic  5.71 us (5%)
  local copies, waits for them, and re-layouts  2.62 us (2%)
    pallas_call x2, Pallas kernels, correlated(): pl.pallas_call(functools.partial(cross_kernel, first=before is None, last...  26.4 us
    ppermute x2, waiting for transfers between devices, shards(): fars = [lax.ppermute(white, 'chan', hop_far) for white in whites]  23.6 us
    pallas_call x1, Pallas kernels, whitened(): pl.pallas_call(spectra_kernel, name='spectra', grid_spec=pltpu.PrefetchSc...  12.4 us
    ppermute x1, waiting for transfers between devices, shards(): passed = lax.ppermute(passing, 'tm', side_swap)  8.29 us
    ppermute x2, starting transfers between devices, shards(): from_even = lax.ppermute(far, 'chan', to_odd)  7.49 us
    ppermute x1, waiting for transfers between devices, shards(): lax.ppermute(valid_mask, 'chan', hop_near)  4.13 us
    ppermute x2, starting transfers between devices, shards(): from_odd = lax.ppermute(white, 'chan', to_even)  2.58 us
    ppermute x2, starting transfers between devices, shards(): fars = [lax.ppermute(white, 'chan', hop_far) for white in whites]  2.57 us
  transfers between devices with their start and end apart: 12, of which 7 were waited for; matrix products, arithmetic and copies ran while one was open for 4% of the time, Pallas kernels for 0%

profile of v2, /device:TPU:0, one launch (start us, length us, event | category | flops | bytes accessed | tf_op | source)
XLA Modules:
  0.0 107.0 jit_solution(4023837499198291196)
XLA Ops:
  0.0 12.4 %spectra.1 = (bf16[2,160,1024]{2,1,0:T(8,128)(2,1)}, bf16[2,160,1024]{2,1,0:T(8,128)(2,1)}) custom-call(s32[1,4]{1,0:T(1,128)} %valid_ref.1, bf16[160,4,7680]{2,1,0:T(4,128)(2,1)} %second_ref.1, bf16[160,4,7680]{2,1,0:T(4,128)(2,1)} %second_ref.1, bf16[3840,1024]{1,0:T(8,128)(2,1)} %constant.38.clone.table_ref), custom_call_target="tpu_custom_call" | custom-call | flops 5033164800 | bytes 17694720 | tf_op jit(solution)/shard_map/spectra/pallas_call | solution.py:98
  12.4 1.3 %collective-permute-start.5 = (bf16[2,160,1024]{2,1,0:T(8,128)(2,1)}, bf16[2,160,1024]{2,1,0:T(8,128)(2,1)S(1)}, u32[]{:S(2)}, u32[]{:S(2)}) collective-permute-start(bf16[2,160,1024]{2,1,0:T(8,128)(2,1)} %get-tuple-element.10.own_ref), channel_id=1, source_target_pairs={{8,0},{12,4},{16,8},{20,12},{24,16},{28,20},{9,1},{13,5},{17,9},{2... | collective-permute-start | bytes 1966088 | tf_op jit(solution)/shard_map/ppermute | solution.py:301
  13.7 1.3 %collective-permute-start.8 = (bf16[2,160,1024]{2,1,0:T(8,128)(2,1)}, bf16[2,160,1024]{2,1,0:T(8,128)(2,1)}, u32[]{:S(2)}, u32[]{:S(2)}) collective-permute-start(bf16[2,160,1024]{2,1,0:T(8,128)(2,1)} %get-tuple-element.11.own_ref), channel_id=1, source_target_pairs={{8,0},{12,4},{16,8},{20,12},{24,16},{28,20},{9,1},{13,5},{17,9},{2... | collective-permute-start | bytes 1966088 | tf_op jit(solution)/shard_map/ppermute | solution.py:301
  15.0 1.3 %collective-permute-start.4 = (bf16[2,160,1024]{2,1,0:T(8,128)(2,1)}, bf16[2,160,1024]{2,1,0:T(8,128)(2,1)S(1)}, u32[]{:S(2)}, u32[]{:S(2)}) collective-permute-start(bf16[2,160,1024]{2,1,0:T(8,128)(2,1)} %get-tuple-element.10.own_ref), channel_id=1, source_target_pairs={{4,0},{12,8},{20,16},{28,24},{5,1},{13,9},{21,17},{29,25},{6,2},{1... | collective-permute-start | bytes 1966088 | tf_op jit(solution)/shard_map/ppermute | solution.py:304
  16.3 16.8 %collective-permute-done.5.far_ref = bf16[2,160,1024]{2,1,0:T(8,128)(2,1)S(1)} collective-permute-done((bf16[2,160,1024]{2,1,0:T(8,128)(2,1)}, bf16[2,160,1024]{2,1,0:T(8,128)(2,1)S(1)}, u32[]{:S(2)}, u32[]{:S(2)}) %collective-permute-start.5) | collective-permute-done | bytes 655392 | tf_op jit(solution)/shard_map/ppermute | solution.py:301
  33.1 3.9 %collective-permute-start.6 = (bf16[2,160,1024]{2,1,0:T(8,128)(2,1)S(1)}, bf16[2,160,1024]{2,1,0:T(8,128)(2,1)S(1)}, u32[]{:S(2)}, u32[]{:S(2)}) collective-permute-start(bf16[2,160,1024]{2,1,0:T(8,128)(2,1)S(1)} %collective-permute-done.5.far_ref), channel_id=1, source_target_pairs={{0,4},{8,12},{16,20},{24,28},{1,5},{9,13},{17,21},{25,29},{2,6},{1... | collective-permute-start | bytes 1966088 | tf_op jit(solution)/shard_map/ppermute | solution.py:305
  37.0 1.3 %collective-permute-start.1 = (s32[1,4]{1,0:T(1,128)S(1)}, s32[1,4]{1,0:T(1,128)S(1)}, u32[]{:S(2)}, u32[]{:S(2)}) collective-permute-start(s32[1,4]{1,0:T(1,128)S(1)} %copy-done), channel_id=1, source_target_pairs={{8,0},{12,4},{16,8},{20,12},{24,16},{28,20},{9,1},{13,5},{17,9},{2... | collective-permute-start | bytes 56 | tf_op jit(solution)/shard_map/ppermute | solution.py:281
  38.3 1.3 %collective-permute-start.7 = (bf16[2,160,1024]{2,1,0:T(8,128)(2,1)}, bf16[2,160,1024]{2,1,0:T(8,128)(2,1)S(1)}, u32[]{:S(2)}, u32[]{:S(2)}) collective-permute-start(bf16[2,160,1024]{2,1,0:T(8,128)(2,1)} %get-tuple-element.11.own_ref), channel_id=1, source_target_pairs={{4,0},{12,8},{20,16},{28,24},{5,1},{13,9},{21,17},{29,25},{6,2},{1... | collective-permute-start | bytes 1966088 | tf_op jit(solution)/shard_map/ppermute | solution.py:304
  39.6 6.8 %collective-permute-done.8.far_ref = bf16[2,160,1024]{2,1,0:T(8,128)(2,1)} collective-permute-done((bf16[2,160,1024]{2,1,0:T(8,128)(2,1)}, bf16[2,160,1024]{2,1,0:T(8,128)(2,1)}, u32[]{:S(2)}, u32[]{:S(2)}) %collective-permute-start.8) | collective-permute-done | bytes 655392 | tf_op jit(solution)/shard_map/ppermute | solution.py:301
  46.4 3.6 %collective-permute-start.9 = (bf16[2,160,1024]{2,1,0:T(8,128)(2,1)}, bf16[2,160,1024]{2,1,0:T(8,128)(2,1)S(1)}, u32[]{:S(2)}, u32[]{:S(2)}) collective-permute-start(bf16[2,160,1024]{2,1,0:T(8,128)(2,1)} %collective-permute-done.8.far_ref), channel_id=1, source_target_pairs={{0,4},{8,12},{16,20},{24,28},{1,5},{9,13},{17,21},{25,29},{2,6},{1... | collective-permute-start | bytes 1966088 | tf_op jit(solution)/shard_map/ppermute | solution.py:305
  50.0 0.7 fusion.3
  50.6 2.0 %stack.31.place_ref = s32[6]{0:T(128)} concatenate(s32[1]{0:T(128)} %bitcast, s32[1]{0:T(128)} %bitcast.1, s32[1]{0:T(128)} %bitcast.2, s32[1]{0:T(128)} %bitcast.3, s32[1]{0:T(128)} %bitcast.4, s32[1]{0:T(128)} %bitcast.5), dimensions={0} | concatenate | bytes 48 | tf_op jit(solution)/shard_map/stack | solution.py:288
  52.6 0.0 collective-permute-done.1
  52.6 1.3 %collective-permute-start = (s32[1,4]{1,0:T(1,128)S(1)}, s32[1,4]{1,0:T(1,128)S(1)}, u32[]{:S(2)}, u32[]{:S(2)}) collective-permute-start(s32[1,4]{1,0:T(1,128)S(1)} %copy-done), channel_id=1, source_target_pairs={{4,0},{8,4},{12,8},{16,12},{20,16},{24,20},{28,24},{5,1},{9,5},{13... | collective-permute-start | bytes 56 | tf_op jit(solution)/shard_map/ppermute | solution.py:280
  53.9 4.1 %collective-permute-done = s32[1,4]{1,0:T(1,128)S(1)} collective-permute-done((s32[1,4]{1,0:T(1,128)S(1)}, s32[1,4]{1,0:T(1,128)S(1)}, u32[]{:S(2)}, u32[]{:S(2)}) %collective-permute-start) | collective-permute-done | bytes 48 | tf_op jit(solution)/shard_map/ppermute | solution.py:280
  58.0 0.2 fusion.2
  58.2 0.1 collective-permute-start.2
  58.2 1.1 %collective-permute-done.2 = s32[3]{0:T(128)S(1)} collective-permute-done((s32[3]{0:T(128)S(1)}, s32[3]{0:T(128)S(1)}, u32[]{:S(2)}, u32[]{:S(2)}) %collective-permute-start.2) | collective-permute-done | bytes 44 | tf_op jit(solution)/shard_map/ppermute | solution.py:285
  59.4 1.5 %collective-permute-start.3 = (s32[3]{0:T(128)S(1)}, s32[3]{0:T(128)S(1)}, u32[]{:S(2)}, u32[]{:S(2)}) collective-permute-start(s32[3]{0:T(128)S(1)} %add.20), channel_id=1, source_target_pairs={{0,2},{1,3},{2,0},{3,1},{4,6},{5,7},{6,4},{7,5},{8,10},{9,11},{10,... | collective-permute-start | bytes 44 | tf_op jit(solution)/shard_map/ppermute | solution.py:286
  60.9 2.0 %collective-permute-done.3 = s32[3]{0:T(128)S(1)} collective-permute-done((s32[3]{0:T(128)S(1)}, s32[3]{0:T(128)S(1)}, u32[]{:S(2)}, u32[]{:S(2)}) %collective-permute-start.3) | collective-permute-done | bytes 44 | tf_op jit(solution)/shard_map/ppermute | solution.py:286
  62.9 0.5 convert_divide_fusion.scale_ref
  63.4 0.0 collective-permute-done.6
  63.4 0.9 broadcast_select_fusion.1.next_ref
  64.4 0.0 collective-permute-done.7
  64.4 0.9 broadcast_select_fusion.next_ref
  65.3 12.9 %cross.2.rest_0_ = f32[10,512,128]{2,1,0:T(8,128)} custom-call(s32[6]{0:T(128)} %stack.31.place_ref, f32[3]{0:T(128)} %convert_divide_fusion.scale_ref, bf16[2,160,1024]{2,1,0:T(8,128)(2,1)} %get-tuple-element.11.own_ref, bf16[2,160,1024]{2,1,0:T(8,128)(2,1)} %broadcast_select_fusion.next_ref, bf16[2,160,1024]{2,1,0:T(8,128)(2,1)} %collective-permute-done.8.far_ref, ...), custom_call_target="tpu_custom_call" | custom-call | flops 1342177280 | bytes 1966080 | tf_op jit(solution)/shard_map/cross/pallas_call | solution.py:236
  78.2 13.5 %cross.3 = (f32[160,8,128]{2,1,0:T(8,128)}, f32[160,8,128]{2,1,0:T(8,128)}, bf16[2,160,8,128]{3,2,1,0:T(8,128)(2,1)}) custom-call(s32[6]{0:T(128)} %stack.31.place_ref, f32[3]{0:T(128)} %convert_divide_fusion.scale_ref, bf16[2,160,1024]{2,1,0:T(8,128)(2,1)} %get-tuple-element.10.own_ref, bf16[2,160,1024]{2,1,0:T(8,128)(2,1)} %broadcast_select_fusion.1.next_ref, ...), custom_call_target="tpu_custom_call" | custom-call | flops 1342177280 | bytes 1966080 | tf_op jit(solution)/shard_map/cross/pallas_call | solution.py:236
  91.7 2.3 %collective-permute-done.10 = bf16[2,160,8,128]{3,2,1,0:T(8,128)(2,1)S(1)} collective-permute-done((bf16[2,160,8,128]{3,2,1,0:T(8,128)(2,1)}, bf16[2,160,8,128]{3,2,1,0:T(8,128)(2,1)S(1)}, u32[]{:S(2)}, u32[]{:S(2)}) %collective-permute-start.10) | collective-permute-done | bytes 655392 | tf_op jit(solution)/shard_map/ppermute | solution.py:311
  94.0 1.2 %fusion = bf16[160,8,128]{2,1,0:T(8,128)(2,1)S(1)} fusion(f32[160,8,128]{2,1,0:T(8,128)} %get-tuple-element.14, bf16[2,160,8,128]{3,2,1,0:T(8,128)(2,1)S(1)} %collective-permute-done.10), kind=kLoop, calls=%fused_computation.1 | loop fusion | flops 491520 | bytes 1310720 | tf_op jit(solution)/shard_map/convert_element_type | solution.py:312
  95.2 1.5 %collective-permute-start.11 = (bf16[160,8,128]{2,1,0:T(8,128)(2,1)S(1)}, bf16[160,8,128]{2,1,0:T(8,128)(2,1)S(1)}, u32[]{:S(2)}, u32[]{:S(2)}) collective-permute-start(bf16[160,8,128]{2,1,0:T(8,128)(2,1)S(1)} %fusion), channel_id=1, source_target_pairs={{0,2},{1,3},{2,0},{3,1},{4,6},{5,7},{6,4},{7,5},{8,10},{9,11},{10,... | collective-permute-start | bytes 983048 | tf_op jit(solution)/shard_map/ppermute | solution.py:313
  96.7 8.3 %collective-permute-done.11 = bf16[160,8,128]{2,1,0:T(8,128)(2,1)S(1)} collective-permute-done((bf16[160,8,128]{2,1,0:T(8,128)(2,1)S(1)}, bf16[160,8,128]{2,1,0:T(8,128)(2,1)S(1)}, u32[]{:S(2)}, u32[]{:S(2)}) %collective-permute-start.11) | collective-permute-done | bytes 327712 | tf_op jit(solution)/shard_map/ppermute | solution.py:313
  105.0 2.0 %fusion.1 = f32[160,8,128]{2,1,0:T(8,128)} fusion(f32[160,8,128]{2,1,0:T(8,128)} %get-tuple-element.12, bf16[160,8,128]{2,1,0:T(8,128)(2,1)S(1)} %collective-permute-done.11, bf16[2,160,8,128]{3,2,1,0:T(8,128)(2,1)S(1)} %collective-permute-done.10), kind=kLoop, calls=%fused_computation.3 | loop fusion | flops 655360 | bytes 1966080 | tf_op jit(solution)/shard_map/add | solution.py:314
  (10 shorter events, 0.0 us)
Async XLA Ops:
  0.0 37.0 %copy-start = (s32[1,4]{1,0:T(1,128)S(1)}, s32[1,4]{1,0:T(1,128)}, u32[]{:S(2)}) copy-start(s32[1,4]{1,0:T(1,128)} %valid_ref.1) | copy-start | bytes 52
  0.0 50.0 %copy-start.1 = (s32[1,2]{1,0:T(1,128)S(1)}, s32[1,2]{1,0:T(1,128)}, u32[]{:S(2)}) copy-start(s32[1,2]{1,0:T(1,128)} %param.7) | copy-start | bytes 28
  12.4 20.7 %collective-permute-start.5 = (bf16[2,160,1024]{2,1,0:T(8,128)(2,1)}, bf16[2,160,1024]{2,1,0:T(8,128)(2,1)S(1)}, u32[]{:S(2)}, u32[]{:S(2)}) collective-permute-start(bf16[2,160,1024]{2,1,0:T(8,128)(2,1)} %get-tuple-element.10.own_ref), channel_id=1, source_target_pairs={{8,0},{12,4},{16,8},{20,12},{24,16},{28,20},{9,1},{13,5},{17,9},{2... | collective-permute-start | bytes 1966088 | tf_op jit(solution)/shard_map/ppermute | solution.py:301
  13.7 32.7 %collective-permute-start.8 = (bf16[2,160,1024]{2,1,0:T(8,128)(2,1)}, bf16[2,160,1024]{2,1,0:T(8,128)(2,1)}, u32[]{:S(2)}, u32[]{:S(2)}) collective-permute-start(bf16[2,160,1024]{2,1,0:T(8,128)(2,1)} %get-tuple-element.11.own_ref), channel_id=1, source_target_pairs={{8,0},{12,4},{16,8},{20,12},{24,16},{28,20},{9,1},{13,5},{17,9},{2... | collective-permute-start | bytes 1966088 | tf_op jit(solution)/shard_map/ppermute | solution.py:301
  15.0 48.5 %collective-permute-start.4 = (bf16[2,160,1024]{2,1,0:T(8,128)(2,1)}, bf16[2,160,1024]{2,1,0:T(8,128)(2,1)S(1)}, u32[]{:S(2)}, u32[]{:S(2)}) collective-permute-start(bf16[2,160,1024]{2,1,0:T(8,128)(2,1)} %get-tuple-element.10.own_ref), channel_id=1, source_target_pairs={{4,0},{12,8},{20,16},{28,24},{5,1},{13,9},{21,17},{29,25},{6,2},{1... | collective-permute-start | bytes 1966088 | tf_op jit(solution)/shard_map/ppermute | solution.py:304
  33.1 45.1 %copy-start.2 = (bf16[2,160,1024]{2,1,0:T(8,128)(2,1)}, bf16[2,160,1024]{2,1,0:T(8,128)(2,1)S(1)}, u32[]{:S(2)}) copy-start(bf16[2,160,1024]{2,1,0:T(8,128)(2,1)S(1)} %collective-permute-done.5.far_ref) | copy-start | bytes 1966084
  33.1 30.4 %collective-permute-start.6 = (bf16[2,160,1024]{2,1,0:T(8,128)(2,1)S(1)}, bf16[2,160,1024]{2,1,0:T(8,128)(2,1)S(1)}, u32[]{:S(2)}, u32[]{:S(2)}) collective-permute-start(bf16[2,160,1024]{2,1,0:T(8,128)(2,1)S(1)} %collective-permute-done.5.far_ref), channel_id=1, source_target_pairs={{0,4},{8,12},{16,20},{24,28},{1,5},{9,13},{17,21},{25,29},{2,6},{1... | collective-permute-start | bytes 1966088 | tf_op jit(solution)/shard_map/ppermute | solution.py:305
  37.0 15.6 %collective-permute-start.1 = (s32[1,4]{1,0:T(1,128)S(1)}, s32[1,4]{1,0:T(1,128)S(1)}, u32[]{:S(2)}, u32[]{:S(2)}) collective-permute-start(s32[1,4]{1,0:T(1,128)S(1)} %copy-done), channel_id=1, source_target_pairs={{8,0},{12,4},{16,8},{20,12},{24,16},{28,20},{9,1},{13,5},{17,9},{2... | collective-permute-start | bytes 56 | tf_op jit(solution)/shard_map/ppermute | solution.py:281
  38.3 26.1 %collective-permute-start.7 = (bf16[2,160,1024]{2,1,0:T(8,128)(2,1)}, bf16[2,160,1024]{2,1,0:T(8,128)(2,1)S(1)}, u32[]{:S(2)}, u32[]{:S(2)}) collective-permute-start(bf16[2,160,1024]{2,1,0:T(8,128)(2,1)} %get-tuple-element.11.own_ref), channel_id=1, source_target_pairs={{4,0},{12,8},{20,16},{28,24},{5,1},{13,9},{21,17},{29,25},{6,2},{1... | collective-permute-start | bytes 1966088 | tf_op jit(solution)/shard_map/ppermute | solution.py:304
  46.4 18.0 %collective-permute-start.9 = (bf16[2,160,1024]{2,1,0:T(8,128)(2,1)}, bf16[2,160,1024]{2,1,0:T(8,128)(2,1)S(1)}, u32[]{:S(2)}, u32[]{:S(2)}) collective-permute-start(bf16[2,160,1024]{2,1,0:T(8,128)(2,1)} %collective-permute-done.8.far_ref), channel_id=1, source_target_pairs={{0,4},{8,12},{16,20},{24,28},{1,5},{9,13},{17,21},{25,29},{2,6},{1... | collective-permute-start | bytes 1966088 | tf_op jit(solution)/shard_map/ppermute | solution.py:305
  52.6 5.4 %collective-permute-start = (s32[1,4]{1,0:T(1,128)S(1)}, s32[1,4]{1,0:T(1,128)S(1)}, u32[]{:S(2)}, u32[]{:S(2)}) collective-permute-start(s32[1,4]{1,0:T(1,128)S(1)} %copy-done), channel_id=1, source_target_pairs={{4,0},{8,4},{12,8},{16,12},{20,16},{24,20},{28,24},{5,1},{9,5},{13... | collective-permute-start | bytes 56 | tf_op jit(solution)/shard_map/ppermute | solution.py:280
  58.2 1.2 %collective-permute-start.2 = (s32[3]{0:T(128)S(1)}, s32[3]{0:T(128)S(1)}, u32[]{:S(2)}, u32[]{:S(2)}) collective-permute-start(s32[3]{0:T(128)S(1)} %fusion.2), channel_id=1, source_target_pairs={{0,1},{1,0},{2,3},{3,2},{4,5},{5,4},{6,7},{7,6},{8,9},{9,8},{10,11... | collective-permute-start | bytes 44 | tf_op jit(solution)/shard_map/ppermute | solution.py:285
  59.4 3.5 %collective-permute-start.3 = (s32[3]{0:T(128)S(1)}, s32[3]{0:T(128)S(1)}, u32[]{:S(2)}, u32[]{:S(2)}) collective-permute-start(s32[3]{0:T(128)S(1)} %add.20), channel_id=1, source_target_pairs={{0,2},{1,3},{2,0},{3,1},{4,6},{5,7},{6,4},{7,5},{8,10},{9,11},{10,... | collective-permute-start | bytes 44 | tf_op jit(solution)/shard_map/ppermute | solution.py:286
  91.7 2.3 %collective-permute-start.10 = (bf16[2,160,8,128]{3,2,1,0:T(8,128)(2,1)}, bf16[2,160,8,128]{3,2,1,0:T(8,128)(2,1)S(1)}, u32[]{:S(2)}, u32[]{:S(2)}) collective-permute-start(bf16[2,160,8,128]{3,2,1,0:T(8,128)(2,1)} %get-tuple-element.13), channel_id=1, source_target_pairs={{0,1},{1,0},{2,3},{3,2},{4,5},{5,4},{6,7},{7,6},{8,9},{9,8},{10,11... | collective-permute-start | bytes 1966088 | tf_op jit(solution)/shard_map/ppermute | solution.py:311
  95.2 9.8 %collective-permute-start.11 = (bf16[160,8,128]{2,1,0:T(8,128)(2,1)S(1)}, bf16[160,8,128]{2,1,0:T(8,128)(2,1)S(1)}, u32[]{:S(2)}, u32[]{:S(2)}) collective-permute-start(bf16[160,8,128]{2,1,0:T(8,128)(2,1)S(1)} %fusion), channel_id=1, source_target_pairs={{0,2},{1,3},{2,0},{3,1},{4,6},{5,7},{6,4},{7,5},{8,10},{9,11},{10,... | collective-permute-start | bytes 983048 | tf_op jit(solution)/shard_map/ppermute | solution.py:313

commit v3 on v2

--- a/solution.py
+++ b/solution.py
@@ -14,7 +14,6 @@
 PAIRS = 32
 REACH = 2
 STEPS = 3
-CHUNKS = 2
 
 
 def bin_order(bins):
@@ -39,14 +38,16 @@
     return (np.concatenate([np.cos(phase), -np.sin(phase)], axis=0) * factor).astype(jnp.bfloat16)
 
 
-def spectra_kernel(valid_ref, first_ref, second_ref, table_ref, *rest):
+def spectra_kernel(valid_ref, first_ref, second_ref, table_ref, *rest, first_seg):
     *white_refs, acc = rest
     step = pl.program_id(0)
-    channels, segs, width = first_ref.shape
+    channels, _, width = first_ref.shape
     lane_tiles = acc.shape[0]
     bins = table_ref.shape[1] // 2
-    first = first_ref[...].astype(jnp.float32)
-    second = second_ref[...].astype(jnp.float32)
+    segs = acc.shape[1] // channels
+    chosen = slice(first_seg, first_seg + segs)
+    first = first_ref[:, chosen, :].astype(jnp.float32)
+    second = second_ref[:, chosen, :].astype(jnp.float32)
     even = (first + second).reshape(channels * segs, width).astype(jnp.bfloat16)
     odd = (first - second).reshape(channels * segs, width).astype(jnp.bfloat16)
     even_part = jnp.dot(even, table_ref[:, :bins], preferred_element_type=jnp.float32)
@@ -80,7 +81,7 @@
                 power = real * real + imag * imag
                 power_sum = power if power_sum is None else power_sum + power
             water = jnp.sum(power_sum, axis=1, keepdims=True) * (1.0 / bins)
-            usable = valid_ref[0, seg].astype(jnp.float32)
+            usable = valid_ref[0, first_seg + seg].astype(jnp.float32)
             for place, tile in enumerate(reals):
                 real, imag = acc[tile, rows, :], acc[tile + quarter, rows, :]
                 power = real * real + imag * imag
@@ -92,11 +93,12 @@
                 white_ref[:, bins + at : bins + at + 128] = (imag * scale).astype(jnp.bfloat16)
 
 
-def whitened(records, valid_mask, table):
+def whitened(records, valid_mask, table, first_seg, groups, group):
     channels, segs, samples = records.shape
     width = samples // 2 // STEPS
+    rows = groups * group * channels
     return pl.pallas_call(
-        spectra_kernel,
+        functools.partial(spectra_kernel, first_seg=first_seg),
         name="spectra",
         grid_spec=pltpu.PrefetchScalarGridSpec(
             num_scalar_prefetch=1,
@@ -106,21 +108,16 @@
                 pl.BlockSpec((channels, segs, width), lambda k, valid: (0, 0, k + STEPS)),
                 pl.BlockSpec((width, 2 * BINS), lambda k, valid: (k, 0)),
             ],
-            out_specs=[
-                pl.BlockSpec((segs // CHUNKS, channels, 2 * BINS), lambda k, valid: (0, 0, 0))
-            ]
-            * CHUNKS,
-            scratch_shapes=[
-                pltpu.VMEM((2 * BINS // 128, channels * segs, 128), jnp.float32),
-            ],
+            out_specs=[pl.BlockSpec((group, channels, 2 * BINS), lambda k, valid: (0, 0, 0))]
+            * groups,
+            scratch_shapes=[pltpu.VMEM((2 * BINS // 128, rows, 128), jnp.float32)],
         ),
-        out_shape=[jax.ShapeDtypeStruct((segs // CHUNKS, channels, 2 * BINS), jnp.bfloat16)]
-        * CHUNKS,
+        out_shape=[jax.ShapeDtypeStruct((group, channels, 2 * BINS), jnp.bfloat16)] * groups,
         compiler_params=pltpu.CompilerParams(vmem_limit_bytes=56 << 20),
         cost_estimate=pl.CostEstimate(
-            flops=2 * channels * segs * samples * BINS,
+            flops=4 * rows * samples * BINS,
             bytes_accessed=2 * channels * segs * samples + 2 * samples * BINS,
-            transcendentals=channels * segs * BINS,
+            transcendentals=rows * BINS,
         ),
     )(valid_mask, records, records, table)
 
@@ -129,7 +126,10 @@
 TILES = 2
 
 
-def cross_kernel(place_ref, scale_ref, own_ref, next_ref, far_ref, lag_ref, *rest, first, last):
+def cross_kernel(place_ref, *rest, first, last):
+    if last:
+        scale_ref, *rest = rest
+    own_ref, next_ref, far_ref, lag_ref, *rest = rest
     if not first:
         before_ref, *rest = rest
     if last:
@@ -237,7 +237,7 @@
         functools.partial(cross_kernel, first=before is None, last=last),
         name="cross",
         grid_spec=pltpu.PrefetchScalarGridSpec(
-            num_scalar_prefetch=2,
+            num_scalar_prefetch=2 if last else 1,
             grid=(channels // rows,),
             in_specs=[
                 whole,
@@ -252,11 +252,19 @@
         out_shape=out_shape,
         compiler_params=pltpu.CompilerParams(vmem_limit_bytes=56 << 20),
         cost_estimate=pl.CostEstimate(
-            flops=2 * channels * PAIRS * columns * LAGS,
+            flops=10 * channels * PAIRS * columns * LAGS,
             bytes_accessed=6 * segs * channels * columns,
             transcendentals=0,
         ),
-    )(places, scales, own, following, far, lag_table, *([] if before is None else [before]))
+    )(
+        places,
+        *([scales] if last else []),
+        own,
+        following,
+        far,
+        lag_table,
+        *([] if before is None else [before]),
+    )
 
 
 def shards(records, valid_mask, band_limits):
@@ -269,8 +277,7 @@
 
     hop_far = [(i + 2, i) for i in range(blocks - 2)]
     hop_near = [(i + 1, i) for i in range(blocks - 1)]
-    to_even = [(i + 1, i) for i in range(0, blocks - 1, 2)]
-    to_odd = [(i - 1, i) for i in range(1, blocks, 2)]
+    pair_swap = [(i ^ 1, i) for i in range(blocks)]
     core_swap = [(i, i ^ 1) for i in range(4)]
     side_swap = [(i, i ^ 2) for i in range(4)]
 
@@ -297,15 +304,19 @@
     )
 
     lag_table = jnp.asarray(lag_table_of(samples, BINS, LAGS))
-    whites = whitened(records, valid_mask, jnp.asarray(dft_table_of(samples, BINS)))
+    table = jnp.asarray(dft_table_of(samples, BINS))
+    half = segs // 2
+    whites = [
+        *whitened(records, valid_mask, table, 0, 1, half),
+        *whitened(records, valid_mask, table, half, half, 1),
+    ]
     fars = [lax.ppermute(white, "chan", hop_far) for white in whites]
     before = None
     for at, (white, far) in enumerate(zip(whites, fars)):
-        from_odd = lax.ppermute(white, "chan", to_even)
-        from_even = lax.ppermute(far, "chan", to_odd)
-        following = jnp.where(block % 2 == 0, from_odd, from_even)
+        passed = jnp.where(block % 2 == 0, far, white)
+        following = lax.ppermute(passed, "chan", pair_swap)
         before = correlated(
-            places, scales, white, following, far, lag_table, before, last=at == CHUNKS - 1
+            places, scales, white, following, far, lag_table, before, last=at == len(whites) - 1
         )
     keep, other, send = before
     got = lax.ppermute(send, "tm", core_swap)

time: 107 us -> 106 us (level)
  the two profiles are of different devices: /device:TPU:0 before, /device:TPU:24 now
where the time goes in v3:
time: 106 us; the launch traced here: 105 us
  Pallas kernels  52.6 us (50%)
  waiting for transfers between devices  25 us (24%)
  starting transfers between devices  18.8 us (18%)
  local copies, waits for them, and re-layouts  4.85 us (5%)
  other arithmetic  4.02 us (4%)
    pallas_call x3, Pallas kernels, correlated(): pl.pallas_call(functools.partial(cross_kernel, first=before is None, last...  31.2 us
    pallas_call x2, Pallas kernels, whitened(): pl.pallas_call(functools.partial(spectra_kernel, first_seg=first_seg), na...  21.4 us
    ppermute x1, waiting for transfers between devices, shards(): passed = lax.ppermute(passing, 'tm', side_swap)  9.29 us
    ppermute x3, waiting for transfers between devices, shards(): following = lax.ppermute(passed, 'chan', pair_swap)  8.17 us
    ppermute x3, starting transfers between devices, shards(): fars = [lax.ppermute(white, 'chan', hop_far) for white in whites]  6.33 us
    ppermute x3, starting transfers between devices, shards(): following = lax.ppermute(passed, 'chan', pair_swap)  4.75 us
    ppermute x3, waiting for transfers between devices, shards(): fars = [lax.ppermute(white, 'chan', hop_far) for white in whites]  3.34 us
    ppermute x1, starting transfers between devices, shards(): lax.ppermute(valid_mask, 'chan', hop_near)  3.28 us
  transfers between devices with their start and end apart: 12, of which 6 were waited for; matrix products, arithmetic and copies ran while one was open for 3% of the time, Pallas kernels for 41%

profile of v3, /device:TPU:24, one launch (start us, length us, event | category | flops | bytes accessed | tf_op | source)
XLA Modules:
  0.0 105.4 jit_solution(10545218714749772004)
XLA Ops:
  0.0 3.3 %collective-permute-start = (s32[1,4]{1,0:T(1,128)}, s32[1,4]{1,0:T(1,128)S(1)}, u32[]{:S(2)}, u32[]{:S(2)}) collective-permute-start(s32[1,4]{1,0:T(1,128)} %valid_ref.3), channel_id=1, source_target_pairs={{4,0},{8,4},{12,8},{16,12},{20,16},{24,20},{28,24},{5,1},{9,5},{13... | collective-permute-start | bytes 56 | tf_op jit(solution)/shard_map/ppermute | solution.py:287
  3.3 2.4 %collective-permute-start.1 = (s32[1,4]{1,0:T(1,128)}, s32[1,4]{1,0:T(1,128)S(1)}, u32[]{:S(2)}, u32[]{:S(2)}) collective-permute-start(s32[1,4]{1,0:T(1,128)} %valid_ref.3), channel_id=1, source_target_pairs={{8,0},{12,4},{16,8},{20,12},{24,16},{28,20},{9,1},{13,5},{17,9},{2... | collective-permute-start | bytes 56 | tf_op jit(solution)/shard_map/ppermute | solution.py:288
  5.6 10.7 %spectra.3.rest_0_ = bf16[2,160,1024]{2,1,0:T(8,128)(2,1)} custom-call(s32[1,4]{1,0:T(1,128)} %valid_ref.3, bf16[160,4,7680]{2,1,0:T(4,128)(2,1)} %second_ref.3, bf16[160,4,7680]{2,1,0:T(4,128)(2,1)} %second_ref.3, bf16[3840,1024]{1,0:T(8,128)(2,1)} %constant.40.clone.table_ref), custom_call_target="tpu_custom_call" | custom-call | flops 5033164800 | bytes 17694720 | tf_op jit(solution)/shard_map/spectra/pallas_call | solution.py:100
  16.4 2.5 %collective-permute-start.8 = (bf16[2,160,1024]{2,1,0:T(8,128)(2,1)}, bf16[2,160,1024]{2,1,0:T(8,128)(2,1)S(1)}, u32[]{:S(2)}, u32[]{:S(2)}) collective-permute-start(bf16[2,160,1024]{2,1,0:T(8,128)(2,1)} %spectra.3.rest_0_), channel_id=1, source_target_pairs={{8,0},{12,4},{16,8},{20,12},{24,16},{28,20},{9,1},{13,5},{17,9},{2... | collective-permute-start | bytes 1966088 | tf_op jit(solution)/shard_map/ppermute | solution.py:313
  18.9 10.7 %spectra.2 = (bf16[1,160,1024]{2,1,0:T(8,128)(2,1)}, bf16[1,160,1024]{2,1,0:T(8,128)(2,1)}) custom-call(s32[1,4]{1,0:T(1,128)} %valid_ref.3, bf16[160,4,7680]{2,1,0:T(4,128)(2,1)} %second_ref.3, bf16[160,4,7680]{2,1,0:T(4,128)(2,1)} %second_ref.3, bf16[3840,1024]{1,0:T(8,128)(2,1)} %constant.40.clone.table_ref), custom_call_target="tpu_custom_call" | custom-call | flops 5033164800 | bytes 17694720 | tf_op jit(solution)/shard_map/spectra/pallas_call | solution.py:100
  29.6 1.9 %collective-permute-start.6 = (bf16[1,160,1024]{2,1,0:T(8,128)(2,1)}, bf16[1,160,1024]{2,1,0:T(8,128)(2,1)S(1)}, u32[]{:S(2)}, u32[]{:S(2)}) collective-permute-start(bf16[1,160,1024]{2,1,0:T(8,128)(2,1)} %get-tuple-element.11.rest_0_), channel_id=1, source_target_pairs={{8,0},{12,4},{16,8},{20,12},{24,16},{28,20},{9,1},{13,5},{17,9},{2... | collective-permute-start | bytes 983048 | tf_op jit(solution)/shard_map/ppermute | solution.py:313
  31.5 1.9 %collective-permute-start.4 = (bf16[1,160,1024]{2,1,0:T(8,128)(2,1)}, bf16[1,160,1024]{2,1,0:T(8,128)(2,1)S(1)}, u32[]{:S(2)}, u32[]{:S(2)}) collective-permute-start(bf16[1,160,1024]{2,1,0:T(8,128)(2,1)} %get-tuple-element.10.rest_1_), channel_id=1, source_target_pairs={{8,0},{12,4},{16,8},{20,12},{24,16},{28,20},{9,1},{13,5},{17,9},{2... | collective-permute-start | bytes 983048 | tf_op jit(solution)/shard_map/ppermute | solution.py:313
  33.5 0.6 fusion.3
  34.1 1.9 %stack.31.place_ref = s32[6]{0:T(128)} concatenate(s32[1]{0:T(128)} %bitcast, s32[1]{0:T(128)} %bitcast.1, s32[1]{0:T(128)} %bitcast.2, s32[1]{0:T(128)} %bitcast.3, s32[1]{0:T(128)} %bitcast.4, s32[1]{0:T(128)} %bitcast.5), dimensions={0} | concatenate | bytes 48 | tf_op jit(solution)/shard_map/stack | solution.py:295
  36.0 0.2 fusion.2
  36.2 0.1 collective-permute-start.2
  36.2 1.1 %collective-permute-done.2 = s32[3]{0:T(128)S(1)} collective-permute-done((s32[3]{0:T(128)S(1)}, s32[3]{0:T(128)S(1)}, u32[]{:S(2)}, u32[]{:S(2)}) %collective-permute-start.2) | collective-permute-done | bytes 44 | tf_op jit(solution)/shard_map/ppermute | solution.py:292
  37.4 1.5 %collective-permute-start.3 = (s32[3]{0:T(128)S(1)}, s32[3]{0:T(128)S(1)}, u32[]{:S(2)}, u32[]{:S(2)}) collective-permute-start(s32[3]{0:T(128)S(1)} %add.21), channel_id=1, source_target_pairs={{0,2},{1,3},{2,0},{3,1},{4,6},{5,7},{6,4},{7,5},{8,10},{9,11},{10,... | collective-permute-start | bytes 44 | tf_op jit(solution)/shard_map/ppermute | solution.py:293
  38.9 0.1 broadcast_select_fusion
  39.0 1.1 %collective-permute-start.9 = (bf16[2,160,1024]{2,1,0:T(8,128)(2,1)S(1)}, bf16[2,160,1024]{2,1,0:T(8,128)(2,1)S(1)}, u32[]{:S(2)}, u32[]{:S(2)}) collective-permute-start(bf16[2,160,1024]{2,1,0:T(8,128)(2,1)S(1)} %broadcast_select_fusion), channel_id=1, source_target_pairs={{4,0},{0,4},{12,8},{8,12},{20,16},{16,20},{28,24},{24,28},{5,1},{1... | collective-permute-start | bytes 1966088 | tf_op jit(solution)/shard_map/ppermute | solution.py:317
  40.1 0.8 collective-permute-done.3
  40.9 0.5 convert_divide_fusion.rest_0_
  41.5 1.8 %collective-permute-start.7 = (bf16[1,160,1024]{2,1,0:T(8,128)(2,1)S(1)}, bf16[1,160,1024]{2,1,0:T(8,128)(2,1)S(1)}, u32[]{:S(2)}, u32[]{:S(2)}) collective-permute-start(bf16[1,160,1024]{2,1,0:T(8,128)(2,1)S(1)} %broadcast_select_fusion.1), channel_id=1, source_target_pairs={{4,0},{0,4},{12,8},{8,12},{20,16},{16,20},{28,24},{24,28},{5,1},{1... | collective-permute-start | bytes 983048 | tf_op jit(solution)/shard_map/ppermute | solution.py:317
  43.3 3.3 %collective-permute-done.4.rest_3_ = bf16[1,160,1024]{2,1,0:T(8,128)(2,1)S(1)} collective-permute-done((bf16[1,160,1024]{2,1,0:T(8,128)(2,1)}, bf16[1,160,1024]{2,1,0:T(8,128)(2,1)S(1)}, u32[]{:S(2)}, u32[]{:S(2)}) %collective-permute-start.4) | collective-permute-done | bytes 327712 | tf_op jit(solution)/shard_map/ppermute | solution.py:313
  46.7 1.8 %collective-permute-start.5 = (bf16[1,160,1024]{2,1,0:T(8,128)(2,1)S(1)}, bf16[1,160,1024]{2,1,0:T(8,128)(2,1)S(1)}, u32[]{:S(2)}, u32[]{:S(2)}) collective-permute-start(bf16[1,160,1024]{2,1,0:T(8,128)(2,1)S(1)} %broadcast_select_fusion.2), channel_id=1, source_target_pairs={{4,0},{0,4},{12,8},{8,12},{20,16},{16,20},{28,24},{24,28},{5,1},{1... | collective-permute-start | bytes 983048 | tf_op jit(solution)/shard_map/ppermute | solution.py:317
  48.5 8.2 %collective-permute-done.9.rest_1_ = bf16[2,160,1024]{2,1,0:T(8,128)(2,1)S(1)} collective-permute-done((bf16[2,160,1024]{2,1,0:T(8,128)(2,1)S(1)}, bf16[2,160,1024]{2,1,0:T(8,128)(2,1)S(1)}, u32[]{:S(2)}, u32[]{:S(2)}) %collective-permute-start.9) | collective-permute-done | bytes 655392 | tf_op jit(solution)/shard_map/ppermute | solution.py:317
  56.6 0.8 copy-done.6
  57.5 12.8 %cross.3.rest_4_ = f32[10,512,128]{2,1,0:T(8,128)} custom-call(s32[6]{0:T(128)} %stack.31.place_ref, bf16[2,160,1024]{2,1,0:T(8,128)(2,1)} %spectra.3.rest_0_, bf16[2,160,1024]{2,1,0:T(8,128)(2,1)} %copy-done.6, bf16[2,160,1024]{2,1,0:T(8,128)(2,1)} %copy-done.1, bf16[1024,128]{1,0:T(8,128)(2,1)} %constant.39.clone.rest_3_.rest_4_), custom_call_target="tpu_custom_call" | custom-call | flops 6710886400 | bytes 1966080 | tf_op jit(solution)/shard_map/cross/pallas_call | solution.py:236
  70.3 0.7 copy-done.8
  71.0 9.0 %cross.4.rest_5_ = f32[10,512,128]{2,1,0:T(8,128)} custom-call(s32[6]{0:T(128)} %stack.31.place_ref, bf16[1,160,1024]{2,1,0:T(8,128)(2,1)} %get-tuple-element.11.rest_0_, bf16[1,160,1024]{2,1,0:T(8,128)(2,1)} %copy-done.8, bf16[1,160,1024]{2,1,0:T(8,128)(2,1)} %copy-done.3, bf16[1024,128]{1,0:T(8,128)(2,1)} %constant.39.clone.rest_3_.rest_4_, ...), custom_call_target="tpu_custom_call" | custom-call | flops 6710886400 | bytes 983040 | tf_op jit(solution)/shard_map/cross/pallas_call | solution.py:236
  80.0 0.7 copy-done.7
  80.8 9.4 %cross.5 = (f32[160,8,128]{2,1,0:T(8,128)}, f32[160,8,128]{2,1,0:T(8,128)}, bf16[2,160,8,128]{3,2,1,0:T(8,128)(2,1)}) custom-call(s32[6]{0:T(128)} %stack.31.place_ref, f32[3]{0:T(128)} %convert_divide_fusion.rest_0_, bf16[1,160,1024]{2,1,0:T(8,128)(2,1)} %get-tuple-element.10.rest_1_, bf16[1,160,1024]{2,1,0:T(8,128)(2,1)} %copy-done.7, ...), custom_call_target="tpu_custom_call" | custom-call | flops 6710886400 | bytes 983040 | tf_op jit(solution)/shard_map/cross/pallas_call | solution.py:236
  90.1 2.3 %collective-permute-done.10 = bf16[2,160,8,128]{3,2,1,0:T(8,128)(2,1)S(1)} collective-permute-done((bf16[2,160,8,128]{3,2,1,0:T(8,128)(2,1)}, bf16[2,160,8,128]{3,2,1,0:T(8,128)(2,1)S(1)}, u32[]{:S(2)}, u32[]{:S(2)}) %collective-permute-start.10) | collective-permute-done | bytes 655392 | tf_op jit(solution)/shard_map/ppermute | solution.py:322
  92.4 1.2 %fusion = bf16[160,8,128]{2,1,0:T(8,128)(2,1)S(1)} fusion(f32[160,8,128]{2,1,0:T(8,128)} %get-tuple-element.14, bf16[2,160,8,128]{3,2,1,0:T(8,128)(2,1)S(1)} %collective-permute-done.10), kind=kLoop, calls=%fused_computation.1 | loop fusion | flops 491520 | bytes 1310720 | tf_op jit(solution)/shard_map/convert_element_type | solution.py:323
  93.6 0.5 collective-permute-start.11
  94.1 9.3 %collective-permute-done.11 = bf16[160,8,128]{2,1,0:T(8,128)(2,1)S(1)} collective-permute-done((bf16[160,8,128]{2,1,0:T(8,128)(2,1)S(1)}, bf16[160,8,128]{2,1,0:T(8,128)(2,1)S(1)}, u32[]{:S(2)}, u32[]{:S(2)}) %collective-permute-start.11) | collective-permute-done | bytes 327712 | tf_op jit(solution)/shard_map/ppermute | solution.py:324
  103.4 2.0 %fusion.1 = f32[160,8,128]{2,1,0:T(8,128)} fusion(f32[160,8,128]{2,1,0:T(8,128)} %get-tuple-element.12, bf16[160,8,128]{2,1,0:T(8,128)(2,1)S(1)} %collective-permute-done.11, bf16[2,160,8,128]{3,2,1,0:T(8,128)(2,1)S(1)} %collective-permute-done.10), kind=kLoop, calls=%fused_computation.3 | loop fusion | flops 655360 | bytes 1966080 | tf_op jit(solution)/shard_map/add | solution.py:325
  (25 shorter events, 0.1 us)
Async XLA Ops:
  0.0 36.0 %collective-permute-start = (s32[1,4]{1,0:T(1,128)}, s32[1,4]{1,0:T(1,128)S(1)}, u32[]{:S(2)}, u32[]{:S(2)}) collective-permute-start(s32[1,4]{1,0:T(1,128)} %valid_ref.3), channel_id=1, source_target_pairs={{4,0},{8,4},{12,8},{16,12},{20,16},{24,20},{28,24},{5,1},{9,5},{13... | collective-permute-start | bytes 56 | tf_op jit(solution)/shard_map/ppermute | solution.py:287
  3.3 32.7 %collective-permute-start.1 = (s32[1,4]{1,0:T(1,128)}, s32[1,4]{1,0:T(1,128)S(1)}, u32[]{:S(2)}, u32[]{:S(2)}) collective-permute-start(s32[1,4]{1,0:T(1,128)} %valid_ref.3), channel_id=1, source_target_pairs={{8,0},{12,4},{16,8},{20,12},{24,16},{28,20},{9,1},{13,5},{17,9},{2... | collective-permute-start | bytes 56 | tf_op jit(solution)/shard_map/ppermute | solution.py:288
  16.3 17.1 %copy-start.5 = (s32[1,2]{1,0:T(1,128)S(1)}, s32[1,2]{1,0:T(1,128)}, u32[]{:S(2)}) copy-start(s32[1,2]{1,0:T(1,128)} %param.7) | copy-start | bytes 28
  16.4 19.7 %copy-start.4 = (s32[1,4]{1,0:T(1,128)S(1)}, s32[1,4]{1,0:T(1,128)}, u32[]{:S(2)}) copy-start(s32[1,4]{1,0:T(1,128)} %valid_ref.3) | copy-start | bytes 52
  16.4 22.5 %copy-start = (bf16[2,160,1024]{2,1,0:T(8,128)(2,1)S(1)}, bf16[2,160,1024]{2,1,0:T(8,128)(2,1)}, u32[]{:S(2)}) copy-start(bf16[2,160,1024]{2,1,0:T(8,128)(2,1)} %spectra.3.rest_0_) | copy-start | bytes 1966084
  16.4 22.5 %collective-permute-start.8 = (bf16[2,160,1024]{2,1,0:T(8,128)(2,1)}, bf16[2,160,1024]{2,1,0:T(8,128)(2,1)S(1)}, u32[]{:S(2)}, u32[]{:S(2)}) collective-permute-start(bf16[2,160,1024]{2,1,0:T(8,128)(2,1)} %spectra.3.rest_0_), channel_id=1, source_target_pairs={{8,0},{12,4},{16,8},{20,12},{24,16},{28,20},{9,1},{13,5},{17,9},{2... | collective-permute-start | bytes 1966088 | tf_op jit(solution)/shard_map/ppermute | solution.py:313
  29.6 11.8 %collective-permute-start.6 = (bf16[1,160,1024]{2,1,0:T(8,128)(2,1)}, bf16[1,160,1024]{2,1,0:T(8,128)(2,1)S(1)}, u32[]{:S(2)}, u32[]{:S(2)}) collective-permute-start(bf16[1,160,1024]{2,1,0:T(8,128)(2,1)} %get-tuple-element.11.rest_0_), channel_id=1, source_target_pairs={{8,0},{12,4},{16,8},{20,12},{24,16},{28,20},{9,1},{13,5},{17,9},{2... | collective-permute-start | bytes 983048 | tf_op jit(solution)/shard_map/ppermute | solution.py:313
  31.5 15.1 %collective-permute-start.4 = (bf16[1,160,1024]{2,1,0:T(8,128)(2,1)}, bf16[1,160,1024]{2,1,0:T(8,128)(2,1)S(1)}, u32[]{:S(2)}, u32[]{:S(2)}) collective-permute-start(bf16[1,160,1024]{2,1,0:T(8,128)(2,1)} %get-tuple-element.10.rest_1_), channel_id=1, source_target_pairs={{8,0},{12,4},{16,8},{20,12},{24,16},{28,20},{9,1},{13,5},{17,9},{2... | collective-permute-start | bytes 983048 | tf_op jit(solution)/shard_map/ppermute | solution.py:313
  36.2 1.2 %collective-permute-start.2 = (s32[3]{0:T(128)S(1)}, s32[3]{0:T(128)S(1)}, u32[]{:S(2)}, u32[]{:S(2)}) collective-permute-start(s32[3]{0:T(128)S(1)} %fusion.2), channel_id=1, source_target_pairs={{0,1},{1,0},{2,3},{3,2},{4,5},{5,4},{6,7},{7,6},{8,9},{9,8},{10,11... | collective-permute-start | bytes 44 | tf_op jit(solution)/shard_map/ppermute | solution.py:292
  37.4 3.5 %collective-permute-start.3 = (s32[3]{0:T(128)S(1)}, s32[3]{0:T(128)S(1)}, u32[]{:S(2)}, u32[]{:S(2)}) collective-permute-start(s32[3]{0:T(128)S(1)} %add.21), channel_id=1, source_target_pairs={{0,2},{1,3},{2,0},{3,1},{4,6},{5,7},{6,4},{7,5},{8,10},{9,11},{10,... | collective-permute-start | bytes 44 | tf_op jit(solution)/shard_map/ppermute | solution.py:293
  38.9 17.8 %copy-start.1 = (bf16[2,160,1024]{2,1,0:T(8,128)(2,1)}, bf16[2,160,1024]{2,1,0:T(8,128)(2,1)S(1)}, u32[]{:S(2)}) copy-start(bf16[2,160,1024]{2,1,0:T(8,128)(2,1)S(1)} %collective-permute-done.8.rest_2_) | copy-start | bytes 1966084
  39.0 17.7 %collective-permute-start.9 = (bf16[2,160,1024]{2,1,0:T(8,128)(2,1)S(1)}, bf16[2,160,1024]{2,1,0:T(8,128)(2,1)S(1)}, u32[]{:S(2)}, u32[]{:S(2)}) collective-permute-start(bf16[2,160,1024]{2,1,0:T(8,128)(2,1)S(1)} %broadcast_select_fusion), channel_id=1, source_target_pairs={{4,0},{0,4},{12,8},{8,12},{20,16},{16,20},{28,24},{24,28},{5,1},{1... | collective-permute-start | bytes 1966088 | tf_op jit(solution)/shard_map/ppermute | solution.py:317
  41.5 28.9 %copy-start.3 = (bf16[1,160,1024]{2,1,0:T(8,128)(2,1)}, bf16[1,160,1024]{2,1,0:T(8,128)(2,1)S(1)}, u32[]{:S(2)}) copy-start(bf16[1,160,1024]{2,1,0:T(8,128)(2,1)S(1)} %collective-permute-done.6.rest_2_) | copy-start | bytes 983044
  41.5 28.8 %collective-permute-start.7 = (bf16[1,160,1024]{2,1,0:T(8,128)(2,1)S(1)}, bf16[1,160,1024]{2,1,0:T(8,128)(2,1)S(1)}, u32[]{:S(2)}, u32[]{:S(2)}) collective-permute-start(bf16[1,160,1024]{2,1,0:T(8,128)(2,1)S(1)} %broadcast_select_fusion.1), channel_id=1, source_target_pairs={{4,0},{0,4},{12,8},{8,12},{20,16},{16,20},{28,24},{24,28},{5,1},{1... | collective-permute-start | bytes 983048 | tf_op jit(solution)/shard_map/ppermute | solution.py:317
  46.6 23.7 %copy-start.2 = (bf16[1,160,1024]{2,1,0:T(8,128)(2,1)}, bf16[1,160,1024]{2,1,0:T(8,128)(2,1)S(1)}, u32[]{:S(2)}) copy-start(bf16[1,160,1024]{2,1,0:T(8,128)(2,1)S(1)} %collective-permute-done.4.rest_3_) | copy-start | bytes 983044
  46.7 33.4 %collective-permute-start.5 = (bf16[1,160,1024]{2,1,0:T(8,128)(2,1)S(1)}, bf16[1,160,1024]{2,1,0:T(8,128)(2,1)S(1)}, u32[]{:S(2)}, u32[]{:S(2)}) collective-permute-start(bf16[1,160,1024]{2,1,0:T(8,128)(2,1)S(1)} %broadcast_select_fusion.2), channel_id=1, source_target_pairs={{4,0},{0,4},{12,8},{8,12},{20,16},{16,20},{28,24},{24,28},{5,1},{1... | collective-permute-start | bytes 983048 | tf_op jit(solution)/shard_map/ppermute | solution.py:317
  56.6 0.9 copy-start.6
  70.3 0.7 copy-start.8
  80.0 0.7 copy-start.7
  90.1 2.3 %collective-permute-start.10 = (bf16[2,160,8,128]{3,2,1,0:T(8,128)(2,1)}, bf16[2,160,8,128]{3,2,1,0:T(8,128)(2,1)S(1)}, u32[]{:S(2)}, u32[]{:S(2)}) collective-permute-start(bf16[2,160,8,128]{3,2,1,0:T(8,128)(2,1)} %get-tuple-element.13), channel_id=1, source_target_pairs={{0,1},{1,0},{2,3},{3,2},{4,5},{5,4},{6,7},{7,6},{8,9},{9,8},{10,11... | collective-permute-start | bytes 1966088 | tf_op jit(solution)/shard_map/ppermute | solution.py:322
  93.6 9.8 %collective-permute-start.11 = (bf16[160,8,128]{2,1,0:T(8,128)(2,1)S(1)}, bf16[160,8,128]{2,1,0:T(8,128)(2,1)S(1)}, u32[]{:S(2)}, u32[]{:S(2)}) collective-permute-start(bf16[160,8,128]{2,1,0:T(8,128)(2,1)S(1)} %fusion), channel_id=1, source_target_pairs={{0,2},{1,3},{2,0},{3,1},{4,6},{5,7},{6,4},{7,5},{8,10},{9,11},{10,... | collective-permute-start | bytes 983048 | tf_op jit(solution)/shard_map/ppermute | solution.py:324

commit v4 on v3

--- a/solution.py
+++ b/solution.py
@@ -35,7 +35,10 @@
     shifts = (np.arange(lags) - lags // 2 + samples) % samples
     phase = (freqs * shifts[None, :] % samples) * (2.0 * math.pi / samples)
     factor = 1.0 / math.sqrt(bins)
-    return (np.concatenate([np.cos(phase), -np.sin(phase)], axis=0) * factor).astype(jnp.bfloat16)
+    parts = np.stack([np.cos(phase), -np.sin(phase)]) * factor
+    tiles = parts.reshape(2, bins // 128, 128, lags).transpose(1, 0, 2, 3)
+    tiles = tiles.reshape(bins // 128, 256, lags)
+    return np.pad(tiles, ((0, 0), (0, 0), (0, 256 - lags))).astype(jnp.bfloat16)
 
 
 def spectra_kernel(valid_ref, first_ref, second_ref, table_ref, *rest, first_seg):
@@ -124,45 +127,62 @@
 
 CH_TILE = 16
 TILES = 2
-
-
-def cross_kernel(place_ref, *rest, first, last):
+WINDOW = 13
+
+
+def cross_kernel(place_ref, *rest, specs, first, last):
     if last:
         scale_ref, *rest = rest
     own_ref, next_ref, far_ref, lag_ref, *rest = rest
     if not first:
         before_ref, *rest = rest
     if last:
-        keep_ref, other_ref, send_ref, wide, mixed, turned = rest
+        keep_ref, other_ref, send_ref, wide, turned = rest
     else:
-        out_ref, wide, mixed = rest
+        out_ref, wide = rest
     segs, channels, columns = own_ref.shape
     bins = columns // 2
     lane_tiles = bins // 128
     lowest = place_ref[0]
+    origin = lowest // CH_TILE * CH_TILE
     step = pl.program_id(0)
 
     @pl.when(step == 0)
     def _():
-        for hop, ref in enumerate((own_ref, next_ref, far_ref)):
-            for seg in range(segs):
-                for lane in range(2 * lane_tiles):
-                    block = ref[seg, :, lane * 128 : lane * 128 + 128]
-                    wide[seg * 2 * lane_tiles + lane, pl.ds(hop * channels, channels), :] = (
-                        block.astype(jnp.float32)
-                    )
-
-    for tile in range(TILES):
+        def one_window(index, carry):
+            row = origin + index * CH_TILE
+            into = pl.ds(pl.multiple_of(index * CH_TILE, CH_TILE), CH_TILE)
+            for hop, ref in enumerate((own_ref, next_ref, far_ref)):
+
+                @pl.when((row >= hop * channels) & (row < (hop + 1) * channels))
+                def _():
+                    rows = pl.ds(pl.multiple_of(row - hop * channels, CH_TILE), CH_TILE)
+                    for seg in range(segs):
+                        for lane in range(2 * lane_tiles):
+                            block = ref[seg, rows, lane * 128 : lane * 128 + 128]
+                            wide[seg * 2 * lane_tiles + lane, into, :] = block.astype(jnp.float32)
+
+            return carry
+
+        lax.fori_loop(0, WINDOW, one_window, 0)
+
+    def all_tiles(*sums):
+        for tile in range(TILES):
+            one_tile(tile, sums)
+
+    def one_tile(tile, sums):
         base = pl.multiple_of((step * TILES + tile) * CH_TILE, CH_TILE)
         for lane in range(lane_tiles):
+            for unit in range(2):
+                pltpu.matmul_push_rhs(lag_ref[lane], 0, unit)
             mine = {}
-            for half in range(2):
-                for seg in range(segs):
-                    for part in range(2):
-                        slab = (seg * 2 + part) * lane_tiles + lane
-                        mine[half, seg, part] = wide[slab, pl.ds(base + 8 * half, 8), :]
+            for seg in range(segs):
+                for part in range(2):
+                    at = (part * lane_tiles + lane) * 128
+                    block = own_ref[seg, pl.ds(base, CH_TILE), at : at + 128].astype(jnp.float32)
+                    mine[0, seg, part], mine[1, seg, part] = block[:8], block[8:]
             for pair in range(PAIRS):
-                start = base + lowest + place_ref[1 + pair // 8] + pair % 8
+                start = base + (lowest - origin) + place_ref[1 + pair // 8] + pair % 8
                 reals, imags = [], []
                 for half in range(2):
                     real = imag = None
@@ -178,22 +198,23 @@
                         imag = im if imag is None else imag + im
                     reals.append(real)
                     imags.append(imag)
-                rows = slice(pair * CH_TILE, pair * CH_TILE + CH_TILE)
-                at = lane * 128
-                mixed[tile, rows, at : at + 128] = jnp.concatenate(reals, axis=0).astype(
-                    jnp.bfloat16
+                mixed = [
+                    jnp.concatenate(part, axis=0).astype(jnp.bfloat16) for part in (reals, imags)
+                ]
+                pltpu.matmul_acc_lhs(
+                    sums[pair],
+                    jnp.concatenate(mixed, axis=1),
+                    load_staged_rhs=0 if pair < 2 else None,
                 )
-                mixed[tile, rows, bins + at : bins + at + 128] = jnp.concatenate(
-                    imags, axis=0
-                ).astype(jnp.bfloat16)
-        lagged = jnp.dot(mixed[tile], lag_ref[...], preferred_element_type=jnp.float32)
-        if not first:
-            lagged += before_ref[tile]
-        if not last:
-            out_ref[tile] = lagged
-            continue
         near = lax.broadcasted_iota(jnp.int32, (CH_TILE, LAGS), 0)
         for pair in range(PAIRS):
+            rows = slice(pair * CH_TILE, pair * CH_TILE + CH_TILE)
+            lagged = pltpu.matmul_pop(sums[pair])[:, :LAGS]
+            if not first:
+                lagged += before_ref[tile, rows]
+            if not last:
+                out_ref[tile, rows] = lagged
+                continue
             offset = lowest + place_ref[1 + pair // 8] + pair % 8
             partner = near + (base + offset)
             scale = jnp.where(
@@ -202,28 +223,25 @@
                 jnp.where(partner < 2 * channels, scale_ref[1], scale_ref[2]),
             )
             inside = jnp.where(offset < place_ref[5], 1.0, 0.0)
-            rows = slice(pair * CH_TILE, pair * CH_TILE + CH_TILE)
-            turned[pair // 8, pl.ds(pair % 8, CH_TILE, stride=8), :] = (
-                lagged[rows] * (scale * inside)
-            )
-        shape = (CH_TILE, 8, LAGS)
-        rows = slice(tile * CH_TILE, tile * CH_TILE + CH_TILE)
-        keep_ref[rows] = turned[0].reshape(shape)
-        other_ref[rows] = turned[1].reshape(shape)
-        for side in range(2):
-            send_ref[side, rows] = turned[2 + side].reshape(shape).astype(jnp.bfloat16)
-
-
-def correlated(places, scales, own, following, far, lag_table, before=None, last=False):
+            turned[pair // 8, pl.ds(pair % 8, CH_TILE, stride=8), :] = lagged * (scale * inside)
+        if last:
+            shape = (CH_TILE, 8, LAGS)
+            rows = slice(tile * CH_TILE, tile * CH_TILE + CH_TILE)
+            keep_ref[rows] = turned[0].reshape(shape)
+            other_ref[rows] = turned[1].reshape(shape)
+            for side in range(2):
+                send_ref[side, rows] = turned[2 + side].reshape(shape).astype(jnp.bfloat16)
+
+    pl.run_scoped(all_tiles, *specs)
+
+
+def correlated(mesh, places, scales, own, following, far, lag_table, before=None, last=False):
     segs, channels, columns = own.shape
     whole = pl.BlockSpec((segs, channels, columns), lambda i, *_: (0, 0, 0))
     rows = TILES * CH_TILE
     raw = pl.BlockSpec((TILES, PAIRS * CH_TILE, LAGS), lambda i, *_: (i, 0, 0))
     raw_shape = jax.ShapeDtypeStruct((channels // CH_TILE, PAIRS * CH_TILE, LAGS), jnp.float32)
-    scratch = [
-        pltpu.VMEM((segs * columns // 128, (REACH + 1) * channels, 128), jnp.float32),
-        pltpu.VMEM((TILES, CH_TILE * PAIRS, columns), jnp.bfloat16),
-    ]
+    scratch = [pltpu.VMEM((segs * columns // 128, WINDOW * CH_TILE, 128), jnp.float32)]
     out_specs, out_shape = raw, raw_shape
     if last:
         kept = pl.BlockSpec((rows, 8, LAGS), lambda i, *_: (i, 0, 0))
@@ -233,8 +251,10 @@
         sent_shape = jax.ShapeDtypeStruct((2, channels, 8, LAGS), jnp.bfloat16)
         out_shape = [kept_shape, kept_shape, sent_shape]
         scratch.append(pltpu.VMEM((4, CH_TILE * 8, LAGS), jnp.float32))
+    with jax.sharding.use_abstract_mesh(mesh.abstract_mesh):
+        specs = [pltpu.ACC(pair % 2)((CH_TILE, 256), jnp.float32) for pair in range(PAIRS)]
     return pl.pallas_call(
-        functools.partial(cross_kernel, first=before is None, last=last),
+        functools.partial(cross_kernel, specs=specs, first=before is None, last=last),
         name="cross",
         grid_spec=pltpu.PrefetchScalarGridSpec(
             num_scalar_prefetch=2 if last else 1,
@@ -243,7 +263,7 @@
                 whole,
                 whole,
                 whole,
-                pl.BlockSpec(lag_table.shape, lambda i, *_: (0, 0)),
+                pl.BlockSpec(lag_table.shape, lambda i, *_: (0, 0, 0)),
                 *([] if before is None else [raw]),
             ],
             out_specs=out_specs,
@@ -267,7 +287,7 @@
     )
 
 
-def shards(records, valid_mask, band_limits):
+def shards(mesh, records, valid_mask, band_limits):
     channels, segs, samples = records.shape
     blocks = lax.axis_size("chan")
     block = lax.axis_index("chan")
@@ -305,18 +325,14 @@
 
     lag_table = jnp.asarray(lag_table_of(samples, BINS, LAGS))
     table = jnp.asarray(dft_table_of(samples, BINS))
-    half = segs // 2
-    whites = [
-        *whitened(records, valid_mask, table, 0, 1, half),
-        *whitened(records, valid_mask, table, half, half, 1),
-    ]
+    whites = whitened(records, valid_mask, table, 0, segs, 1)
     fars = [lax.ppermute(white, "chan", hop_far) for white in whites]
     before = None
     for at, (white, far) in enumerate(zip(whites, fars)):
         passed = jnp.where(block % 2 == 0, far, white)
         following = lax.ppermute(passed, "chan", pair_swap)
         before = correlated(
-            places, scales, white, following, far, lag_table, before, last=at == len(whites) - 1
+            mesh, places, scales, white, following, far, lag_table, before, last=at == len(whites) - 1
         )
     keep, other, send = before
     got = lax.ppermute(send, "tm", core_swap)
@@ -328,5 +344,9 @@
 def solution(mesh):
     placed = (P("chan", "tm", None), P("chan", "tm"), P("chan", None))
     return jax.shard_map(
-        shards, mesh=mesh, in_specs=placed, out_specs=P("chan", "tm", None), check_vma=False
+        functools.partial(shards, mesh),
+        mesh=mesh,
+        in_specs=placed,
+        out_specs=P("chan", "tm", None),
+        check_vma=False,
     )

time: 106 us -> 103 us (0.972)
  the two profiles are of different devices: /device:TPU:24 before, /device:TPU:0 now
where the time goes in v4:
time: 103 us; the launch traced here: 102 us
  Pallas kernels  44.3 us (43%)
  waiting for transfers between devices  29.3 us (28%)
  starting transfers between devices  19.3 us (19%)
  local copies, waits for them, and re-layouts  5.37 us (5%)
  other arithmetic  4 us (4%)
    pallas_call x4, Pallas kernels, correlated(): pl.pallas_call(functools.partial(cross_kernel, specs=specs, first=before...  32.1 us
    ppermute x4, waiting for transfers between devices, shards(): fars = [lax.ppermute(white, 'chan', hop_far) for white in whites]  16.7 us
    pallas_call x1, Pallas kernels, whitened(): pl.pallas_call(functools.partial(spectra_kernel, first_seg=first_seg), na...  12.2 us
    ppermute x1, waiting for transfers between devices, shards(): passed = lax.ppermute(passing, 'tm', side_swap)  8.01 us
    ppermute x4, starting transfers between devices, shards(): following = lax.ppermute(passed, 'chan', pair_swap)  6.12 us
    ppermute x4, starting transfers between devices, shards(): fars = [lax.ppermute(white, 'chan', hop_far) for white in whites]  5.28 us
    unnamed x22, local copies, waits for them, and re-layouts  2.92 us
    ppermute x1, starting transfers between devices, shards(): counts += lax.ppermute(counts, 'tm', side_swap)  2.82 us
  transfers between devices with their start and end apart: 14, of which 8 were waited for; matrix products, arithmetic and copies ran while one was open for 3% of the time, Pallas kernels for 35%

profile of v4, /device:TPU:0, one launch (start us, length us, event | category | flops | bytes accessed | tf_op | source)
XLA Modules:
  0.0 102.5 jit_solution(4353170851094360575)
XLA Ops:
  0.0 1.4 %collective-permute-start = (s32[1,4]{1,0:T(1,128)}, s32[1,4]{1,0:T(1,128)S(1)}, u32[]{:S(2)}, u32[]{:S(2)}) collective-permute-start(s32[1,4]{1,0:T(1,128)} %valid_ref.1), channel_id=1, source_target_pairs={{4,0},{8,4},{12,8},{16,12},{20,16},{24,20},{28,24},{5,1},{9,5},{13... | collective-permute-start | bytes 56 | tf_op jit(solution)/shard_map/ppermute | solution.py:307
  1.4 1.3 %collective-permute-start.1 = (s32[1,4]{1,0:T(1,128)}, s32[1,4]{1,0:T(1,128)S(1)}, u32[]{:S(2)}, u32[]{:S(2)}) collective-permute-start(s32[1,4]{1,0:T(1,128)} %valid_ref.1), channel_id=1, source_target_pairs={{8,0},{12,4},{16,8},{20,12},{24,16},{28,20},{9,1},{13,5},{17,9},{2... | collective-permute-start | bytes 56 | tf_op jit(solution)/shard_map/ppermute | solution.py:308
  2.7 12.2 %spectra.1 = (bf16[1,160,1024]{2,1,0:T(8,128)(2,1)}, bf16[1,160,1024]{2,1,0:T(8,128)(2,1)}, bf16[1,160,1024]{2,1,0:T(8,128)(2,1)}, bf16[1,160,1024]{2,1,0:T(8,128)(2,1)}) custom-call(s32[1,4]{1,0:T(1,128)} %valid_ref.1, bf16[160,4,7680]{2,1,0:T(4,128)(2,1)} %second_ref.1, bf16[160,4,7680]{2,1,0:T(4,128)(2,1)} %second_ref.1, ...), custom_call_target="tpu_custom_call" | custom-call | flops 10066329600 | bytes 17694720 | tf_op jit(solution)/shard_map/spectra/pallas_call | solution.py:103
  15.0 1.4 %collective-permute-start.10 = (bf16[1,160,1024]{2,1,0:T(8,128)(2,1)}, bf16[1,160,1024]{2,1,0:T(8,128)(2,1)S(1)}, u32[]{:S(2)}, u32[]{:S(2)}) collective-permute-start(bf16[1,160,1024]{2,1,0:T(8,128)(2,1)} %get-tuple-element.15.rest_0_), channel_id=1, source_target_pairs={{8,0},{12,4},{16,8},{20,12},{24,16},{28,20},{9,1},{13,5},{17,9},{2... | collective-permute-start | bytes 983048 | tf_op jit(solution)/shard_map/ppermute | solution.py:329
  16.4 1.3 %collective-permute-start.8 = (bf16[1,160,1024]{2,1,0:T(8,128)(2,1)}, bf16[1,160,1024]{2,1,0:T(8,128)(2,1)S(1)}, u32[]{:S(2)}, u32[]{:S(2)}) collective-permute-start(bf16[1,160,1024]{2,1,0:T(8,128)(2,1)} %get-tuple-element.14.rest_0_), channel_id=1, source_target_pairs={{8,0},{12,4},{16,8},{20,12},{24,16},{28,20},{9,1},{13,5},{17,9},{2... | collective-permute-start | bytes 983048 | tf_op jit(solution)/shard_map/ppermute | solution.py:329
  17.7 1.3 %collective-permute-start.6 = (bf16[1,160,1024]{2,1,0:T(8,128)(2,1)}, bf16[1,160,1024]{2,1,0:T(8,128)(2,1)S(1)}, u32[]{:S(2)}, u32[]{:S(2)}) collective-permute-start(bf16[1,160,1024]{2,1,0:T(8,128)(2,1)} %get-tuple-element.13.rest_0_), channel_id=1, source_target_pairs={{8,0},{12,4},{16,8},{20,12},{24,16},{28,20},{9,1},{13,5},{17,9},{2... | collective-permute-start | bytes 983048 | tf_op jit(solution)/shard_map/ppermute | solution.py:329
  19.6 1.9 %stack.31.place_ref = s32[6]{0:T(128)} concatenate(s32[1]{0:T(128)} %bitcast, s32[1]{0:T(128)} %bitcast.1, s32[1]{0:T(128)} %bitcast.2, s32[1]{0:T(128)} %bitcast.3, s32[1]{0:T(128)} %bitcast.4, s32[1]{0:T(128)} %bitcast.5), dimensions={0} | concatenate | bytes 48 | tf_op jit(solution)/shard_map/stack | solution.py:315
  21.5 1.3 %collective-permute-start.4 = (bf16[1,160,1024]{2,1,0:T(8,128)(2,1)}, bf16[1,160,1024]{2,1,0:T(8,128)(2,1)S(1)}, u32[]{:S(2)}, u32[]{:S(2)}) collective-permute-start(bf16[1,160,1024]{2,1,0:T(8,128)(2,1)} %get-tuple-element.12.rest_1_), channel_id=1, source_target_pairs={{8,0},{12,4},{16,8},{20,12},{24,16},{28,20},{9,1},{13,5},{17,9},{2... | collective-permute-start | bytes 983048 | tf_op jit(solution)/shard_map/ppermute | solution.py:329
  23.5 0.8 collective-permute-done.2
  24.3 2.8 %collective-permute-start.3 = (s32[3]{0:T(128)S(1)}, s32[3]{0:T(128)S(1)}, u32[]{:S(2)}, u32[]{:S(2)}) collective-permute-start(s32[3]{0:T(128)S(1)} %add.22), channel_id=1, source_target_pairs={{0,2},{1,3},{2,0},{3,1},{4,6},{5,7},{6,4},{7,5},{8,10},{9,11},{10,... | collective-permute-start | bytes 44 | tf_op jit(solution)/shard_map/ppermute | solution.py:313
  27.1 1.5 %collective-permute-done.3 = s32[3]{0:T(128)S(1)} collective-permute-done((s32[3]{0:T(128)S(1)}, s32[3]{0:T(128)S(1)}, u32[]{:S(2)}, u32[]{:S(2)}) %collective-permute-start.3) | collective-permute-done | bytes 44 | tf_op jit(solution)/shard_map/ppermute | solution.py:313
  29.1 2.3 %collective-permute-done.10.rest_2_ = bf16[1,160,1024]{2,1,0:T(8,128)(2,1)S(1)} collective-permute-done((bf16[1,160,1024]{2,1,0:T(8,128)(2,1)}, bf16[1,160,1024]{2,1,0:T(8,128)(2,1)S(1)}, u32[]{:S(2)}, u32[]{:S(2)}) %collective-permute-start.10) | collective-permute-done | bytes 327712 | tf_op jit(solution)/shard_map/ppermute | solution.py:329
  31.5 1.8 %collective-permute-start.11 = (bf16[1,160,1024]{2,1,0:T(8,128)(2,1)S(1)}, bf16[1,160,1024]{2,1,0:T(8,128)(2,1)S(1)}, u32[]{:S(2)}, u32[]{:S(2)}) collective-permute-start(bf16[1,160,1024]{2,1,0:T(8,128)(2,1)S(1)} %broadcast_select_fusion), channel_id=1, source_target_pairs={{4,0},{0,4},{12,8},{8,12},{20,16},{16,20},{28,24},{24,28},{5,1},{1... | collective-permute-start | bytes 983048 | tf_op jit(solution)/shard_map/ppermute | solution.py:333
  33.3 5.2 %collective-permute-done.8.rest_2_ = bf16[1,160,1024]{2,1,0:T(8,128)(2,1)S(1)} collective-permute-done((bf16[1,160,1024]{2,1,0:T(8,128)(2,1)}, bf16[1,160,1024]{2,1,0:T(8,128)(2,1)S(1)}, u32[]{:S(2)}, u32[]{:S(2)}) %collective-permute-start.8) | collective-permute-done | bytes 327712 | tf_op jit(solution)/shard_map/ppermute | solution.py:329
  38.5 1.8 %collective-permute-start.9 = (bf16[1,160,1024]{2,1,0:T(8,128)(2,1)S(1)}, bf16[1,160,1024]{2,1,0:T(8,128)(2,1)S(1)}, u32[]{:S(2)}, u32[]{:S(2)}) collective-permute-start(bf16[1,160,1024]{2,1,0:T(8,128)(2,1)S(1)} %broadcast_select_fusion.1), channel_id=1, source_target_pairs={{4,0},{0,4},{12,8},{8,12},{20,16},{16,20},{28,24},{24,28},{5,1},{1... | collective-permute-start | bytes 983048 | tf_op jit(solution)/shard_map/ppermute | solution.py:333
  40.3 5.2 %collective-permute-done.6.rest_2_ = bf16[1,160,1024]{2,1,0:T(8,128)(2,1)S(1)} collective-permute-done((bf16[1,160,1024]{2,1,0:T(8,128)(2,1)}, bf16[1,160,1024]{2,1,0:T(8,128)(2,1)S(1)}, u32[]{:S(2)}, u32[]{:S(2)}) %collective-permute-start.6) | collective-permute-done | bytes 327712 | tf_op jit(solution)/shard_map/ppermute | solution.py:329
  45.5 1.8 %collective-permute-start.7 = (bf16[1,160,1024]{2,1,0:T(8,128)(2,1)S(1)}, bf16[1,160,1024]{2,1,0:T(8,128)(2,1)S(1)}, u32[]{:S(2)}, u32[]{:S(2)}) collective-permute-start(bf16[1,160,1024]{2,1,0:T(8,128)(2,1)S(1)} %broadcast_select_fusion.2), channel_id=1, source_target_pairs={{4,0},{0,4},{12,8},{8,12},{20,16},{16,20},{28,24},{24,28},{5,1},{1... | collective-permute-start | bytes 983048 | tf_op jit(solution)/shard_map/ppermute | solution.py:333
  47.3 4.0 %collective-permute-done.4.rest_3_ = bf16[1,160,1024]{2,1,0:T(8,128)(2,1)S(1)} collective-permute-done((bf16[1,160,1024]{2,1,0:T(8,128)(2,1)}, bf16[1,160,1024]{2,1,0:T(8,128)(2,1)S(1)}, u32[]{:S(2)}, u32[]{:S(2)}) %collective-permute-start.4) | collective-permute-done | bytes 327712 | tf_op jit(solution)/shard_map/ppermute | solution.py:329
  51.4 0.7 collective-permute-start.5
  52.1 0.7 copy-done.9
  52.8 7.3 %cross.4.rest_4_ = f32[10,512,128]{2,1,0:T(8,128)} custom-call(s32[6]{0:T(128)} %stack.31.place_ref, bf16[1,160,1024]{2,1,0:T(8,128)(2,1)} %get-tuple-element.15.rest_0_, bf16[1,160,1024]{2,1,0:T(8,128)(2,1)} %copy-done.9, bf16[1,160,1024]{2,1,0:T(8,128)(2,1)} %copy-done.3, bf16[4,256,256]{2,1,0:T(8,128)(2,1)} %constant.41.clone.rest_3_.rest_4_), custom_call_target="tpu_custom_call" | custom-call | flops 6710886400 | bytes 983040 | tf_op jit(solution)/shard_map/cross/pallas_call | solution.py:256
  60.2 0.7 copy-done.10
  60.9 8.3 %cross.5.rest_4_ = f32[10,512,128]{2,1,0:T(8,128)} custom-call(s32[6]{0:T(128)} %stack.31.place_ref, bf16[1,160,1024]{2,1,0:T(8,128)(2,1)} %get-tuple-element.14.rest_0_, bf16[1,160,1024]{2,1,0:T(8,128)(2,1)} %copy-done.10, bf16[1,160,1024]{2,1,0:T(8,128)(2,1)} %copy-done.2, bf16[4,256,256]{2,1,0:T(8,128)(2,1)} %constant.41.clone.rest_3_.rest_4_, ...), custom_call_target="tpu_custom_call" | custom-call | flops 6710886400 | bytes 983040 | tf_op jit(solution)/shard_map/cross/pallas_call | solution.py:256
  69.2 0.7 copy-done.8
  70.0 8.3 %cross.6.rest_5_ = f32[10,512,128]{2,1,0:T(8,128)} custom-call(s32[6]{0:T(128)} %stack.31.place_ref, bf16[1,160,1024]{2,1,0:T(8,128)(2,1)} %get-tuple-element.13.rest_0_, bf16[1,160,1024]{2,1,0:T(8,128)(2,1)} %copy-done.8, bf16[1,160,1024]{2,1,0:T(8,128)(2,1)} %copy-done.1, bf16[4,256,256]{2,1,0:T(8,128)(2,1)} %constant.41.clone.rest_3_.rest_4_, ...), custom_call_target="tpu_custom_call" | custom-call | flops 6710886400 | bytes 983040 | tf_op jit(solution)/shard_map/cross/pallas_call | solution.py:256
  78.2 0.7 copy-done.7
  79.0 8.2 %cross.7 = (f32[160,8,128]{2,1,0:T(8,128)}, f32[160,8,128]{2,1,0:T(8,128)}, bf16[2,160,8,128]{3,2,1,0:T(8,128)(2,1)}) custom-call(s32[6]{0:T(128)} %stack.31.place_ref, f32[3]{0:T(128)} %convert_divide_fusion.rest_0_, bf16[1,160,1024]{2,1,0:T(8,128)(2,1)} %get-tuple-element.12.rest_1_, bf16[1,160,1024]{2,1,0:T(8,128)(2,1)} %copy-done.7, ...), custom_call_target="tpu_custom_call" | custom-call | flops 6710886400 | bytes 983040 | tf_op jit(solution)/shard_map/cross/pallas_call | solution.py:256
  87.2 2.3 %collective-permute-done.12 = bf16[2,160,8,128]{3,2,1,0:T(8,128)(2,1)S(1)} collective-permute-done((bf16[2,160,8,128]{3,2,1,0:T(8,128)(2,1)}, bf16[2,160,8,128]{3,2,1,0:T(8,128)(2,1)S(1)}, u32[]{:S(2)}, u32[]{:S(2)}) %collective-permute-start.12) | collective-permute-done | bytes 655392 | tf_op jit(solution)/shard_map/ppermute | solution.py:338
  89.5 1.2 %fusion = bf16[160,8,128]{2,1,0:T(8,128)(2,1)S(1)} fusion(f32[160,8,128]{2,1,0:T(8,128)} %get-tuple-element.18, bf16[2,160,8,128]{3,2,1,0:T(8,128)(2,1)S(1)} %collective-permute-done.12), kind=kLoop, calls=%fused_computation.1 | loop fusion | flops 491520 | bytes 1310720 | tf_op jit(solution)/shard_map/convert_element_type | solution.py:339
  90.6 1.8 %collective-permute-start.13 = (bf16[160,8,128]{2,1,0:T(8,128)(2,1)S(1)}, bf16[160,8,128]{2,1,0:T(8,128)(2,1)S(1)}, u32[]{:S(2)}, u32[]{:S(2)}) collective-permute-start(bf16[160,8,128]{2,1,0:T(8,128)(2,1)S(1)} %fusion), channel_id=1, source_target_pairs={{0,2},{1,3},{2,0},{3,1},{4,6},{5,7},{6,4},{7,5},{8,10},{9,11},{10,... | collective-permute-start | bytes 983048 | tf_op jit(solution)/shard_map/ppermute | solution.py:340
  92.5 8.0 %collective-permute-done.13 = bf16[160,8,128]{2,1,0:T(8,128)(2,1)S(1)} collective-permute-done((bf16[160,8,128]{2,1,0:T(8,128)(2,1)S(1)}, bf16[160,8,128]{2,1,0:T(8,128)(2,1)S(1)}, u32[]{:S(2)}, u32[]{:S(2)}) %collective-permute-start.13) | collective-permute-done | bytes 327712 | tf_op jit(solution)/shard_map/ppermute | solution.py:340
  100.5 2.0 %fusion.1 = f32[160,8,128]{2,1,0:T(8,128)} fusion(f32[160,8,128]{2,1,0:T(8,128)} %get-tuple-element.16, bf16[160,8,128]{2,1,0:T(8,128)(2,1)S(1)} %collective-permute-done.13, bf16[2,160,8,128]{3,2,1,0:T(8,128)(2,1)S(1)} %collective-permute-done.12), kind=kLoop, calls=%fused_computation.3 | loop fusion | flops 655360 | bytes 1966080 | tf_op jit(solution)/shard_map/add | solution.py:341
  (34 shorter events, 2.0 us)
Async XLA Ops:
  0.0 22.8 %copy-start.5 = (s32[1,4]{1,0:T(1,128)S(1)}, s32[1,4]{1,0:T(1,128)}, u32[]{:S(2)}) copy-start(s32[1,4]{1,0:T(1,128)} %valid_ref.1) | copy-start | bytes 52
  0.0 19.0 %copy-start.6 = (s32[1,2]{1,0:T(1,128)S(1)}, s32[1,2]{1,0:T(1,128)}, u32[]{:S(2)}) copy-start(s32[1,2]{1,0:T(1,128)} %param.7) | copy-start | bytes 28
  0.0 21.5 %collective-permute-start = (s32[1,4]{1,0:T(1,128)}, s32[1,4]{1,0:T(1,128)S(1)}, u32[]{:S(2)}, u32[]{:S(2)}) collective-permute-start(s32[1,4]{1,0:T(1,128)} %valid_ref.1), channel_id=1, source_target_pairs={{4,0},{8,4},{12,8},{16,12},{20,16},{24,20},{28,24},{5,1},{9,5},{13... | collective-permute-start | bytes 56 | tf_op jit(solution)/shard_map/ppermute | solution.py:307
  1.4 21.3 %collective-permute-start.1 = (s32[1,4]{1,0:T(1,128)}, s32[1,4]{1,0:T(1,128)S(1)}, u32[]{:S(2)}, u32[]{:S(2)}) collective-permute-start(s32[1,4]{1,0:T(1,128)} %valid_ref.1), channel_id=1, source_target_pairs={{8,0},{12,4},{16,8},{20,12},{24,16},{28,20},{9,1},{13,5},{17,9},{2... | collective-permute-start | bytes 56 | tf_op jit(solution)/shard_map/ppermute | solution.py:308
  15.0 36.4 %copy-start = (bf16[1,160,1024]{2,1,0:T(8,128)(2,1)S(1)}, bf16[1,160,1024]{2,1,0:T(8,128)(2,1)}, u32[]{:S(2)}) copy-start(bf16[1,160,1024]{2,1,0:T(8,128)(2,1)} %get-tuple-element.12.rest_1_) | copy-start | bytes 983044
  15.0 16.5 %collective-permute-start.10 = (bf16[1,160,1024]{2,1,0:T(8,128)(2,1)}, bf16[1,160,1024]{2,1,0:T(8,128)(2,1)S(1)}, u32[]{:S(2)}, u32[]{:S(2)}) collective-permute-start(bf16[1,160,1024]{2,1,0:T(8,128)(2,1)} %get-tuple-element.15.rest_0_), channel_id=1, source_target_pairs={{8,0},{12,4},{16,8},{20,12},{24,16},{28,20},{9,1},{13,5},{17,9},{2... | collective-permute-start | bytes 983048 | tf_op jit(solution)/shard_map/ppermute | solution.py:329
  16.4 22.1 %collective-permute-start.8 = (bf16[1,160,1024]{2,1,0:T(8,128)(2,1)}, bf16[1,160,1024]{2,1,0:T(8,128)(2,1)S(1)}, u32[]{:S(2)}, u32[]{:S(2)}) collective-permute-start(bf16[1,160,1024]{2,1,0:T(8,128)(2,1)} %get-tuple-element.14.rest_0_), channel_id=1, source_target_pairs={{8,0},{12,4},{16,8},{20,12},{24,16},{28,20},{9,1},{13,5},{17,9},{2... | collective-permute-start | bytes 983048 | tf_op jit(solution)/shard_map/ppermute | solution.py:329
  17.7 27.8 %collective-permute-start.6 = (bf16[1,160,1024]{2,1,0:T(8,128)(2,1)}, bf16[1,160,1024]{2,1,0:T(8,128)(2,1)S(1)}, u32[]{:S(2)}, u32[]{:S(2)}) collective-permute-start(bf16[1,160,1024]{2,1,0:T(8,128)(2,1)} %get-tuple-element.13.rest_0_), channel_id=1, source_target_pairs={{8,0},{12,4},{16,8},{20,12},{24,16},{28,20},{9,1},{13,5},{17,9},{2... | collective-permute-start | bytes 983048 | tf_op jit(solution)/shard_map/ppermute | solution.py:329
  21.5 29.9 %collective-permute-start.4 = (bf16[1,160,1024]{2,1,0:T(8,128)(2,1)}, bf16[1,160,1024]{2,1,0:T(8,128)(2,1)S(1)}, u32[]{:S(2)}, u32[]{:S(2)}) collective-permute-start(bf16[1,160,1024]{2,1,0:T(8,128)(2,1)} %get-tuple-element.12.rest_1_), channel_id=1, source_target_pairs={{8,0},{12,4},{16,8},{20,12},{24,16},{28,20},{9,1},{13,5},{17,9},{2... | collective-permute-start | bytes 983048 | tf_op jit(solution)/shard_map/ppermute | solution.py:329
  22.9 1.3 %collective-permute-start.2 = (s32[3]{0:T(128)S(1)}, s32[3]{0:T(128)S(1)}, u32[]{:S(2)}, u32[]{:S(2)}) collective-permute-start(s32[3]{0:T(128)S(1)} %fusion.2), channel_id=1, source_target_pairs={{0,1},{1,0},{2,3},{3,2},{4,5},{5,4},{6,7},{7,6},{8,9},{9,8},{10,11... | collective-permute-start | bytes 44 | tf_op jit(solution)/shard_map/ppermute | solution.py:312
  24.3 4.3 %collective-permute-start.3 = (s32[3]{0:T(128)S(1)}, s32[3]{0:T(128)S(1)}, u32[]{:S(2)}, u32[]{:S(2)}) collective-permute-start(s32[3]{0:T(128)S(1)} %add.22), channel_id=1, source_target_pairs={{0,2},{1,3},{2,0},{3,1},{4,6},{5,7},{6,4},{7,5},{8,10},{9,11},{10,... | collective-permute-start | bytes 44 | tf_op jit(solution)/shard_map/ppermute | solution.py:313
  31.4 20.7 %copy-start.3 = (bf16[1,160,1024]{2,1,0:T(8,128)(2,1)}, bf16[1,160,1024]{2,1,0:T(8,128)(2,1)S(1)}, u32[]{:S(2)}) copy-start(bf16[1,160,1024]{2,1,0:T(8,128)(2,1)S(1)} %collective-permute-done.10.rest_2_) | copy-start | bytes 983044
  31.5 20.6 %collective-permute-start.11 = (bf16[1,160,1024]{2,1,0:T(8,128)(2,1)S(1)}, bf16[1,160,1024]{2,1,0:T(8,128)(2,1)S(1)}, u32[]{:S(2)}, u32[]{:S(2)}) collective-permute-start(bf16[1,160,1024]{2,1,0:T(8,128)(2,1)S(1)} %broadcast_select_fusion), channel_id=1, source_target_pairs={{4,0},{0,4},{12,8},{8,12},{20,16},{16,20},{28,24},{24,28},{5,1},{1... | collective-permute-start | bytes 983048 | tf_op jit(solution)/shard_map/ppermute | solution.py:333
  38.5 21.7 %copy-start.2 = (bf16[1,160,1024]{2,1,0:T(8,128)(2,1)}, bf16[1,160,1024]{2,1,0:T(8,128)(2,1)S(1)}, u32[]{:S(2)}) copy-start(bf16[1,160,1024]{2,1,0:T(8,128)(2,1)S(1)} %collective-permute-done.8.rest_2_) | copy-start | bytes 983044
  38.5 21.7 %collective-permute-start.9 = (bf16[1,160,1024]{2,1,0:T(8,128)(2,1)S(1)}, bf16[1,160,1024]{2,1,0:T(8,128)(2,1)S(1)}, u32[]{:S(2)}, u32[]{:S(2)}) collective-permute-start(bf16[1,160,1024]{2,1,0:T(8,128)(2,1)S(1)} %broadcast_select_fusion.1), channel_id=1, source_target_pairs={{4,0},{0,4},{12,8},{8,12},{20,16},{16,20},{28,24},{24,28},{5,1},{1... | collective-permute-start | bytes 983048 | tf_op jit(solution)/shard_map/ppermute | solution.py:333
  45.5 14.7 %copy-start.1 = (bf16[1,160,1024]{2,1,0:T(8,128)(2,1)}, bf16[1,160,1024]{2,1,0:T(8,128)(2,1)S(1)}, u32[]{:S(2)}) copy-start(bf16[1,160,1024]{2,1,0:T(8,128)(2,1)S(1)} %collective-permute-done.6.rest_2_) | copy-start | bytes 983044
  45.5 23.7 %collective-permute-start.7 = (bf16[1,160,1024]{2,1,0:T(8,128)(2,1)S(1)}, bf16[1,160,1024]{2,1,0:T(8,128)(2,1)S(1)}, u32[]{:S(2)}, u32[]{:S(2)}) collective-permute-start(bf16[1,160,1024]{2,1,0:T(8,128)(2,1)S(1)} %broadcast_select_fusion.2), channel_id=1, source_target_pairs={{4,0},{0,4},{12,8},{8,12},{20,16},{16,20},{28,24},{24,28},{5,1},{1... | collective-permute-start | bytes 983048 | tf_op jit(solution)/shard_map/ppermute | solution.py:333
  51.4 8.8 %copy-start.4 = (bf16[1,160,1024]{2,1,0:T(8,128)(2,1)}, bf16[1,160,1024]{2,1,0:T(8,128)(2,1)S(1)}, u32[]{:S(2)}) copy-start(bf16[1,160,1024]{2,1,0:T(8,128)(2,1)S(1)} %collective-permute-done.4.rest_3_) | copy-start | bytes 983044
  51.4 26.8 %collective-permute-start.5 = (bf16[1,160,1024]{2,1,0:T(8,128)(2,1)S(1)}, bf16[1,160,1024]{2,1,0:T(8,128)(2,1)S(1)}, u32[]{:S(2)}, u32[]{:S(2)}) collective-permute-start(bf16[1,160,1024]{2,1,0:T(8,128)(2,1)S(1)} %broadcast_select_fusion.3), channel_id=1, source_target_pairs={{4,0},{0,4},{12,8},{8,12},{20,16},{16,20},{28,24},{24,28},{5,1},{1... | collective-permute-start | bytes 983048 | tf_op jit(solution)/shard_map/ppermute | solution.py:333
  52.1 0.7 copy-start.9
  60.2 0.7 copy-start.10
  69.2 0.7 copy-start.8
  78.2 0.7 copy-start.7
  87.2 2.3 %collective-permute-start.12 = (bf16[2,160,8,128]{3,2,1,0:T(8,128)(2,1)}, bf16[2,160,8,128]{3,2,1,0:T(8,128)(2,1)S(1)}, u32[]{:S(2)}, u32[]{:S(2)}) collective-permute-start(bf16[2,160,8,128]{3,2,1,0:T(8,128)(2,1)} %get-tuple-element.17), channel_id=1, source_target_pairs={{0,1},{1,0},{2,3},{3,2},{4,5},{5,4},{6,7},{7,6},{8,9},{9,8},{10,11... | collective-permute-start | bytes 1966088 | tf_op jit(solution)/shard_map/ppermute | solution.py:338
  90.6 9.8 %collective-permute-start.13 = (bf16[160,8,128]{2,1,0:T(8,128)(2,1)S(1)}, bf16[160,8,128]{2,1,0:T(8,128)(2,1)S(1)}, u32[]{:S(2)}, u32[]{:S(2)}) collective-permute-start(bf16[160,8,128]{2,1,0:T(8,128)(2,1)S(1)} %fusion), channel_id=1, source_target_pairs={{0,2},{1,3},{2,0},{3,1},{4,6},{5,7},{6,4},{7,5},{8,10},{9,11},{10,... | collective-permute-start | bytes 983048 | tf_op jit(solution)/shard_map/ppermute | solution.py:340

commit v5 on v4

--- a/solution.py
+++ b/solution.py
@@ -128,92 +128,129 @@
 CH_TILE = 16
 TILES = 2
 WINDOW = 13
-
-
-def cross_kernel(place_ref, *rest, specs, first, last):
+GROUPS = (slice(0, 2), slice(2, 4))
+
+
+def cross_kernel(place_ref, *rest, segs, specs, first, last):
     if last:
         scale_ref, *rest = rest
-    own_ref, next_ref, far_ref, lag_ref, *rest = rest
+    sources, rest = rest[: 3 * segs], rest[3 * segs :]
+    lag_hbm, *rest = rest
     if not first:
-        before_ref, *rest = rest
+        before_hbm, *rest = rest
+    outs, rest = (rest[:3], rest[3:]) if last else (rest[:1], rest[1:])
+    extended, lag_ref, wide, before, in_sems, out_sems, *results = rest
     if last:
-        keep_ref, other_ref, send_ref, wide, turned = rest
-    else:
-        out_ref, wide = rest
-    segs, channels, columns = own_ref.shape
-    bins = columns // 2
-    lane_tiles = bins // 128
+        turned, *results = results
+    columns = extended.shape[2]
+    channels = extended.shape[1] // (REACH + 1)
+    lane_tiles = columns // 256
+    steps = channels // (TILES * CH_TILE)
     lowest = place_ref[0]
     origin = lowest // CH_TILE * CH_TILE
-    step = pl.program_id(0)
-
-    @pl.when(step == 0)
-    def _():
-        def one_window(index, carry):
-            row = origin + index * CH_TILE
-            into = pl.ds(pl.multiple_of(index * CH_TILE, CH_TILE), CH_TILE)
-            for hop, ref in enumerate((own_ref, next_ref, far_ref)):
-
-                @pl.when((row >= hop * channels) & (row < (hop + 1) * channels))
-                def _():
-                    rows = pl.ds(pl.multiple_of(row - hop * channels, CH_TILE), CH_TILE)
-                    for seg in range(segs):
-                        for lane in range(2 * lane_tiles):
-                            block = ref[seg, rows, lane * 128 : lane * 128 + 128]
-                            wide[seg * 2 * lane_tiles + lane, into, :] = block.astype(jnp.float32)
-
-            return carry
-
-        lax.fori_loop(0, WINDOW, one_window, 0)
-
-    def all_tiles(*sums):
-        for tile in range(TILES):
-            one_tile(tile, sums)
-
-    def one_tile(tile, sums):
-        base = pl.multiple_of((step * TILES + tile) * CH_TILE, CH_TILE)
+
+    loads = [
+        pltpu.make_async_copy(
+            sources[hop * segs + seg],
+            extended.at[seg, pl.ds(hop * channels, channels), :],
+            in_sems.at[hop * segs + seg],
+        )
+        for hop in range(REACH + 1)
+        for seg in range(segs)
+    ]
+    loads.append(pltpu.make_async_copy(lag_hbm, lag_ref, in_sems.at[3 * segs]))
+    if not first:
+        earlier = pltpu.make_async_copy(before_hbm, before, in_sems.at[3 * segs + 1])
+    for load in loads:
+        load.start()
+    if not first:
+        earlier.start()
+    for load in loads:
+        load.wait()
+
+    def one_window(index, carry):
+        row = jnp.minimum(origin + index * CH_TILE, (REACH + 1) * channels - CH_TILE)
+        rows = pl.ds(pl.multiple_of(row, CH_TILE), CH_TILE)
+        into = pl.ds(pl.multiple_of(index * CH_TILE, CH_TILE), CH_TILE)
+        for seg in range(segs):
+            for lane in range(2 * lane_tiles):
+                block = extended[seg, rows, lane * 128 : lane * 128 + 128]
+                wide[seg * 2 * lane_tiles + lane, into, :] = block.astype(jnp.float32)
+        return carry
+
+    lax.fori_loop(0, WINDOW, one_window, 0)
+    if not first:
+        earlier.wait()
+
+    def stores(step):
+        rows = pl.ds(pl.multiple_of(step * TILES * CH_TILE, TILES * CH_TILE), TILES * CH_TILE)
+        if last:
+            picks = [(rows,), (rows,), (slice(None), rows)]
+        else:
+            picks = [(pl.ds(step * TILES, TILES),)]
+        return [
+            pltpu.make_async_copy(result.at[pick], out.at[pick], out_sems.at[step, number])
+            for number, (result, out, pick) in enumerate(zip(results, outs, picks))
+        ]
+
+    def one_step(step, sums):
+        bases = [
+            pl.multiple_of((step * TILES + tile) * CH_TILE, CH_TILE) for tile in range(TILES)
+        ]
         for lane in range(lane_tiles):
             for unit in range(2):
                 pltpu.matmul_push_rhs(lag_ref[lane], 0, unit)
             mine = {}
-            for seg in range(segs):
-                for part in range(2):
-                    at = (part * lane_tiles + lane) * 128
-                    block = own_ref[seg, pl.ds(base, CH_TILE), at : at + 128].astype(jnp.float32)
-                    mine[0, seg, part], mine[1, seg, part] = block[:8], block[8:]
+            for tile in range(TILES):
+                for seg in range(segs):
+                    for part in range(2):
+                        at = (part * lane_tiles + lane) * 128
+                        rows = pl.ds(bases[tile], CH_TILE)
+                        block = extended[seg, rows, at : at + 128].astype(jnp.float32)
+                        mine[tile, 0, seg, part] = block[:8]
+                        mine[tile, 1, seg, part] = block[8:]
             for pair in range(PAIRS):
-                start = base + (lowest - origin) + place_ref[1 + pair // 8] + pair % 8
-                reals, imags = [], []
-                for half in range(2):
-                    real = imag = None
-                    for seg in range(segs):
-                        slab = seg * 2 * lane_tiles + lane
-                        rows = pl.ds(start + 8 * half, 8)
-                        their_real = wide[slab, rows, :]
-                        their_imag = wide[slab + lane_tiles, rows, :]
-                        my_real, my_imag = mine[half, seg, 0], mine[half, seg, 1]
-                        re = my_real * their_real + my_imag * their_imag
-                        im = my_imag * their_real - my_real * their_imag
-                        real = re if real is None else real + re
-                        imag = im if imag is None else imag + im
-                    reals.append(real)
-                    imags.append(imag)
-                mixed = [
-                    jnp.concatenate(part, axis=0).astype(jnp.bfloat16) for part in (reals, imags)
-                ]
-                pltpu.matmul_acc_lhs(
-                    sums[pair],
-                    jnp.concatenate(mixed, axis=1),
-                    load_staged_rhs=0 if pair < 2 else None,
-                )
+                offset = (lowest - origin) + place_ref[1 + pair // 8] + pair % 8
+                for tile in range(TILES):
+                    reals, imags = [], []
+                    for half in range(2):
+                        real = imag = None
+                        for seg in range(segs):
+                            slab = seg * 2 * lane_tiles + lane
+                            rows = pl.ds(bases[tile] + offset + 8 * half, 8)
+                            their_real = wide[slab, rows, :]
+                            their_imag = wide[slab + lane_tiles, rows, :]
+                            my_real = mine[tile, half, seg, 0]
+                            my_imag = mine[tile, half, seg, 1]
+                            re = my_real * their_real + my_imag * their_imag
+                            im = my_imag * their_real - my_real * their_imag
+                            real = re if real is None else real + re
+                            imag = im if imag is None else imag + im
+                        reals.append(real)
+                        imags.append(imag)
+                    mixed = [
+                        jnp.concatenate(part, axis=0).astype(jnp.bfloat16)
+                        for part in (reals, imags)
+                    ]
+                    pltpu.matmul_acc_lhs(
+                        sums[TILES * pair + tile],
+                        jnp.concatenate(mixed, axis=1),
+                        load_staged_rhs=0 if pair == 0 else None,
+                    )
+        for tile in range(TILES):
+            finish(step * TILES + tile, bases[tile], sums[tile::TILES])
+        for store in stores(step):
+            store.start()
+
+    def finish(tile, base, sums):
         near = lax.broadcasted_iota(jnp.int32, (CH_TILE, LAGS), 0)
         for pair in range(PAIRS):
             rows = slice(pair * CH_TILE, pair * CH_TILE + CH_TILE)
             lagged = pltpu.matmul_pop(sums[pair])[:, :LAGS]
             if not first:
-                lagged += before_ref[tile, rows]
+                lagged += before[tile, rows].astype(jnp.float32)
             if not last:
-                out_ref[tile, rows] = lagged
+                results[0][tile, rows] = lagged.astype(jnp.bfloat16)
                 continue
             offset = lowest + place_ref[1 + pair // 8] + pair % 8
             partner = near + (base + offset)
@@ -226,65 +263,77 @@
             turned[pair // 8, pl.ds(pair % 8, CH_TILE, stride=8), :] = lagged * (scale * inside)
         if last:
             shape = (CH_TILE, 8, LAGS)
-            rows = slice(tile * CH_TILE, tile * CH_TILE + CH_TILE)
+            rows = pl.ds(base, CH_TILE)
+            keep_ref, other_ref, send_ref = results
             keep_ref[rows] = turned[0].reshape(shape)
             other_ref[rows] = turned[1].reshape(shape)
             for side in range(2):
                 send_ref[side, rows] = turned[2 + side].reshape(shape).astype(jnp.bfloat16)
 
-    pl.run_scoped(all_tiles, *specs)
-
-
-def correlated(mesh, places, scales, own, following, far, lag_table, before=None, last=False):
-    segs, channels, columns = own.shape
-    whole = pl.BlockSpec((segs, channels, columns), lambda i, *_: (0, 0, 0))
-    rows = TILES * CH_TILE
-    raw = pl.BlockSpec((TILES, PAIRS * CH_TILE, LAGS), lambda i, *_: (i, 0, 0))
-    raw_shape = jax.ShapeDtypeStruct((channels // CH_TILE, PAIRS * CH_TILE, LAGS), jnp.float32)
-    scratch = [pltpu.VMEM((segs * columns // 128, WINDOW * CH_TILE, 128), jnp.float32)]
-    out_specs, out_shape = raw, raw_shape
+    def all_steps(*sums):
+        def body(step, carry):
+            one_step(step, sums)
+            return carry
+
+        lax.fori_loop(0, steps, body, 0)
+
+    pl.run_scoped(all_steps, *specs)
+
+    def drain(step, carry):
+        for store in stores(step):
+            store.wait()
+        return carry
+
+    lax.fori_loop(0, steps, drain, 0)
+
+
+def correlated(mesh, places, scales, owns, nexts, fars, lag_table, before=None, last=False):
+    segs = len(owns)
+    channels, columns = owns[0].shape
+    steps = channels // (TILES * CH_TILE)
+    raw_shape = (channels // CH_TILE, PAIRS * CH_TILE, LAGS)
     if last:
-        kept = pl.BlockSpec((rows, 8, LAGS), lambda i, *_: (i, 0, 0))
-        sent = pl.BlockSpec((2, rows, 8, LAGS), lambda i, *_: (0, i, 0, 0))
-        out_specs = [kept, kept, sent]
-        kept_shape = jax.ShapeDtypeStruct((channels, 8, LAGS), jnp.float32)
-        sent_shape = jax.ShapeDtypeStruct((2, channels, 8, LAGS), jnp.bfloat16)
-        out_shape = [kept_shape, kept_shape, sent_shape]
-        scratch.append(pltpu.VMEM((4, CH_TILE * 8, LAGS), jnp.float32))
+        out_shape = [
+            jax.ShapeDtypeStruct((channels, 8, LAGS), jnp.float32),
+            jax.ShapeDtypeStruct((channels, 8, LAGS), jnp.float32),
+            jax.ShapeDtypeStruct((2, channels, 8, LAGS), jnp.bfloat16),
+        ]
+    else:
+        out_shape = [jax.ShapeDtypeStruct(raw_shape, jnp.bfloat16)]
+    scratch = [
+        pltpu.VMEM((segs, (REACH + 1) * channels, columns), jnp.bfloat16),
+        pltpu.VMEM(lag_table.shape, lag_table.dtype),
+        pltpu.VMEM((segs * columns // 128, WINDOW * CH_TILE, 128), jnp.float32),
+        pltpu.VMEM((8, 128) if before is None else raw_shape, jnp.bfloat16),
+        pltpu.SemaphoreType.DMA((3 * segs + 2,)),
+        pltpu.SemaphoreType.DMA((steps, 3)),
+        *([pltpu.VMEM((4, CH_TILE * 8, LAGS), jnp.float32)] if last else []),
+        *[pltpu.VMEM(shape.shape, shape.dtype) for shape in out_shape],
+    ]
     with jax.sharding.use_abstract_mesh(mesh.abstract_mesh):
-        specs = [pltpu.ACC(pair % 2)((CH_TILE, 256), jnp.float32) for pair in range(PAIRS)]
+        specs = [
+            pltpu.ACC(tile)((CH_TILE, 256), jnp.float32)
+            for _ in range(PAIRS)
+            for tile in range(TILES)
+        ]
+    smem = pl.BlockSpec(memory_space=pltpu.SMEM)
+    anywhere = pl.BlockSpec(memory_space=pltpu.HBM)
+    small = [places, scales] if last else [places]
+    large = [*owns, *nexts, *fars, lag_table, *([] if before is None else [before])]
     return pl.pallas_call(
-        functools.partial(cross_kernel, specs=specs, first=before is None, last=last),
+        functools.partial(cross_kernel, segs=segs, specs=specs, first=before is None, last=last),
         name="cross",
-        grid_spec=pltpu.PrefetchScalarGridSpec(
-            num_scalar_prefetch=2 if last else 1,
-            grid=(channels // rows,),
-            in_specs=[
-                whole,
-                whole,
-                whole,
-                pl.BlockSpec(lag_table.shape, lambda i, *_: (0, 0, 0)),
-                *([] if before is None else [raw]),
-            ],
-            out_specs=out_specs,
-            scratch_shapes=scratch,
-        ),
+        in_specs=[smem] * len(small) + [anywhere] * len(large),
+        out_specs=[anywhere] * len(out_shape),
         out_shape=out_shape,
-        compiler_params=pltpu.CompilerParams(vmem_limit_bytes=56 << 20),
+        scratch_shapes=scratch,
+        compiler_params=pltpu.CompilerParams(vmem_limit_bytes=40 << 20),
         cost_estimate=pl.CostEstimate(
             flops=10 * channels * PAIRS * columns * LAGS,
             bytes_accessed=6 * segs * channels * columns,
             transcendentals=0,
         ),
-    )(
-        places,
-        *([scales] if last else []),
-        own,
-        following,
-        far,
-        lag_table,
-        *([] if before is None else [before]),
-    )
+    )(*small, *large)
 
 
 def shards(mesh, records, valid_mask, band_limits):
@@ -325,16 +374,20 @@
 
     lag_table = jnp.asarray(lag_table_of(samples, BINS, LAGS))
     table = jnp.asarray(dft_table_of(samples, BINS))
-    whites = whitened(records, valid_mask, table, 0, segs, 1)
+    whites = [white[0] for white in whitened(records, valid_mask, table, 0, segs, 1)]
     fars = [lax.ppermute(white, "chan", hop_far) for white in whites]
+    nexts = []
+    for white, far in zip(whites, fars):
+        passed = jnp.where(block % 2 == 0, far, white)
+        nexts.append(lax.ppermute(passed, "chan", pair_swap))
     before = None
-    for at, (white, far) in enumerate(zip(whites, fars)):
-        passed = jnp.where(block % 2 == 0, far, white)
-        following = lax.ppermute(passed, "chan", pair_swap)
-        before = correlated(
-            mesh, places, scales, white, following, far, lag_table, before, last=at == len(whites) - 1
+    for part in GROUPS:
+        last = part.stop == segs
+        found = correlated(
+            mesh, places, scales, whites[part], nexts[part], fars[part], lag_table, before, last
         )
-    keep, other, send = before
+        before = found[0]
+    keep, other, send = found
     got = lax.ppermute(send, "tm", core_swap)
     passing = (other + got[1].astype(jnp.float32)).astype(jnp.bfloat16)
     passed = lax.ppermute(passing, "tm", side_swap)

time: 103 us -> 98.3 us (0.954)
  Pallas kernels: 44.3 us -> 30.3 us
  waiting for transfers between devices: 29.3 us -> 40.3 us
  starting transfers between devices: 19.3 us -> 17.8 us
  local copies, waits for them, and re-layouts: 5.37 us -> 3.94 us
  other arithmetic: 4 us -> 5.23 us
    pallas_call x4 -> x2, Pallas kernels: 32.1 us -> 18 us  [correlated(): pl.pallas_call(functools.partial(cross_kernel, segs=segs, specs=specs, fi...]
    ppermute x4, waiting for transfers between devices: 0.01 us -> 7.52 us  [shards(): nexts.append(lax.ppermute(passed, 'chan', pair_swap))]
    select_n x4, other arithmetic: 0.15 us -> 4.05 us  [shards(): passed = jnp.where(block % 2 == 0, far, white)]
    ppermute x4, waiting for transfers between devices: 16.7 us -> 20.2 us  [shards(): fars = [lax.ppermute(white, 'chan', hop_far) for white in whites]]
    ppermute x4, starting transfers between devices: 6.12 us -> 4.86 us  [shards(): nexts.append(lax.ppermute(passed, 'chan', pair_swap))]
    convert_element_type x1, other arithmetic: 1.15 us -> 0.07 us  [shards(): passing = (other + got[1].astype(jnp.float32)).astype(jnp.bfloat16)]
    add x1, other arithmetic: 2.01 us -> 0.95 us  [shards(): return keep + got[0].astype(jnp.float32) + passed.astype(jnp.float32)]
    unnamed x22 -> x14, local copies, waits for them, and re-layouts: 2.92 us -> 1.96 us
  transfers between devices with their start and end apart: 14 -> 14, of which waited for: 8 -> 8; matrix products, arithmetic and copies ran while one was open for 3% -> 6% of each run, Pallas kernels for 35% -> 20%
where the time goes in v5:
time: 98.3 us; the launch traced here: 97.8 us
  waiting for transfers between devices  40.3 us (41%)
  Pallas kernels  30.3 us (31%)
  starting transfers between devices  17.8 us (18%)
  other arithmetic  5.23 us (5%)
  local copies, waits for them, and re-layouts  3.94 us (4%)
    ppermute x4, waiting for transfers between devices, shards(): fars = [lax.ppermute(white, 'chan', hop_far) for white in whites]  20.2 us
    pallas_call x2, Pallas kernels, correlated(): pl.pallas_call(functools.partial(cross_kernel, segs=segs, specs=specs, fi...  18 us
    pallas_call x1, Pallas kernels, whitened(): pl.pallas_call(functools.partial(spectra_kernel, first_seg=first_seg), na...  12.3 us
    ppermute x1, waiting for transfers between devices, shards(): passed = lax.ppermute(passing, 'tm', side_swap)  8.16 us
    ppermute x4, waiting for transfers between devices, shards(): nexts.append(lax.ppermute(passed, 'chan', pair_swap))  7.52 us
    ppermute x4, starting transfers between devices, shards(): fars = [lax.ppermute(white, 'chan', hop_far) for white in whites]  5.15 us
    ppermute x4, starting transfers between devices, shards(): nexts.append(lax.ppermute(passed, 'chan', pair_swap))  4.86 us
    select_n x4, other arithmetic, shards(): passed = jnp.where(block % 2 == 0, far, white)  4.05 us
  transfers between devices with their start and end apart: 14, of which 8 were waited for; matrix products, arithmetic and copies ran while one was open for 6% of the time, Pallas kernels for 20%

profile of v5, /device:TPU:0, one launch (start us, length us, event | category | flops | bytes accessed | tf_op | source)
XLA Modules:
  0.0 97.8 jit_solution(14996193657660523304)
XLA Ops:
  0.0 1.4 %collective-permute-start.1 = (s32[1,4]{1,0:T(1,128)}, s32[1,4]{1,0:T(1,128)S(1)}, u32[]{:S(2)}, u32[]{:S(2)}) collective-permute-start(s32[1,4]{1,0:T(1,128)} %valid_ref.1), channel_id=1, source_target_pairs={{8,0},{12,4},{16,8},{20,12},{24,16},{28,20},{9,1},{13,5},{17,9},{2... | collective-permute-start | bytes 56 | tf_op jit(solution)/shard_map/ppermute | solution.py:357
  1.4 1.3 %collective-permute-start = (s32[1,4]{1,0:T(1,128)}, s32[1,4]{1,0:T(1,128)S(1)}, u32[]{:S(2)}, u32[]{:S(2)}) collective-permute-start(s32[1,4]{1,0:T(1,128)} %valid_ref.1), channel_id=1, source_target_pairs={{4,0},{8,4},{12,8},{16,12},{20,16},{24,20},{28,24},{5,1},{9,5},{13... | collective-permute-start | bytes 56 | tf_op jit(solution)/shard_map/ppermute | solution.py:356
  2.7 12.3 %spectra.1 = (bf16[1,160,1024]{2,1,0:T(8,128)(2,1)}, bf16[1,160,1024]{2,1,0:T(8,128)(2,1)}, bf16[1,160,1024]{2,1,0:T(8,128)(2,1)}, bf16[1,160,1024]{2,1,0:T(8,128)(2,1)}) custom-call(s32[1,4]{1,0:T(1,128)} %valid_ref.1, bf16[160,4,7680]{2,1,0:T(4,128)(2,1)} %second_ref.1, bf16[160,4,7680]{2,1,0:T(4,128)(2,1)} %second_ref.1, ...), custom_call_target="tpu_custom_call" | custom-call | flops 10066329600 | bytes 17694720 | tf_op jit(solution)/shard_map/spectra/pallas_call | solution.py:103
  15.0 1.3 %collective-permute-start.6 = (bf16[160,1024]{1,0:T(8,128)(2,1)}, bf16[160,1024]{1,0:T(8,128)(2,1)S(1)}, u32[]{:S(2)}, u32[]{:S(2)}) collective-permute-start(bf16[160,1024]{1,0:T(8,128)(2,1)} %bitcast.30), channel_id=1, source_target_pairs={{8,0},{12,4},{16,8},{20,12},{24,16},{28,20},{9,1},{13,5},{17,9},{2... | collective-permute-start | bytes 983048 | tf_op jit(solution)/shard_map/ppermute | solution.py:378
  16.3 1.3 %collective-permute-start.4 = (bf16[160,1024]{1,0:T(8,128)(2,1)}, bf16[160,1024]{1,0:T(8,128)(2,1)S(1)}, u32[]{:S(2)}, u32[]{:S(2)}) collective-permute-start(bf16[160,1024]{1,0:T(8,128)(2,1)} %bitcast.28), channel_id=1, source_target_pairs={{8,0},{12,4},{16,8},{20,12},{24,16},{28,20},{9,1},{13,5},{17,9},{2... | collective-permute-start | bytes 983048 | tf_op jit(solution)/shard_map/ppermute | solution.py:378
  17.6 1.3 %collective-permute-start.8 = (bf16[160,1024]{1,0:T(8,128)(2,1)}, bf16[160,1024]{1,0:T(8,128)(2,1)S(1)}, u32[]{:S(2)}, u32[]{:S(2)}) collective-permute-start(bf16[160,1024]{1,0:T(8,128)(2,1)} %bitcast.32), channel_id=1, source_target_pairs={{8,0},{12,4},{16,8},{20,12},{24,16},{28,20},{9,1},{13,5},{17,9},{2... | collective-permute-start | bytes 983048 | tf_op jit(solution)/shard_map/ppermute | solution.py:378
  18.9 0.6 fusion.3
  19.6 1.3 %stack.31.place_ref = s32[6]{0:T(128)S(1)} concatenate(s32[1]{0:T(128)} %bitcast, s32[1]{0:T(128)} %bitcast.1, s32[1]{0:T(128)} %bitcast.2, s32[1]{0:T(128)} %bitcast.3, s32[1]{0:T(128)} %bitcast.4, s32[1]{0:T(128)} %bitcast.5), dimensions={0} | concatenate | bytes 48 | tf_op jit(solution)/shard_map/stack | solution.py:364
  20.9 1.3 %collective-permute-start.10 = (bf16[160,1024]{1,0:T(8,128)(2,1)}, bf16[160,1024]{1,0:T(8,128)(2,1)S(1)}, u32[]{:S(2)}, u32[]{:S(2)}) collective-permute-start(bf16[160,1024]{1,0:T(8,128)(2,1)} %bitcast.34), channel_id=1, source_target_pairs={{8,0},{12,4},{16,8},{20,12},{24,16},{28,20},{9,1},{13,5},{17,9},{2... | collective-permute-start | bytes 983048 | tf_op jit(solution)/shard_map/ppermute | solution.py:378
  22.9 0.8 collective-permute-done.2
  23.7 2.8 %collective-permute-start.3 = (s32[3]{0:T(128)S(1)}, s32[3]{0:T(128)S(1)}, u32[]{:S(2)}, u32[]{:S(2)}) collective-permute-start(s32[3]{0:T(128)S(1)} %add.22), channel_id=1, source_target_pairs={{0,2},{1,3},{2,0},{3,1},{4,6},{5,7},{6,4},{7,5},{8,10},{9,11},{10,... | collective-permute-start | bytes 44 | tf_op jit(solution)/shard_map/ppermute | solution.py:362
  26.6 1.5 %collective-permute-done.3 = s32[3]{0:T(128)S(1)} collective-permute-done((s32[3]{0:T(128)S(1)}, s32[3]{0:T(128)S(1)}, u32[]{:S(2)}, u32[]{:S(2)}) %collective-permute-start.3) | collective-permute-done | bytes 44 | tf_op jit(solution)/shard_map/ppermute | solution.py:362
  28.1 16.7 %collective-permute-done.8.rest_4_ = bf16[160,1024]{1,0:T(8,128)(2,1)S(1)} collective-permute-done((bf16[160,1024]{1,0:T(8,128)(2,1)}, bf16[160,1024]{1,0:T(8,128)(2,1)S(1)}, u32[]{:S(2)}, u32[]{:S(2)}) %collective-permute-start.8) | collective-permute-done | bytes 327712 | tf_op jit(solution)/shard_map/ppermute | solution.py:378
  44.8 1.0 %broadcast_select_fusion.1 = bf16[160,1024]{1,0:T(8,128)(2,1)S(1)} fusion(bf16[160,1024]{1,0:T(8,128)(2,1)S(1)} %collective-permute-done.8.rest_4_, pred[]{:T(512)S(6)} %eq.11, bf16[1,160,1024]{2,1,0:T(8,128)(2,1)} %get-tuple-element.14), kind=kLoop, calls=%fused_computation.7 | loop fusion | flops 163840 | bytes 983041 | tf_op jit(solution)/shard_map/jit(_where)/select_n | solution.py:381
  45.8 1.3 %collective-permute-start.9 = (bf16[160,1024]{1,0:T(8,128)(2,1)S(1)}, bf16[160,1024]{1,0:T(8,128)(2,1)S(1)}, u32[]{:S(2)}, u32[]{:S(2)}) collective-permute-start(bf16[160,1024]{1,0:T(8,128)(2,1)S(1)} %broadcast_select_fusion.1), channel_id=1, source_target_pairs={{4,0},{0,4},{12,8},{8,12},{20,16},{16,20},{28,24},{24,28},{5,1},{1... | collective-permute-start | bytes 983048 | tf_op jit(solution)/shard_map/ppermute | solution.py:382
  47.1 3.5 %collective-permute-done.10.rest_5_ = bf16[160,1024]{1,0:T(8,128)(2,1)S(1)} collective-permute-done((bf16[160,1024]{1,0:T(8,128)(2,1)}, bf16[160,1024]{1,0:T(8,128)(2,1)S(1)}, u32[]{:S(2)}, u32[]{:S(2)}) %collective-permute-start.10) | collective-permute-done | bytes 327712 | tf_op jit(solution)/shard_map/ppermute | solution.py:378
  50.6 1.0 %broadcast_select_fusion = bf16[160,1024]{1,0:T(8,128)(2,1)S(1)} fusion(bf16[160,1024]{1,0:T(8,128)(2,1)S(1)} %collective-permute-done.10.rest_5_, pred[]{:T(512)S(6)} %eq.11, bf16[1,160,1024]{2,1,0:T(8,128)(2,1)} %get-tuple-element.15), kind=kLoop, calls=%fused_computation.6 | loop fusion | flops 163840 | bytes 983041 | tf_op jit(solution)/shard_map/jit(_where)/select_n | solution.py:381
  51.7 1.4 %collective-permute-start.11 = (bf16[160,1024]{1,0:T(8,128)(2,1)S(1)}, bf16[160,1024]{1,0:T(8,128)(2,1)S(1)}, u32[]{:S(2)}, u32[]{:S(2)}) collective-permute-start(bf16[160,1024]{1,0:T(8,128)(2,1)S(1)} %broadcast_select_fusion), channel_id=1, source_target_pairs={{4,0},{0,4},{12,8},{8,12},{20,16},{16,20},{28,24},{24,28},{5,1},{1... | collective-permute-start | bytes 983048 | tf_op jit(solution)/shard_map/ppermute | solution.py:382
  53.0 1.0 %broadcast_select_fusion.2 = bf16[160,1024]{1,0:T(8,128)(2,1)S(1)} fusion(bf16[160,1024]{1,0:T(8,128)(2,1)S(1)} %collective-permute-done.6.rest_6_, pred[]{:T(512)S(6)} %eq.11, bf16[1,160,1024]{2,1,0:T(8,128)(2,1)} %get-tuple-element.13), kind=kLoop, calls=%fused_computation.8 | loop fusion | flops 163840 | bytes 983041 | tf_op jit(solution)/shard_map/jit(_where)/select_n | solution.py:381
  54.0 0.8 collective-permute-start.7
  54.8 1.0 %broadcast_select_fusion.3 = bf16[160,1024]{1,0:T(8,128)(2,1)S(1)} fusion(bf16[160,1024]{1,0:T(8,128)(2,1)S(1)} %collective-permute-done.4.rest_5_, pred[]{:T(512)S(6)} %eq.11, bf16[1,160,1024]{2,1,0:T(8,128)(2,1)} %get-tuple-element.12), kind=kLoop, calls=%fused_computation.9 | loop fusion | flops 163840 | bytes 983041 | tf_op jit(solution)/shard_map/jit(_where)/select_n | solution.py:381
  55.9 1.4 %collective-permute-start.5 = (bf16[160,1024]{1,0:T(8,128)(2,1)S(1)}, bf16[160,1024]{1,0:T(8,128)(2,1)S(1)}, u32[]{:S(2)}, u32[]{:S(2)}) collective-permute-start(bf16[160,1024]{1,0:T(8,128)(2,1)S(1)} %broadcast_select_fusion.3), channel_id=1, source_target_pairs={{4,0},{0,4},{12,8},{8,12},{20,16},{16,20},{28,24},{24,28},{5,1},{1... | collective-permute-start | bytes 983048 | tf_op jit(solution)/shard_map/ppermute | solution.py:382
  57.2 5.1 %collective-permute-done.11.rest_3_ = bf16[160,1024]{1,0:T(8,128)(2,1)S(1)} collective-permute-done((bf16[160,1024]{1,0:T(8,128)(2,1)S(1)}, bf16[160,1024]{1,0:T(8,128)(2,1)S(1)}, u32[]{:S(2)}, u32[]{:S(2)}) %collective-permute-start.11) | collective-permute-done | bytes 327712 | tf_op jit(solution)/shard_map/ppermute | solution.py:382
  62.4 1.0 copy-done.2
  63.4 1.0 copy-done.3
  64.3 7.6 %cross.2.rest_8_ = bf16[10,512,128]{2,1,0:T(8,128)(2,1)S(1)} custom-call(s32[6]{0:T(128)S(1)} %stack.31.place_ref, bf16[160,1024]{1,0:T(8,128)(2,1)S(1)} %bitcast.33, bf16[160,1024]{1,0:T(8,128)(2,1)S(1)} %bitcast.35, bf16[160,1024]{1,0:T(8,128)(2,1)S(1)} %collective-permute-done.9.rest_2_, bf16[160,1024]{1,0:T(8,128)(2,1)S(1)} %collective-permute-done.11.rest_3_, ...), custom_call_target="tpu_custom_call" | custom-call | flops 6710886400 | bytes 1966080 | tf_op jit(solution)/shard_map/cross/pallas_call | solution.py:323
  72.0 2.4 %collective-permute-done.5.rest_3_ = bf16[160,1024]{1,0:T(8,128)(2,1)S(1)} collective-permute-done((bf16[160,1024]{1,0:T(8,128)(2,1)S(1)}, bf16[160,1024]{1,0:T(8,128)(2,1)S(1)}, u32[]{:S(2)}, u32[]{:S(2)}) %collective-permute-start.5) | collective-permute-done | bytes 327712 | tf_op jit(solution)/shard_map/ppermute | solution.py:382
  74.4 10.4 %cross.3 = (f32[160,8,128]{2,1,0:T(8,128)S(1)}, f32[160,8,128]{2,1,0:T(8,128)S(1)}, bf16[2,160,8,128]{3,2,1,0:T(8,128)(2,1)S(1)}) custom-call(s32[6]{0:T(128)S(1)} %stack.31.place_ref, f32[3]{0:T(128)S(1)} %convert_divide_fusion.rest_0_, bf16[160,1024]{1,0:T(8,128)(2,1)S(1)} %bitcast.29, bf16[160,1024]{1,0:T(8,128)(2,1)S(1)} %bitcast.31, ...), custom_call_target="tpu_custom_call" | custom-call | flops 6710886400 | bytes 1966080 | tf_op jit(solution)/shard_map/cross/pallas_call | solution.py:323
  84.8 2.1 %collective-permute-done.12 = bf16[2,160,8,128]{3,2,1,0:T(8,128)(2,1)S(1)} collective-permute-done((bf16[2,160,8,128]{3,2,1,0:T(8,128)(2,1)S(1)}, bf16[2,160,8,128]{3,2,1,0:T(8,128)(2,1)S(1)}, u32[]{:S(2)}, u32[]{:S(2)}) %collective-permute-start.12) | collective-permute-done | bytes 655392 | tf_op jit(solution)/shard_map/ppermute | solution.py:391
  87.0 1.7 %collective-permute-start.13 = (bf16[160,8,128]{2,1,0:T(8,128)(2,1)S(1)}, bf16[160,8,128]{2,1,0:T(8,128)(2,1)S(1)}, u32[]{:S(2)}, u32[]{:S(2)}) collective-permute-start(bf16[160,8,128]{2,1,0:T(8,128)(2,1)S(1)} %fusion), channel_id=1, source_target_pairs={{0,2},{1,3},{2,0},{3,1},{4,6},{5,7},{6,4},{7,5},{8,10},{9,11},{10,... | collective-permute-start | bytes 983048 | tf_op jit(solution)/shard_map/ppermute | solution.py:393
  88.7 8.2 %collective-permute-done.13 = bf16[160,8,128]{2,1,0:T(8,128)(2,1)S(1)} collective-permute-done((bf16[160,8,128]{2,1,0:T(8,128)(2,1)S(1)}, bf16[160,8,128]{2,1,0:T(8,128)(2,1)S(1)}, u32[]{:S(2)}, u32[]{:S(2)}) %collective-permute-start.13) | collective-permute-done | bytes 327712 | tf_op jit(solution)/shard_map/ppermute | solution.py:393
  96.8 0.9 fusion.1
  (24 shorter events, 0.9 us)
Async XLA Ops:
  0.0 62.4 %copy-start.4 = (bf16[4,256,256]{2,1,0:T(8,128)(2,1)S(1)}, bf16[4,256,256]{2,1,0:T(8,128)(2,1)}, u32[]{:S(2)}) copy-start(bf16[4,256,256]{2,1,0:T(8,128)(2,1)} %constant.41.clone.rest_6_.rest_7_) | copy-start | bytes 1572868
  0.0 22.2 %copy-start.5 = (s32[1,4]{1,0:T(1,128)S(1)}, s32[1,4]{1,0:T(1,128)}, u32[]{:S(2)}) copy-start(s32[1,4]{1,0:T(1,128)} %valid_ref.1) | copy-start | bytes 52
  0.0 18.9 %copy-start.6 = (s32[1,2]{1,0:T(1,128)S(1)}, s32[1,2]{1,0:T(1,128)}, u32[]{:S(2)}) copy-start(s32[1,2]{1,0:T(1,128)} %param.7) | copy-start | bytes 28
  0.0 20.9 %collective-permute-start.1 = (s32[1,4]{1,0:T(1,128)}, s32[1,4]{1,0:T(1,128)S(1)}, u32[]{:S(2)}, u32[]{:S(2)}) collective-permute-start(s32[1,4]{1,0:T(1,128)} %valid_ref.1), channel_id=1, source_target_pairs={{8,0},{12,4},{16,8},{20,12},{24,16},{28,20},{9,1},{13,5},{17,9},{2... | collective-permute-start | bytes 56 | tf_op jit(solution)/shard_map/ppermute | solution.py:357
  1.4 20.8 %collective-permute-start = (s32[1,4]{1,0:T(1,128)}, s32[1,4]{1,0:T(1,128)S(1)}, u32[]{:S(2)}, u32[]{:S(2)}) collective-permute-start(s32[1,4]{1,0:T(1,128)} %valid_ref.1), channel_id=1, source_target_pairs={{4,0},{8,4},{12,8},{16,12},{20,16},{24,20},{28,24},{5,1},{9,5},{13... | collective-permute-start | bytes 56 | tf_op jit(solution)/shard_map/ppermute | solution.py:356
  15.0 38.0 %collective-permute-start.6 = (bf16[160,1024]{1,0:T(8,128)(2,1)}, bf16[160,1024]{1,0:T(8,128)(2,1)S(1)}, u32[]{:S(2)}, u32[]{:S(2)}) collective-permute-start(bf16[160,1024]{1,0:T(8,128)(2,1)} %bitcast.30), channel_id=1, source_target_pairs={{8,0},{12,4},{16,8},{20,12},{24,16},{28,20},{9,1},{13,5},{17,9},{2... | collective-permute-start | bytes 983048 | tf_op jit(solution)/shard_map/ppermute | solution.py:378
  16.3 38.5 %collective-permute-start.4 = (bf16[160,1024]{1,0:T(8,128)(2,1)}, bf16[160,1024]{1,0:T(8,128)(2,1)S(1)}, u32[]{:S(2)}, u32[]{:S(2)}) collective-permute-start(bf16[160,1024]{1,0:T(8,128)(2,1)} %bitcast.28), channel_id=1, source_target_pairs={{8,0},{12,4},{16,8},{20,12},{24,16},{28,20},{9,1},{13,5},{17,9},{2... | collective-permute-start | bytes 983048 | tf_op jit(solution)/shard_map/ppermute | solution.py:378
  17.6 27.2 %collective-permute-start.8 = (bf16[160,1024]{1,0:T(8,128)(2,1)}, bf16[160,1024]{1,0:T(8,128)(2,1)S(1)}, u32[]{:S(2)}, u32[]{:S(2)}) collective-permute-start(bf16[160,1024]{1,0:T(8,128)(2,1)} %bitcast.32), channel_id=1, source_target_pairs={{8,0},{12,4},{16,8},{20,12},{24,16},{28,20},{9,1},{13,5},{17,9},{2... | collective-permute-start | bytes 983048 | tf_op jit(solution)/shard_map/ppermute | solution.py:378
  20.9 29.7 %collective-permute-start.10 = (bf16[160,1024]{1,0:T(8,128)(2,1)}, bf16[160,1024]{1,0:T(8,128)(2,1)S(1)}, u32[]{:S(2)}, u32[]{:S(2)}) collective-permute-start(bf16[160,1024]{1,0:T(8,128)(2,1)} %bitcast.34), channel_id=1, source_target_pairs={{8,0},{12,4},{16,8},{20,12},{24,16},{28,20},{9,1},{13,5},{17,9},{2... | collective-permute-start | bytes 983048 | tf_op jit(solution)/shard_map/ppermute | solution.py:378
  22.4 1.4 %collective-permute-start.2 = (s32[3]{0:T(128)S(1)}, s32[3]{0:T(128)S(1)}, u32[]{:S(2)}, u32[]{:S(2)}) collective-permute-start(s32[3]{0:T(128)S(1)} %fusion.2), channel_id=1, source_target_pairs={{0,1},{1,0},{2,3},{3,2},{4,5},{5,4},{6,7},{7,6},{8,9},{9,8},{10,11... | collective-permute-start | bytes 44 | tf_op jit(solution)/shard_map/ppermute | solution.py:361
  23.7 4.3 %collective-permute-start.3 = (s32[3]{0:T(128)S(1)}, s32[3]{0:T(128)S(1)}, u32[]{:S(2)}, u32[]{:S(2)}) collective-permute-start(s32[3]{0:T(128)S(1)} %add.22), channel_id=1, source_target_pairs={{0,2},{1,3},{2,0},{3,1},{4,6},{5,7},{6,4},{7,5},{8,10},{9,11},{10,... | collective-permute-start | bytes 44 | tf_op jit(solution)/shard_map/ppermute | solution.py:362
  45.8 11.4 %collective-permute-start.9 = (bf16[160,1024]{1,0:T(8,128)(2,1)S(1)}, bf16[160,1024]{1,0:T(8,128)(2,1)S(1)}, u32[]{:S(2)}, u32[]{:S(2)}) collective-permute-start(bf16[160,1024]{1,0:T(8,128)(2,1)S(1)} %broadcast_select_fusion.1), channel_id=1, source_target_pairs={{4,0},{0,4},{12,8},{8,12},{20,16},{16,20},{28,24},{24,28},{5,1},{1... | collective-permute-start | bytes 983048 | tf_op jit(solution)/shard_map/ppermute | solution.py:382
  51.7 10.7 %collective-permute-start.11 = (bf16[160,1024]{1,0:T(8,128)(2,1)S(1)}, bf16[160,1024]{1,0:T(8,128)(2,1)S(1)}, u32[]{:S(2)}, u32[]{:S(2)}) collective-permute-start(bf16[160,1024]{1,0:T(8,128)(2,1)S(1)} %broadcast_select_fusion), channel_id=1, source_target_pairs={{4,0},{0,4},{12,8},{8,12},{20,16},{16,20},{28,24},{24,28},{5,1},{1... | collective-permute-start | bytes 983048 | tf_op jit(solution)/shard_map/ppermute | solution.py:382
  54.0 17.9 %collective-permute-start.7 = (bf16[160,1024]{1,0:T(8,128)(2,1)S(1)}, bf16[160,1024]{1,0:T(8,128)(2,1)S(1)}, u32[]{:S(2)}, u32[]{:S(2)}) collective-permute-start(bf16[160,1024]{1,0:T(8,128)(2,1)S(1)} %broadcast_select_fusion.2), channel_id=1, source_target_pairs={{4,0},{0,4},{12,8},{8,12},{20,16},{16,20},{28,24},{24,28},{5,1},{1... | collective-permute-start | bytes 983048 | tf_op jit(solution)/shard_map/ppermute | solution.py:382
  55.9 18.5 %copy-start = (bf16[1,160,1024]{2,1,0:T(8,128)(2,1)S(1)}, bf16[1,160,1024]{2,1,0:T(8,128)(2,1)}, u32[]{:S(2)}) copy-start(bf16[1,160,1024]{2,1,0:T(8,128)(2,1)} %get-tuple-element.12) | copy-start | bytes 983044
  55.9 18.5 %copy-start.1 = (bf16[1,160,1024]{2,1,0:T(8,128)(2,1)S(1)}, bf16[1,160,1024]{2,1,0:T(8,128)(2,1)}, u32[]{:S(2)}) copy-start(bf16[1,160,1024]{2,1,0:T(8,128)(2,1)} %get-tuple-element.13) | copy-start | bytes 983044
  55.9 18.5 %collective-permute-start.5 = (bf16[160,1024]{1,0:T(8,128)(2,1)S(1)}, bf16[160,1024]{1,0:T(8,128)(2,1)S(1)}, u32[]{:S(2)}, u32[]{:S(2)}) collective-permute-start(bf16[160,1024]{1,0:T(8,128)(2,1)S(1)} %broadcast_select_fusion.3), channel_id=1, source_target_pairs={{4,0},{0,4},{12,8},{8,12},{20,16},{16,20},{28,24},{24,28},{5,1},{1... | collective-permute-start | bytes 983048 | tf_op jit(solution)/shard_map/ppermute | solution.py:382
  62.4 1.0 copy-start.2
  63.4 1.0 copy-start.3
  84.8 2.2 %collective-permute-start.12 = (bf16[2,160,8,128]{3,2,1,0:T(8,128)(2,1)S(1)}, bf16[2,160,8,128]{3,2,1,0:T(8,128)(2,1)S(1)}, u32[]{:S(2)}, u32[]{:S(2)}) collective-permute-start(bf16[2,160,8,128]{3,2,1,0:T(8,128)(2,1)S(1)} %get-tuple-element.17), channel_id=1, source_target_pairs={{0,1},{1,0},{2,3},{3,2},{4,5},{5,4},{6,7},{7,6},{8,9},{9,8},{10,11... | collective-permute-start | bytes 1966088 | tf_op jit(solution)/shard_map/ppermute | solution.py:391
  87.0 9.8 %collective-permute-start.13 = (bf16[160,8,128]{2,1,0:T(8,128)(2,1)S(1)}, bf16[160,8,128]{2,1,0:T(8,128)(2,1)S(1)}, u32[]{:S(2)}, u32[]{:S(2)}) collective-permute-start(bf16[160,8,128]{2,1,0:T(8,128)(2,1)S(1)} %fusion), channel_id=1, source_target_pairs={{0,2},{1,3},{2,0},{3,1},{4,6},{5,7},{6,4},{7,5},{8,10},{9,11},{10,... | collective-permute-start | bytes 983048 | tf_op jit(solution)/shard_map/ppermute | solution.py:393

commit v6 on v5

--- a/solution.py
+++ b/solution.py
@@ -128,17 +128,17 @@
 CH_TILE = 16
 TILES = 2
 WINDOW = 13
-GROUPS = (slice(0, 2), slice(2, 4))
-
-
-def cross_kernel(place_ref, *rest, segs, specs, first, last):
+
+
+def cross_kernel(place_ref, *rest, segs, specs, quarters, first, last):
     if last:
         scale_ref, *rest = rest
     sources, rest = rest[: 3 * segs], rest[3 * segs :]
     lag_hbm, *rest = rest
     if not first:
         before_hbm, *rest = rest
-    outs, rest = (rest[:3], rest[3:]) if last else (rest[:1], rest[1:])
+    count = len(quarters) if last else 1
+    outs, rest = rest[:count], rest[count:]
     extended, lag_ref, wide, before, in_sems, out_sems, *results = rest
     if last:
         turned, *results = results
@@ -185,7 +185,7 @@
     def stores(step):
         rows = pl.ds(pl.multiple_of(step * TILES * CH_TILE, TILES * CH_TILE), TILES * CH_TILE)
         if last:
-            picks = [(rows,), (rows,), (slice(None), rows)]
+            picks = [(rows,)] * len(results)
         else:
             picks = [(pl.ds(step * TILES, TILES),)]
         return [
@@ -209,8 +209,9 @@
                         block = extended[seg, rows, at : at + 128].astype(jnp.float32)
                         mine[tile, 0, seg, part] = block[:8]
                         mine[tile, 1, seg, part] = block[8:]
-            for pair in range(PAIRS):
-                offset = (lowest - origin) + place_ref[1 + pair // 8] + pair % 8
+            for pair in range(8 * len(quarters)):
+                quarter = quarters[pair // 8]
+                offset = (lowest - origin) + place_ref[1 + quarter] + pair % 8
                 for tile in range(TILES):
                     reals, imags = [], []
                     for half in range(2):
@@ -244,15 +245,17 @@
 
     def finish(tile, base, sums):
         near = lax.broadcasted_iota(jnp.int32, (CH_TILE, LAGS), 0)
-        for pair in range(PAIRS):
-            rows = slice(pair * CH_TILE, pair * CH_TILE + CH_TILE)
+        for pair in range(8 * len(quarters)):
+            quarter = quarters[pair // 8]
+            at = pair * CH_TILE
+            rows = slice(at, at + CH_TILE)
             lagged = pltpu.matmul_pop(sums[pair])[:, :LAGS]
             if not first:
                 lagged += before[tile, rows].astype(jnp.float32)
             if not last:
                 results[0][tile, rows] = lagged.astype(jnp.bfloat16)
                 continue
-            offset = lowest + place_ref[1 + pair // 8] + pair % 8
+            offset = lowest + place_ref[1 + quarter] + pair % 8
             partner = near + (base + offset)
             scale = jnp.where(
                 partner < channels,
@@ -264,11 +267,8 @@
         if last:
             shape = (CH_TILE, 8, LAGS)
             rows = pl.ds(base, CH_TILE)
-            keep_ref, other_ref, send_ref = results
-            keep_ref[rows] = turned[0].reshape(shape)
-            other_ref[rows] = turned[1].reshape(shape)
-            for side in range(2):
-                send_ref[side, rows] = turned[2 + side].reshape(shape).astype(jnp.bfloat16)
+            for number, result in enumerate(results):
+                result[rows] = turned[number].reshape(shape).astype(result.dtype)
 
     def all_steps(*sums):
         def body(step, carry):
@@ -287,16 +287,17 @@
     lax.fori_loop(0, steps, drain, 0)
 
 
-def correlated(mesh, places, scales, owns, nexts, fars, lag_table, before=None, last=False):
+def correlated(
+    mesh, places, scales, owns, nexts, fars, lag_table, before, quarters, last
+):
     segs = len(owns)
     channels, columns = owns[0].shape
     steps = channels // (TILES * CH_TILE)
-    raw_shape = (channels // CH_TILE, PAIRS * CH_TILE, LAGS)
+    raw_shape = (channels // CH_TILE, 8 * 3 * CH_TILE, LAGS)
     if last:
         out_shape = [
-            jax.ShapeDtypeStruct((channels, 8, LAGS), jnp.float32),
-            jax.ShapeDtypeStruct((channels, 8, LAGS), jnp.float32),
-            jax.ShapeDtypeStruct((2, channels, 8, LAGS), jnp.bfloat16),
+            jax.ShapeDtypeStruct((channels, 8, LAGS), jnp.float32 if q < 2 else jnp.bfloat16)
+            for q in quarters
         ]
     else:
         out_shape = [jax.ShapeDtypeStruct(raw_shape, jnp.bfloat16)]
@@ -307,13 +308,13 @@
         pltpu.VMEM((8, 128) if before is None else raw_shape, jnp.bfloat16),
         pltpu.SemaphoreType.DMA((3 * segs + 2,)),
         pltpu.SemaphoreType.DMA((steps, 3)),
-        *([pltpu.VMEM((4, CH_TILE * 8, LAGS), jnp.float32)] if last else []),
+        *([pltpu.VMEM((len(quarters), CH_TILE * 8, LAGS), jnp.float32)] if last else []),
         *[pltpu.VMEM(shape.shape, shape.dtype) for shape in out_shape],
     ]
     with jax.sharding.use_abstract_mesh(mesh.abstract_mesh):
         specs = [
             pltpu.ACC(tile)((CH_TILE, 256), jnp.float32)
-            for _ in range(PAIRS)
+            for _ in range(8 * len(quarters))
             for tile in range(TILES)
         ]
     smem = pl.BlockSpec(memory_space=pltpu.SMEM)
@@ -321,15 +322,22 @@
     small = [places, scales] if last else [places]
     large = [*owns, *nexts, *fars, lag_table, *([] if before is None else [before])]
     return pl.pallas_call(
-        functools.partial(cross_kernel, segs=segs, specs=specs, first=before is None, last=last),
+        functools.partial(
+            cross_kernel,
+            segs=segs,
+            specs=specs,
+            quarters=quarters,
+            first=before is None,
+            last=last,
+        ),
         name="cross",
         in_specs=[smem] * len(small) + [anywhere] * len(large),
         out_specs=[anywhere] * len(out_shape),
         out_shape=out_shape,
         scratch_shapes=scratch,
-        compiler_params=pltpu.CompilerParams(vmem_limit_bytes=40 << 20),
+        compiler_params=pltpu.CompilerParams(vmem_limit_bytes=60 << 20),
         cost_estimate=pl.CostEstimate(
-            flops=10 * channels * PAIRS * columns * LAGS,
+            flops=20 * channels * 8 * len(quarters) * columns * LAGS,
             bytes_accessed=6 * segs * channels * columns,
             transcendentals=0,
         ),
@@ -377,21 +385,27 @@
     whites = [white[0] for white in whitened(records, valid_mask, table, 0, segs, 1)]
     fars = [lax.ppermute(white, "chan", hop_far) for white in whites]
     nexts = []
+    passed = None
     for white, far in zip(whites, fars):
+        if passed is not None:
+            far, _ = lax.optimization_barrier((far, passed))
         passed = jnp.where(block % 2 == 0, far, white)
         nexts.append(lax.ppermute(passed, "chan", pair_swap))
-    before = None
-    for part in GROUPS:
-        last = part.stop == segs
-        found = correlated(
-            mesh, places, scales, whites[part], nexts[part], fars[part], lag_table, before, last
-        )
-        before = found[0]
-    keep, other, send = found
+
+    def stacked(part, quarters, before=None, last=True):
+        chosen = (whites[part], nexts[part], fars[part])
+        return correlated(mesh, places, scales, *chosen, lag_table, before, quarters, last)
+
+    half = segs // 2
+    (before,) = stacked(slice(0, half), (1, 3, 2), last=False)
+    other, send_far, send = stacked(slice(half, segs), (1, 3, 2), before)
+    got_far = lax.ppermute(send_far, "tm", core_swap)
     got = lax.ppermute(send, "tm", core_swap)
-    passing = (other + got[1].astype(jnp.float32)).astype(jnp.bfloat16)
-    passed = lax.ppermute(passing, "tm", side_swap)
-    return keep + got[0].astype(jnp.float32) + passed.astype(jnp.float32)
+    passing = (other + got_far.astype(jnp.float32)).astype(jnp.bfloat16)
+    crossed = lax.ppermute(passing, "tm", side_swap)
+    scales, _ = lax.optimization_barrier((scales, passing))
+    (keep,) = stacked(slice(0, segs), (0,))
+    return keep + got.astype(jnp.float32) + crossed.astype(jnp.float32)
 
 
 def solution(mesh):

time: 98.3 us -> 107 us (1.089)
  Pallas kernels: 30.3 us -> 36.4 us
  other arithmetic: 5.23 us -> 8.38 us
  waiting for transfers between devices: 40.3 us -> 38.1 us
  local copies, waits for them, and re-layouts: 3.94 us -> 5.43 us
    ppermute x1 -> x2, waiting for transfers between devices: 8.16 us -> 1.75 us  [the longest x1 1.33 us: shards(): got_far = lax.ppermute(send_far, 'tm', core_swap)]
    pallas_call x2 -> x3, Pallas kernels: 18 us -> 24.1 us  [correlated(): pl.pallas_call(functools.partial(cross_kernel, segs=segs, specs=specs, qu...]
    ppermute x4, waiting for transfers between devices: 7.52 us -> 12.5 us  [shards(): nexts.append(lax.ppermute(passed, 'chan', pair_swap))]
    ppermute x1, waiting for transfers between devices: 2.08 us -> 0.01 us  [shards(): got = lax.ppermute(send, 'tm', core_swap)]
    ppermute x4, waiting for transfers between devices: 20.2 us -> 21.5 us  [shards(): fars = [lax.ppermute(white, 'chan', hop_far) for white in whites]]
    convert_element_type x1, other arithmetic: 0.07 us -> 1.15 us  [shards(): passing = (other + got_far.astype(jnp.float32)).astype(jnp.bfloat16)]
    unnamed x14 -> x20, local copies, waits for them, and re-layouts: 1.96 us -> 2.89 us
  transfers between devices with their start and end apart: 14 -> 15, of which waited for: 8 -> 7; matrix products, arithmetic and copies ran while one was open for 6% -> 8% of each run, Pallas kernels for 20% -> 26%
where the time goes in v6:
time: 107 us; the launch traced here: 106 us
  waiting for transfers between devices  38.1 us (36%)
  Pallas kernels  36.4 us (34%)
  starting transfers between devices  17.7 us (17%)
  other arithmetic  8.38 us (8%)
  local copies, waits for them, and re-layouts  5.43 us (5%)
    pallas_call x3, Pallas kernels, correlated(): pl.pallas_call(functools.partial(cross_kernel, segs=segs, specs=specs, qu...  24.1 us
    ppermute x4, waiting for transfers between devices, shards(): fars = [lax.ppermute(white, 'chan', hop_far) for white in whites]  21.5 us
    ppermute x4, waiting for transfers between devices, shards(): nexts.append(lax.ppermute(passed, 'chan', pair_swap))  12.5 us
    pallas_call x1, Pallas kernels, whitened(): pl.pallas_call(functools.partial(spectra_kernel, first_seg=first_seg), na...  12.3 us
    ppermute x4, starting transfers between devices, shards(): fars = [lax.ppermute(white, 'chan', hop_far) for white in whites]  5.15 us
    select_n x4, other arithmetic, shards(): passed = jnp.where(block % 2 == 0, far, white)  4.51 us
    ppermute x4, starting transfers between devices, shards(): nexts.append(lax.ppermute(passed, 'chan', pair_swap))  4.31 us
    unnamed x20, local copies, waits for them, and re-layouts  2.89 us
  transfers between devices with their start and end apart: 15, of which 7 were waited for; matrix products, arithmetic and copies ran while one was open for 8% of the time, Pallas kernels for 26%

profile of v6, /device:TPU:0, one launch (start us, length us, event | category | flops | bytes accessed | tf_op | source)
XLA Modules:
  0.0 106.2 jit_solution(726763809070656484)
XLA Ops:
  0.0 1.4 %collective-permute-start.1 = (s32[1,4]{1,0:T(1,128)}, s32[1,4]{1,0:T(1,128)S(1)}, u32[]{:S(2)}, u32[]{:S(2)}) collective-permute-start(s32[1,4]{1,0:T(1,128)} %valid_ref.1), channel_id=1, source_target_pairs={{8,0},{12,4},{16,8},{20,12},{24,16},{28,20},{9,1},{13,5},{17,9},{2... | collective-permute-start | bytes 56 | tf_op jit(solution)/shard_map/ppermute | solution.py:365
  1.4 1.3 %collective-permute-start = (s32[1,4]{1,0:T(1,128)}, s32[1,4]{1,0:T(1,128)S(1)}, u32[]{:S(2)}, u32[]{:S(2)}) collective-permute-start(s32[1,4]{1,0:T(1,128)} %valid_ref.1), channel_id=1, source_target_pairs={{4,0},{8,4},{12,8},{16,12},{20,16},{24,20},{28,24},{5,1},{9,5},{13... | collective-permute-start | bytes 56 | tf_op jit(solution)/shard_map/ppermute | solution.py:364
  2.7 12.3 %spectra.1 = (bf16[1,160,1024]{2,1,0:T(8,128)(2,1)}, bf16[1,160,1024]{2,1,0:T(8,128)(2,1)}, bf16[1,160,1024]{2,1,0:T(8,128)(2,1)}, bf16[1,160,1024]{2,1,0:T(8,128)(2,1)}) custom-call(s32[1,4]{1,0:T(1,128)} %valid_ref.1, bf16[160,4,7680]{2,1,0:T(4,128)(2,1)} %second_ref.1, bf16[160,4,7680]{2,1,0:T(4,128)(2,1)} %second_ref.1, ...), custom_call_target="tpu_custom_call" | custom-call | flops 10066329600 | bytes 17694720 | tf_op jit(solution)/shard_map/spectra/pallas_call | solution.py:103
  15.0 1.3 %collective-permute-start.8 = (bf16[160,1024]{1,0:T(8,128)(2,1)}, bf16[160,1024]{1,0:T(8,128)(2,1)S(1)}, u32[]{:S(2)}, u32[]{:S(2)}) collective-permute-start(bf16[160,1024]{1,0:T(8,128)(2,1)} %bitcast.27), channel_id=1, source_target_pairs={{8,0},{12,4},{16,8},{20,12},{24,16},{28,20},{9,1},{13,5},{17,9},{2... | collective-permute-start | bytes 983048 | tf_op jit(solution)/shard_map/ppermute | solution.py:386
  16.3 1.3 %collective-permute-start.4 = (bf16[160,1024]{1,0:T(8,128)(2,1)}, bf16[160,1024]{1,0:T(8,128)(2,1)S(1)}, u32[]{:S(2)}, u32[]{:S(2)}) collective-permute-start(bf16[160,1024]{1,0:T(8,128)(2,1)} %bitcast.24), channel_id=1, source_target_pairs={{8,0},{12,4},{16,8},{20,12},{24,16},{28,20},{9,1},{13,5},{17,9},{2... | collective-permute-start | bytes 983048 | tf_op jit(solution)/shard_map/ppermute | solution.py:386
  17.6 1.3 %collective-permute-start.5 = (bf16[160,1024]{1,0:T(8,128)(2,1)}, bf16[160,1024]{1,0:T(8,128)(2,1)S(1)}, u32[]{:S(2)}, u32[]{:S(2)}) collective-permute-start(bf16[160,1024]{1,0:T(8,128)(2,1)} %bitcast.21), channel_id=1, source_target_pairs={{8,0},{12,4},{16,8},{20,12},{24,16},{28,20},{9,1},{13,5},{17,9},{2... | collective-permute-start | bytes 983048 | tf_op jit(solution)/shard_map/ppermute | solution.py:386
  19.5 1.9 %stack.31.place_ref = s32[6]{0:T(128)} concatenate(s32[1]{0:T(128)} %bitcast, s32[1]{0:T(128)} %bitcast.1, s32[1]{0:T(128)} %bitcast.2, s32[1]{0:T(128)} %bitcast.3, s32[1]{0:T(128)} %bitcast.4, s32[1]{0:T(128)} %bitcast.5), dimensions={0} | concatenate | bytes 48 | tf_op jit(solution)/shard_map/stack | solution.py:372
  21.5 1.3 %collective-permute-start.6 = (bf16[160,1024]{1,0:T(8,128)(2,1)}, bf16[160,1024]{1,0:T(8,128)(2,1)S(1)}, u32[]{:S(2)}, u32[]{:S(2)}) collective-permute-start(bf16[160,1024]{1,0:T(8,128)(2,1)} %bitcast.18), channel_id=1, source_target_pairs={{8,0},{12,4},{16,8},{20,12},{24,16},{28,20},{9,1},{13,5},{17,9},{2... | collective-permute-start | bytes 983048 | tf_op jit(solution)/shard_map/ppermute | solution.py:386
  23.4 0.8 collective-permute-done.2
  24.3 2.8 %collective-permute-start.3 = (s32[3]{0:T(128)S(1)}, s32[3]{0:T(128)S(1)}, u32[]{:S(2)}, u32[]{:S(2)}) collective-permute-start(s32[3]{0:T(128)S(1)} %add.22), channel_id=1, source_target_pairs={{0,2},{1,3},{2,0},{3,1},{4,6},{5,7},{6,4},{7,5},{8,10},{9,11},{10,... | collective-permute-start | bytes 44 | tf_op jit(solution)/shard_map/ppermute | solution.py:370
  27.1 1.5 %collective-permute-done.3 = s32[3]{0:T(128)S(1)} collective-permute-done((s32[3]{0:T(128)S(1)}, s32[3]{0:T(128)S(1)}, u32[]{:S(2)}, u32[]{:S(2)}) %collective-permute-start.3) | collective-permute-done | bytes 44 | tf_op jit(solution)/shard_map/ppermute | solution.py:370
  29.2 21.5 %collective-permute-done.6.rest_4_.rest_9_ = bf16[160,1024]{1,0:T(8,128)(2,1)S(1)} collective-permute-done((bf16[160,1024]{1,0:T(8,128)(2,1)}, bf16[160,1024]{1,0:T(8,128)(2,1)S(1)}, u32[]{:S(2)}, u32[]{:S(2)}) %collective-permute-start.6) | collective-permute-done | bytes 327712 | tf_op jit(solution)/shard_map/ppermute | solution.py:386
  50.6 1.1 %broadcast_select_fusion.3 = bf16[160,1024]{1,0:T(8,128)(2,1)S(1)} fusion(bf16[160,1024]{1,0:T(8,128)(2,1)S(1)} %collective-permute-done.6.rest_4_.rest_9_, pred[]{:T(512)S(6)} %eq.11, bf16[1,160,1024]{2,1,0:T(8,128)(2,1)} %get-tuple-element.19), kind=kLoop, calls=%fused_computation.5 | loop fusion | flops 163840 | bytes 983041 | tf_op jit(solution)/shard_map/jit(_where)/select_n | solution.py:392
  51.7 1.4 %collective-permute-start.10 = (bf16[160,1024]{1,0:T(8,128)(2,1)S(1)}, bf16[160,1024]{1,0:T(8,128)(2,1)S(1)}, u32[]{:S(2)}, u32[]{:S(2)}) collective-permute-start(bf16[160,1024]{1,0:T(8,128)(2,1)S(1)} %broadcast_select_fusion.3), channel_id=1, source_target_pairs={{4,0},{0,4},{12,8},{8,12},{20,16},{16,20},{28,24},{24,28},{5,1},{1... | collective-permute-start | bytes 983048 | tf_op jit(solution)/shard_map/ppermute | solution.py:393
  53.1 1.1 %broadcast_select_fusion.2 = bf16[160,1024]{1,0:T(8,128)(2,1)S(1)} fusion(bf16[160,1024]{1,0:T(8,128)(2,1)S(1)} %collective-permute-done.5.rest_5_.rest_10_, pred[]{:T(512)S(6)} %eq.11, bf16[1,160,1024]{2,1,0:T(8,128)(2,1)} %get-tuple-element.18), kind=kLoop, calls=%fused_computation.4 | loop fusion | flops 163840 | bytes 983041 | tf_op jit(solution)/shard_map/jit(_where)/select_n | solution.py:392
  54.2 0.8 collective-permute-start.11
  55.0 1.1 %broadcast_select_fusion.1 = bf16[160,1024]{1,0:T(8,128)(2,1)S(1)} fusion(bf16[160,1024]{1,0:T(8,128)(2,1)S(1)} %collective-permute-done.4.rest_5_.rest_11_, pred[]{:T(512)S(6)} %eq.11, bf16[1,160,1024]{2,1,0:T(8,128)(2,1)} %get-tuple-element.16), kind=kLoop, calls=%fused_computation.3 | loop fusion | flops 163840 | bytes 983041 | tf_op jit(solution)/shard_map/jit(_where)/select_n | solution.py:392
  56.2 1.4 %collective-permute-start.7 = (bf16[160,1024]{1,0:T(8,128)(2,1)S(1)}, bf16[160,1024]{1,0:T(8,128)(2,1)S(1)}, u32[]{:S(2)}, u32[]{:S(2)}) collective-permute-start(bf16[160,1024]{1,0:T(8,128)(2,1)S(1)} %broadcast_select_fusion.1), channel_id=1, source_target_pairs={{4,0},{0,4},{12,8},{8,12},{20,16},{16,20},{28,24},{24,28},{5,1},{1... | collective-permute-start | bytes 983048 | tf_op jit(solution)/shard_map/ppermute | solution.py:393
  57.5 1.1 %broadcast_select_fusion = bf16[160,1024]{1,0:T(8,128)(2,1)S(1)} fusion(bf16[160,1024]{1,0:T(8,128)(2,1)S(1)} %collective-permute-done.8.rest_6_.rest_12_, pred[]{:T(512)S(6)} %eq.11, bf16[1,160,1024]{2,1,0:T(8,128)(2,1)} %get-tuple-element.17), kind=kLoop, calls=%fused_computation.2 | loop fusion | flops 163840 | bytes 983041 | tf_op jit(solution)/shard_map/jit(_where)/select_n | solution.py:392
  58.7 0.8 collective-permute-start.9
  59.5 10.0 %collective-permute-done.11.rest_3_.rest_6_ = bf16[160,1024]{1,0:T(8,128)(2,1)S(1)} collective-permute-done((bf16[160,1024]{1,0:T(8,128)(2,1)S(1)}, bf16[160,1024]{1,0:T(8,128)(2,1)S(1)}, u32[]{:S(2)}, u32[]{:S(2)}) %collective-permute-start.11) | collective-permute-done | bytes 327712 | tf_op jit(solution)/shard_map/ppermute | solution.py:393
  70.2 0.7 copy-done.6
  70.9 8.0 %cross.3.rest_8_ = bf16[10,384,128]{2,1,0:T(8,128)(2,1)} custom-call(s32[6]{0:T(128)} %stack.31.place_ref, bf16[160,1024]{1,0:T(8,128)(2,1)} %bitcast.19, bf16[160,1024]{1,0:T(8,128)(2,1)} %bitcast.22, bf16[160,1024]{1,0:T(8,128)(2,1)} %copy-done.6, bf16[160,1024]{1,0:T(8,128)(2,1)} %copy-done.7, bf16[160,1024]{1,0:T(8,128)(2,1)} %copy-done.3, ...), custom_call_target="tpu_custom_call" | custom-call | flops 10066329600 | bytes 1966080 | tf_op jit(solution)/shard_map/cross/pallas_call | solution.py:324
  78.9 2.5 %collective-permute-done.9.rest_4_.rest_8_ = bf16[160,1024]{1,0:T(8,128)(2,1)S(1)} collective-permute-done((bf16[160,1024]{1,0:T(8,128)(2,1)S(1)}, bf16[160,1024]{1,0:T(8,128)(2,1)S(1)}, u32[]{:S(2)}, u32[]{:S(2)}) %collective-permute-start.9) | collective-permute-done | bytes 327712 | tf_op jit(solution)/shard_map/ppermute | solution.py:393
  81.5 0.7 copy-done.9
  82.2 0.7 copy-done.8
  82.9 8.4 %cross.4 = (f32[160,8,128]{2,1,0:T(8,128)}, bf16[160,8,128]{2,1,0:T(8,128)(2,1)}, bf16[160,8,128]{2,1,0:T(8,128)(2,1)}) custom-call(s32[6]{0:T(128)} %stack.31.place_ref, f32[3]{0:T(128)} %convert_divide_fusion.rest_0_, bf16[160,1024]{1,0:T(8,128)(2,1)} %bitcast.25, bf16[160,1024]{1,0:T(8,128)(2,1)} %bitcast.28, bf16[160,1024]{1,0:T(8,128)(2,1)} %copy-done.8, ...), custom_call_target="tpu_custom_call" | custom-call | flops 10066329600 | bytes 1966080 | tf_op jit(solution)/shard_map/cross/pallas_call | solution.py:324
  91.9 1.3 %collective-permute-done.12 = bf16[160,8,128]{2,1,0:T(8,128)(2,1)S(1)} collective-permute-done((bf16[160,8,128]{2,1,0:T(8,128)(2,1)}, bf16[160,8,128]{2,1,0:T(8,128)(2,1)S(1)}, u32[]{:S(2)}, u32[]{:S(2)}) %collective-permute-start.12) | collective-permute-done | bytes 327712 | tf_op jit(solution)/shard_map/ppermute | solution.py:402
  93.2 1.2 %add_convert_fusion = bf16[160,8,128]{2,1,0:T(8,128)(2,1)S(1)} fusion(f32[160,8,128]{2,1,0:T(8,128)} %get-tuple-element.23, bf16[160,8,128]{2,1,0:T(8,128)(2,1)S(1)} %collective-permute-done.12), kind=kLoop, calls=%fused_computation.1 | loop fusion | flops 491520 | bytes 1310720 | tf_op jit(solution)/shard_map/convert_element_type | solution.py:404
  94.4 1.6 %collective-permute-start.14 = (bf16[160,8,128]{2,1,0:T(8,128)(2,1)S(1)}, bf16[160,8,128]{2,1,0:T(8,128)(2,1)S(1)}, u32[]{:S(2)}, u32[]{:S(2)}) collective-permute-start(bf16[160,8,128]{2,1,0:T(8,128)(2,1)S(1)} %add_convert_fusion), channel_id=1, source_target_pairs={{0,2},{1,3},{2,0},{3,1},{4,6},{5,7},{6,4},{7,5},{8,10},{9,11},{10,... | collective-permute-start | bytes 983048 | tf_op jit(solution)/shard_map/ppermute | solution.py:405
  96.0 7.7 %cross.5 = f32[160,8,128]{2,1,0:T(8,128)} custom-call(s32[6]{0:T(128)} %stack.31.place_ref, f32[3]{0:T(128)} %convert_divide_fusion.rest_0_, bf16[160,1024]{1,0:T(8,128)(2,1)} %bitcast.20, bf16[160,1024]{1,0:T(8,128)(2,1)} %bitcast.23, bf16[160,1024]{1,0:T(8,128)(2,1)} %bitcast.26, bf16[160,1024]{1,0:T(8,128)(2,1)} %bitcast.29, bf16[160,1024]{1,0:T(8,128)(2,1)} %copy-done.6, ...), custom_call_target="tpu_custom_call" | custom-call | flops 3355443200 | bytes 3932160 | tf_op jit(solution)/shard_map/cross/pallas_call | solution.py:324
  104.2 2.0 %convert_add_fusion = f32[160,8,128]{2,1,0:T(8,128)} fusion(bf16[160,8,128]{2,1,0:T(8,128)(2,1)S(1)} %collective-permute-done.14, f32[160,8,128]{2,1,0:T(8,128)} %cross.5, bf16[160,8,128]{2,1,0:T(8,128)(2,1)S(1)} %collective-permute-done.13), kind=kLoop, calls=%fused_computation | loop fusion | flops 655360 | bytes 1966080 | tf_op jit(solution)/shard_map/add | solution.py:408
  (33 shorter events, 3.5 us)
Async XLA Ops:
  0.0 22.8 %copy-start.4 = (s32[1,4]{1,0:T(1,128)S(1)}, s32[1,4]{1,0:T(1,128)}, u32[]{:S(2)}) copy-start(s32[1,4]{1,0:T(1,128)} %valid_ref.1) | copy-start | bytes 52
  0.0 18.9 %copy-start.5 = (s32[1,2]{1,0:T(1,128)S(1)}, s32[1,2]{1,0:T(1,128)}, u32[]{:S(2)}) copy-start(s32[1,2]{1,0:T(1,128)} %param.7) | copy-start | bytes 28
  0.0 21.5 %collective-permute-start.1 = (s32[1,4]{1,0:T(1,128)}, s32[1,4]{1,0:T(1,128)S(1)}, u32[]{:S(2)}, u32[]{:S(2)}) collective-permute-start(s32[1,4]{1,0:T(1,128)} %valid_ref.1), channel_id=1, source_target_pairs={{8,0},{12,4},{16,8},{20,12},{24,16},{28,20},{9,1},{13,5},{17,9},{2... | collective-permute-start | bytes 56 | tf_op jit(solution)/shard_map/ppermute | solution.py:365
  1.4 21.3 %collective-permute-start = (s32[1,4]{1,0:T(1,128)}, s32[1,4]{1,0:T(1,128)S(1)}, u32[]{:S(2)}, u32[]{:S(2)}) collective-permute-start(s32[1,4]{1,0:T(1,128)} %valid_ref.1), channel_id=1, source_target_pairs={{4,0},{8,4},{12,8},{16,12},{20,16},{24,20},{28,24},{5,1},{9,5},{13... | collective-permute-start | bytes 56 | tf_op jit(solution)/shard_map/ppermute | solution.py:364
  15.0 42.5 %collective-permute-start.8 = (bf16[160,1024]{1,0:T(8,128)(2,1)}, bf16[160,1024]{1,0:T(8,128)(2,1)S(1)}, u32[]{:S(2)}, u32[]{:S(2)}) collective-permute-start(bf16[160,1024]{1,0:T(8,128)(2,1)} %bitcast.27), channel_id=1, source_target_pairs={{8,0},{12,4},{16,8},{20,12},{24,16},{28,20},{9,1},{13,5},{17,9},{2... | collective-permute-start | bytes 983048 | tf_op jit(solution)/shard_map/ppermute | solution.py:386
  16.3 38.8 %collective-permute-start.4 = (bf16[160,1024]{1,0:T(8,128)(2,1)}, bf16[160,1024]{1,0:T(8,128)(2,1)S(1)}, u32[]{:S(2)}, u32[]{:S(2)}) collective-permute-start(bf16[160,1024]{1,0:T(8,128)(2,1)} %bitcast.24), channel_id=1, source_target_pairs={{8,0},{12,4},{16,8},{20,12},{24,16},{28,20},{9,1},{13,5},{17,9},{2... | collective-permute-start | bytes 983048 | tf_op jit(solution)/shard_map/ppermute | solution.py:386
  17.6 35.5 %collective-permute-start.5 = (bf16[160,1024]{1,0:T(8,128)(2,1)}, bf16[160,1024]{1,0:T(8,128)(2,1)S(1)}, u32[]{:S(2)}, u32[]{:S(2)}) collective-permute-start(bf16[160,1024]{1,0:T(8,128)(2,1)} %bitcast.21), channel_id=1, source_target_pairs={{8,0},{12,4},{16,8},{20,12},{24,16},{28,20},{9,1},{13,5},{17,9},{2... | collective-permute-start | bytes 983048 | tf_op jit(solution)/shard_map/ppermute | solution.py:386
  21.5 29.1 %collective-permute-start.6 = (bf16[160,1024]{1,0:T(8,128)(2,1)}, bf16[160,1024]{1,0:T(8,128)(2,1)S(1)}, u32[]{:S(2)}, u32[]{:S(2)}) collective-permute-start(bf16[160,1024]{1,0:T(8,128)(2,1)} %bitcast.18), channel_id=1, source_target_pairs={{8,0},{12,4},{16,8},{20,12},{24,16},{28,20},{9,1},{13,5},{17,9},{2... | collective-permute-start | bytes 983048 | tf_op jit(solution)/shard_map/ppermute | solution.py:386
  22.9 1.3 %collective-permute-start.2 = (s32[3]{0:T(128)S(1)}, s32[3]{0:T(128)S(1)}, u32[]{:S(2)}, u32[]{:S(2)}) collective-permute-start(s32[3]{0:T(128)S(1)} %fusion), channel_id=1, source_target_pairs={{0,1},{1,0},{2,3},{3,2},{4,5},{5,4},{6,7},{7,6},{8,9},{9,8},{10,11... | collective-permute-start | bytes 44 | tf_op jit(solution)/shard_map/ppermute | solution.py:369
  24.3 4.3 %collective-permute-start.3 = (s32[3]{0:T(128)S(1)}, s32[3]{0:T(128)S(1)}, u32[]{:S(2)}, u32[]{:S(2)}) collective-permute-start(s32[3]{0:T(128)S(1)} %add.22), channel_id=1, source_target_pairs={{0,2},{1,3},{2,0},{3,1},{4,6},{5,7},{6,4},{7,5},{8,10},{9,11},{10,... | collective-permute-start | bytes 44 | tf_op jit(solution)/shard_map/ppermute | solution.py:370
  50.6 18.9 %copy-start.3 = (bf16[160,1024]{1,0:T(8,128)(2,1)}, bf16[160,1024]{1,0:T(8,128)(2,1)S(1)}, u32[]{:S(2)}) copy-start(bf16[160,1024]{1,0:T(8,128)(2,1)S(1)} %collective-permute-done.6.rest_4_.rest_9_) | copy-start | bytes 983044
  51.7 17.7 %collective-permute-start.10 = (bf16[160,1024]{1,0:T(8,128)(2,1)S(1)}, bf16[160,1024]{1,0:T(8,128)(2,1)S(1)}, u32[]{:S(2)}, u32[]{:S(2)}) collective-permute-start(bf16[160,1024]{1,0:T(8,128)(2,1)S(1)} %broadcast_select_fusion.3), channel_id=1, source_target_pairs={{4,0},{0,4},{12,8},{8,12},{20,16},{16,20},{28,24},{24,28},{5,1},{1... | collective-permute-start | bytes 983048 | tf_op jit(solution)/shard_map/ppermute | solution.py:393
  53.1 16.4 %copy-start.2 = (bf16[160,1024]{1,0:T(8,128)(2,1)}, bf16[160,1024]{1,0:T(8,128)(2,1)S(1)}, u32[]{:S(2)}) copy-start(bf16[160,1024]{1,0:T(8,128)(2,1)S(1)} %collective-permute-done.5.rest_5_.rest_10_) | copy-start | bytes 983044
  54.2 15.2 %collective-permute-start.11 = (bf16[160,1024]{1,0:T(8,128)(2,1)S(1)}, bf16[160,1024]{1,0:T(8,128)(2,1)S(1)}, u32[]{:S(2)}, u32[]{:S(2)}) collective-permute-start(bf16[160,1024]{1,0:T(8,128)(2,1)S(1)} %broadcast_select_fusion.2), channel_id=1, source_target_pairs={{4,0},{0,4},{12,8},{8,12},{20,16},{16,20},{28,24},{24,28},{5,1},{1... | collective-permute-start | bytes 983048 | tf_op jit(solution)/shard_map/ppermute | solution.py:393
  55.0 23.9 %copy-start.1 = (bf16[160,1024]{1,0:T(8,128)(2,1)}, bf16[160,1024]{1,0:T(8,128)(2,1)S(1)}, u32[]{:S(2)}) copy-start(bf16[160,1024]{1,0:T(8,128)(2,1)S(1)} %collective-permute-done.4.rest_5_.rest_11_) | copy-start | bytes 983044
  56.2 25.3 %collective-permute-start.7 = (bf16[160,1024]{1,0:T(8,128)(2,1)S(1)}, bf16[160,1024]{1,0:T(8,128)(2,1)S(1)}, u32[]{:S(2)}, u32[]{:S(2)}) collective-permute-start(bf16[160,1024]{1,0:T(8,128)(2,1)S(1)} %broadcast_select_fusion.1), channel_id=1, source_target_pairs={{4,0},{0,4},{12,8},{8,12},{20,16},{16,20},{28,24},{24,28},{5,1},{1... | collective-permute-start | bytes 983048 | tf_op jit(solution)/shard_map/ppermute | solution.py:393
  57.5 21.4 %copy-start = (bf16[160,1024]{1,0:T(8,128)(2,1)}, bf16[160,1024]{1,0:T(8,128)(2,1)S(1)}, u32[]{:S(2)}) copy-start(bf16[160,1024]{1,0:T(8,128)(2,1)S(1)} %collective-permute-done.8.rest_6_.rest_12_) | copy-start | bytes 983044
  58.7 22.8 %collective-permute-start.9 = (bf16[160,1024]{1,0:T(8,128)(2,1)S(1)}, bf16[160,1024]{1,0:T(8,128)(2,1)S(1)}, u32[]{:S(2)}, u32[]{:S(2)}) collective-permute-start(bf16[160,1024]{1,0:T(8,128)(2,1)S(1)} %broadcast_select_fusion), channel_id=1, source_target_pairs={{4,0},{0,4},{12,8},{8,12},{20,16},{16,20},{28,24},{24,28},{5,1},{1... | collective-permute-start | bytes 983048 | tf_op jit(solution)/shard_map/ppermute | solution.py:393
  69.5 0.7 copy-start.7
  70.2 0.7 copy-start.6
  81.5 0.7 copy-start.9
  82.2 0.7 copy-start.8
  91.3 1.9 %collective-permute-start.12 = (bf16[160,8,128]{2,1,0:T(8,128)(2,1)}, bf16[160,8,128]{2,1,0:T(8,128)(2,1)S(1)}, u32[]{:S(2)}, u32[]{:S(2)}) collective-permute-start(bf16[160,8,128]{2,1,0:T(8,128)(2,1)} %get-tuple-element.24), channel_id=1, source_target_pairs={{0,1},{1,0},{2,3},{3,2},{4,5},{5,4},{6,7},{7,6},{8,9},{9,8},{10,11... | collective-permute-start | bytes 983048 | tf_op jit(solution)/shard_map/ppermute | solution.py:402
  91.4 12.4 %collective-permute-start.13 = (bf16[160,8,128]{2,1,0:T(8,128)(2,1)}, bf16[160,8,128]{2,1,0:T(8,128)(2,1)S(1)}, u32[]{:S(2)}, u32[]{:S(2)}) collective-permute-start(bf16[160,8,128]{2,1,0:T(8,128)(2,1)} %get-tuple-element.26), channel_id=1, source_target_pairs={{0,1},{1,0},{2,3},{3,2},{4,5},{5,4},{6,7},{7,6},{8,9},{9,8},{10,11... | collective-permute-start | bytes 983048 | tf_op jit(solution)/shard_map/ppermute | solution.py:403
  94.4 9.8 %collective-permute-start.14 = (bf16[160,8,128]{2,1,0:T(8,128)(2,1)S(1)}, bf16[160,8,128]{2,1,0:T(8,128)(2,1)S(1)}, u32[]{:S(2)}, u32[]{:S(2)}) collective-permute-start(bf16[160,8,128]{2,1,0:T(8,128)(2,1)S(1)} %add_convert_fusion), channel_id=1, source_target_pairs={{0,2},{1,3},{2,0},{3,1},{4,6},{5,7},{6,4},{7,5},{8,10},{9,11},{10,... | collective-permute-start | bytes 983048 | tf_op jit(solution)/shard_map/ppermute | solution.py:405

commit v7 on v6

--- a/solution.py
+++ b/solution.py
@@ -13,7 +13,7 @@
 LAGS = 128
 PAIRS = 32
 REACH = 2
-STEPS = 3
+STEPS = 5
 
 
 def bin_order(bins):
@@ -130,10 +130,10 @@
 WINDOW = 13
 
 
-def cross_kernel(place_ref, *rest, segs, specs, quarters, first, last):
+def cross_kernel(place_ref, *rest, segs, parts, specs, quarters, first, last):
     if last:
         scale_ref, *rest = rest
-    sources, rest = rest[: 3 * segs], rest[3 * segs :]
+    sources, rest = rest[: 3 * parts], rest[3 * parts :]
     lag_hbm, *rest = rest
     if not first:
         before_hbm, *rest = rest
@@ -149,18 +149,19 @@
     lowest = place_ref[0]
     origin = lowest // CH_TILE * CH_TILE
 
+    group = segs // parts
     loads = [
         pltpu.make_async_copy(
-            sources[hop * segs + seg],
-            extended.at[seg, pl.ds(hop * channels, channels), :],
-            in_sems.at[hop * segs + seg],
+            sources[hop * parts + part],
+            extended.at[pl.ds(part * group, group), pl.ds(hop * channels, channels), :],
+            in_sems.at[hop * parts + part],
         )
         for hop in range(REACH + 1)
-        for seg in range(segs)
+        for part in range(parts)
     ]
-    loads.append(pltpu.make_async_copy(lag_hbm, lag_ref, in_sems.at[3 * segs]))
+    loads.append(pltpu.make_async_copy(lag_hbm, lag_ref, in_sems.at[3 * parts]))
     if not first:
-        earlier = pltpu.make_async_copy(before_hbm, before, in_sems.at[3 * segs + 1])
+        earlier = pltpu.make_async_copy(before_hbm, before, in_sems.at[3 * parts + 1])
     for load in loads:
         load.start()
     if not first:
@@ -290,8 +291,8 @@
 def correlated(
     mesh, places, scales, owns, nexts, fars, lag_table, before, quarters, last
 ):
-    segs = len(owns)
-    channels, columns = owns[0].shape
+    group, channels, columns = owns[0].shape
+    segs = group * len(owns)
     steps = channels // (TILES * CH_TILE)
     raw_shape = (channels // CH_TILE, 8 * 3 * CH_TILE, LAGS)
     if last:
@@ -306,7 +307,7 @@
         pltpu.VMEM(lag_table.shape, lag_table.dtype),
         pltpu.VMEM((segs * columns // 128, WINDOW * CH_TILE, 128), jnp.float32),
         pltpu.VMEM((8, 128) if before is None else raw_shape, jnp.bfloat16),
-        pltpu.SemaphoreType.DMA((3 * segs + 2,)),
+        pltpu.SemaphoreType.DMA((3 * len(owns) + 2,)),
         pltpu.SemaphoreType.DMA((steps, 3)),
         *([pltpu.VMEM((len(quarters), CH_TILE * 8, LAGS), jnp.float32)] if last else []),
         *[pltpu.VMEM(shape.shape, shape.dtype) for shape in out_shape],
@@ -325,6 +326,7 @@
         functools.partial(
             cross_kernel,
             segs=segs,
+            parts=len(owns),
             specs=specs,
             quarters=quarters,
             first=before is None,
@@ -358,17 +360,6 @@
     core_swap = [(i, i ^ 1) for i in range(4)]
     side_swap = [(i, i ^ 2) for i in range(4)]
 
-    marks = jnp.stack(
-        [
-            valid_mask,
-            lax.ppermute(valid_mask, "chan", hop_near),
-            lax.ppermute(valid_mask, "chan", hop_far),
-        ]
-    )
-    counts = jnp.sum(marks * valid_mask[None], axis=(1, 2))
-    counts += lax.ppermute(counts, "tm", core_swap)
-    counts += lax.ppermute(counts, "tm", side_swap)
-    scales = 1.0 / jnp.maximum(counts, 1).astype(jnp.float32)
     places = jnp.stack(
         [
             lowest,
@@ -382,13 +373,23 @@
 
     lag_table = jnp.asarray(lag_table_of(samples, BINS, LAGS))
     table = jnp.asarray(dft_table_of(samples, BINS))
-    whites = [white[0] for white in whitened(records, valid_mask, table, 0, segs, 1)]
+    half = segs // 2
+    whites = [whitened(records, valid_mask, table, first, 1, half)[0] for first in (0, half)]
     fars = [lax.ppermute(white, "chan", hop_far) for white in whites]
+    valid_mask, _ = lax.optimization_barrier((valid_mask, whites[1]))
+    marks = jnp.stack(
+        [
+            valid_mask,
+            lax.ppermute(valid_mask, "chan", hop_near),
+            lax.ppermute(valid_mask, "chan", hop_far),
+        ]
+    )
+    counts = jnp.sum(marks * valid_mask[None], axis=(1, 2))
+    counts += lax.ppermute(counts, "tm", core_swap)
+    counts += lax.ppermute(counts, "tm", side_swap)
+    scales = 1.0 / jnp.maximum(counts, 1).astype(jnp.float32)
     nexts = []
-    passed = None
     for white, far in zip(whites, fars):
-        if passed is not None:
-            far, _ = lax.optimization_barrier((far, passed))
         passed = jnp.where(block % 2 == 0, far, white)
         nexts.append(lax.ppermute(passed, "chan", pair_swap))
 
@@ -396,15 +397,14 @@
         chosen = (whites[part], nexts[part], fars[part])
         return correlated(mesh, places, scales, *chosen, lag_table, before, quarters, last)
 
-    half = segs // 2
-    (before,) = stacked(slice(0, half), (1, 3, 2), last=False)
-    other, send_far, send = stacked(slice(half, segs), (1, 3, 2), before)
+    (before,) = stacked(slice(0, 1), (1, 3, 2), last=False)
+    other, send_far, send = stacked(slice(1, 2), (1, 3, 2), before)
     got_far = lax.ppermute(send_far, "tm", core_swap)
     got = lax.ppermute(send, "tm", core_swap)
     passing = (other + got_far.astype(jnp.float32)).astype(jnp.bfloat16)
     crossed = lax.ppermute(passing, "tm", side_swap)
     scales, _ = lax.optimization_barrier((scales, passing))
-    (keep,) = stacked(slice(0, segs), (0,))
+    (keep,) = stacked(slice(0, 2), (0,))
     return keep + got.astype(jnp.float32) + crossed.astype(jnp.float32)
 
 

time: 107 us -> 89.3 us (0.83)
  waiting for transfers between devices: 38.1 us -> 21.2 us
  Pallas kernels: 36.4 us -> 46.5 us
  other arithmetic: 8.38 us -> 4.06 us
  starting transfers between devices: 17.7 us -> 13.7 us
  local copies, waits for them, and re-layouts: 5.43 us -> 3.26 us
    ppermute x4 -> x2, waiting for transfers between devices: 21.5 us -> 10.7 us  [shards(): fars = [lax.ppermute(white, 'chan', hop_far) for white in whites]]
    pallas_call x1 -> x2, Pallas kernels: 12.3 us -> 22.6 us  [whitened(): pl.pallas_call(functools.partial(spectra_kernel, first_seg=first_seg), na...]
    ppermute x4 -> x2, waiting for transfers between devices: 12.5 us -> 5.13 us  [shards(): nexts.append(lax.ppermute(passed, 'chan', pair_swap))]
    select_n x4 -> x2, other arithmetic: 4.51 us -> 0.14 us  [shards(): passed = jnp.where(block % 2 == 0, far, white)]
    ppermute x4 -> x2, starting transfers between devices: 5.15 us -> 2.72 us  [shards(): fars = [lax.ppermute(white, 'chan', hop_far) for white in whites]]
    unnamed x20 -> x12, local copies, waits for them, and re-layouts: 2.89 us -> 0.85 us
    ppermute x1, starting transfers between devices: 2.82 us -> 1.52 us  [shards(): counts += lax.ppermute(counts, 'tm', side_swap)]
    ppermute x4 -> x2, starting transfers between devices: 4.31 us -> 4.84 us  [shards(): nexts.append(lax.ppermute(passed, 'chan', pair_swap))]
  transfers between devices with their start and end apart: 15 -> 11, of which waited for: 7 -> 7; matrix products, arithmetic and copies ran while one was open for 8% -> 5% of each run, Pallas kernels for 26% -> 30%
where the time goes in v7:
time: 89.3 us; the launch traced here: 88.8 us
  Pallas kernels  46.5 us (52%)
  waiting for transfers between devices  21.2 us (24%)
  starting transfers between devices  13.7 us (15%)
  other arithmetic  4.06 us (5%)
  local copies, waits for them, and re-layouts  3.26 us (4%)
    pallas_call x3, Pallas kernels, correlated(): pl.pallas_call(functools.partial(cross_kernel, segs=segs, parts=len(owns)...  23.9 us
    pallas_call x2, Pallas kernels, whitened(): pl.pallas_call(functools.partial(spectra_kernel, first_seg=first_seg), na...  22.6 us
    ppermute x2, waiting for transfers between devices, shards(): fars = [lax.ppermute(white, 'chan', hop_far) for white in whites]  10.7 us
    ppermute x2, waiting for transfers between devices, shards(): nexts.append(lax.ppermute(passed, 'chan', pair_swap))  5.13 us
    ppermute x2, starting transfers between devices, shards(): nexts.append(lax.ppermute(passed, 'chan', pair_swap))  4.84 us
    ppermute x2, starting transfers between devices, shards(): fars = [lax.ppermute(white, 'chan', hop_far) for white in whites]  2.72 us
    ppermute x1, waiting for transfers between devices, shards(): counts += lax.ppermute(counts, 'tm', side_swap)  2.02 us
    add x1, other arithmetic, shards(): return keep + got.astype(jnp.float32) + crossed.astype(jnp.float32)  2.01 us
  transfers between devices with their start and end apart: 11, of which 7 were waited for; matrix products, arithmetic and copies ran while one was open for 5% of the time, Pallas kernels for 30%

profile of v7, /device:TPU:0, one launch (start us, length us, event | category | flops | bytes accessed | tf_op | source)
XLA Modules:
  0.0 88.8 jit_solution(6474156869833319910)
XLA Ops:
  0.0 11.3 %spectra.3.rest_0_.rest_1_ = bf16[2,160,1024]{2,1,0:T(8,128)(2,1)} custom-call(s32[1,4]{1,0:T(1,128)} %valid_ref.3, bf16[160,4,7680]{2,1,0:T(4,128)(2,1)} %second_ref.3, bf16[160,4,7680]{2,1,0:T(4,128)(2,1)} %second_ref.3, bf16[3840,1024]{1,0:T(8,128)(2,1)} %constant.38.clone.table_ref), custom_call_target="tpu_custom_call" | custom-call | flops 5033164800 | bytes 17694720 | tf_op jit(solution)/shard_map/spectra/pallas_call | solution.py:103
  11.3 1.4 %collective-permute-start.6 = (bf16[2,160,1024]{2,1,0:T(8,128)(2,1)}, bf16[2,160,1024]{2,1,0:T(8,128)(2,1)S(1)}, u32[]{:S(2)}, u32[]{:S(2)}) collective-permute-start(bf16[2,160,1024]{2,1,0:T(8,128)(2,1)} %spectra.3.rest_0_.rest_1_), channel_id=1, source_target_pairs={{8,0},{12,4},{16,8},{20,12},{24,16},{28,20},{9,1},{13,5},{17,9},{2... | collective-permute-start | bytes 1966088 | tf_op jit(solution)/shard_map/ppermute | solution.py:378
  12.8 11.3 %spectra.2.rest_1_.rest_2_ = bf16[2,160,1024]{2,1,0:T(8,128)(2,1)} custom-call(s32[1,4]{1,0:T(1,128)} %valid_ref.3, bf16[160,4,7680]{2,1,0:T(4,128)(2,1)} %second_ref.3, bf16[160,4,7680]{2,1,0:T(4,128)(2,1)} %second_ref.3, bf16[3840,1024]{1,0:T(8,128)(2,1)} %constant.38.clone.table_ref), custom_call_target="tpu_custom_call" | custom-call | flops 5033164800 | bytes 17694720 | tf_op jit(solution)/shard_map/spectra/pallas_call | solution.py:103
  24.1 1.3 %collective-permute-start.1 = (s32[1,4]{1,0:T(1,128)S(1)}, s32[1,4]{1,0:T(1,128)S(1)}, u32[]{:S(2)}, u32[]{:S(2)}) collective-permute-start(s32[1,4]{1,0:T(1,128)S(1)} %copy-done.3), channel_id=1, source_target_pairs={{8,0},{12,4},{16,8},{20,12},{24,16},{28,20},{9,1},{13,5},{17,9},{2... | collective-permute-start | bytes 56 | tf_op jit(solution)/shard_map/ppermute | solution.py:384
  25.4 1.3 %collective-permute-start = (s32[1,4]{1,0:T(1,128)S(1)}, s32[1,4]{1,0:T(1,128)S(1)}, u32[]{:S(2)}, u32[]{:S(2)}) collective-permute-start(s32[1,4]{1,0:T(1,128)S(1)} %copy-done.3), channel_id=1, source_target_pairs={{4,0},{8,4},{12,8},{16,12},{20,16},{24,20},{28,24},{5,1},{9,5},{13... | collective-permute-start | bytes 56 | tf_op jit(solution)/shard_map/ppermute | solution.py:383
  26.7 1.3 %collective-permute-start.4 = (bf16[2,160,1024]{2,1,0:T(8,128)(2,1)}, bf16[2,160,1024]{2,1,0:T(8,128)(2,1)S(1)}, u32[]{:S(2)}, u32[]{:S(2)}) collective-permute-start(bf16[2,160,1024]{2,1,0:T(8,128)(2,1)} %spectra.2.rest_1_.rest_2_), channel_id=1, source_target_pairs={{8,0},{12,4},{16,8},{20,12},{24,16},{28,20},{9,1},{13,5},{17,9},{2... | collective-permute-start | bytes 1966088 | tf_op jit(solution)/shard_map/ppermute | solution.py:378
  28.0 3.4 %collective-permute-done.6.rest_2_.rest_5_ = bf16[2,160,1024]{2,1,0:T(8,128)(2,1)S(1)} collective-permute-done((bf16[2,160,1024]{2,1,0:T(8,128)(2,1)}, bf16[2,160,1024]{2,1,0:T(8,128)(2,1)S(1)}, u32[]{:S(2)}, u32[]{:S(2)}) %collective-permute-start.6) | collective-permute-done | bytes 655392 | tf_op jit(solution)/shard_map/ppermute | solution.py:378
  31.3 0.1 broadcast_select_fusion
  31.4 1.7 %collective-permute-start.7 = (bf16[2,160,1024]{2,1,0:T(8,128)(2,1)S(1)}, bf16[2,160,1024]{2,1,0:T(8,128)(2,1)S(1)}, u32[]{:S(2)}, u32[]{:S(2)}) collective-permute-start(bf16[2,160,1024]{2,1,0:T(8,128)(2,1)S(1)} %broadcast_select_fusion), channel_id=1, source_target_pairs={{4,0},{0,4},{12,8},{8,12},{20,16},{16,20},{28,24},{24,28},{5,1},{1... | collective-permute-start | bytes 1966088 | tf_op jit(solution)/shard_map/ppermute | solution.py:394
  33.1 0.6 fusion.1
  33.7 1.8 %stack.31.place_ref = s32[6]{0:T(128)} concatenate(s32[1]{0:T(128)} %bitcast, s32[1]{0:T(128)} %bitcast.1, s32[1]{0:T(128)} %bitcast.2, s32[1]{0:T(128)} %bitcast.3, s32[1]{0:T(128)} %bitcast.4, s32[1]{0:T(128)} %bitcast.5), dimensions={0} | concatenate | bytes 48 | tf_op jit(solution)/shard_map/stack | solution.py:363
  35.5 0.2 fusion
  35.7 0.1 collective-permute-start.2
  35.8 1.1 %collective-permute-done.2 = s32[3]{0:T(128)S(1)} collective-permute-done((s32[3]{0:T(128)S(1)}, s32[3]{0:T(128)S(1)}, u32[]{:S(2)}, u32[]{:S(2)}) %collective-permute-start.2) | collective-permute-done | bytes 44 | tf_op jit(solution)/shard_map/ppermute | solution.py:388
  36.9 1.5 %collective-permute-start.3 = (s32[3]{0:T(128)S(1)}, s32[3]{0:T(128)S(1)}, u32[]{:S(2)}, u32[]{:S(2)}) collective-permute-start(s32[3]{0:T(128)S(1)} %add.20), channel_id=1, source_target_pairs={{0,2},{1,3},{2,0},{3,1},{4,6},{5,7},{6,4},{7,5},{8,10},{9,11},{10,... | collective-permute-start | bytes 44 | tf_op jit(solution)/shard_map/ppermute | solution.py:389
  38.4 2.0 %collective-permute-done.3 = s32[3]{0:T(128)S(1)} collective-permute-done((s32[3]{0:T(128)S(1)}, s32[3]{0:T(128)S(1)}, u32[]{:S(2)}, u32[]{:S(2)}) %collective-permute-start.3) | collective-permute-done | bytes 44 | tf_op jit(solution)/shard_map/ppermute | solution.py:389
  40.4 0.6 convert_divide_fusion.rest_0_
  41.0 7.4 %collective-permute-done.4.rest_3_.rest_6_ = bf16[2,160,1024]{2,1,0:T(8,128)(2,1)S(1)} collective-permute-done((bf16[2,160,1024]{2,1,0:T(8,128)(2,1)}, bf16[2,160,1024]{2,1,0:T(8,128)(2,1)S(1)}, u32[]{:S(2)}, u32[]{:S(2)}) %collective-permute-start.4) | collective-permute-done | bytes 655392 | tf_op jit(solution)/shard_map/ppermute | solution.py:378
  48.4 0.1 broadcast_select_fusion.1
  48.5 3.1 %collective-permute-start.5 = (bf16[2,160,1024]{2,1,0:T(8,128)(2,1)S(1)}, bf16[2,160,1024]{2,1,0:T(8,128)(2,1)}, u32[]{:S(2)}, u32[]{:S(2)}) collective-permute-start(bf16[2,160,1024]{2,1,0:T(8,128)(2,1)S(1)} %broadcast_select_fusion.1), channel_id=1, source_target_pairs={{4,0},{0,4},{12,8},{8,12},{20,16},{16,20},{28,24},{24,28},{5,1},{1... | collective-permute-start | bytes 1966088 | tf_op jit(solution)/shard_map/ppermute | solution.py:394
  51.6 0.8 copy-done.5
  52.4 8.0 %cross.3.rest_5_ = bf16[10,384,128]{2,1,0:T(8,128)(2,1)} custom-call(s32[6]{0:T(128)} %stack.31.place_ref, bf16[2,160,1024]{2,1,0:T(8,128)(2,1)} %spectra.3.rest_0_.rest_1_, bf16[2,160,1024]{2,1,0:T(8,128)(2,1)} %copy-done.5, bf16[2,160,1024]{2,1,0:T(8,128)(2,1)} %copy-done.1, bf16[4,256,256]{2,1,0:T(8,128)(2,1)} %constant.37.clone.rest_3_.rest_4_.rest_7_), custom_call_target="tpu_custom_call" | custom-call | flops 10066329600 | bytes 1966080 | tf_op jit(solution)/shard_map/cross/pallas_call | solution.py:325
  60.5 5.1 %collective-permute-done.5.rest_2_.rest_4_ = bf16[2,160,1024]{2,1,0:T(8,128)(2,1)} collective-permute-done((bf16[2,160,1024]{2,1,0:T(8,128)(2,1)S(1)}, bf16[2,160,1024]{2,1,0:T(8,128)(2,1)}, u32[]{:S(2)}, u32[]{:S(2)}) %collective-permute-start.5) | collective-permute-done | bytes 655392 | tf_op jit(solution)/shard_map/ppermute | solution.py:394
  65.6 8.4 %cross.4 = (f32[160,8,128]{2,1,0:T(8,128)}, bf16[160,8,128]{2,1,0:T(8,128)(2,1)}, bf16[160,8,128]{2,1,0:T(8,128)(2,1)}) custom-call(s32[6]{0:T(128)} %stack.31.place_ref, f32[3]{0:T(128)} %convert_divide_fusion.rest_0_, bf16[2,160,1024]{2,1,0:T(8,128)(2,1)} %spectra.2.rest_1_.rest_2_, bf16[2,160,1024]{2,1,0:T(8,128)(2,1)} %collective-permute-done.5.rest_2_.rest_4_, ...), custom_call_target="tpu_custom_call" | custom-call | flops 10066329600 | bytes 1966080 | tf_op jit(solution)/shard_map/cross/pallas_call | solution.py:325
  73.9 0.1 collective-permute-start.8
  74.0 0.5 collective-permute-start.9
  74.5 1.3 %collective-permute-done.8 = bf16[160,8,128]{2,1,0:T(8,128)(2,1)S(1)} collective-permute-done((bf16[160,8,128]{2,1,0:T(8,128)(2,1)}, bf16[160,8,128]{2,1,0:T(8,128)(2,1)S(1)}, u32[]{:S(2)}, u32[]{:S(2)}) %collective-permute-start.8) | collective-permute-done | bytes 327712 | tf_op jit(solution)/shard_map/ppermute | solution.py:402
  75.8 1.2 %add_convert_fusion = bf16[160,8,128]{2,1,0:T(8,128)(2,1)S(1)} fusion(f32[160,8,128]{2,1,0:T(8,128)} %get-tuple-element.11, bf16[160,8,128]{2,1,0:T(8,128)(2,1)S(1)} %collective-permute-done.8), kind=kLoop, calls=%fused_computation.1 | loop fusion | flops 491520 | bytes 1310720 | tf_op jit(solution)/shard_map/convert_element_type | solution.py:404
  77.0 1.4 %collective-permute-start.10 = (bf16[160,8,128]{2,1,0:T(8,128)(2,1)S(1)}, bf16[160,8,128]{2,1,0:T(8,128)(2,1)S(1)}, u32[]{:S(2)}, u32[]{:S(2)}) collective-permute-start(bf16[160,8,128]{2,1,0:T(8,128)(2,1)S(1)} %add_convert_fusion), channel_id=1, source_target_pairs={{0,2},{1,3},{2,0},{3,1},{4,6},{5,7},{6,4},{7,5},{8,10},{9,11},{10,... | collective-permute-start | bytes 983048 | tf_op jit(solution)/shard_map/ppermute | solution.py:405
  78.4 7.5 %cross.5 = f32[160,8,128]{2,1,0:T(8,128)} custom-call(s32[6]{0:T(128)} %stack.31.place_ref, f32[3]{0:T(128)} %convert_divide_fusion.rest_0_, bf16[2,160,1024]{2,1,0:T(8,128)(2,1)} %spectra.3.rest_0_.rest_1_, bf16[2,160,1024]{2,1,0:T(8,128)(2,1)} %spectra.2.rest_1_.rest_2_, bf16[2,160,1024]{2,1,0:T(8,128)(2,1)} %copy-done.5, ...), custom_call_target="tpu_custom_call" | custom-call | flops 3355443200 | bytes 3932160 | tf_op jit(solution)/shard_map/cross/pallas_call | solution.py:325
  85.9 0.9 %collective-permute-done.10 = bf16[160,8,128]{2,1,0:T(8,128)(2,1)S(1)} collective-permute-done((bf16[160,8,128]{2,1,0:T(8,128)(2,1)S(1)}, bf16[160,8,128]{2,1,0:T(8,128)(2,1)S(1)}, u32[]{:S(2)}, u32[]{:S(2)}) %collective-permute-start.10) | collective-permute-done | bytes 327712 | tf_op jit(solution)/shard_map/ppermute | solution.py:405
  86.8 2.0 %convert_add_fusion = f32[160,8,128]{2,1,0:T(8,128)} fusion(bf16[160,8,128]{2,1,0:T(8,128)(2,1)S(1)} %collective-permute-done.10, f32[160,8,128]{2,1,0:T(8,128)} %cross.5, bf16[160,8,128]{2,1,0:T(8,128)(2,1)S(1)} %collective-permute-done.9), kind=kLoop, calls=%fused_computation | loop fusion | flops 655360 | bytes 1966080 | tf_op jit(solution)/shard_map/add | solution.py:408
  (16 shorter events, 0.0 us)
Async XLA Ops:
  11.3 12.7 %copy-start.3 = (s32[1,4]{1,0:T(1,128)S(1)}, s32[1,4]{1,0:T(1,128)}, u32[]{:S(2)}) copy-start(s32[1,4]{1,0:T(1,128)} %valid_ref.3) | copy-start | bytes 52
  11.3 20.0 %copy-start = (bf16[2,160,1024]{2,1,0:T(8,128)(2,1)S(1)}, bf16[2,160,1024]{2,1,0:T(8,128)(2,1)}, u32[]{:S(2)}) copy-start(bf16[2,160,1024]{2,1,0:T(8,128)(2,1)} %spectra.3.rest_0_.rest_1_) | copy-start | bytes 1966084
  11.3 21.8 %copy-start.4 = (s32[1,2]{1,0:T(1,128)S(1)}, s32[1,2]{1,0:T(1,128)}, u32[]{:S(2)}) copy-start(s32[1,2]{1,0:T(1,128)} %param.7) | copy-start | bytes 28
  11.3 20.0 %collective-permute-start.6 = (bf16[2,160,1024]{2,1,0:T(8,128)(2,1)}, bf16[2,160,1024]{2,1,0:T(8,128)(2,1)S(1)}, u32[]{:S(2)}, u32[]{:S(2)}) collective-permute-start(bf16[2,160,1024]{2,1,0:T(8,128)(2,1)} %spectra.3.rest_0_.rest_1_), channel_id=1, source_target_pairs={{8,0},{12,4},{16,8},{20,12},{24,16},{28,20},{9,1},{13,5},{17,9},{2... | collective-permute-start | bytes 1966088 | tf_op jit(solution)/shard_map/ppermute | solution.py:378
  24.1 11.5 %collective-permute-start.1 = (s32[1,4]{1,0:T(1,128)S(1)}, s32[1,4]{1,0:T(1,128)S(1)}, u32[]{:S(2)}, u32[]{:S(2)}) collective-permute-start(s32[1,4]{1,0:T(1,128)S(1)} %copy-done.3), channel_id=1, source_target_pairs={{8,0},{12,4},{16,8},{20,12},{24,16},{28,20},{9,1},{13,5},{17,9},{2... | collective-permute-start | bytes 56 | tf_op jit(solution)/shard_map/ppermute | solution.py:384
  25.4 10.2 %collective-permute-start = (s32[1,4]{1,0:T(1,128)S(1)}, s32[1,4]{1,0:T(1,128)S(1)}, u32[]{:S(2)}, u32[]{:S(2)}) collective-permute-start(s32[1,4]{1,0:T(1,128)S(1)} %copy-done.3), channel_id=1, source_target_pairs={{4,0},{8,4},{12,8},{16,12},{20,16},{24,20},{28,24},{5,1},{9,5},{13... | collective-permute-start | bytes 56 | tf_op jit(solution)/shard_map/ppermute | solution.py:383
  26.7 21.8 %collective-permute-start.4 = (bf16[2,160,1024]{2,1,0:T(8,128)(2,1)}, bf16[2,160,1024]{2,1,0:T(8,128)(2,1)S(1)}, u32[]{:S(2)}, u32[]{:S(2)}) collective-permute-start(bf16[2,160,1024]{2,1,0:T(8,128)(2,1)} %spectra.2.rest_1_.rest_2_), channel_id=1, source_target_pairs={{8,0},{12,4},{16,8},{20,12},{24,16},{28,20},{9,1},{13,5},{17,9},{2... | collective-permute-start | bytes 1966088 | tf_op jit(solution)/shard_map/ppermute | solution.py:378
  31.3 20.3 %copy-start.1 = (bf16[2,160,1024]{2,1,0:T(8,128)(2,1)}, bf16[2,160,1024]{2,1,0:T(8,128)(2,1)S(1)}, u32[]{:S(2)}) copy-start(bf16[2,160,1024]{2,1,0:T(8,128)(2,1)S(1)} %collective-permute-done.6.rest_2_.rest_5_) | copy-start | bytes 1966084
  31.4 20.2 %collective-permute-start.7 = (bf16[2,160,1024]{2,1,0:T(8,128)(2,1)S(1)}, bf16[2,160,1024]{2,1,0:T(8,128)(2,1)S(1)}, u32[]{:S(2)}, u32[]{:S(2)}) collective-permute-start(bf16[2,160,1024]{2,1,0:T(8,128)(2,1)S(1)} %broadcast_select_fusion), channel_id=1, source_target_pairs={{4,0},{0,4},{12,8},{8,12},{20,16},{16,20},{28,24},{24,28},{5,1},{1... | collective-permute-start | bytes 1966088 | tf_op jit(solution)/shard_map/ppermute | solution.py:394
  35.7 1.2 %collective-permute-start.2 = (s32[3]{0:T(128)S(1)}, s32[3]{0:T(128)S(1)}, u32[]{:S(2)}, u32[]{:S(2)}) collective-permute-start(s32[3]{0:T(128)S(1)} %fusion), channel_id=1, source_target_pairs={{0,1},{1,0},{2,3},{3,2},{4,5},{5,4},{6,7},{7,6},{8,9},{9,8},{10,11... | collective-permute-start | bytes 44 | tf_op jit(solution)/shard_map/ppermute | solution.py:388
  36.9 3.5 %collective-permute-start.3 = (s32[3]{0:T(128)S(1)}, s32[3]{0:T(128)S(1)}, u32[]{:S(2)}, u32[]{:S(2)}) collective-permute-start(s32[3]{0:T(128)S(1)} %add.20), channel_id=1, source_target_pairs={{0,2},{1,3},{2,0},{3,1},{4,6},{5,7},{6,4},{7,5},{8,10},{9,11},{10,... | collective-permute-start | bytes 44 | tf_op jit(solution)/shard_map/ppermute | solution.py:389
  48.4 12.0 %copy-start.2 = (bf16[2,160,1024]{2,1,0:T(8,128)(2,1)}, bf16[2,160,1024]{2,1,0:T(8,128)(2,1)S(1)}, u32[]{:S(2)}) copy-start(bf16[2,160,1024]{2,1,0:T(8,128)(2,1)S(1)} %collective-permute-done.4.rest_3_.rest_6_) | copy-start | bytes 1966084
  48.5 17.1 %collective-permute-start.5 = (bf16[2,160,1024]{2,1,0:T(8,128)(2,1)S(1)}, bf16[2,160,1024]{2,1,0:T(8,128)(2,1)}, u32[]{:S(2)}, u32[]{:S(2)}) collective-permute-start(bf16[2,160,1024]{2,1,0:T(8,128)(2,1)S(1)} %broadcast_select_fusion.1), channel_id=1, source_target_pairs={{4,0},{0,4},{12,8},{8,12},{20,16},{16,20},{28,24},{24,28},{5,1},{1... | collective-permute-start | bytes 1966088 | tf_op jit(solution)/shard_map/ppermute | solution.py:394
  51.6 0.8 copy-start.5
  73.9 1.9 %collective-permute-start.8 = (bf16[160,8,128]{2,1,0:T(8,128)(2,1)}, bf16[160,8,128]{2,1,0:T(8,128)(2,1)S(1)}, u32[]{:S(2)}, u32[]{:S(2)}) collective-permute-start(bf16[160,8,128]{2,1,0:T(8,128)(2,1)} %get-tuple-element.12), channel_id=1, source_target_pairs={{0,1},{1,0},{2,3},{3,2},{4,5},{5,4},{6,7},{7,6},{8,9},{9,8},{10,11... | collective-permute-start | bytes 983048 | tf_op jit(solution)/shard_map/ppermute | solution.py:402
  74.0 11.9 %collective-permute-start.9 = (bf16[160,8,128]{2,1,0:T(8,128)(2,1)}, bf16[160,8,128]{2,1,0:T(8,128)(2,1)S(1)}, u32[]{:S(2)}, u32[]{:S(2)}) collective-permute-start(bf16[160,8,128]{2,1,0:T(8,128)(2,1)} %get-tuple-element.14), channel_id=1, source_target_pairs={{0,1},{1,0},{2,3},{3,2},{4,5},{5,4},{6,7},{7,6},{8,9},{9,8},{10,11... | collective-permute-start | bytes 983048 | tf_op jit(solution)/shard_map/ppermute | solution.py:403
  77.0 9.8 %collective-permute-start.10 = (bf16[160,8,128]{2,1,0:T(8,128)(2,1)S(1)}, bf16[160,8,128]{2,1,0:T(8,128)(2,1)S(1)}, u32[]{:S(2)}, u32[]{:S(2)}) collective-permute-start(bf16[160,8,128]{2,1,0:T(8,128)(2,1)S(1)} %add_convert_fusion), channel_id=1, source_target_pairs={{0,2},{1,3},{2,0},{3,1},{4,6},{5,7},{6,4},{7,5},{8,10},{9,11},{10,... | collective-permute-start | bytes 983048 | tf_op jit(solution)/shard_map/ppermute | solution.py:405

commit v8 on v7

--- a/solution.py
+++ b/solution.py
@@ -130,9 +130,10 @@
 WINDOW = 13
 
 
-def cross_kernel(place_ref, *rest, segs, parts, specs, quarters, first, last):
+def cross_kernel(place_ref, *rest, groups, specs, quarters, first, last):
     if last:
         scale_ref, *rest = rest
+    parts, segs = len(groups), sum(groups)
     sources, rest = rest[: 3 * parts], rest[3 * parts :]
     lag_hbm, *rest = rest
     if not first:
@@ -149,16 +150,12 @@
     lowest = place_ref[0]
     origin = lowest // CH_TILE * CH_TILE
 
-    group = segs // parts
-    loads = [
-        pltpu.make_async_copy(
-            sources[hop * parts + part],
-            extended.at[pl.ds(part * group, group), pl.ds(hop * channels, channels), :],
-            in_sems.at[hop * parts + part],
-        )
-        for hop in range(REACH + 1)
-        for part in range(parts)
-    ]
+    loads = []
+    for number, source in enumerate(sources):
+        hop, part = divmod(number, parts)
+        into = pl.ds(sum(groups[:part]), groups[part])
+        into = extended.at[into, pl.ds(hop * channels, channels), :]
+        loads.append(pltpu.make_async_copy(source, into, in_sems.at[number]))
     loads.append(pltpu.make_async_copy(lag_hbm, lag_ref, in_sems.at[3 * parts]))
     if not first:
         earlier = pltpu.make_async_copy(before_hbm, before, in_sems.at[3 * parts + 1])
@@ -291,8 +288,9 @@
 def correlated(
     mesh, places, scales, owns, nexts, fars, lag_table, before, quarters, last
 ):
-    group, channels, columns = owns[0].shape
-    segs = group * len(owns)
+    groups = [own.shape[0] for own in owns]
+    segs = sum(groups)
+    _, channels, columns = owns[0].shape
     steps = channels // (TILES * CH_TILE)
     raw_shape = (channels // CH_TILE, 8 * 3 * CH_TILE, LAGS)
     if last:
@@ -325,8 +323,7 @@
     return pl.pallas_call(
         functools.partial(
             cross_kernel,
-            segs=segs,
-            parts=len(owns),
+            groups=groups,
             specs=specs,
             quarters=quarters,
             first=before is None,
@@ -374,7 +371,10 @@
     lag_table = jnp.asarray(lag_table_of(samples, BINS, LAGS))
     table = jnp.asarray(dft_table_of(samples, BINS))
     half = segs // 2
-    whites = [whitened(records, valid_mask, table, first, 1, half)[0] for first in (0, half)]
+    whites = [
+        *whitened(records, valid_mask, table, 0, 1, half),
+        *whitened(records, valid_mask, table, half, half, 1),
+    ]
     fars = [lax.ppermute(white, "chan", hop_far) for white in whites]
     valid_mask, _ = lax.optimization_barrier((valid_mask, whites[1]))
     marks = jnp.stack(
@@ -389,7 +389,10 @@
     counts += lax.ppermute(counts, "tm", side_swap)
     scales = 1.0 / jnp.maximum(counts, 1).astype(jnp.float32)
     nexts = []
+    passed = None
     for white, far in zip(whites, fars):
+        if nexts:
+            far, _ = lax.optimization_barrier((far, passed))
         passed = jnp.where(block % 2 == 0, far, white)
         nexts.append(lax.ppermute(passed, "chan", pair_swap))
 
@@ -398,13 +401,13 @@
         return correlated(mesh, places, scales, *chosen, lag_table, before, quarters, last)
 
     (before,) = stacked(slice(0, 1), (1, 3, 2), last=False)
-    other, send_far, send = stacked(slice(1, 2), (1, 3, 2), before)
+    other, send_far, send = stacked(slice(1, None), (1, 3, 2), before)
     got_far = lax.ppermute(send_far, "tm", core_swap)
     got = lax.ppermute(send, "tm", core_swap)
     passing = (other + got_far.astype(jnp.float32)).astype(jnp.bfloat16)
     crossed = lax.ppermute(passing, "tm", side_swap)
     scales, _ = lax.optimization_barrier((scales, passing))
-    (keep,) = stacked(slice(0, 2), (0,))
+    (keep,) = stacked(slice(None), (0,))
     return keep + got.astype(jnp.float32) + crossed.astype(jnp.float32)
 
 

time: 89.3 us -> 96 us (1.075)
  the two profiles are of different devices: /device:TPU:0 before, /device:TPU:24 now
where the time goes in v8:
time: 96 us; the launch traced here: 95.5 us
  Pallas kernels  46.6 us (49%)
  waiting for transfers between devices  20.3 us (21%)
  starting transfers between devices  19.5 us (20%)
  local copies, waits for them, and re-layouts  4.79 us (5%)
  other arithmetic  4.07 us (4%)
    pallas_call x3, Pallas kernels, correlated(): pl.pallas_call(functools.partial(cross_kernel, groups=groups, specs=specs...  24 us
    pallas_call x2, Pallas kernels, whitened(): pl.pallas_call(functools.partial(spectra_kernel, first_seg=first_seg), na...  22.6 us
    ppermute x3, waiting for transfers between devices, shards(): nexts.append(lax.ppermute(passed, 'chan', pair_swap))  13.6 us
    ppermute x3, starting transfers between devices, shards(): fars = [lax.ppermute(white, 'chan', hop_far) for white in whites]  6.37 us
    ppermute x3, starting transfers between devices, shards(): nexts.append(lax.ppermute(passed, 'chan', pair_swap))  4.74 us
    ppermute x1, starting transfers between devices, shards(): lax.ppermute(valid_mask, 'chan', hop_near)  3.29 us
    unnamed x18, local copies, waits for them, and re-layouts  2.38 us
    ppermute x1, starting transfers between devices, shards(): lax.ppermute(valid_mask, 'chan', hop_far)  2.31 us
  transfers between devices with their start and end apart: 13, of which 7 were waited for; matrix products, arithmetic and copies ran while one was open for 5% of the time, Pallas kernels for 28%

profile of v8, /device:TPU:24, one launch (start us, length us, event | category | flops | bytes accessed | tf_op | source)
XLA Modules:
  0.0 95.5 jit_solution(7954434969344494496)
XLA Ops:
  0.0 11.3 %spectra.3.rest_0_.rest_1_ = bf16[2,160,1024]{2,1,0:T(8,128)(2,1)} custom-call(s32[1,4]{1,0:T(1,128)} %valid_ref.3, bf16[160,4,7680]{2,1,0:T(4,128)(2,1)} %second_ref.3, bf16[160,4,7680]{2,1,0:T(4,128)(2,1)} %second_ref.3, bf16[3840,1024]{1,0:T(8,128)(2,1)} %constant.40.clone.table_ref), custom_call_target="tpu_custom_call" | custom-call | flops 5033164800 | bytes 17694720 | tf_op jit(solution)/shard_map/spectra/pallas_call | solution.py:103
  11.3 2.5 %collective-permute-start.5 = (bf16[2,160,1024]{2,1,0:T(8,128)(2,1)}, bf16[2,160,1024]{2,1,0:T(8,128)(2,1)S(1)}, u32[]{:S(2)}, u32[]{:S(2)}) collective-permute-start(bf16[2,160,1024]{2,1,0:T(8,128)(2,1)} %spectra.3.rest_0_.rest_1_), channel_id=1, source_target_pairs={{8,0},{12,4},{16,8},{20,12},{24,16},{28,20},{9,1},{13,5},{17,9},{2... | collective-permute-start | bytes 1966088 | tf_op jit(solution)/shard_map/ppermute | solution.py:378
  13.8 11.3 %spectra.2 = (bf16[1,160,1024]{2,1,0:T(8,128)(2,1)}, bf16[1,160,1024]{2,1,0:T(8,128)(2,1)}) custom-call(s32[1,4]{1,0:T(1,128)} %valid_ref.3, bf16[160,4,7680]{2,1,0:T(4,128)(2,1)} %second_ref.3, bf16[160,4,7680]{2,1,0:T(4,128)(2,1)} %second_ref.3, bf16[3840,1024]{1,0:T(8,128)(2,1)} %constant.40.clone.table_ref), custom_call_target="tpu_custom_call" | custom-call | flops 5033164800 | bytes 17694720 | tf_op jit(solution)/shard_map/spectra/pallas_call | solution.py:103
  25.1 2.3 %collective-permute-start.1 = (s32[1,4]{1,0:T(1,128)S(1)}, s32[1,4]{1,0:T(1,128)S(1)}, u32[]{:S(2)}, u32[]{:S(2)}) collective-permute-start(s32[1,4]{1,0:T(1,128)S(1)} %copy-done.4), channel_id=1, source_target_pairs={{8,0},{12,4},{16,8},{20,12},{24,16},{28,20},{9,1},{13,5},{17,9},{2... | collective-permute-start | bytes 56 | tf_op jit(solution)/shard_map/ppermute | solution.py:384
  27.5 3.3 %collective-permute-start = (s32[1,4]{1,0:T(1,128)S(1)}, s32[1,4]{1,0:T(1,128)S(1)}, u32[]{:S(2)}, u32[]{:S(2)}) collective-permute-start(s32[1,4]{1,0:T(1,128)S(1)} %copy-done.4), channel_id=1, source_target_pairs={{4,0},{8,4},{12,8},{16,12},{20,16},{24,20},{28,24},{5,1},{9,5},{13... | collective-permute-start | bytes 56 | tf_op jit(solution)/shard_map/ppermute | solution.py:383
  30.8 1.9 %collective-permute-start.4 = (bf16[1,160,1024]{2,1,0:T(8,128)(2,1)}, bf16[1,160,1024]{2,1,0:T(8,128)(2,1)S(1)}, u32[]{:S(2)}, u32[]{:S(2)}) collective-permute-start(bf16[1,160,1024]{2,1,0:T(8,128)(2,1)} %get-tuple-element.14.rest_1_.rest_2_), channel_id=1, source_target_pairs={{8,0},{12,4},{16,8},{20,12},{24,16},{28,20},{9,1},{13,5},{17,9},{2... | collective-permute-start | bytes 983048 | tf_op jit(solution)/shard_map/ppermute | solution.py:378
  32.7 1.9 %collective-permute-start.7 = (bf16[1,160,1024]{2,1,0:T(8,128)(2,1)}, bf16[1,160,1024]{2,1,0:T(8,128)(2,1)S(1)}, u32[]{:S(2)}, u32[]{:S(2)}) collective-permute-start(bf16[1,160,1024]{2,1,0:T(8,128)(2,1)} %get-tuple-element.16.rest_2_.rest_3_), channel_id=1, source_target_pairs={{8,0},{12,4},{16,8},{20,12},{24,16},{28,20},{9,1},{13,5},{17,9},{2... | collective-permute-start | bytes 983048 | tf_op jit(solution)/shard_map/ppermute | solution.py:378
  34.7 0.6 fusion.1
  35.3 1.8 %stack.31.place_ref = s32[6]{0:T(128)} concatenate(s32[1]{0:T(128)} %bitcast, s32[1]{0:T(128)} %bitcast.1, s32[1]{0:T(128)} %bitcast.2, s32[1]{0:T(128)} %bitcast.3, s32[1]{0:T(128)} %bitcast.4, s32[1]{0:T(128)} %bitcast.5), dimensions={0} | concatenate | bytes 48 | tf_op jit(solution)/shard_map/stack | solution.py:360
  37.1 0.2 fusion
  37.3 1.1 %collective-permute-done.2 = s32[3]{0:T(128)S(1)} collective-permute-done((s32[3]{0:T(128)S(1)}, s32[3]{0:T(128)S(1)}, u32[]{:S(2)}, u32[]{:S(2)}) %collective-permute-start.2) | collective-permute-done | bytes 44 | tf_op jit(solution)/shard_map/ppermute | solution.py:388
  38.4 1.5 %collective-permute-start.3 = (s32[3]{0:T(128)S(1)}, s32[3]{0:T(128)S(1)}, u32[]{:S(2)}, u32[]{:S(2)}) collective-permute-start(s32[3]{0:T(128)S(1)} %add.21), channel_id=1, source_target_pairs={{0,2},{1,3},{2,0},{3,1},{4,6},{5,7},{6,4},{7,5},{8,10},{9,11},{10,... | collective-permute-start | bytes 44 | tf_op jit(solution)/shard_map/ppermute | solution.py:389
  40.0 1.1 %collective-permute-start.9 = (bf16[2,160,1024]{2,1,0:T(8,128)(2,1)S(1)}, bf16[2,160,1024]{2,1,0:T(8,128)(2,1)S(1)}, u32[]{:S(2)}, u32[]{:S(2)}) collective-permute-start(bf16[2,160,1024]{2,1,0:T(8,128)(2,1)S(1)} %broadcast_select_fusion), channel_id=1, source_target_pairs={{4,0},{0,4},{12,8},{8,12},{20,16},{16,20},{28,24},{24,28},{5,1},{1... | collective-permute-start | bytes 1966088 | tf_op jit(solution)/shard_map/ppermute | solution.py:397
  41.2 0.8 collective-permute-done.3
  42.0 0.6 convert_divide_fusion.rest_0_
  42.6 1.8 %collective-permute-start.6 = (bf16[1,160,1024]{2,1,0:T(8,128)(2,1)S(1)}, bf16[1,160,1024]{2,1,0:T(8,128)(2,1)S(1)}, u32[]{:S(2)}, u32[]{:S(2)}) collective-permute-start(bf16[1,160,1024]{2,1,0:T(8,128)(2,1)S(1)} %broadcast_select_fusion.2), channel_id=1, source_target_pairs={{4,0},{0,4},{12,8},{8,12},{20,16},{16,20},{28,24},{24,28},{5,1},{1... | collective-permute-start | bytes 983048 | tf_op jit(solution)/shard_map/ppermute | solution.py:397
  44.4 2.0 %collective-permute-done.7.rest_6_.rest_9_ = bf16[1,160,1024]{2,1,0:T(8,128)(2,1)S(1)} collective-permute-done((bf16[1,160,1024]{2,1,0:T(8,128)(2,1)}, bf16[1,160,1024]{2,1,0:T(8,128)(2,1)S(1)}, u32[]{:S(2)}, u32[]{:S(2)}) %collective-permute-start.7) | collective-permute-done | bytes 327712 | tf_op jit(solution)/shard_map/ppermute | solution.py:378
  46.5 1.8 %collective-permute-start.8 = (bf16[1,160,1024]{2,1,0:T(8,128)(2,1)S(1)}, bf16[1,160,1024]{2,1,0:T(8,128)(2,1)S(1)}, u32[]{:S(2)}, u32[]{:S(2)}) collective-permute-start(bf16[1,160,1024]{2,1,0:T(8,128)(2,1)S(1)} %broadcast_select_fusion.1), channel_id=1, source_target_pairs={{4,0},{0,4},{12,8},{8,12},{20,16},{16,20},{28,24},{24,28},{5,1},{1... | collective-permute-start | bytes 983048 | tf_op jit(solution)/shard_map/ppermute | solution.py:397
  48.3 9.4 %collective-permute-done.9.rest_1_.rest_4_ = bf16[2,160,1024]{2,1,0:T(8,128)(2,1)S(1)} collective-permute-done((bf16[2,160,1024]{2,1,0:T(8,128)(2,1)S(1)}, bf16[2,160,1024]{2,1,0:T(8,128)(2,1)S(1)}, u32[]{:S(2)}, u32[]{:S(2)}) %collective-permute-start.9) | collective-permute-done | bytes 655392 | tf_op jit(solution)/shard_map/ppermute | solution.py:397
  57.7 0.9 copy-done.6
  58.6 7.9 %cross.3.rest_8_ = bf16[10,384,128]{2,1,0:T(8,128)(2,1)} custom-call(s32[6]{0:T(128)} %stack.31.place_ref, bf16[2,160,1024]{2,1,0:T(8,128)(2,1)} %spectra.3.rest_0_.rest_1_, bf16[2,160,1024]{2,1,0:T(8,128)(2,1)} %copy-done.6, bf16[2,160,1024]{2,1,0:T(8,128)(2,1)} %copy-done.1, bf16[4,256,256]{2,1,0:T(8,128)(2,1)} %constant.39.clone.rest_3_.rest_7_.rest_10_), custom_call_target="tpu_custom_call" | custom-call | flops 10066329600 | bytes 1966080 | tf_op jit(solution)/shard_map/cross/pallas_call | solution.py:323
  66.6 4.1 %collective-permute-done.8.rest_4_.rest_6_ = bf16[1,160,1024]{2,1,0:T(8,128)(2,1)S(1)} collective-permute-done((bf16[1,160,1024]{2,1,0:T(8,128)(2,1)S(1)}, bf16[1,160,1024]{2,1,0:T(8,128)(2,1)S(1)}, u32[]{:S(2)}, u32[]{:S(2)}) %collective-permute-start.8) | collective-permute-done | bytes 327712 | tf_op jit(solution)/shard_map/ppermute | solution.py:397
  70.7 0.7 copy-done.8
  71.4 0.7 copy-done.7
  72.2 8.4 %cross.4 = (f32[160,8,128]{2,1,0:T(8,128)}, bf16[160,8,128]{2,1,0:T(8,128)(2,1)}, bf16[160,8,128]{2,1,0:T(8,128)(2,1)}) custom-call(s32[6]{0:T(128)} %stack.31.place_ref, f32[3]{0:T(128)} %convert_divide_fusion.rest_0_, bf16[1,160,1024]{2,1,0:T(8,128)(2,1)} %get-tuple-element.14.rest_1_.rest_2_, bf16[1,160,1024]{2,1,0:T(8,128)(2,1)} %get-tuple-element.16.rest_2_.rest_3_, ...), custom_call_target="tpu_custom_call" | custom-call | flops 10066329600 | bytes 1966080 | tf_op jit(solution)/shard_map/cross/pallas_call | solution.py:323
  80.7 0.5 collective-permute-start.11
  81.2 1.3 %collective-permute-done.10 = bf16[160,8,128]{2,1,0:T(8,128)(2,1)S(1)} collective-permute-done((bf16[160,8,128]{2,1,0:T(8,128)(2,1)}, bf16[160,8,128]{2,1,0:T(8,128)(2,1)S(1)}, u32[]{:S(2)}, u32[]{:S(2)}) %collective-permute-start.10) | collective-permute-done | bytes 327712 | tf_op jit(solution)/shard_map/ppermute | solution.py:405
  82.5 1.2 %add_convert_fusion = bf16[160,8,128]{2,1,0:T(8,128)(2,1)S(1)} fusion(f32[160,8,128]{2,1,0:T(8,128)} %get-tuple-element.19, bf16[160,8,128]{2,1,0:T(8,128)(2,1)S(1)} %collective-permute-done.10), kind=kLoop, calls=%fused_computation.1 | loop fusion | flops 491520 | bytes 1310720 | tf_op jit(solution)/shard_map/convert_element_type | solution.py:407
  83.6 0.6 collective-permute-start.12
  84.3 7.7 %cross.5 = f32[160,8,128]{2,1,0:T(8,128)} custom-call(s32[6]{0:T(128)} %stack.31.place_ref, f32[3]{0:T(128)} %convert_divide_fusion.rest_0_, bf16[2,160,1024]{2,1,0:T(8,128)(2,1)} %spectra.3.rest_0_.rest_1_, bf16[1,160,1024]{2,1,0:T(8,128)(2,1)} %get-tuple-element.14.rest_1_.rest_2_, bf16[1,160,1024]{2,1,0:T(8,128)(2,1)} %get-tuple-element.16.rest_2_.rest_3_, ...), custom_call_target="tpu_custom_call" | custom-call | flops 3355443200 | bytes 3932160 | tf_op jit(solution)/shard_map/cross/pallas_call | solution.py:323
  92.0 1.5 %collective-permute-done.12 = bf16[160,8,128]{2,1,0:T(8,128)(2,1)S(1)} collective-permute-done((bf16[160,8,128]{2,1,0:T(8,128)(2,1)S(1)}, bf16[160,8,128]{2,1,0:T(8,128)(2,1)S(1)}, u32[]{:S(2)}, u32[]{:S(2)}) %collective-permute-start.12) | collective-permute-done | bytes 327712 | tf_op jit(solution)/shard_map/ppermute | solution.py:408
  93.5 2.0 %convert_add_fusion = f32[160,8,128]{2,1,0:T(8,128)} fusion(bf16[160,8,128]{2,1,0:T(8,128)(2,1)S(1)} %collective-permute-done.12, f32[160,8,128]{2,1,0:T(8,128)} %cross.5, bf16[160,8,128]{2,1,0:T(8,128)(2,1)S(1)} %collective-permute-done.11), kind=kLoop, calls=%fused_computation | loop fusion | flops 655360 | bytes 1966080 | tf_op jit(solution)/shard_map/add | solution.py:411
  (27 shorter events, 0.3 us)
Async XLA Ops:
  11.3 13.8 %copy-start.4 = (s32[1,4]{1,0:T(1,128)S(1)}, s32[1,4]{1,0:T(1,128)}, u32[]{:S(2)}) copy-start(s32[1,4]{1,0:T(1,128)} %valid_ref.3) | copy-start | bytes 52
  11.3 23.4 %copy-start.5 = (s32[1,2]{1,0:T(1,128)S(1)}, s32[1,2]{1,0:T(1,128)}, u32[]{:S(2)}) copy-start(s32[1,2]{1,0:T(1,128)} %param.7) | copy-start | bytes 28
  11.3 28.6 %copy-start = (bf16[2,160,1024]{2,1,0:T(8,128)(2,1)S(1)}, bf16[2,160,1024]{2,1,0:T(8,128)(2,1)}, u32[]{:S(2)}) copy-start(bf16[2,160,1024]{2,1,0:T(8,128)(2,1)} %spectra.3.rest_0_.rest_1_) | copy-start | bytes 1966084
  11.3 28.6 %collective-permute-start.5 = (bf16[2,160,1024]{2,1,0:T(8,128)(2,1)}, bf16[2,160,1024]{2,1,0:T(8,128)(2,1)S(1)}, u32[]{:S(2)}, u32[]{:S(2)}) collective-permute-start(bf16[2,160,1024]{2,1,0:T(8,128)(2,1)} %spectra.3.rest_0_.rest_1_), channel_id=1, source_target_pairs={{8,0},{12,4},{16,8},{20,12},{24,16},{28,20},{9,1},{13,5},{17,9},{2... | collective-permute-start | bytes 1966088 | tf_op jit(solution)/shard_map/ppermute | solution.py:378
  25.1 11.9 %collective-permute-start.1 = (s32[1,4]{1,0:T(1,128)S(1)}, s32[1,4]{1,0:T(1,128)S(1)}, u32[]{:S(2)}, u32[]{:S(2)}) collective-permute-start(s32[1,4]{1,0:T(1,128)S(1)} %copy-done.4), channel_id=1, source_target_pairs={{8,0},{12,4},{16,8},{20,12},{24,16},{28,20},{9,1},{13,5},{17,9},{2... | collective-permute-start | bytes 56 | tf_op jit(solution)/shard_map/ppermute | solution.py:384
  27.5 9.6 %collective-permute-start = (s32[1,4]{1,0:T(1,128)S(1)}, s32[1,4]{1,0:T(1,128)S(1)}, u32[]{:S(2)}, u32[]{:S(2)}) collective-permute-start(s32[1,4]{1,0:T(1,128)S(1)} %copy-done.4), channel_id=1, source_target_pairs={{4,0},{8,4},{12,8},{16,12},{20,16},{24,20},{28,24},{5,1},{9,5},{13... | collective-permute-start | bytes 56 | tf_op jit(solution)/shard_map/ppermute | solution.py:383
  30.8 11.8 %collective-permute-start.4 = (bf16[1,160,1024]{2,1,0:T(8,128)(2,1)}, bf16[1,160,1024]{2,1,0:T(8,128)(2,1)S(1)}, u32[]{:S(2)}, u32[]{:S(2)}) collective-permute-start(bf16[1,160,1024]{2,1,0:T(8,128)(2,1)} %get-tuple-element.14.rest_1_.rest_2_), channel_id=1, source_target_pairs={{8,0},{12,4},{16,8},{20,12},{24,16},{28,20},{9,1},{13,5},{17,9},{2... | collective-permute-start | bytes 983048 | tf_op jit(solution)/shard_map/ppermute | solution.py:378
  32.7 13.7 %collective-permute-start.7 = (bf16[1,160,1024]{2,1,0:T(8,128)(2,1)}, bf16[1,160,1024]{2,1,0:T(8,128)(2,1)S(1)}, u32[]{:S(2)}, u32[]{:S(2)}) collective-permute-start(bf16[1,160,1024]{2,1,0:T(8,128)(2,1)} %get-tuple-element.16.rest_2_.rest_3_), channel_id=1, source_target_pairs={{8,0},{12,4},{16,8},{20,12},{24,16},{28,20},{9,1},{13,5},{17,9},{2... | collective-permute-start | bytes 983048 | tf_op jit(solution)/shard_map/ppermute | solution.py:378
  37.2 1.2 %collective-permute-start.2 = (s32[3]{0:T(128)S(1)}, s32[3]{0:T(128)S(1)}, u32[]{:S(2)}, u32[]{:S(2)}) collective-permute-start(s32[3]{0:T(128)S(1)} %fusion), channel_id=1, source_target_pairs={{0,1},{1,0},{2,3},{3,2},{4,5},{5,4},{6,7},{7,6},{8,9},{9,8},{10,11... | collective-permute-start | bytes 44 | tf_op jit(solution)/shard_map/ppermute | solution.py:388
  38.4 3.5 %collective-permute-start.3 = (s32[3]{0:T(128)S(1)}, s32[3]{0:T(128)S(1)}, u32[]{:S(2)}, u32[]{:S(2)}) collective-permute-start(s32[3]{0:T(128)S(1)} %add.21), channel_id=1, source_target_pairs={{0,2},{1,3},{2,0},{3,1},{4,6},{5,7},{6,4},{7,5},{8,10},{9,11},{10,... | collective-permute-start | bytes 44 | tf_op jit(solution)/shard_map/ppermute | solution.py:389
  39.9 17.8 %copy-start.1 = (bf16[2,160,1024]{2,1,0:T(8,128)(2,1)}, bf16[2,160,1024]{2,1,0:T(8,128)(2,1)S(1)}, u32[]{:S(2)}) copy-start(bf16[2,160,1024]{2,1,0:T(8,128)(2,1)S(1)} %collective-permute-done.5.rest_2_.rest_7_) | copy-start | bytes 1966084
  40.0 17.7 %collective-permute-start.9 = (bf16[2,160,1024]{2,1,0:T(8,128)(2,1)S(1)}, bf16[2,160,1024]{2,1,0:T(8,128)(2,1)S(1)}, u32[]{:S(2)}, u32[]{:S(2)}) collective-permute-start(bf16[2,160,1024]{2,1,0:T(8,128)(2,1)S(1)} %broadcast_select_fusion), channel_id=1, source_target_pairs={{4,0},{0,4},{12,8},{8,12},{20,16},{16,20},{28,24},{24,28},{5,1},{1... | collective-permute-start | bytes 1966088 | tf_op jit(solution)/shard_map/ppermute | solution.py:397
  42.6 24.0 %copy-start.2 = (bf16[1,160,1024]{2,1,0:T(8,128)(2,1)}, bf16[1,160,1024]{2,1,0:T(8,128)(2,1)S(1)}, u32[]{:S(2)}) copy-start(bf16[1,160,1024]{2,1,0:T(8,128)(2,1)S(1)} %collective-permute-done.4.rest_5_.rest_8_) | copy-start | bytes 983044
  42.6 28.1 %collective-permute-start.6 = (bf16[1,160,1024]{2,1,0:T(8,128)(2,1)S(1)}, bf16[1,160,1024]{2,1,0:T(8,128)(2,1)S(1)}, u32[]{:S(2)}, u32[]{:S(2)}) collective-permute-start(bf16[1,160,1024]{2,1,0:T(8,128)(2,1)S(1)} %broadcast_select_fusion.2), channel_id=1, source_target_pairs={{4,0},{0,4},{12,8},{8,12},{20,16},{16,20},{28,24},{24,28},{5,1},{1... | collective-permute-start | bytes 983048 | tf_op jit(solution)/shard_map/ppermute | solution.py:397
  46.4 20.1 %copy-start.3 = (bf16[1,160,1024]{2,1,0:T(8,128)(2,1)}, bf16[1,160,1024]{2,1,0:T(8,128)(2,1)S(1)}, u32[]{:S(2)}) copy-start(bf16[1,160,1024]{2,1,0:T(8,128)(2,1)S(1)} %collective-permute-done.7.rest_6_.rest_9_) | copy-start | bytes 983044
  46.5 24.2 %collective-permute-start.8 = (bf16[1,160,1024]{2,1,0:T(8,128)(2,1)S(1)}, bf16[1,160,1024]{2,1,0:T(8,128)(2,1)S(1)}, u32[]{:S(2)}, u32[]{:S(2)}) collective-permute-start(bf16[1,160,1024]{2,1,0:T(8,128)(2,1)S(1)} %broadcast_select_fusion.1), channel_id=1, source_target_pairs={{4,0},{0,4},{12,8},{8,12},{20,16},{16,20},{28,24},{24,28},{5,1},{1... | collective-permute-start | bytes 983048 | tf_op jit(solution)/shard_map/ppermute | solution.py:397
  57.7 0.9 copy-start.6
  70.7 0.7 copy-start.8
  71.4 0.7 copy-start.7
  80.6 1.9 %collective-permute-start.10 = (bf16[160,8,128]{2,1,0:T(8,128)(2,1)}, bf16[160,8,128]{2,1,0:T(8,128)(2,1)S(1)}, u32[]{:S(2)}, u32[]{:S(2)}) collective-permute-start(bf16[160,8,128]{2,1,0:T(8,128)(2,1)} %get-tuple-element.20), channel_id=1, source_target_pairs={{0,1},{1,0},{2,3},{3,2},{4,5},{5,4},{6,7},{7,6},{8,9},{9,8},{10,11... | collective-permute-start | bytes 983048 | tf_op jit(solution)/shard_map/ppermute | solution.py:405
  80.7 11.3 %collective-permute-start.11 = (bf16[160,8,128]{2,1,0:T(8,128)(2,1)}, bf16[160,8,128]{2,1,0:T(8,128)(2,1)S(1)}, u32[]{:S(2)}, u32[]{:S(2)}) collective-permute-start(bf16[160,8,128]{2,1,0:T(8,128)(2,1)} %get-tuple-element.22), channel_id=1, source_target_pairs={{0,1},{1,0},{2,3},{3,2},{4,5},{5,4},{6,7},{7,6},{8,9},{9,8},{10,11... | collective-permute-start | bytes 983048 | tf_op jit(solution)/shard_map/ppermute | solution.py:406
  83.6 9.8 %collective-permute-start.12 = (bf16[160,8,128]{2,1,0:T(8,128)(2,1)S(1)}, bf16[160,8,128]{2,1,0:T(8,128)(2,1)S(1)}, u32[]{:S(2)}, u32[]{:S(2)}) collective-permute-start(bf16[160,8,128]{2,1,0:T(8,128)(2,1)S(1)} %add_convert_fusion), channel_id=1, source_target_pairs={{0,2},{1,3},{2,0},{3,1},{4,6},{5,7},{6,4},{7,5},{8,10},{9,11},{10,... | collective-permute-start | bytes 983048 | tf_op jit(solution)/shard_map/ppermute | solution.py:408

commit v9 on v8

--- a/solution.py
+++ b/solution.py
@@ -385,16 +385,17 @@
         ]
     )
     counts = jnp.sum(marks * valid_mask[None], axis=(1, 2))
-    counts += lax.ppermute(counts, "tm", core_swap)
-    counts += lax.ppermute(counts, "tm", side_swap)
-    scales = 1.0 / jnp.maximum(counts, 1).astype(jnp.float32)
     nexts = []
-    passed = None
     for white, far in zip(whites, fars):
         if nexts:
-            far, _ = lax.optimization_barrier((far, passed))
+            far, _ = lax.optimization_barrier((far, (passed, counts)))
         passed = jnp.where(block % 2 == 0, far, white)
+        if not nexts:
+            counts, _ = lax.optimization_barrier((counts, passed))
+            counts += lax.ppermute(counts, "tm", core_swap)
+            counts += lax.ppermute(counts, "tm", side_swap)
         nexts.append(lax.ppermute(passed, "chan", pair_swap))
+    scales = 1.0 / jnp.maximum(counts, 1).astype(jnp.float32)
 
     def stacked(part, quarters, before=None, last=True):
         chosen = (whites[part], nexts[part], fars[part])

time: 96 us -> 92.4 us (0.963)
  waiting for transfers between devices: 20.3 us -> 15.2 us
  starting transfers between devices: 19.5 us -> 21.1 us
    ppermute x3, waiting for transfers between devices: 13.6 us -> 9.93 us  [shards(): nexts.append(lax.ppermute(passed, 'chan', pair_swap))]
    ppermute x3, waiting for transfers between devices: 2.01 us -> 0.52 us  [shards(): fars = [lax.ppermute(white, 'chan', hop_far) for white in whites]]
  transfers between devices with their start and end apart: 13 -> 13, of which waited for: 7 -> 7; matrix products, arithmetic and copies ran while one was open for 5% -> 5% of each run, Pallas kernels for 28% -> 29%
where the time goes in v9:
time: 92.4 us; the launch traced here: 91.9 us
  Pallas kernels  46.6 us (50%)
  starting transfers between devices  21.1 us (23%)
  waiting for transfers between devices  15.2 us (16%)
  local copies, waits for them, and re-layouts  4.79 us (5%)
  other arithmetic  4.07 us (4%)
    pallas_call x3, Pallas kernels, correlated(): pl.pallas_call(functools.partial(cross_kernel, groups=groups, specs=specs...  24 us
    pallas_call x2, Pallas kernels, whitened(): pl.pallas_call(functools.partial(spectra_kernel, first_seg=first_seg), na...  22.6 us
    ppermute x3, waiting for transfers between devices, shards(): nexts.append(lax.ppermute(passed, 'chan', pair_swap))  9.93 us
    ppermute x3, starting transfers between devices, shards(): fars = [lax.ppermute(white, 'chan', hop_far) for white in whites]  6.37 us
    ppermute x3, starting transfers between devices, shards(): nexts.append(lax.ppermute(passed, 'chan', pair_swap))  5.04 us
    ppermute x1, starting transfers between devices, shards(): lax.ppermute(valid_mask, 'chan', hop_near)  3.29 us
    unnamed x18, local copies, waits for them, and re-layouts  2.38 us
    ppermute x1, starting transfers between devices, shards(): lax.ppermute(valid_mask, 'chan', hop_far)  2.31 us
  transfers between devices with their start and end apart: 13, of which 7 were waited for; matrix products, arithmetic and copies ran while one was open for 5% of the time, Pallas kernels for 29%

profile of v9, /device:TPU:24, one launch (start us, length us, event | category | flops | bytes accessed | tf_op | source)
XLA Modules:
  0.0 91.9 jit_solution(3399564546053794180)
XLA Ops:
  0.0 11.3 %spectra.3.rest_0_.rest_1_ = bf16[2,160,1024]{2,1,0:T(8,128)(2,1)} custom-call(s32[1,4]{1,0:T(1,128)} %valid_ref.3, bf16[160,4,7680]{2,1,0:T(4,128)(2,1)} %second_ref.3, bf16[160,4,7680]{2,1,0:T(4,128)(2,1)} %second_ref.3, bf16[3840,1024]{1,0:T(8,128)(2,1)} %constant.40.clone.table_ref), custom_call_target="tpu_custom_call" | custom-call | flops 5033164800 | bytes 17694720 | tf_op jit(solution)/shard_map/spectra/pallas_call | solution.py:103
  11.3 2.5 %collective-permute-start.2 = (bf16[2,160,1024]{2,1,0:T(8,128)(2,1)}, bf16[2,160,1024]{2,1,0:T(8,128)(2,1)S(1)}, u32[]{:S(2)}, u32[]{:S(2)}) collective-permute-start(bf16[2,160,1024]{2,1,0:T(8,128)(2,1)} %spectra.3.rest_0_.rest_1_), channel_id=1, source_target_pairs={{8,0},{12,4},{16,8},{20,12},{24,16},{28,20},{9,1},{13,5},{17,9},{2... | collective-permute-start | bytes 1966088 | tf_op jit(solution)/shard_map/ppermute | solution.py:378
  13.8 11.3 %spectra.2 = (bf16[1,160,1024]{2,1,0:T(8,128)(2,1)}, bf16[1,160,1024]{2,1,0:T(8,128)(2,1)}) custom-call(s32[1,4]{1,0:T(1,128)} %valid_ref.3, bf16[160,4,7680]{2,1,0:T(4,128)(2,1)} %second_ref.3, bf16[160,4,7680]{2,1,0:T(4,128)(2,1)} %second_ref.3, bf16[3840,1024]{1,0:T(8,128)(2,1)} %constant.40.clone.table_ref), custom_call_target="tpu_custom_call" | custom-call | flops 5033164800 | bytes 17694720 | tf_op jit(solution)/shard_map/spectra/pallas_call | solution.py:103
  25.1 2.3 %collective-permute-start.1 = (s32[1,4]{1,0:T(1,128)S(1)}, s32[1,4]{1,0:T(1,128)S(1)}, u32[]{:S(2)}, u32[]{:S(2)}) collective-permute-start(s32[1,4]{1,0:T(1,128)S(1)} %copy-done.4), channel_id=1, source_target_pairs={{8,0},{12,4},{16,8},{20,12},{24,16},{28,20},{9,1},{13,5},{17,9},{2... | collective-permute-start | bytes 56 | tf_op jit(solution)/shard_map/ppermute | solution.py:384
  27.5 3.3 %collective-permute-start = (s32[1,4]{1,0:T(1,128)S(1)}, s32[1,4]{1,0:T(1,128)S(1)}, u32[]{:S(2)}, u32[]{:S(2)}) collective-permute-start(s32[1,4]{1,0:T(1,128)S(1)} %copy-done.4), channel_id=1, source_target_pairs={{4,0},{8,4},{12,8},{16,12},{20,16},{24,20},{28,24},{5,1},{9,5},{13... | collective-permute-start | bytes 56 | tf_op jit(solution)/shard_map/ppermute | solution.py:383
  30.8 1.9 %collective-permute-start.5 = (bf16[1,160,1024]{2,1,0:T(8,128)(2,1)}, bf16[1,160,1024]{2,1,0:T(8,128)(2,1)S(1)}, u32[]{:S(2)}, u32[]{:S(2)}) collective-permute-start(bf16[1,160,1024]{2,1,0:T(8,128)(2,1)} %get-tuple-element.15.rest_1_.rest_2_), channel_id=1, source_target_pairs={{8,0},{12,4},{16,8},{20,12},{24,16},{28,20},{9,1},{13,5},{17,9},{2... | collective-permute-start | bytes 983048 | tf_op jit(solution)/shard_map/ppermute | solution.py:378
  32.7 1.9 %collective-permute-start.7 = (bf16[1,160,1024]{2,1,0:T(8,128)(2,1)}, bf16[1,160,1024]{2,1,0:T(8,128)(2,1)S(1)}, u32[]{:S(2)}, u32[]{:S(2)}) collective-permute-start(bf16[1,160,1024]{2,1,0:T(8,128)(2,1)} %get-tuple-element.18.rest_2_.rest_3_), channel_id=1, source_target_pairs={{8,0},{12,4},{16,8},{20,12},{24,16},{28,20},{9,1},{13,5},{17,9},{2... | collective-permute-start | bytes 983048 | tf_op jit(solution)/shard_map/ppermute | solution.py:378
  34.7 0.6 fusion.1
  35.3 1.8 %stack.31.place_ref = s32[6]{0:T(128)} concatenate(s32[1]{0:T(128)} %bitcast, s32[1]{0:T(128)} %bitcast.1, s32[1]{0:T(128)} %bitcast.2, s32[1]{0:T(128)} %bitcast.3, s32[1]{0:T(128)} %bitcast.4, s32[1]{0:T(128)} %bitcast.5), dimensions={0} | concatenate | bytes 48 | tf_op jit(solution)/shard_map/stack | solution.py:360
  37.1 0.2 fusion
  37.3 0.7 collective-permute-start.9
  38.0 1.1 %collective-permute-done.3 = s32[3]{0:T(128)S(1)} collective-permute-done((s32[3]{0:T(128)S(1)}, s32[3]{0:T(128)S(1)}, u32[]{:S(2)}, u32[]{:S(2)}) %collective-permute-start.3) | collective-permute-done | bytes 44 | tf_op jit(solution)/shard_map/ppermute | solution.py:395
  39.2 2.0 %collective-permute-start.4 = (s32[3]{0:T(128)S(1)}, s32[3]{0:T(128)S(1)}, u32[]{:S(2)}, u32[]{:S(2)}) collective-permute-start(s32[3]{0:T(128)S(1)} %add.22), channel_id=1, source_target_pairs={{0,2},{1,3},{2,0},{3,1},{4,6},{5,7},{6,4},{7,5},{8,10},{9,11},{10,... | collective-permute-start | bytes 44 | tf_op jit(solution)/shard_map/ppermute | solution.py:396
  41.1 1.6 %collective-permute-done.4 = s32[3]{0:T(128)S(1)} collective-permute-done((s32[3]{0:T(128)S(1)}, s32[3]{0:T(128)S(1)}, u32[]{:S(2)}, u32[]{:S(2)}) %collective-permute-start.4) | collective-permute-done | bytes 44 | tf_op jit(solution)/shard_map/ppermute | solution.py:396
  42.7 0.6 convert_divide_fusion
  43.4 2.5 %collective-permute-start.6 = (bf16[1,160,1024]{2,1,0:T(8,128)(2,1)S(1)}, bf16[1,160,1024]{2,1,0:T(8,128)(2,1)S(1)}, u32[]{:S(2)}, u32[]{:S(2)}) collective-permute-start(bf16[1,160,1024]{2,1,0:T(8,128)(2,1)S(1)} %broadcast_select_fusion.2), channel_id=1, source_target_pairs={{4,0},{0,4},{12,8},{8,12},{20,16},{16,20},{28,24},{24,28},{5,1},{1... | collective-permute-start | bytes 983048 | tf_op jit(solution)/shard_map/ppermute | solution.py:397
  45.9 0.5 collective-permute-done.7.rest_6_.rest_9_
  46.5 1.8 %collective-permute-start.8 = (bf16[1,160,1024]{2,1,0:T(8,128)(2,1)S(1)}, bf16[1,160,1024]{2,1,0:T(8,128)(2,1)S(1)}, u32[]{:S(2)}, u32[]{:S(2)}) collective-permute-start(bf16[1,160,1024]{2,1,0:T(8,128)(2,1)S(1)} %broadcast_select_fusion.1), channel_id=1, source_target_pairs={{4,0},{0,4},{12,8},{8,12},{20,16},{16,20},{28,24},{24,28},{5,1},{1... | collective-permute-start | bytes 983048 | tf_op jit(solution)/shard_map/ppermute | solution.py:397
  48.3 6.8 %collective-permute-done.9.rest_1_.rest_4_ = bf16[2,160,1024]{2,1,0:T(8,128)(2,1)S(1)} collective-permute-done((bf16[2,160,1024]{2,1,0:T(8,128)(2,1)S(1)}, bf16[2,160,1024]{2,1,0:T(8,128)(2,1)S(1)}, u32[]{:S(2)}, u32[]{:S(2)}) %collective-permute-start.9) | collective-permute-done | bytes 655392 | tf_op jit(solution)/shard_map/ppermute | solution.py:397
  55.1 0.9 copy-done.6
  56.0 8.0 %cross.3.rest_8_ = bf16[10,384,128]{2,1,0:T(8,128)(2,1)} custom-call(s32[6]{0:T(128)} %stack.31.place_ref, bf16[2,160,1024]{2,1,0:T(8,128)(2,1)} %spectra.3.rest_0_.rest_1_, bf16[2,160,1024]{2,1,0:T(8,128)(2,1)} %copy-done.6, bf16[2,160,1024]{2,1,0:T(8,128)(2,1)} %copy-done.1, bf16[4,256,256]{2,1,0:T(8,128)(2,1)} %constant.39.clone.rest_3_.rest_7_.rest_10_), custom_call_target="tpu_custom_call" | custom-call | flops 10066329600 | bytes 1966080 | tf_op jit(solution)/shard_map/cross/pallas_call | solution.py:323
  64.0 3.1 %collective-permute-done.8.rest_4_.rest_6_ = bf16[1,160,1024]{2,1,0:T(8,128)(2,1)S(1)} collective-permute-done((bf16[1,160,1024]{2,1,0:T(8,128)(2,1)S(1)}, bf16[1,160,1024]{2,1,0:T(8,128)(2,1)S(1)}, u32[]{:S(2)}, u32[]{:S(2)}) %collective-permute-start.8) | collective-permute-done | bytes 327712 | tf_op jit(solution)/shard_map/ppermute | solution.py:397
  67.1 0.7 copy-done.8
  67.8 0.7 copy-done.7
  68.6 8.4 %cross.4 = (f32[160,8,128]{2,1,0:T(8,128)}, bf16[160,8,128]{2,1,0:T(8,128)(2,1)}, bf16[160,8,128]{2,1,0:T(8,128)(2,1)}) custom-call(s32[6]{0:T(128)} %stack.31.place_ref, f32[3]{0:T(128)} %convert_divide_fusion, bf16[1,160,1024]{2,1,0:T(8,128)(2,1)} %get-tuple-element.15.rest_1_.rest_2_, bf16[1,160,1024]{2,1,0:T(8,128)(2,1)} %get-tuple-element.18.rest_2_.rest_3_, ...), custom_call_target="tpu_custom_call" | custom-call | flops 10066329600 | bytes 1966080 | tf_op jit(solution)/shard_map/cross/pallas_call | solution.py:323
  77.1 0.5 collective-permute-start.11
  77.6 1.3 %collective-permute-done.10 = bf16[160,8,128]{2,1,0:T(8,128)(2,1)S(1)} collective-permute-done((bf16[160,8,128]{2,1,0:T(8,128)(2,1)}, bf16[160,8,128]{2,1,0:T(8,128)(2,1)S(1)}, u32[]{:S(2)}, u32[]{:S(2)}) %collective-permute-start.10) | collective-permute-done | bytes 327712 | tf_op jit(solution)/shard_map/ppermute | solution.py:406
  78.9 1.2 %add_convert_fusion = bf16[160,8,128]{2,1,0:T(8,128)(2,1)S(1)} fusion(f32[160,8,128]{2,1,0:T(8,128)} %get-tuple-element.21, bf16[160,8,128]{2,1,0:T(8,128)(2,1)S(1)} %collective-permute-done.10), kind=kLoop, calls=%fused_computation.1 | loop fusion | flops 491520 | bytes 1310720 | tf_op jit(solution)/shard_map/convert_element_type | solution.py:408
  80.1 1.5 %collective-permute-start.12 = (bf16[160,8,128]{2,1,0:T(8,128)(2,1)S(1)}, bf16[160,8,128]{2,1,0:T(8,128)(2,1)S(1)}, u32[]{:S(2)}, u32[]{:S(2)}) collective-permute-start(bf16[160,8,128]{2,1,0:T(8,128)(2,1)S(1)} %add_convert_fusion), channel_id=1, source_target_pairs={{0,2},{1,3},{2,0},{3,1},{4,6},{5,7},{6,4},{7,5},{8,10},{9,11},{10,... | collective-permute-start | bytes 983048 | tf_op jit(solution)/shard_map/ppermute | solution.py:409
  81.6 7.6 %cross.5 = f32[160,8,128]{2,1,0:T(8,128)} custom-call(s32[6]{0:T(128)} %stack.31.place_ref, f32[3]{0:T(128)} %convert_divide_fusion, bf16[2,160,1024]{2,1,0:T(8,128)(2,1)} %spectra.3.rest_0_.rest_1_, bf16[1,160,1024]{2,1,0:T(8,128)(2,1)} %get-tuple-element.15.rest_1_.rest_2_, bf16[1,160,1024]{2,1,0:T(8,128)(2,1)} %get-tuple-element.18.rest_2_.rest_3_, ...), custom_call_target="tpu_custom_call" | custom-call | flops 3355443200 | bytes 3932160 | tf_op jit(solution)/shard_map/cross/pallas_call | solution.py:323
  89.2 0.7 collective-permute-done.12
  89.9 2.0 %convert_add_fusion = f32[160,8,128]{2,1,0:T(8,128)} fusion(bf16[160,8,128]{2,1,0:T(8,128)(2,1)S(1)} %collective-permute-done.12, f32[160,8,128]{2,1,0:T(8,128)} %cross.5, bf16[160,8,128]{2,1,0:T(8,128)(2,1)S(1)} %collective-permute-done.11), kind=kLoop, calls=%fused_computation | loop fusion | flops 655360 | bytes 1966080 | tf_op jit(solution)/shard_map/add | solution.py:412
  (27 shorter events, 0.3 us)
Async XLA Ops:
  11.3 13.8 %copy-start.4 = (s32[1,4]{1,0:T(1,128)S(1)}, s32[1,4]{1,0:T(1,128)}, u32[]{:S(2)}) copy-start(s32[1,4]{1,0:T(1,128)} %valid_ref.3) | copy-start | bytes 52
  11.3 23.4 %copy-start.5 = (s32[1,2]{1,0:T(1,128)S(1)}, s32[1,2]{1,0:T(1,128)}, u32[]{:S(2)}) copy-start(s32[1,2]{1,0:T(1,128)} %param.7) | copy-start | bytes 28
  11.3 25.9 %copy-start = (bf16[2,160,1024]{2,1,0:T(8,128)(2,1)S(1)}, bf16[2,160,1024]{2,1,0:T(8,128)(2,1)}, u32[]{:S(2)}) copy-start(bf16[2,160,1024]{2,1,0:T(8,128)(2,1)} %spectra.3.rest_0_.rest_1_) | copy-start | bytes 1966084
  11.3 25.9 %collective-permute-start.2 = (bf16[2,160,1024]{2,1,0:T(8,128)(2,1)}, bf16[2,160,1024]{2,1,0:T(8,128)(2,1)S(1)}, u32[]{:S(2)}, u32[]{:S(2)}) collective-permute-start(bf16[2,160,1024]{2,1,0:T(8,128)(2,1)} %spectra.3.rest_0_.rest_1_), channel_id=1, source_target_pairs={{8,0},{12,4},{16,8},{20,12},{24,16},{28,20},{9,1},{13,5},{17,9},{2... | collective-permute-start | bytes 1966088 | tf_op jit(solution)/shard_map/ppermute | solution.py:378
  25.1 11.9 %collective-permute-start.1 = (s32[1,4]{1,0:T(1,128)S(1)}, s32[1,4]{1,0:T(1,128)S(1)}, u32[]{:S(2)}, u32[]{:S(2)}) collective-permute-start(s32[1,4]{1,0:T(1,128)S(1)} %copy-done.4), channel_id=1, source_target_pairs={{8,0},{12,4},{16,8},{20,12},{24,16},{28,20},{9,1},{13,5},{17,9},{2... | collective-permute-start | bytes 56 | tf_op jit(solution)/shard_map/ppermute | solution.py:384
  27.5 9.6 %collective-permute-start = (s32[1,4]{1,0:T(1,128)S(1)}, s32[1,4]{1,0:T(1,128)S(1)}, u32[]{:S(2)}, u32[]{:S(2)}) collective-permute-start(s32[1,4]{1,0:T(1,128)S(1)} %copy-done.4), channel_id=1, source_target_pairs={{4,0},{8,4},{12,8},{16,12},{20,16},{24,20},{28,24},{5,1},{9,5},{13... | collective-permute-start | bytes 56 | tf_op jit(solution)/shard_map/ppermute | solution.py:383
  30.8 12.6 %collective-permute-start.5 = (bf16[1,160,1024]{2,1,0:T(8,128)(2,1)}, bf16[1,160,1024]{2,1,0:T(8,128)(2,1)S(1)}, u32[]{:S(2)}, u32[]{:S(2)}) collective-permute-start(bf16[1,160,1024]{2,1,0:T(8,128)(2,1)} %get-tuple-element.15.rest_1_.rest_2_), channel_id=1, source_target_pairs={{8,0},{12,4},{16,8},{20,12},{24,16},{28,20},{9,1},{13,5},{17,9},{2... | collective-permute-start | bytes 983048 | tf_op jit(solution)/shard_map/ppermute | solution.py:378
  32.7 13.7 %collective-permute-start.7 = (bf16[1,160,1024]{2,1,0:T(8,128)(2,1)}, bf16[1,160,1024]{2,1,0:T(8,128)(2,1)S(1)}, u32[]{:S(2)}, u32[]{:S(2)}) collective-permute-start(bf16[1,160,1024]{2,1,0:T(8,128)(2,1)} %get-tuple-element.18.rest_2_.rest_3_), channel_id=1, source_target_pairs={{8,0},{12,4},{16,8},{20,12},{24,16},{28,20},{9,1},{13,5},{17,9},{2... | collective-permute-start | bytes 983048 | tf_op jit(solution)/shard_map/ppermute | solution.py:378
  37.2 17.8 %copy-start.1 = (bf16[2,160,1024]{2,1,0:T(8,128)(2,1)}, bf16[2,160,1024]{2,1,0:T(8,128)(2,1)S(1)}, u32[]{:S(2)}) copy-start(bf16[2,160,1024]{2,1,0:T(8,128)(2,1)S(1)} %collective-permute-done.2.rest_2_.rest_7_) | copy-start | bytes 1966084
  37.3 17.7 %collective-permute-start.9 = (bf16[2,160,1024]{2,1,0:T(8,128)(2,1)S(1)}, bf16[2,160,1024]{2,1,0:T(8,128)(2,1)S(1)}, u32[]{:S(2)}, u32[]{:S(2)}) collective-permute-start(bf16[2,160,1024]{2,1,0:T(8,128)(2,1)S(1)} %broadcast_select_fusion), channel_id=1, source_target_pairs={{4,0},{0,4},{12,8},{8,12},{20,16},{16,20},{28,24},{24,28},{5,1},{1... | collective-permute-start | bytes 1966088 | tf_op jit(solution)/shard_map/ppermute | solution.py:397
  38.0 1.1 %collective-permute-start.3 = (s32[3]{0:T(128)S(1)}, s32[3]{0:T(128)S(1)}, u32[]{:S(2)}, u32[]{:S(2)}) collective-permute-start(s32[3]{0:T(128)S(1)} %fusion), channel_id=1, source_target_pairs={{0,1},{1,0},{2,3},{3,2},{4,5},{5,4},{6,7},{7,6},{8,9},{9,8},{10,11... | collective-permute-start | bytes 44 | tf_op jit(solution)/shard_map/ppermute | solution.py:395
  39.2 3.5 %collective-permute-start.4 = (s32[3]{0:T(128)S(1)}, s32[3]{0:T(128)S(1)}, u32[]{:S(2)}, u32[]{:S(2)}) collective-permute-start(s32[3]{0:T(128)S(1)} %add.22), channel_id=1, source_target_pairs={{0,2},{1,3},{2,0},{3,1},{4,6},{5,7},{6,4},{7,5},{8,10},{9,11},{10,... | collective-permute-start | bytes 44 | tf_op jit(solution)/shard_map/ppermute | solution.py:396
  43.3 20.6 %copy-start.2 = (bf16[1,160,1024]{2,1,0:T(8,128)(2,1)}, bf16[1,160,1024]{2,1,0:T(8,128)(2,1)S(1)}, u32[]{:S(2)}) copy-start(bf16[1,160,1024]{2,1,0:T(8,128)(2,1)S(1)} %collective-permute-done.5.rest_5_.rest_8_) | copy-start | bytes 983044
  43.4 23.7 %collective-permute-start.6 = (bf16[1,160,1024]{2,1,0:T(8,128)(2,1)S(1)}, bf16[1,160,1024]{2,1,0:T(8,128)(2,1)S(1)}, u32[]{:S(2)}, u32[]{:S(2)}) collective-permute-start(bf16[1,160,1024]{2,1,0:T(8,128)(2,1)S(1)} %broadcast_select_fusion.2), channel_id=1, source_target_pairs={{4,0},{0,4},{12,8},{8,12},{20,16},{16,20},{28,24},{24,28},{5,1},{1... | collective-permute-start | bytes 983048 | tf_op jit(solution)/shard_map/ppermute | solution.py:397
  46.4 17.6 %copy-start.3 = (bf16[1,160,1024]{2,1,0:T(8,128)(2,1)}, bf16[1,160,1024]{2,1,0:T(8,128)(2,1)S(1)}, u32[]{:S(2)}) copy-start(bf16[1,160,1024]{2,1,0:T(8,128)(2,1)S(1)} %collective-permute-done.7.rest_6_.rest_9_) | copy-start | bytes 983044
  46.5 20.6 %collective-permute-start.8 = (bf16[1,160,1024]{2,1,0:T(8,128)(2,1)S(1)}, bf16[1,160,1024]{2,1,0:T(8,128)(2,1)S(1)}, u32[]{:S(2)}, u32[]{:S(2)}) collective-permute-start(bf16[1,160,1024]{2,1,0:T(8,128)(2,1)S(1)} %broadcast_select_fusion.1), channel_id=1, source_target_pairs={{4,0},{0,4},{12,8},{8,12},{20,16},{16,20},{28,24},{24,28},{5,1},{1... | collective-permute-start | bytes 983048 | tf_op jit(solution)/shard_map/ppermute | solution.py:397
  55.1 0.9 copy-start.6
  67.1 0.7 copy-start.8
  67.8 0.7 copy-start.7
  77.0 1.9 %collective-permute-start.10 = (bf16[160,8,128]{2,1,0:T(8,128)(2,1)}, bf16[160,8,128]{2,1,0:T(8,128)(2,1)S(1)}, u32[]{:S(2)}, u32[]{:S(2)}) collective-permute-start(bf16[160,8,128]{2,1,0:T(8,128)(2,1)} %get-tuple-element.22), channel_id=1, source_target_pairs={{0,1},{1,0},{2,3},{3,2},{4,5},{5,4},{6,7},{7,6},{8,9},{9,8},{10,11... | collective-permute-start | bytes 983048 | tf_op jit(solution)/shard_map/ppermute | solution.py:406
  77.1 12.1 %collective-permute-start.11 = (bf16[160,8,128]{2,1,0:T(8,128)(2,1)}, bf16[160,8,128]{2,1,0:T(8,128)(2,1)S(1)}, u32[]{:S(2)}, u32[]{:S(2)}) collective-permute-start(bf16[160,8,128]{2,1,0:T(8,128)(2,1)} %get-tuple-element.24), channel_id=1, source_target_pairs={{0,1},{1,0},{2,3},{3,2},{4,5},{5,4},{6,7},{7,6},{8,9},{9,8},{10,11... | collective-permute-start | bytes 983048 | tf_op jit(solution)/shard_map/ppermute | solution.py:407
  80.1 9.8 %collective-permute-start.12 = (bf16[160,8,128]{2,1,0:T(8,128)(2,1)S(1)}, bf16[160,8,128]{2,1,0:T(8,128)(2,1)S(1)}, u32[]{:S(2)}, u32[]{:S(2)}) collective-permute-start(bf16[160,8,128]{2,1,0:T(8,128)(2,1)S(1)} %add_convert_fusion), channel_id=1, source_target_pairs={{0,2},{1,3},{2,0},{3,1},{4,6},{5,7},{6,4},{7,5},{8,10},{9,11},{10,... | collective-permute-start | bytes 983048 | tf_op jit(solution)/shard_map/ppermute | solution.py:409

commit v10 on v9

--- a/solution.py
+++ b/solution.py
@@ -13,7 +13,7 @@
 LAGS = 128
 PAIRS = 32
 REACH = 2
-STEPS = 5
+STEPS = 3
 
 
 def bin_order(bins):
@@ -41,16 +41,38 @@
     return np.pad(tiles, ((0, 0), (0, 0), (0, 256 - lags))).astype(jnp.bfloat16)
 
 
-def spectra_kernel(valid_ref, first_ref, second_ref, table_ref, *rest, first_seg):
-    *white_refs, acc = rest
+def spectra_kernel(valid_ref, records_hbm, table_ref, *rest, first_seg):
+    *white_refs, acc, buffer, sems = rest
     step = pl.program_id(0)
-    channels, _, width = first_ref.shape
+    steps, _, channels, _, width = buffer.shape
     lane_tiles = acc.shape[0]
     bins = table_ref.shape[1] // 2
     segs = acc.shape[1] // channels
-    chosen = slice(first_seg, first_seg + segs)
-    first = first_ref[:, chosen, :].astype(jnp.float32)
-    second = second_ref[:, chosen, :].astype(jnp.float32)
+
+    def loads(at):
+        copies = []
+        for side in range(2):
+            columns = pl.ds(pl.multiple_of((at + side * steps) * width, 128), width)
+            source = records_hbm.at[:, first_seg : first_seg + segs, columns]
+            copies.append(
+                pltpu.make_async_copy(source, buffer.at[at, side], sems.at[at, side])
+            )
+        return copies
+
+    @pl.when(step == 0)
+    def _():
+        for load in loads(0) + loads(1):
+            load.start()
+
+    @pl.when(step + 2 < steps)
+    def _():
+        for load in loads(step + 2):
+            load.start()
+
+    for load in loads(step):
+        load.wait()
+    first = buffer[step, 0].astype(jnp.float32)
+    second = buffer[step, 1].astype(jnp.float32)
     even = (first + second).reshape(channels * segs, width).astype(jnp.bfloat16)
     odd = (first - second).reshape(channels * segs, width).astype(jnp.bfloat16)
     even_part = jnp.dot(even, table_ref[:, :bins], preferred_element_type=jnp.float32)
@@ -107,13 +129,16 @@
             num_scalar_prefetch=1,
             grid=(STEPS,),
             in_specs=[
-                pl.BlockSpec((channels, segs, width), lambda k, valid: (0, 0, k)),
-                pl.BlockSpec((channels, segs, width), lambda k, valid: (0, 0, k + STEPS)),
+                pl.BlockSpec(memory_space=pltpu.HBM),
                 pl.BlockSpec((width, 2 * BINS), lambda k, valid: (k, 0)),
             ],
             out_specs=[pl.BlockSpec((group, channels, 2 * BINS), lambda k, valid: (0, 0, 0))]
             * groups,
-            scratch_shapes=[pltpu.VMEM((2 * BINS // 128, rows, 128), jnp.float32)],
+            scratch_shapes=[
+                pltpu.VMEM((2 * BINS // 128, rows, 128), jnp.float32),
+                pltpu.VMEM((STEPS, 2, channels, groups * group, width), jnp.bfloat16),
+                pltpu.SemaphoreType.DMA((STEPS, 2)),
+            ],
         ),
         out_shape=[jax.ShapeDtypeStruct((group, channels, 2 * BINS), jnp.bfloat16)] * groups,
         compiler_params=pltpu.CompilerParams(vmem_limit_bytes=56 << 20),
@@ -122,7 +147,7 @@
             bytes_accessed=2 * channels * segs * samples + 2 * samples * BINS,
             transcendentals=rows * BINS,
         ),
-    )(valid_mask, records, records, table)
+    )(valid_mask, records, table)
 
 
 CH_TILE = 16
@@ -130,7 +155,7 @@
 WINDOW = 13
 
 
-def cross_kernel(place_ref, *rest, groups, specs, quarters, first, last):
+def cross_kernel(band_ref, rank_ref, *rest, groups, specs, quarters, first, last):
     if last:
         scale_ref, *rest = rest
     parts, segs = len(groups), sum(groups)
@@ -147,7 +172,8 @@
     channels = extended.shape[1] // (REACH + 1)
     lane_tiles = columns // 256
     steps = channels // (TILES * CH_TILE)
-    lowest = place_ref[0]
+    lowest, highest, rank = band_ref[0, 0], band_ref[0, 1], rank_ref[0]
+    starts = [8 * (rank ^ flip) for flip in (0, 2, 1, 3)]
     origin = lowest // CH_TILE * CH_TILE
 
     loads = []
@@ -209,7 +235,7 @@
                         mine[tile, 1, seg, part] = block[8:]
             for pair in range(8 * len(quarters)):
                 quarter = quarters[pair // 8]
-                offset = (lowest - origin) + place_ref[1 + quarter] + pair % 8
+                offset = (lowest - origin) + starts[quarter] + pair % 8
                 for tile in range(TILES):
                     reals, imags = [], []
                     for half in range(2):
@@ -253,14 +279,14 @@
             if not last:
                 results[0][tile, rows] = lagged.astype(jnp.bfloat16)
                 continue
-            offset = lowest + place_ref[1 + quarter] + pair % 8
+            offset = lowest + starts[quarter] + pair % 8
             partner = near + (base + offset)
             scale = jnp.where(
                 partner < channels,
                 scale_ref[0],
                 jnp.where(partner < 2 * channels, scale_ref[1], scale_ref[2]),
             )
-            inside = jnp.where(offset < place_ref[5], 1.0, 0.0)
+            inside = jnp.where(offset < highest, 1.0, 0.0)
             turned[pair // 8, pl.ds(pair % 8, CH_TILE, stride=8), :] = lagged * (scale * inside)
         if last:
             shape = (CH_TILE, 8, LAGS)
@@ -318,7 +344,7 @@
         ]
     smem = pl.BlockSpec(memory_space=pltpu.SMEM)
     anywhere = pl.BlockSpec(memory_space=pltpu.HBM)
-    small = [places, scales] if last else [places]
+    small = [*places, scales] if last else places
     large = [*owns, *nexts, *fars, lag_table, *([] if before is None else [before])]
     return pl.pallas_call(
         functools.partial(
@@ -347,26 +373,13 @@
     channels, segs, samples = records.shape
     blocks = lax.axis_size("chan")
     block = lax.axis_index("chan")
-    rank = lax.axis_index("tm")
-    lowest = band_limits[0, 0]
-    highest = band_limits[0, 1]
+    rank = lax.axis_index("tm")[None]
 
     hop_far = [(i + 2, i) for i in range(blocks - 2)]
     hop_near = [(i + 1, i) for i in range(blocks - 1)]
     pair_swap = [(i ^ 1, i) for i in range(blocks)]
     core_swap = [(i, i ^ 1) for i in range(4)]
     side_swap = [(i, i ^ 2) for i in range(4)]
-
-    places = jnp.stack(
-        [
-            lowest,
-            8 * rank,
-            8 * (rank ^ 2),
-            8 * (rank ^ 1),
-            8 * (rank ^ 3),
-            highest,
-        ]
-    )
 
     lag_table = jnp.asarray(lag_table_of(samples, BINS, LAGS))
     table = jnp.asarray(dft_table_of(samples, BINS))
@@ -399,7 +412,7 @@
 
     def stacked(part, quarters, before=None, last=True):
         chosen = (whites[part], nexts[part], fars[part])
-        return correlated(mesh, places, scales, *chosen, lag_table, before, quarters, last)
+        return correlated(mesh, [band_limits, rank], scales, *chosen, lag_table, before, quarters, last)
 
     (before,) = stacked(slice(0, 1), (1, 3, 2), last=False)
     other, send_far, send = stacked(slice(1, None), (1, 3, 2), before)

time: 92.4 us -> 86.1 us (0.932)
  the two profiles are of different devices: /device:TPU:24 before, /device:TPU:0 now
where the time goes in v10:
time: 86.1 us; the launch traced here: 84.4 us
  Pallas kernels  42.6 us (49%)
  starting transfers between devices  17.7 us (21%)
  waiting for transfers between devices  17.6 us (20%)
  other arithmetic  4 us (5%)
  local copies, waits for them, and re-layouts  2.34 us (3%)
    pallas_call x3, Pallas kernels, correlated(): pl.pallas_call(functools.partial(cross_kernel, groups=groups, specs=specs...  23.9 us
    pallas_call x2, Pallas kernels, whitened(): pl.pallas_call(functools.partial(spectra_kernel, first_seg=first_seg), na...  18.7 us
    ppermute x3, starting transfers between devices, shards(): nexts.append(lax.ppermute(passed, 'chan', pair_swap))  7.67 us
    ppermute x3, waiting for transfers between devices, shards(): fars = [lax.ppermute(white, 'chan', hop_far) for white in whites]  4.78 us
    ppermute x1, waiting for transfers between devices, shards(): lax.ppermute(valid_mask, 'chan', hop_far)  4.07 us
    ppermute x3, starting transfers between devices, shards(): fars = [lax.ppermute(white, 'chan', hop_far) for white in whites]  4.01 us
    ppermute x3, waiting for transfers between devices, shards(): nexts.append(lax.ppermute(passed, 'chan', pair_swap))  3.36 us
    unnamed x16, local copies, waits for them, and re-layouts  2.34 us
  transfers between devices with their start and end apart: 13, of which 8 were waited for; matrix products, arithmetic and copies ran while one was open for 2% of the time, Pallas kernels for 29%

profile of v10, /device:TPU:0, one launch (start us, length us, event | category | flops | bytes accessed | tf_op | source)
XLA Modules:
  0.0 84.4 jit_solution(8110584948938207550)
XLA Ops:
  0.0 9.3 %spectra.3.rest_0_.rest_1_ = bf16[2,160,1024]{2,1,0:T(8,128)(2,1)} custom-call(s32[1,4]{1,0:T(1,128)} %valid_ref.3, bf16[160,4,7680]{2,1,0:T(4,128)(2,1)} %records_hbm.3, bf16[3840,1024]{1,0:T(8,128)(2,1)} %constant.35.clone.table_ref), custom_call_target="tpu_custom_call" | custom-call | flops 5033164800 | bytes 17694720 | tf_op jit(solution)/shard_map/spectra/pallas_call | solution.py:125
  9.4 1.4 %collective-permute-start.2 = (bf16[2,160,1024]{2,1,0:T(8,128)(2,1)}, bf16[2,160,1024]{2,1,0:T(8,128)(2,1)S(1)}, u32[]{:S(2)}, u32[]{:S(2)}) collective-permute-start(bf16[2,160,1024]{2,1,0:T(8,128)(2,1)} %spectra.3.rest_0_.rest_1_), channel_id=1, source_target_pairs={{8,0},{12,4},{16,8},{20,12},{24,16},{28,20},{9,1},{13,5},{17,9},{2... | collective-permute-start | bytes 1966088 | tf_op jit(solution)/shard_map/ppermute | solution.py:391
  10.8 9.3 %spectra.2 = (bf16[1,160,1024]{2,1,0:T(8,128)(2,1)}, bf16[1,160,1024]{2,1,0:T(8,128)(2,1)}) custom-call(s32[1,4]{1,0:T(1,128)} %valid_ref.3, bf16[160,4,7680]{2,1,0:T(4,128)(2,1)} %records_hbm.3, bf16[3840,1024]{1,0:T(8,128)(2,1)} %constant.35.clone.table_ref), custom_call_target="tpu_custom_call" | custom-call | flops 5033164800 | bytes 17694720 | tf_op jit(solution)/shard_map/spectra/pallas_call | solution.py:125
  20.1 1.3 %collective-permute-start.1 = (s32[1,4]{1,0:T(1,128)S(1)}, s32[1,4]{1,0:T(1,128)S(1)}, u32[]{:S(2)}, u32[]{:S(2)}) collective-permute-start(s32[1,4]{1,0:T(1,128)S(1)} %copy-done.4), channel_id=1, source_target_pairs={{8,0},{12,4},{16,8},{20,12},{24,16},{28,20},{9,1},{13,5},{17,9},{2... | collective-permute-start | bytes 56 | tf_op jit(solution)/shard_map/ppermute | solution.py:397
  21.4 1.3 %collective-permute-start = (s32[1,4]{1,0:T(1,128)S(1)}, s32[1,4]{1,0:T(1,128)S(1)}, u32[]{:S(2)}, u32[]{:S(2)}) collective-permute-start(s32[1,4]{1,0:T(1,128)S(1)} %copy-done.4), channel_id=1, source_target_pairs={{4,0},{8,4},{12,8},{16,12},{20,16},{24,20},{28,24},{5,1},{9,5},{13... | collective-permute-start | bytes 56 | tf_op jit(solution)/shard_map/ppermute | solution.py:396
  22.7 1.3 %collective-permute-start.5 = (bf16[1,160,1024]{2,1,0:T(8,128)(2,1)}, bf16[1,160,1024]{2,1,0:T(8,128)(2,1)S(1)}, u32[]{:S(2)}, u32[]{:S(2)}) collective-permute-start(bf16[1,160,1024]{2,1,0:T(8,128)(2,1)} %get-tuple-element.15.rest_1_.rest_2_), channel_id=1, source_target_pairs={{8,0},{12,4},{16,8},{20,12},{24,16},{28,20},{9,1},{13,5},{17,9},{2... | collective-permute-start | bytes 983048 | tf_op jit(solution)/shard_map/ppermute | solution.py:391
  24.0 1.3 %collective-permute-start.7 = (bf16[1,160,1024]{2,1,0:T(8,128)(2,1)}, bf16[1,160,1024]{2,1,0:T(8,128)(2,1)S(1)}, u32[]{:S(2)}, u32[]{:S(2)}) collective-permute-start(bf16[1,160,1024]{2,1,0:T(8,128)(2,1)} %get-tuple-element.18.rest_2_.rest_3_), channel_id=1, source_target_pairs={{8,0},{12,4},{16,8},{20,12},{24,16},{28,20},{9,1},{13,5},{17,9},{2... | collective-permute-start | bytes 983048 | tf_op jit(solution)/shard_map/ppermute | solution.py:391
  25.4 4.1 %collective-permute-done.1 = s32[1,4]{1,0:T(1,128)S(1)} collective-permute-done((s32[1,4]{1,0:T(1,128)S(1)}, s32[1,4]{1,0:T(1,128)S(1)}, u32[]{:S(2)}, u32[]{:S(2)}) %collective-permute-start.1) | collective-permute-done | bytes 48 | tf_op jit(solution)/shard_map/ppermute | solution.py:397
  29.4 0.2 fusion
  29.6 0.1 broadcast_select_fusion
  29.7 1.7 %collective-permute-start.9 = (bf16[2,160,1024]{2,1,0:T(8,128)(2,1)S(1)}, bf16[2,160,1024]{2,1,0:T(8,128)(2,1)S(1)}, u32[]{:S(2)}, u32[]{:S(2)}) collective-permute-start(bf16[2,160,1024]{2,1,0:T(8,128)(2,1)S(1)} %broadcast_select_fusion), channel_id=1, source_target_pairs={{4,0},{0,4},{12,8},{8,12},{20,16},{16,20},{28,24},{24,28},{5,1},{1... | collective-permute-start | bytes 1966088 | tf_op jit(solution)/shard_map/ppermute | solution.py:410
  31.4 1.1 %collective-permute-done.3 = s32[3]{0:T(128)S(1)} collective-permute-done((s32[3]{0:T(128)S(1)}, s32[3]{0:T(128)S(1)}, u32[]{:S(2)}, u32[]{:S(2)}) %collective-permute-start.3) | collective-permute-done | bytes 44 | tf_op jit(solution)/shard_map/ppermute | solution.py:408
  32.5 1.5 %collective-permute-start.4 = (s32[3]{0:T(128)S(1)}, s32[3]{0:T(128)S(1)}, u32[]{:S(2)}, u32[]{:S(2)}) collective-permute-start(s32[3]{0:T(128)S(1)} %add.22), channel_id=1, source_target_pairs={{0,2},{1,3},{2,0},{3,1},{4,6},{5,7},{6,4},{7,5},{8,10},{9,11},{10,... | collective-permute-start | bytes 44 | tf_op jit(solution)/shard_map/ppermute | solution.py:409
  34.1 2.0 %collective-permute-done.4 = s32[3]{0:T(128)S(1)} collective-permute-done((s32[3]{0:T(128)S(1)}, s32[3]{0:T(128)S(1)}, u32[]{:S(2)}, u32[]{:S(2)}) %collective-permute-start.4) | collective-permute-done | bytes 44 | tf_op jit(solution)/shard_map/ppermute | solution.py:409
  36.1 0.5 convert_divide_fusion
  36.6 1.8 %collective-permute-done.5.rest_5_.rest_8_ = bf16[1,160,1024]{2,1,0:T(8,128)(2,1)S(1)} collective-permute-done((bf16[1,160,1024]{2,1,0:T(8,128)(2,1)}, bf16[1,160,1024]{2,1,0:T(8,128)(2,1)S(1)}, u32[]{:S(2)}, u32[]{:S(2)}) %collective-permute-start.5) | collective-permute-done | bytes 327712 | tf_op jit(solution)/shard_map/ppermute | solution.py:391
  38.5 3.1 %collective-permute-start.6 = (bf16[1,160,1024]{2,1,0:T(8,128)(2,1)S(1)}, bf16[1,160,1024]{2,1,0:T(8,128)(2,1)S(1)}, u32[]{:S(2)}, u32[]{:S(2)}) collective-permute-start(bf16[1,160,1024]{2,1,0:T(8,128)(2,1)S(1)} %broadcast_select_fusion.2), channel_id=1, source_target_pairs={{4,0},{0,4},{12,8},{8,12},{20,16},{16,20},{28,24},{24,28},{5,1},{1... | collective-permute-start | bytes 983048 | tf_op jit(solution)/shard_map/ppermute | solution.py:410
  41.6 2.9 %collective-permute-done.7.rest_6_.rest_9_ = bf16[1,160,1024]{2,1,0:T(8,128)(2,1)S(1)} collective-permute-done((bf16[1,160,1024]{2,1,0:T(8,128)(2,1)}, bf16[1,160,1024]{2,1,0:T(8,128)(2,1)S(1)}, u32[]{:S(2)}, u32[]{:S(2)}) %collective-permute-start.7) | collective-permute-done | bytes 327712 | tf_op jit(solution)/shard_map/ppermute | solution.py:391
  44.5 2.9 %collective-permute-start.8 = (bf16[1,160,1024]{2,1,0:T(8,128)(2,1)S(1)}, bf16[1,160,1024]{2,1,0:T(8,128)(2,1)S(1)}, u32[]{:S(2)}, u32[]{:S(2)}) collective-permute-start(bf16[1,160,1024]{2,1,0:T(8,128)(2,1)S(1)} %broadcast_select_fusion.1), channel_id=1, source_target_pairs={{4,0},{0,4},{12,8},{8,12},{20,16},{16,20},{28,24},{24,28},{5,1},{1... | collective-permute-start | bytes 983048 | tf_op jit(solution)/shard_map/ppermute | solution.py:410
  47.4 0.9 %copy-done.5 = bf16[2,160,1024]{2,1,0:T(8,128)(2,1)} copy-done((bf16[2,160,1024]{2,1,0:T(8,128)(2,1)}, bf16[2,160,1024]{2,1,0:T(8,128)(2,1)S(1)}, u32[]{:S(2)}) %copy-start.5) | copy-done | bytes 655384
  48.3 8.0 %cross.3.rest_8_ = bf16[10,384,128]{2,1,0:T(8,128)(2,1)} custom-call(s32[1,2]{1,0:T(1,128)} %band_ref.5, s32[1]{0:T(128)} %bitcast.rank_ref, bf16[2,160,1024]{2,1,0:T(8,128)(2,1)} %spectra.3.rest_0_.rest_1_, bf16[2,160,1024]{2,1,0:T(8,128)(2,1)} %copy-done.5, bf16[2,160,1024]{2,1,0:T(8,128)(2,1)} %copy-done.1, ...), custom_call_target="tpu_custom_call" | custom-call | flops 10066329600 | bytes 1966080 | tf_op jit(solution)/shard_map/cross/pallas_call | solution.py:349
  56.3 3.3 %collective-permute-done.8.rest_4_.rest_6_ = bf16[1,160,1024]{2,1,0:T(8,128)(2,1)S(1)} collective-permute-done((bf16[1,160,1024]{2,1,0:T(8,128)(2,1)S(1)}, bf16[1,160,1024]{2,1,0:T(8,128)(2,1)S(1)}, u32[]{:S(2)}, u32[]{:S(2)}) %collective-permute-start.8) | collective-permute-done | bytes 327712 | tf_op jit(solution)/shard_map/ppermute | solution.py:410
  59.7 0.7 copy-done.7
  60.4 0.7 copy-done.6
  61.1 8.4 %cross.4 = (f32[160,8,128]{2,1,0:T(8,128)}, bf16[160,8,128]{2,1,0:T(8,128)(2,1)}, bf16[160,8,128]{2,1,0:T(8,128)(2,1)}) custom-call(s32[1,2]{1,0:T(1,128)} %band_ref.5, s32[1]{0:T(128)} %bitcast.rank_ref, f32[3]{0:T(128)} %convert_divide_fusion, bf16[1,160,1024]{2,1,0:T(8,128)(2,1)} %get-tuple-element.15.rest_1_.rest_2_, ...), custom_call_target="tpu_custom_call" | custom-call | flops 10066329600 | bytes 1966080 | tf_op jit(solution)/shard_map/cross/pallas_call | solution.py:349
  69.6 0.5 collective-permute-start.11
  70.1 1.3 %collective-permute-done.10 = bf16[160,8,128]{2,1,0:T(8,128)(2,1)S(1)} collective-permute-done((bf16[160,8,128]{2,1,0:T(8,128)(2,1)}, bf16[160,8,128]{2,1,0:T(8,128)(2,1)S(1)}, u32[]{:S(2)}, u32[]{:S(2)}) %collective-permute-start.10) | collective-permute-done | bytes 327712 | tf_op jit(solution)/shard_map/ppermute | solution.py:419
  71.4 1.2 %add_convert_fusion = bf16[160,8,128]{2,1,0:T(8,128)(2,1)S(1)} fusion(f32[160,8,128]{2,1,0:T(8,128)} %get-tuple-element.21, bf16[160,8,128]{2,1,0:T(8,128)(2,1)S(1)} %collective-permute-done.10), kind=kLoop, calls=%fused_computation.1 | loop fusion | flops 491520 | bytes 1310720 | tf_op jit(solution)/shard_map/convert_element_type | solution.py:421
  72.6 1.4 %collective-permute-start.12 = (bf16[160,8,128]{2,1,0:T(8,128)(2,1)S(1)}, bf16[160,8,128]{2,1,0:T(8,128)(2,1)S(1)}, u32[]{:S(2)}, u32[]{:S(2)}) collective-permute-start(bf16[160,8,128]{2,1,0:T(8,128)(2,1)S(1)} %add_convert_fusion), channel_id=1, source_target_pairs={{0,2},{1,3},{2,0},{3,1},{4,6},{5,7},{6,4},{7,5},{8,10},{9,11},{10,... | collective-permute-start | bytes 983048 | tf_op jit(solution)/shard_map/ppermute | solution.py:422
  73.9 7.6 %cross.5 = f32[160,8,128]{2,1,0:T(8,128)} custom-call(s32[1,2]{1,0:T(1,128)} %band_ref.5, s32[1]{0:T(128)} %bitcast.rank_ref, f32[3]{0:T(128)} %convert_divide_fusion, bf16[2,160,1024]{2,1,0:T(8,128)(2,1)} %spectra.3.rest_0_.rest_1_, bf16[1,160,1024]{2,1,0:T(8,128)(2,1)} %get-tuple-element.15.rest_1_.rest_2_, ...), custom_call_target="tpu_custom_call" | custom-call | flops 3355443200 | bytes 3932160 | tf_op jit(solution)/shard_map/cross/pallas_call | solution.py:349
  81.5 0.9 %collective-permute-done.12 = bf16[160,8,128]{2,1,0:T(8,128)(2,1)S(1)} collective-permute-done((bf16[160,8,128]{2,1,0:T(8,128)(2,1)S(1)}, bf16[160,8,128]{2,1,0:T(8,128)(2,1)S(1)}, u32[]{:S(2)}, u32[]{:S(2)}) %collective-permute-start.12) | collective-permute-done | bytes 327712 | tf_op jit(solution)/shard_map/ppermute | solution.py:422
  82.4 2.0 %convert_add_fusion = f32[160,8,128]{2,1,0:T(8,128)} fusion(bf16[160,8,128]{2,1,0:T(8,128)(2,1)S(1)} %collective-permute-done.12, f32[160,8,128]{2,1,0:T(8,128)} %cross.5, bf16[160,8,128]{2,1,0:T(8,128)(2,1)S(1)} %collective-permute-done.11), kind=kLoop, calls=%fused_computation | loop fusion | flops 655360 | bytes 1966080 | tf_op jit(solution)/shard_map/add | solution.py:425
  (23 shorter events, 0.2 us)
Async XLA Ops:
  9.3 10.8 %copy-start.4 = (s32[1,4]{1,0:T(1,128)S(1)}, s32[1,4]{1,0:T(1,128)}, u32[]{:S(2)}) copy-start(s32[1,4]{1,0:T(1,128)} %valid_ref.3) | copy-start | bytes 52
  9.3 20.3 %copy-start = (bf16[2,160,1024]{2,1,0:T(8,128)(2,1)S(1)}, bf16[2,160,1024]{2,1,0:T(8,128)(2,1)}, u32[]{:S(2)}) copy-start(bf16[2,160,1024]{2,1,0:T(8,128)(2,1)} %spectra.3.rest_0_.rest_1_) | copy-start | bytes 1966084
  9.4 20.2 %collective-permute-start.2 = (bf16[2,160,1024]{2,1,0:T(8,128)(2,1)}, bf16[2,160,1024]{2,1,0:T(8,128)(2,1)S(1)}, u32[]{:S(2)}, u32[]{:S(2)}) collective-permute-start(bf16[2,160,1024]{2,1,0:T(8,128)(2,1)} %spectra.3.rest_0_.rest_1_), channel_id=1, source_target_pairs={{8,0},{12,4},{16,8},{20,12},{24,16},{28,20},{9,1},{13,5},{17,9},{2... | collective-permute-start | bytes 1966088 | tf_op jit(solution)/shard_map/ppermute | solution.py:391
  20.1 9.3 %collective-permute-start.1 = (s32[1,4]{1,0:T(1,128)S(1)}, s32[1,4]{1,0:T(1,128)S(1)}, u32[]{:S(2)}, u32[]{:S(2)}) collective-permute-start(s32[1,4]{1,0:T(1,128)S(1)} %copy-done.4), channel_id=1, source_target_pairs={{8,0},{12,4},{16,8},{20,12},{24,16},{28,20},{9,1},{13,5},{17,9},{2... | collective-permute-start | bytes 56 | tf_op jit(solution)/shard_map/ppermute | solution.py:397
  21.4 8.0 %collective-permute-start = (s32[1,4]{1,0:T(1,128)S(1)}, s32[1,4]{1,0:T(1,128)S(1)}, u32[]{:S(2)}, u32[]{:S(2)}) collective-permute-start(s32[1,4]{1,0:T(1,128)S(1)} %copy-done.4), channel_id=1, source_target_pairs={{4,0},{8,4},{12,8},{16,12},{20,16},{24,20},{28,24},{5,1},{9,5},{13... | collective-permute-start | bytes 56 | tf_op jit(solution)/shard_map/ppermute | solution.py:396
  22.7 15.7 %collective-permute-start.5 = (bf16[1,160,1024]{2,1,0:T(8,128)(2,1)}, bf16[1,160,1024]{2,1,0:T(8,128)(2,1)S(1)}, u32[]{:S(2)}, u32[]{:S(2)}) collective-permute-start(bf16[1,160,1024]{2,1,0:T(8,128)(2,1)} %get-tuple-element.15.rest_1_.rest_2_), channel_id=1, source_target_pairs={{8,0},{12,4},{16,8},{20,12},{24,16},{28,20},{9,1},{13,5},{17,9},{2... | collective-permute-start | bytes 983048 | tf_op jit(solution)/shard_map/ppermute | solution.py:391
  24.0 20.4 %collective-permute-start.7 = (bf16[1,160,1024]{2,1,0:T(8,128)(2,1)}, bf16[1,160,1024]{2,1,0:T(8,128)(2,1)S(1)}, u32[]{:S(2)}, u32[]{:S(2)}) collective-permute-start(bf16[1,160,1024]{2,1,0:T(8,128)(2,1)} %get-tuple-element.18.rest_2_.rest_3_), channel_id=1, source_target_pairs={{8,0},{12,4},{16,8},{20,12},{24,16},{28,20},{9,1},{13,5},{17,9},{2... | collective-permute-start | bytes 983048 | tf_op jit(solution)/shard_map/ppermute | solution.py:391
  29.6 17.8 %copy-start.1 = (bf16[2,160,1024]{2,1,0:T(8,128)(2,1)}, bf16[2,160,1024]{2,1,0:T(8,128)(2,1)S(1)}, u32[]{:S(2)}) copy-start(bf16[2,160,1024]{2,1,0:T(8,128)(2,1)S(1)} %collective-permute-done.2.rest_2_.rest_7_) | copy-start | bytes 1966084
  29.7 17.7 %collective-permute-start.9 = (bf16[2,160,1024]{2,1,0:T(8,128)(2,1)S(1)}, bf16[2,160,1024]{2,1,0:T(8,128)(2,1)S(1)}, u32[]{:S(2)}, u32[]{:S(2)}) collective-permute-start(bf16[2,160,1024]{2,1,0:T(8,128)(2,1)S(1)} %broadcast_select_fusion), channel_id=1, source_target_pairs={{4,0},{0,4},{12,8},{8,12},{20,16},{16,20},{28,24},{24,28},{5,1},{1... | collective-permute-start | bytes 1966088 | tf_op jit(solution)/shard_map/ppermute | solution.py:410
  31.4 1.1 %collective-permute-start.3 = (s32[3]{0:T(128)S(1)}, s32[3]{0:T(128)S(1)}, u32[]{:S(2)}, u32[]{:S(2)}) collective-permute-start(s32[3]{0:T(128)S(1)} %fusion), channel_id=1, source_target_pairs={{0,1},{1,0},{2,3},{3,2},{4,5},{5,4},{6,7},{7,6},{8,9},{9,8},{10,11... | collective-permute-start | bytes 44 | tf_op jit(solution)/shard_map/ppermute | solution.py:408
  32.5 3.5 %collective-permute-start.4 = (s32[3]{0:T(128)S(1)}, s32[3]{0:T(128)S(1)}, u32[]{:S(2)}, u32[]{:S(2)}) collective-permute-start(s32[3]{0:T(128)S(1)} %add.22), channel_id=1, source_target_pairs={{0,2},{1,3},{2,0},{3,1},{4,6},{5,7},{6,4},{7,5},{8,10},{9,11},{10,... | collective-permute-start | bytes 44 | tf_op jit(solution)/shard_map/ppermute | solution.py:409
  38.4 17.9 %copy-start.2 = (bf16[1,160,1024]{2,1,0:T(8,128)(2,1)}, bf16[1,160,1024]{2,1,0:T(8,128)(2,1)S(1)}, u32[]{:S(2)}) copy-start(bf16[1,160,1024]{2,1,0:T(8,128)(2,1)S(1)} %collective-permute-done.5.rest_5_.rest_8_) | copy-start | bytes 983044
  38.5 21.2 %collective-permute-start.6 = (bf16[1,160,1024]{2,1,0:T(8,128)(2,1)S(1)}, bf16[1,160,1024]{2,1,0:T(8,128)(2,1)S(1)}, u32[]{:S(2)}, u32[]{:S(2)}) collective-permute-start(bf16[1,160,1024]{2,1,0:T(8,128)(2,1)S(1)} %broadcast_select_fusion.2), channel_id=1, source_target_pairs={{4,0},{0,4},{12,8},{8,12},{20,16},{16,20},{28,24},{24,28},{5,1},{1... | collective-permute-start | bytes 983048 | tf_op jit(solution)/shard_map/ppermute | solution.py:410
  44.5 11.8 %copy-start.3 = (bf16[1,160,1024]{2,1,0:T(8,128)(2,1)}, bf16[1,160,1024]{2,1,0:T(8,128)(2,1)S(1)}, u32[]{:S(2)}) copy-start(bf16[1,160,1024]{2,1,0:T(8,128)(2,1)S(1)} %collective-permute-done.7.rest_6_.rest_9_) | copy-start | bytes 983044
  44.5 15.1 %collective-permute-start.8 = (bf16[1,160,1024]{2,1,0:T(8,128)(2,1)S(1)}, bf16[1,160,1024]{2,1,0:T(8,128)(2,1)S(1)}, u32[]{:S(2)}, u32[]{:S(2)}) collective-permute-start(bf16[1,160,1024]{2,1,0:T(8,128)(2,1)S(1)} %broadcast_select_fusion.1), channel_id=1, source_target_pairs={{4,0},{0,4},{12,8},{8,12},{20,16},{16,20},{28,24},{24,28},{5,1},{1... | collective-permute-start | bytes 983048 | tf_op jit(solution)/shard_map/ppermute | solution.py:410
  47.4 0.9 %copy-start.5 = (bf16[2,160,1024]{2,1,0:T(8,128)(2,1)}, bf16[2,160,1024]{2,1,0:T(8,128)(2,1)S(1)}, u32[]{:S(2)}) copy-start(bf16[2,160,1024]{2,1,0:T(8,128)(2,1)S(1)} %collective-permute-done.9.rest_1_.rest_4_) | copy-start | bytes 1966084
  59.7 0.7 copy-start.7
  60.4 0.7 copy-start.6
  69.5 1.9 %collective-permute-start.10 = (bf16[160,8,128]{2,1,0:T(8,128)(2,1)}, bf16[160,8,128]{2,1,0:T(8,128)(2,1)S(1)}, u32[]{:S(2)}, u32[]{:S(2)}) collective-permute-start(bf16[160,8,128]{2,1,0:T(8,128)(2,1)} %get-tuple-element.22), channel_id=1, source_target_pairs={{0,1},{1,0},{2,3},{3,2},{4,5},{5,4},{6,7},{7,6},{8,9},{9,8},{10,11... | collective-permute-start | bytes 983048 | tf_op jit(solution)/shard_map/ppermute | solution.py:419
  69.6 11.9 %collective-permute-start.11 = (bf16[160,8,128]{2,1,0:T(8,128)(2,1)}, bf16[160,8,128]{2,1,0:T(8,128)(2,1)S(1)}, u32[]{:S(2)}, u32[]{:S(2)}) collective-permute-start(bf16[160,8,128]{2,1,0:T(8,128)(2,1)} %get-tuple-element.24), channel_id=1, source_target_pairs={{0,1},{1,0},{2,3},{3,2},{4,5},{5,4},{6,7},{7,6},{8,9},{9,8},{10,11... | collective-permute-start | bytes 983048 | tf_op jit(solution)/shard_map/ppermute | solution.py:420
  72.6 9.8 %collective-permute-start.12 = (bf16[160,8,128]{2,1,0:T(8,128)(2,1)S(1)}, bf16[160,8,128]{2,1,0:T(8,128)(2,1)S(1)}, u32[]{:S(2)}, u32[]{:S(2)}) collective-permute-start(bf16[160,8,128]{2,1,0:T(8,128)(2,1)S(1)} %add_convert_fusion), channel_id=1, source_target_pairs={{0,2},{1,3},{2,0},{3,1},{4,6},{5,7},{6,4},{7,5},{8,10},{9,11},{10,... | collective-permute-start | bytes 983048 | tf_op jit(solution)/shard_map/ppermute | solution.py:422

commit v11 on v10

--- a/solution.py
+++ b/solution.py
@@ -390,21 +390,16 @@
     ]
     fars = [lax.ppermute(white, "chan", hop_far) for white in whites]
     valid_mask, _ = lax.optimization_barrier((valid_mask, whites[1]))
-    marks = jnp.stack(
-        [
-            valid_mask,
-            lax.ppermute(valid_mask, "chan", hop_near),
-            lax.ppermute(valid_mask, "chan", hop_far),
-        ]
-    )
-    counts = jnp.sum(marks * valid_mask[None], axis=(1, 2))
+    marks = [valid_mask] + [lax.ppermute(valid_mask, "chan", hop) for hop in (hop_near, hop_far)]
+    counts = None
     nexts = []
     for white, far in zip(whites, fars):
         if nexts:
             far, _ = lax.optimization_barrier((far, (passed, counts)))
         passed = jnp.where(block % 2 == 0, far, white)
         if not nexts:
-            counts, _ = lax.optimization_barrier((counts, passed))
+            marks, _ = lax.optimization_barrier((marks, passed))
+            counts = jnp.sum(jnp.stack(marks) * marks[0][None], axis=(1, 2))
             counts += lax.ppermute(counts, "tm", core_swap)
             counts += lax.ppermute(counts, "tm", side_swap)
         nexts.append(lax.ppermute(passed, "chan", pair_swap))

time: 86.1 us -> 85.9 us (level)
    ppermute x2, waiting for transfers between devices: 4.07 us -> 0.01 us  [shards(): lax.ppermute(valid_mask, 'chan', hop)]
    ppermute x3, waiting for transfers between devices: 4.78 us -> 8.81 us  [shards(): fars = [lax.ppermute(white, 'chan', hop_far) for white in whites]]
  transfers between devices with their start and end apart: 13 -> 13, of which waited for: 8 -> 8; matrix products, arithmetic and copies ran while one was open for 2% -> 2% of each run, Pallas kernels for 29% -> 30%
where the time goes in v11:
time: 85.9 us; the launch traced here: 84.2 us
  Pallas kernels  42.7 us (50%)
  starting transfers between devices  17.9 us (21%)
  waiting for transfers between devices  17.1 us (20%)
  other arithmetic  4 us (5%)
  local copies, waits for them, and re-layouts  2.34 us (3%)
    pallas_call x3, Pallas kernels, correlated(): pl.pallas_call(functools.partial(cross_kernel, groups=groups, specs=specs...  24.1 us
    pallas_call x2, Pallas kernels, whitened(): pl.pallas_call(functools.partial(spectra_kernel, first_seg=first_seg), na...  18.7 us
    ppermute x3, waiting for transfers between devices, shards(): fars = [lax.ppermute(white, 'chan', hop_far) for white in whites]  8.81 us
    ppermute x3, starting transfers between devices, shards(): nexts.append(lax.ppermute(passed, 'chan', pair_swap))  7.67 us
    ppermute x3, starting transfers between devices, shards(): fars = [lax.ppermute(white, 'chan', hop_far) for white in whites]  4.01 us
    ppermute x3, waiting for transfers between devices, shards(): nexts.append(lax.ppermute(passed, 'chan', pair_swap))  3.17 us
    ppermute x2, starting transfers between devices, shards(): lax.ppermute(valid_mask, 'chan', hop)  2.58 us
    unnamed x16, local copies, waits for them, and re-layouts  2.34 us
  transfers between devices with their start and end apart: 13, of which 8 were waited for; matrix products, arithmetic and copies ran while one was open for 2% of the time, Pallas kernels for 30%

profile of v11, /device:TPU:0, one launch (start us, length us, event | category | flops | bytes accessed | tf_op | source)
XLA Modules:
  0.0 84.2 jit_solution(4447428871184368998)
XLA Ops:
  0.0 9.3 %spectra.3.rest_0_.rest_1_ = bf16[2,160,1024]{2,1,0:T(8,128)(2,1)} custom-call(s32[1,4]{1,0:T(1,128)} %valid_ref.3, bf16[160,4,7680]{2,1,0:T(4,128)(2,1)} %records_hbm.3, bf16[3840,1024]{1,0:T(8,128)(2,1)} %constant.35.clone.table_ref), custom_call_target="tpu_custom_call" | custom-call | flops 5033164800 | bytes 17694720 | tf_op jit(solution)/shard_map/spectra/pallas_call | solution.py:125
  9.4 1.4 %collective-permute-start.2 = (bf16[2,160,1024]{2,1,0:T(8,128)(2,1)}, bf16[2,160,1024]{2,1,0:T(8,128)(2,1)S(1)}, u32[]{:S(2)}, u32[]{:S(2)}) collective-permute-start(bf16[2,160,1024]{2,1,0:T(8,128)(2,1)} %spectra.3.rest_0_.rest_1_), channel_id=1, source_target_pairs={{8,0},{12,4},{16,8},{20,12},{24,16},{28,20},{9,1},{13,5},{17,9},{2... | collective-permute-start | bytes 1966088 | tf_op jit(solution)/shard_map/ppermute | solution.py:391
  10.8 9.3 %spectra.2 = (bf16[1,160,1024]{2,1,0:T(8,128)(2,1)}, bf16[1,160,1024]{2,1,0:T(8,128)(2,1)}) custom-call(s32[1,4]{1,0:T(1,128)} %valid_ref.3, bf16[160,4,7680]{2,1,0:T(4,128)(2,1)} %records_hbm.3, bf16[3840,1024]{1,0:T(8,128)(2,1)} %constant.35.clone.table_ref), custom_call_target="tpu_custom_call" | custom-call | flops 5033164800 | bytes 17694720 | tf_op jit(solution)/shard_map/spectra/pallas_call | solution.py:125
  20.1 1.3 %collective-permute-start.1 = (s32[1,4]{1,0:T(1,128)S(1)}, s32[1,4]{1,0:T(1,128)S(1)}, u32[]{:S(2)}, u32[]{:S(2)}) collective-permute-start(s32[1,4]{1,0:T(1,128)S(1)} %copy-done.4), channel_id=1, source_target_pairs={{8,0},{12,4},{16,8},{20,12},{24,16},{28,20},{9,1},{13,5},{17,9},{2... | collective-permute-start | bytes 56 | tf_op jit(solution)/shard_map/ppermute | solution.py:393
  21.4 1.3 %collective-permute-start = (s32[1,4]{1,0:T(1,128)S(1)}, s32[1,4]{1,0:T(1,128)S(1)}, u32[]{:S(2)}, u32[]{:S(2)}) collective-permute-start(s32[1,4]{1,0:T(1,128)S(1)} %copy-done.4), channel_id=1, source_target_pairs={{4,0},{8,4},{12,8},{16,12},{20,16},{24,20},{28,24},{5,1},{9,5},{13... | collective-permute-start | bytes 56 | tf_op jit(solution)/shard_map/ppermute | solution.py:393
  22.7 1.3 %collective-permute-start.5 = (bf16[1,160,1024]{2,1,0:T(8,128)(2,1)}, bf16[1,160,1024]{2,1,0:T(8,128)(2,1)S(1)}, u32[]{:S(2)}, u32[]{:S(2)}) collective-permute-start(bf16[1,160,1024]{2,1,0:T(8,128)(2,1)} %get-tuple-element.17.rest_1_.rest_2_), channel_id=1, source_target_pairs={{8,0},{12,4},{16,8},{20,12},{24,16},{28,20},{9,1},{13,5},{17,9},{2... | collective-permute-start | bytes 983048 | tf_op jit(solution)/shard_map/ppermute | solution.py:391
  24.0 1.3 %collective-permute-start.7 = (bf16[1,160,1024]{2,1,0:T(8,128)(2,1)}, bf16[1,160,1024]{2,1,0:T(8,128)(2,1)S(1)}, u32[]{:S(2)}, u32[]{:S(2)}) collective-permute-start(bf16[1,160,1024]{2,1,0:T(8,128)(2,1)} %get-tuple-element.22.rest_2_.rest_3_), channel_id=1, source_target_pairs={{8,0},{12,4},{16,8},{20,12},{24,16},{28,20},{9,1},{13,5},{17,9},{2... | collective-permute-start | bytes 983048 | tf_op jit(solution)/shard_map/ppermute | solution.py:391
  25.4 4.0 %collective-permute-done.2.rest_2_.rest_7_ = bf16[2,160,1024]{2,1,0:T(8,128)(2,1)S(1)} collective-permute-done((bf16[2,160,1024]{2,1,0:T(8,128)(2,1)}, bf16[2,160,1024]{2,1,0:T(8,128)(2,1)S(1)}, u32[]{:S(2)}, u32[]{:S(2)}) %collective-permute-start.2) | collective-permute-done | bytes 655392 | tf_op jit(solution)/shard_map/ppermute | solution.py:391
  29.4 1.7 %collective-permute-start.9 = (bf16[2,160,1024]{2,1,0:T(8,128)(2,1)S(1)}, bf16[2,160,1024]{2,1,0:T(8,128)(2,1)S(1)}, u32[]{:S(2)}, u32[]{:S(2)}) collective-permute-start(bf16[2,160,1024]{2,1,0:T(8,128)(2,1)S(1)} %broadcast_select_fusion), channel_id=1, source_target_pairs={{4,0},{0,4},{12,8},{8,12},{20,16},{16,20},{28,24},{24,28},{5,1},{1... | collective-permute-start | bytes 1966088 | tf_op jit(solution)/shard_map/ppermute | solution.py:405
  31.2 0.2 fusion
  31.3 0.1 collective-permute-start.3
  31.4 1.1 %collective-permute-done.3 = s32[3]{0:T(128)S(1)} collective-permute-done((s32[3]{0:T(128)S(1)}, s32[3]{0:T(128)S(1)}, u32[]{:S(2)}, u32[]{:S(2)}) %collective-permute-start.3) | collective-permute-done | bytes 44 | tf_op jit(solution)/shard_map/ppermute | solution.py:403
  32.5 1.5 %collective-permute-start.4 = (s32[3]{0:T(128)S(1)}, s32[3]{0:T(128)S(1)}, u32[]{:S(2)}, u32[]{:S(2)}) collective-permute-start(s32[3]{0:T(128)S(1)} %add.22), channel_id=1, source_target_pairs={{0,2},{1,3},{2,0},{3,1},{4,6},{5,7},{6,4},{7,5},{8,10},{9,11},{10,... | collective-permute-start | bytes 44 | tf_op jit(solution)/shard_map/ppermute | solution.py:404
  34.0 2.0 %collective-permute-done.4 = s32[3]{0:T(128)S(1)} collective-permute-done((s32[3]{0:T(128)S(1)}, s32[3]{0:T(128)S(1)}, u32[]{:S(2)}, u32[]{:S(2)}) %collective-permute-start.4) | collective-permute-done | bytes 44 | tf_op jit(solution)/shard_map/ppermute | solution.py:404
  36.1 0.5 convert_divide_fusion
  36.6 1.9 %collective-permute-done.5.rest_5_.rest_8_ = bf16[1,160,1024]{2,1,0:T(8,128)(2,1)S(1)} collective-permute-done((bf16[1,160,1024]{2,1,0:T(8,128)(2,1)}, bf16[1,160,1024]{2,1,0:T(8,128)(2,1)S(1)}, u32[]{:S(2)}, u32[]{:S(2)}) %collective-permute-start.5) | collective-permute-done | bytes 327712 | tf_op jit(solution)/shard_map/ppermute | solution.py:391
  38.5 3.1 %collective-permute-start.6 = (bf16[1,160,1024]{2,1,0:T(8,128)(2,1)S(1)}, bf16[1,160,1024]{2,1,0:T(8,128)(2,1)S(1)}, u32[]{:S(2)}, u32[]{:S(2)}) collective-permute-start(bf16[1,160,1024]{2,1,0:T(8,128)(2,1)S(1)} %broadcast_select_fusion.2), channel_id=1, source_target_pairs={{4,0},{0,4},{12,8},{8,12},{20,16},{16,20},{28,24},{24,28},{5,1},{1... | collective-permute-start | bytes 983048 | tf_op jit(solution)/shard_map/ppermute | solution.py:405
  41.6 2.9 %collective-permute-done.7.rest_6_.rest_9_ = bf16[1,160,1024]{2,1,0:T(8,128)(2,1)S(1)} collective-permute-done((bf16[1,160,1024]{2,1,0:T(8,128)(2,1)}, bf16[1,160,1024]{2,1,0:T(8,128)(2,1)S(1)}, u32[]{:S(2)}, u32[]{:S(2)}) %collective-permute-start.7) | collective-permute-done | bytes 327712 | tf_op jit(solution)/shard_map/ppermute | solution.py:391
  44.5 2.9 %collective-permute-start.8 = (bf16[1,160,1024]{2,1,0:T(8,128)(2,1)S(1)}, bf16[1,160,1024]{2,1,0:T(8,128)(2,1)S(1)}, u32[]{:S(2)}, u32[]{:S(2)}) collective-permute-start(bf16[1,160,1024]{2,1,0:T(8,128)(2,1)S(1)} %broadcast_select_fusion.1), channel_id=1, source_target_pairs={{4,0},{0,4},{12,8},{8,12},{20,16},{16,20},{28,24},{24,28},{5,1},{1... | collective-permute-start | bytes 983048 | tf_op jit(solution)/shard_map/ppermute | solution.py:405
  47.4 0.9 %copy-done.5 = bf16[2,160,1024]{2,1,0:T(8,128)(2,1)} copy-done((bf16[2,160,1024]{2,1,0:T(8,128)(2,1)}, bf16[2,160,1024]{2,1,0:T(8,128)(2,1)S(1)}, u32[]{:S(2)}) %copy-start.5) | copy-done | bytes 655384
  48.3 8.0 %cross.3.rest_8_ = bf16[10,384,128]{2,1,0:T(8,128)(2,1)} custom-call(s32[1,2]{1,0:T(1,128)} %band_ref.5, s32[1]{0:T(128)} %bitcast.rank_ref, bf16[2,160,1024]{2,1,0:T(8,128)(2,1)} %spectra.3.rest_0_.rest_1_, bf16[2,160,1024]{2,1,0:T(8,128)(2,1)} %copy-done.5, bf16[2,160,1024]{2,1,0:T(8,128)(2,1)} %copy-done.1, ...), custom_call_target="tpu_custom_call" | custom-call | flops 10066329600 | bytes 1966080 | tf_op jit(solution)/shard_map/cross/pallas_call | solution.py:349
  56.3 3.2 %collective-permute-done.8.rest_4_.rest_6_ = bf16[1,160,1024]{2,1,0:T(8,128)(2,1)S(1)} collective-permute-done((bf16[1,160,1024]{2,1,0:T(8,128)(2,1)S(1)}, bf16[1,160,1024]{2,1,0:T(8,128)(2,1)S(1)}, u32[]{:S(2)}, u32[]{:S(2)}) %collective-permute-start.8) | collective-permute-done | bytes 327712 | tf_op jit(solution)/shard_map/ppermute | solution.py:405
  59.5 0.7 copy-done.7
  60.2 0.7 copy-done.6
  60.9 8.4 %cross.4 = (f32[160,8,128]{2,1,0:T(8,128)}, bf16[160,8,128]{2,1,0:T(8,128)(2,1)}, bf16[160,8,128]{2,1,0:T(8,128)(2,1)}) custom-call(s32[1,2]{1,0:T(1,128)} %band_ref.5, s32[1]{0:T(128)} %bitcast.rank_ref, f32[3]{0:T(128)} %convert_divide_fusion, bf16[1,160,1024]{2,1,0:T(8,128)(2,1)} %get-tuple-element.17.rest_1_.rest_2_, ...), custom_call_target="tpu_custom_call" | custom-call | flops 10066329600 | bytes 1966080 | tf_op jit(solution)/shard_map/cross/pallas_call | solution.py:349
  69.4 0.5 collective-permute-start.11
  69.9 1.3 %collective-permute-done.10 = bf16[160,8,128]{2,1,0:T(8,128)(2,1)S(1)} collective-permute-done((bf16[160,8,128]{2,1,0:T(8,128)(2,1)}, bf16[160,8,128]{2,1,0:T(8,128)(2,1)S(1)}, u32[]{:S(2)}, u32[]{:S(2)}) %collective-permute-start.10) | collective-permute-done | bytes 327712 | tf_op jit(solution)/shard_map/ppermute | solution.py:414
  71.2 1.2 %add_convert_fusion = bf16[160,8,128]{2,1,0:T(8,128)(2,1)S(1)} fusion(f32[160,8,128]{2,1,0:T(8,128)} %get-tuple-element.25, bf16[160,8,128]{2,1,0:T(8,128)(2,1)S(1)} %collective-permute-done.10), kind=kLoop, calls=%fused_computation.1 | loop fusion | flops 491520 | bytes 1310720 | tf_op jit(solution)/shard_map/convert_element_type | solution.py:416
  72.4 1.4 %collective-permute-start.12 = (bf16[160,8,128]{2,1,0:T(8,128)(2,1)S(1)}, bf16[160,8,128]{2,1,0:T(8,128)(2,1)S(1)}, u32[]{:S(2)}, u32[]{:S(2)}) collective-permute-start(bf16[160,8,128]{2,1,0:T(8,128)(2,1)S(1)} %add_convert_fusion), channel_id=1, source_target_pairs={{0,2},{1,3},{2,0},{3,1},{4,6},{5,7},{6,4},{7,5},{8,10},{9,11},{10,... | collective-permute-start | bytes 983048 | tf_op jit(solution)/shard_map/ppermute | solution.py:417
  73.8 7.7 %cross.5 = f32[160,8,128]{2,1,0:T(8,128)} custom-call(s32[1,2]{1,0:T(1,128)} %band_ref.5, s32[1]{0:T(128)} %bitcast.rank_ref, f32[3]{0:T(128)} %convert_divide_fusion, bf16[2,160,1024]{2,1,0:T(8,128)(2,1)} %spectra.3.rest_0_.rest_1_, bf16[1,160,1024]{2,1,0:T(8,128)(2,1)} %get-tuple-element.17.rest_1_.rest_2_, ...), custom_call_target="tpu_custom_call" | custom-call | flops 3355443200 | bytes 3932160 | tf_op jit(solution)/shard_map/cross/pallas_call | solution.py:349
  81.6 0.6 collective-permute-done.12
  82.2 2.0 %convert_add_fusion = f32[160,8,128]{2,1,0:T(8,128)} fusion(bf16[160,8,128]{2,1,0:T(8,128)(2,1)S(1)} %collective-permute-done.12, f32[160,8,128]{2,1,0:T(8,128)} %cross.5, bf16[160,8,128]{2,1,0:T(8,128)(2,1)S(1)} %collective-permute-done.11), kind=kLoop, calls=%fused_computation | loop fusion | flops 655360 | bytes 1966080 | tf_op jit(solution)/shard_map/add | solution.py:420
  (23 shorter events, 0.3 us)
Async XLA Ops:
  9.3 10.8 %copy-start.4 = (s32[1,4]{1,0:T(1,128)S(1)}, s32[1,4]{1,0:T(1,128)}, u32[]{:S(2)}) copy-start(s32[1,4]{1,0:T(1,128)} %valid_ref.3) | copy-start | bytes 52
  9.3 20.0 %copy-start = (bf16[2,160,1024]{2,1,0:T(8,128)(2,1)S(1)}, bf16[2,160,1024]{2,1,0:T(8,128)(2,1)}, u32[]{:S(2)}) copy-start(bf16[2,160,1024]{2,1,0:T(8,128)(2,1)} %spectra.3.rest_0_.rest_1_) | copy-start | bytes 1966084
  9.4 20.0 %collective-permute-start.2 = (bf16[2,160,1024]{2,1,0:T(8,128)(2,1)}, bf16[2,160,1024]{2,1,0:T(8,128)(2,1)S(1)}, u32[]{:S(2)}, u32[]{:S(2)}) collective-permute-start(bf16[2,160,1024]{2,1,0:T(8,128)(2,1)} %spectra.3.rest_0_.rest_1_), channel_id=1, source_target_pairs={{8,0},{12,4},{16,8},{20,12},{24,16},{28,20},{9,1},{13,5},{17,9},{2... | collective-permute-start | bytes 1966088 | tf_op jit(solution)/shard_map/ppermute | solution.py:391
  20.1 11.0 %collective-permute-start.1 = (s32[1,4]{1,0:T(1,128)S(1)}, s32[1,4]{1,0:T(1,128)S(1)}, u32[]{:S(2)}, u32[]{:S(2)}) collective-permute-start(s32[1,4]{1,0:T(1,128)S(1)} %copy-done.4), channel_id=1, source_target_pairs={{8,0},{12,4},{16,8},{20,12},{24,16},{28,20},{9,1},{13,5},{17,9},{2... | collective-permute-start | bytes 56 | tf_op jit(solution)/shard_map/ppermute | solution.py:393
  21.4 9.7 %collective-permute-start = (s32[1,4]{1,0:T(1,128)S(1)}, s32[1,4]{1,0:T(1,128)S(1)}, u32[]{:S(2)}, u32[]{:S(2)}) collective-permute-start(s32[1,4]{1,0:T(1,128)S(1)} %copy-done.4), channel_id=1, source_target_pairs={{4,0},{8,4},{12,8},{16,12},{20,16},{24,20},{28,24},{5,1},{9,5},{13... | collective-permute-start | bytes 56 | tf_op jit(solution)/shard_map/ppermute | solution.py:393
  22.7 15.7 %collective-permute-start.5 = (bf16[1,160,1024]{2,1,0:T(8,128)(2,1)}, bf16[1,160,1024]{2,1,0:T(8,128)(2,1)S(1)}, u32[]{:S(2)}, u32[]{:S(2)}) collective-permute-start(bf16[1,160,1024]{2,1,0:T(8,128)(2,1)} %get-tuple-element.17.rest_1_.rest_2_), channel_id=1, source_target_pairs={{8,0},{12,4},{16,8},{20,12},{24,16},{28,20},{9,1},{13,5},{17,9},{2... | collective-permute-start | bytes 983048 | tf_op jit(solution)/shard_map/ppermute | solution.py:391
  24.0 20.4 %collective-permute-start.7 = (bf16[1,160,1024]{2,1,0:T(8,128)(2,1)}, bf16[1,160,1024]{2,1,0:T(8,128)(2,1)S(1)}, u32[]{:S(2)}, u32[]{:S(2)}) collective-permute-start(bf16[1,160,1024]{2,1,0:T(8,128)(2,1)} %get-tuple-element.22.rest_2_.rest_3_), channel_id=1, source_target_pairs={{8,0},{12,4},{16,8},{20,12},{24,16},{28,20},{9,1},{13,5},{17,9},{2... | collective-permute-start | bytes 983048 | tf_op jit(solution)/shard_map/ppermute | solution.py:391
  29.4 18.1 %copy-start.1 = (bf16[2,160,1024]{2,1,0:T(8,128)(2,1)}, bf16[2,160,1024]{2,1,0:T(8,128)(2,1)S(1)}, u32[]{:S(2)}) copy-start(bf16[2,160,1024]{2,1,0:T(8,128)(2,1)S(1)} %collective-permute-done.2.rest_2_.rest_7_) | copy-start | bytes 1966084
  29.4 18.0 %collective-permute-start.9 = (bf16[2,160,1024]{2,1,0:T(8,128)(2,1)S(1)}, bf16[2,160,1024]{2,1,0:T(8,128)(2,1)S(1)}, u32[]{:S(2)}, u32[]{:S(2)}) collective-permute-start(bf16[2,160,1024]{2,1,0:T(8,128)(2,1)S(1)} %broadcast_select_fusion), channel_id=1, source_target_pairs={{4,0},{0,4},{12,8},{8,12},{20,16},{16,20},{28,24},{24,28},{5,1},{1... | collective-permute-start | bytes 1966088 | tf_op jit(solution)/shard_map/ppermute | solution.py:405
  31.3 1.2 %collective-permute-start.3 = (s32[3]{0:T(128)S(1)}, s32[3]{0:T(128)S(1)}, u32[]{:S(2)}, u32[]{:S(2)}) collective-permute-start(s32[3]{0:T(128)S(1)} %fusion), channel_id=1, source_target_pairs={{0,1},{1,0},{2,3},{3,2},{4,5},{5,4},{6,7},{7,6},{8,9},{9,8},{10,11... | collective-permute-start | bytes 44 | tf_op jit(solution)/shard_map/ppermute | solution.py:403
  32.5 3.5 %collective-permute-start.4 = (s32[3]{0:T(128)S(1)}, s32[3]{0:T(128)S(1)}, u32[]{:S(2)}, u32[]{:S(2)}) collective-permute-start(s32[3]{0:T(128)S(1)} %add.22), channel_id=1, source_target_pairs={{0,2},{1,3},{2,0},{3,1},{4,6},{5,7},{6,4},{7,5},{8,10},{9,11},{10,... | collective-permute-start | bytes 44 | tf_op jit(solution)/shard_map/ppermute | solution.py:404
  38.4 17.8 %copy-start.2 = (bf16[1,160,1024]{2,1,0:T(8,128)(2,1)}, bf16[1,160,1024]{2,1,0:T(8,128)(2,1)S(1)}, u32[]{:S(2)}) copy-start(bf16[1,160,1024]{2,1,0:T(8,128)(2,1)S(1)} %collective-permute-done.5.rest_5_.rest_8_) | copy-start | bytes 983044
  38.5 21.0 %collective-permute-start.6 = (bf16[1,160,1024]{2,1,0:T(8,128)(2,1)S(1)}, bf16[1,160,1024]{2,1,0:T(8,128)(2,1)S(1)}, u32[]{:S(2)}, u32[]{:S(2)}) collective-permute-start(bf16[1,160,1024]{2,1,0:T(8,128)(2,1)S(1)} %broadcast_select_fusion.2), channel_id=1, source_target_pairs={{4,0},{0,4},{12,8},{8,12},{20,16},{16,20},{28,24},{24,28},{5,1},{1... | collective-permute-start | bytes 983048 | tf_op jit(solution)/shard_map/ppermute | solution.py:405
  44.5 11.8 %copy-start.3 = (bf16[1,160,1024]{2,1,0:T(8,128)(2,1)}, bf16[1,160,1024]{2,1,0:T(8,128)(2,1)S(1)}, u32[]{:S(2)}) copy-start(bf16[1,160,1024]{2,1,0:T(8,128)(2,1)S(1)} %collective-permute-done.7.rest_6_.rest_9_) | copy-start | bytes 983044
  44.5 14.9 %collective-permute-start.8 = (bf16[1,160,1024]{2,1,0:T(8,128)(2,1)S(1)}, bf16[1,160,1024]{2,1,0:T(8,128)(2,1)S(1)}, u32[]{:S(2)}, u32[]{:S(2)}) collective-permute-start(bf16[1,160,1024]{2,1,0:T(8,128)(2,1)S(1)} %broadcast_select_fusion.1), channel_id=1, source_target_pairs={{4,0},{0,4},{12,8},{8,12},{20,16},{16,20},{28,24},{24,28},{5,1},{1... | collective-permute-start | bytes 983048 | tf_op jit(solution)/shard_map/ppermute | solution.py:405
  47.4 0.9 %copy-start.5 = (bf16[2,160,1024]{2,1,0:T(8,128)(2,1)}, bf16[2,160,1024]{2,1,0:T(8,128)(2,1)S(1)}, u32[]{:S(2)}) copy-start(bf16[2,160,1024]{2,1,0:T(8,128)(2,1)S(1)} %collective-permute-done.9.rest_1_.rest_4_) | copy-start | bytes 1966084
  59.5 0.7 copy-start.7
  60.2 0.7 copy-start.6
  69.3 1.9 %collective-permute-start.10 = (bf16[160,8,128]{2,1,0:T(8,128)(2,1)}, bf16[160,8,128]{2,1,0:T(8,128)(2,1)S(1)}, u32[]{:S(2)}, u32[]{:S(2)}) collective-permute-start(bf16[160,8,128]{2,1,0:T(8,128)(2,1)} %get-tuple-element.26), channel_id=1, source_target_pairs={{0,1},{1,0},{2,3},{3,2},{4,5},{5,4},{6,7},{7,6},{8,9},{9,8},{10,11... | collective-permute-start | bytes 983048 | tf_op jit(solution)/shard_map/ppermute | solution.py:414
  69.4 12.2 %collective-permute-start.11 = (bf16[160,8,128]{2,1,0:T(8,128)(2,1)}, bf16[160,8,128]{2,1,0:T(8,128)(2,1)S(1)}, u32[]{:S(2)}, u32[]{:S(2)}) collective-permute-start(bf16[160,8,128]{2,1,0:T(8,128)(2,1)} %get-tuple-element.28), channel_id=1, source_target_pairs={{0,1},{1,0},{2,3},{3,2},{4,5},{5,4},{6,7},{7,6},{8,9},{9,8},{10,11... | collective-permute-start | bytes 983048 | tf_op jit(solution)/shard_map/ppermute | solution.py:415
  72.4 9.8 %collective-permute-start.12 = (bf16[160,8,128]{2,1,0:T(8,128)(2,1)S(1)}, bf16[160,8,128]{2,1,0:T(8,128)(2,1)S(1)}, u32[]{:S(2)}, u32[]{:S(2)}) collective-permute-start(bf16[160,8,128]{2,1,0:T(8,128)(2,1)S(1)} %add_convert_fusion), channel_id=1, source_target_pairs={{0,2},{1,3},{2,0},{3,1},{4,6},{5,7},{6,4},{7,5},{8,10},{9,11},{10,... | collective-permute-start | bytes 983048 | tf_op jit(solution)/shard_map/ppermute | solution.py:417

commit v12 on v11

--- a/solution.py
+++ b/solution.py
@@ -343,7 +343,7 @@
             for tile in range(TILES)
         ]
     smem = pl.BlockSpec(memory_space=pltpu.SMEM)
-    anywhere = pl.BlockSpec(memory_space=pltpu.HBM)
+    anywhere = pl.BlockSpec(memory_space=pl.ANY)
     small = [*places, scales] if last else places
     large = [*owns, *nexts, *fars, lag_table, *([] if before is None else [before])]
     return pl.pallas_call(
@@ -360,7 +360,7 @@
         out_specs=[anywhere] * len(out_shape),
         out_shape=out_shape,
         scratch_shapes=scratch,
-        compiler_params=pltpu.CompilerParams(vmem_limit_bytes=60 << 20),
+        compiler_params=pltpu.CompilerParams(vmem_limit_bytes=24 << 20),
         cost_estimate=pl.CostEstimate(
             flops=20 * channels * 8 * len(quarters) * columns * LAGS,
             bytes_accessed=6 * segs * channels * columns,

time: 85.9 us -> 82.1 us (0.956)
  waiting for transfers between devices: 17.1 us -> 20.4 us
  other arithmetic: 4 us -> 1.31 us
  local copies, waits for them, and re-layouts: 2.34 us -> 0.03 us
  Pallas kernels: 42.7 us -> 41 us
    unnamed x16 -> x12, local copies, waits for them, and re-layouts: 2.34 us -> 0.03 us
    ppermute x3, waiting for transfers between devices: 3.17 us -> 4.89 us  [shards(): nexts.append(lax.ppermute(passed, 'chan', pair_swap))]
    pallas_call x3, Pallas kernels: 24.1 us -> 22.4 us  [correlated(): pl.pallas_call(functools.partial(cross_kernel, groups=groups, specs=specs...]
    ppermute x1, waiting for transfers between devices: 0.63 us -> 1.81 us  [shards(): crossed = lax.ppermute(passing, 'tm', side_swap)]
    convert_element_type x1, other arithmetic: 1.15 us -> 0.07 us  [shards(): passing = (other + got_far.astype(jnp.float32)).astype(jnp.bfloat16)]
    add x1, other arithmetic: 2.01 us -> 0.94 us  [shards(): return keep + got.astype(jnp.float32) + crossed.astype(jnp.float32)]
  transfers between devices with their start and end apart: 13 -> 13, of which waited for: 8 -> 8; matrix products, arithmetic and copies ran while one was open for 2% -> 0% of each run, Pallas kernels for 30% -> 29%
where the time goes in v12:
time: 82.1 us; the launch traced here: 80.6 us
  Pallas kernels  41 us (50%)
  waiting for transfers between devices  20.4 us (25%)
  starting transfers between devices  17.6 us (21%)
  other arithmetic  1.31 us (2%)
    pallas_call x3, Pallas kernels, correlated(): pl.pallas_call(functools.partial(cross_kernel, groups=groups, specs=specs...  22.4 us
    pallas_call x2, Pallas kernels, whitened(): pl.pallas_call(functools.partial(spectra_kernel, first_seg=first_seg), na...  18.7 us
    ppermute x3, waiting for transfers between devices, shards(): fars = [lax.ppermute(white, 'chan', hop_far) for white in whites]  9.45 us
    ppermute x3, starting transfers between devices, shards(): nexts.append(lax.ppermute(passed, 'chan', pair_swap))  7.43 us
    ppermute x3, waiting for transfers between devices, shards(): nexts.append(lax.ppermute(passed, 'chan', pair_swap))  4.89 us
    ppermute x3, starting transfers between devices, shards(): fars = [lax.ppermute(white, 'chan', hop_far) for white in whites]  4.01 us
    ppermute x2, starting transfers between devices, shards(): lax.ppermute(valid_mask, 'chan', hop)  2.58 us
    ppermute x1, waiting for transfers between devices, shards(): counts += lax.ppermute(counts, 'tm', side_swap)  2.02 us
  transfers between devices with their start and end apart: 13, of which 8 were waited for; matrix products, arithmetic and copies ran while one was open for 0% of the time, Pallas kernels for 29%

profile of v12, /device:TPU:0, one launch (start us, length us, event | category | flops | bytes accessed | tf_op | source)
XLA Modules:
  0.0 80.6 jit_solution(9891557288392008894)
XLA Ops:
  0.0 9.3 %spectra.3.rest_0_.rest_1_ = bf16[2,160,1024]{2,1,0:T(8,128)(2,1)} custom-call(s32[1,4]{1,0:T(1,128)} %valid_ref.3, bf16[160,4,7680]{2,1,0:T(4,128)(2,1)} %records_hbm.3, bf16[3840,1024]{1,0:T(8,128)(2,1)} %constant.35.clone.table_ref), custom_call_target="tpu_custom_call" | custom-call | flops 5033164800 | bytes 17694720 | tf_op jit(solution)/shard_map/spectra/pallas_call | solution.py:125
  9.3 0.0 copy-start
  9.4 0.0 copy-start.4
  9.4 1.4 %collective-permute-start.2 = (bf16[2,160,1024]{2,1,0:T(8,128)(2,1)}, bf16[2,160,1024]{2,1,0:T(8,128)(2,1)S(1)}, u32[]{:S(2)}, u32[]{:S(2)}) collective-permute-start(bf16[2,160,1024]{2,1,0:T(8,128)(2,1)} %spectra.3.rest_0_.rest_1_), channel_id=1, source_target_pairs={{8,0},{12,4},{16,8},{20,12},{24,16},{28,20},{9,1},{13,5},{17,9},{2... | collective-permute-start | bytes 1966088 | tf_op jit(solution)/shard_map/ppermute | solution.py:391
  10.8 9.3 %spectra.2 = (bf16[1,160,1024]{2,1,0:T(8,128)(2,1)}, bf16[1,160,1024]{2,1,0:T(8,128)(2,1)}) custom-call(s32[1,4]{1,0:T(1,128)} %valid_ref.3, bf16[160,4,7680]{2,1,0:T(4,128)(2,1)} %records_hbm.3, bf16[3840,1024]{1,0:T(8,128)(2,1)} %constant.35.clone.table_ref), custom_call_target="tpu_custom_call" | custom-call | flops 5033164800 | bytes 17694720 | tf_op jit(solution)/shard_map/spectra/pallas_call | solution.py:125
  20.2 1.3 %collective-permute-start.1 = (s32[1,4]{1,0:T(1,128)S(1)}, s32[1,4]{1,0:T(1,128)S(1)}, u32[]{:S(2)}, u32[]{:S(2)}) collective-permute-start(s32[1,4]{1,0:T(1,128)S(1)} %copy-done.5), channel_id=1, source_target_pairs={{8,0},{12,4},{16,8},{20,12},{24,16},{28,20},{9,1},{13,5},{17,9},{2... | collective-permute-start | bytes 56 | tf_op jit(solution)/shard_map/ppermute | solution.py:393
  21.5 1.3 %collective-permute-start = (s32[1,4]{1,0:T(1,128)S(1)}, s32[1,4]{1,0:T(1,128)S(1)}, u32[]{:S(2)}, u32[]{:S(2)}) collective-permute-start(s32[1,4]{1,0:T(1,128)S(1)} %copy-done.5), channel_id=1, source_target_pairs={{4,0},{8,4},{12,8},{16,12},{20,16},{24,20},{28,24},{5,1},{9,5},{13... | collective-permute-start | bytes 56 | tf_op jit(solution)/shard_map/ppermute | solution.py:393
  22.8 1.3 %collective-permute-start.5 = (bf16[1,160,1024]{2,1,0:T(8,128)(2,1)}, bf16[1,160,1024]{2,1,0:T(8,128)(2,1)S(1)}, u32[]{:S(2)}, u32[]{:S(2)}) collective-permute-start(bf16[1,160,1024]{2,1,0:T(8,128)(2,1)} %get-tuple-element.17.rest_1_.rest_2_), channel_id=1, source_target_pairs={{8,0},{12,4},{16,8},{20,12},{24,16},{28,20},{9,1},{13,5},{17,9},{2... | collective-permute-start | bytes 983048 | tf_op jit(solution)/shard_map/ppermute | solution.py:391
  24.1 1.3 %collective-permute-start.7 = (bf16[1,160,1024]{2,1,0:T(8,128)(2,1)}, bf16[1,160,1024]{2,1,0:T(8,128)(2,1)S(1)}, u32[]{:S(2)}, u32[]{:S(2)}) collective-permute-start(bf16[1,160,1024]{2,1,0:T(8,128)(2,1)} %get-tuple-element.22.rest_2_.rest_3_), channel_id=1, source_target_pairs={{8,0},{12,4},{16,8},{20,12},{24,16},{28,20},{9,1},{13,5},{17,9},{2... | collective-permute-start | bytes 983048 | tf_op jit(solution)/shard_map/ppermute | solution.py:391
  25.4 4.0 %collective-permute-done.2.rest_2_.rest_7_ = bf16[2,160,1024]{2,1,0:T(8,128)(2,1)S(1)} collective-permute-done((bf16[2,160,1024]{2,1,0:T(8,128)(2,1)}, bf16[2,160,1024]{2,1,0:T(8,128)(2,1)S(1)}, u32[]{:S(2)}, u32[]{:S(2)}) %collective-permute-start.2) | collective-permute-done | bytes 655392 | tf_op jit(solution)/shard_map/ppermute | solution.py:391
  29.4 0.1 broadcast_select_fusion
  29.5 1.7 %collective-permute-start.9 = (bf16[2,160,1024]{2,1,0:T(8,128)(2,1)S(1)}, bf16[2,160,1024]{2,1,0:T(8,128)(2,1)S(1)}, u32[]{:S(2)}, u32[]{:S(2)}) collective-permute-start(bf16[2,160,1024]{2,1,0:T(8,128)(2,1)S(1)} %broadcast_select_fusion), channel_id=1, source_target_pairs={{4,0},{0,4},{12,8},{8,12},{20,16},{16,20},{28,24},{24,28},{5,1},{1... | collective-permute-start | bytes 1966088 | tf_op jit(solution)/shard_map/ppermute | solution.py:405
  31.2 0.2 fusion
  31.3 0.1 collective-permute-start.3
  31.4 1.1 %collective-permute-done.3 = s32[3]{0:T(128)S(1)} collective-permute-done((s32[3]{0:T(128)S(1)}, s32[3]{0:T(128)S(1)}, u32[]{:S(2)}, u32[]{:S(2)}) %collective-permute-start.3) | collective-permute-done | bytes 44 | tf_op jit(solution)/shard_map/ppermute | solution.py:403
  32.5 1.5 %collective-permute-start.4 = (s32[3]{0:T(128)S(1)}, s32[3]{0:T(128)S(1)}, u32[]{:S(2)}, u32[]{:S(2)}) collective-permute-start(s32[3]{0:T(128)S(1)} %add.22), channel_id=1, source_target_pairs={{0,2},{1,3},{2,0},{3,1},{4,6},{5,7},{6,4},{7,5},{8,10},{9,11},{10,... | collective-permute-start | bytes 44 | tf_op jit(solution)/shard_map/ppermute | solution.py:404
  34.1 2.0 %collective-permute-done.4 = s32[3]{0:T(128)S(1)} collective-permute-done((s32[3]{0:T(128)S(1)}, s32[3]{0:T(128)S(1)}, u32[]{:S(2)}, u32[]{:S(2)}) %collective-permute-start.4) | collective-permute-done | bytes 44 | tf_op jit(solution)/shard_map/ppermute | solution.py:404
  36.1 2.4 %collective-permute-done.5.rest_5_.rest_8_ = bf16[1,160,1024]{2,1,0:T(8,128)(2,1)S(1)} collective-permute-done((bf16[1,160,1024]{2,1,0:T(8,128)(2,1)}, bf16[1,160,1024]{2,1,0:T(8,128)(2,1)S(1)}, u32[]{:S(2)}, u32[]{:S(2)}) %collective-permute-start.5) | collective-permute-done | bytes 327712 | tf_op jit(solution)/shard_map/ppermute | solution.py:391
  38.5 3.0 %collective-permute-start.6 = (bf16[1,160,1024]{2,1,0:T(8,128)(2,1)S(1)}, bf16[1,160,1024]{2,1,0:T(8,128)(2,1)S(1)}, u32[]{:S(2)}, u32[]{:S(2)}) collective-permute-start(bf16[1,160,1024]{2,1,0:T(8,128)(2,1)S(1)} %broadcast_select_fusion.2), channel_id=1, source_target_pairs={{4,0},{0,4},{12,8},{8,12},{20,16},{16,20},{28,24},{24,28},{5,1},{1... | collective-permute-start | bytes 983048 | tf_op jit(solution)/shard_map/ppermute | solution.py:405
  41.5 3.1 %collective-permute-done.7.rest_6_.rest_9_ = bf16[1,160,1024]{2,1,0:T(8,128)(2,1)S(1)} collective-permute-done((bf16[1,160,1024]{2,1,0:T(8,128)(2,1)}, bf16[1,160,1024]{2,1,0:T(8,128)(2,1)S(1)}, u32[]{:S(2)}, u32[]{:S(2)}) %collective-permute-start.7) | collective-permute-done | bytes 327712 | tf_op jit(solution)/shard_map/ppermute | solution.py:391
  44.6 2.8 %collective-permute-start.8 = (bf16[1,160,1024]{2,1,0:T(8,128)(2,1)S(1)}, bf16[1,160,1024]{2,1,0:T(8,128)(2,1)S(1)}, u32[]{:S(2)}, u32[]{:S(2)}) collective-permute-start(bf16[1,160,1024]{2,1,0:T(8,128)(2,1)S(1)} %broadcast_select_fusion.1), channel_id=1, source_target_pairs={{4,0},{0,4},{12,8},{8,12},{20,16},{16,20},{28,24},{24,28},{5,1},{1... | collective-permute-start | bytes 983048 | tf_op jit(solution)/shard_map/ppermute | solution.py:405
  47.4 7.2 %cross.3.rest_8_ = bf16[10,384,128]{2,1,0:T(8,128)(2,1)S(1)} custom-call(s32[1,2]{1,0:T(1,128)S(1)} %copy-done.3, s32[1]{0:T(128)} %bitcast.rank_ref, bf16[2,160,1024]{2,1,0:T(8,128)(2,1)S(1)} %copy-done, bf16[2,160,1024]{2,1,0:T(8,128)(2,1)S(1)} %collective-permute-done.9.rest_1_.rest_4_, bf16[2,160,1024]{2,1,0:T(8,128)(2,1)S(1)} %collective-permute-done.2.rest_2_.rest_7_, ...), custom_call_target="tpu_custom_call" | custom-call | flops 10066329600 | bytes 1966080 | tf_op jit(solution)/shard_map/cross/pallas_call | solution.py:349
  54.6 4.9 %collective-permute-done.8.rest_4_.rest_6_ = bf16[1,160,1024]{2,1,0:T(8,128)(2,1)S(1)} collective-permute-done((bf16[1,160,1024]{2,1,0:T(8,128)(2,1)S(1)}, bf16[1,160,1024]{2,1,0:T(8,128)(2,1)S(1)}, u32[]{:S(2)}, u32[]{:S(2)}) %collective-permute-start.8) | collective-permute-done | bytes 327712 | tf_op jit(solution)/shard_map/ppermute | solution.py:405
  59.5 8.5 %cross.4 = (f32[160,8,128]{2,1,0:T(8,128)S(1)}, bf16[160,8,128]{2,1,0:T(8,128)(2,1)S(1)}, bf16[160,8,128]{2,1,0:T(8,128)(2,1)S(1)}) custom-call(s32[1,2]{1,0:T(1,128)S(1)} %copy-done.3, s32[1]{0:T(128)} %bitcast.rank_ref, f32[3]{0:T(128)S(1)} %convert_divide_fusion, bf16[1,160,1024]{2,1,0:T(8,128)(2,1)S(1)} %copy-done.1, ...), custom_call_target="tpu_custom_call" | custom-call | flops 10066329600 | bytes 1966080 | tf_op jit(solution)/shard_map/cross/pallas_call | solution.py:349
  68.1 0.1 collective-permute-start.10
  68.1 0.5 collective-permute-start.11
  68.6 1.1 %collective-permute-done.10 = bf16[160,8,128]{2,1,0:T(8,128)(2,1)S(1)} collective-permute-done((bf16[160,8,128]{2,1,0:T(8,128)(2,1)S(1)}, bf16[160,8,128]{2,1,0:T(8,128)(2,1)S(1)}, u32[]{:S(2)}, u32[]{:S(2)}) %collective-permute-start.10) | collective-permute-done | bytes 327712 | tf_op jit(solution)/shard_map/ppermute | solution.py:414
  69.7 0.1 add_convert_fusion
  69.8 1.4 %collective-permute-start.12 = (bf16[160,8,128]{2,1,0:T(8,128)(2,1)S(1)}, bf16[160,8,128]{2,1,0:T(8,128)(2,1)S(1)}, u32[]{:S(2)}, u32[]{:S(2)}) collective-permute-start(bf16[160,8,128]{2,1,0:T(8,128)(2,1)S(1)} %add_convert_fusion), channel_id=1, source_target_pairs={{0,2},{1,3},{2,0},{3,1},{4,6},{5,7},{6,4},{7,5},{8,10},{9,11},{10,... | collective-permute-start | bytes 983048 | tf_op jit(solution)/shard_map/ppermute | solution.py:417
  71.2 6.6 %cross.5 = f32[160,8,128]{2,1,0:T(8,128)S(1)} custom-call(s32[1,2]{1,0:T(1,128)S(1)} %copy-done.3, s32[1]{0:T(128)} %bitcast.rank_ref, f32[3]{0:T(128)S(1)} %convert_divide_fusion, bf16[2,160,1024]{2,1,0:T(8,128)(2,1)S(1)} %copy-done, bf16[1,160,1024]{2,1,0:T(8,128)(2,1)S(1)} %copy-done.1, bf16[1,160,1024]{2,1,0:T(8,128)(2,1)S(1)} %copy-done.2, ...), custom_call_target="tpu_custom_call" | custom-call | flops 3355443200 | bytes 3932160 | tf_op jit(solution)/shard_map/cross/pallas_call | solution.py:349
  77.8 1.8 %collective-permute-done.12 = bf16[160,8,128]{2,1,0:T(8,128)(2,1)S(1)} collective-permute-done((bf16[160,8,128]{2,1,0:T(8,128)(2,1)S(1)}, bf16[160,8,128]{2,1,0:T(8,128)(2,1)S(1)}, u32[]{:S(2)}, u32[]{:S(2)}) %collective-permute-start.12) | collective-permute-done | bytes 327712 | tf_op jit(solution)/shard_map/ppermute | solution.py:417
  79.6 0.9 %convert_add_fusion = f32[160,8,128]{2,1,0:T(8,128)} fusion(bf16[160,8,128]{2,1,0:T(8,128)(2,1)S(1)} %collective-permute-done.12, f32[160,8,128]{2,1,0:T(8,128)S(1)} %cross.5, bf16[160,8,128]{2,1,0:T(8,128)(2,1)S(1)} %collective-permute-done.11), kind=kLoop, calls=%fused_computation | loop fusion | flops 655360 | bytes 1966080 | tf_op jit(solution)/shard_map/add | solution.py:420
  (19 shorter events, 0.1 us)
Async XLA Ops:
  9.3 10.8 %copy-start.5 = (s32[1,4]{1,0:T(1,128)S(1)}, s32[1,4]{1,0:T(1,128)}, u32[]{:S(2)}) copy-start(s32[1,4]{1,0:T(1,128)} %valid_ref.3) | copy-start | bytes 52
  9.3 20.0 %copy-start = (bf16[2,160,1024]{2,1,0:T(8,128)(2,1)S(1)}, bf16[2,160,1024]{2,1,0:T(8,128)(2,1)}, u32[]{:S(2)}) copy-start(bf16[2,160,1024]{2,1,0:T(8,128)(2,1)} %spectra.3.rest_0_.rest_1_) | copy-start | bytes 1966084
  9.4 38.0 %copy-start.3 = (s32[1,2]{1,0:T(1,128)S(1)}, s32[1,2]{1,0:T(1,128)}, u32[]{:S(2)}) copy-start(s32[1,2]{1,0:T(1,128)} %band_ref.5) | copy-start | bytes 28
  9.4 38.0 %copy-start.4 = (bf16[4,256,256]{2,1,0:T(8,128)(2,1)S(1)}, bf16[4,256,256]{2,1,0:T(8,128)(2,1)}, u32[]{:S(2)}) copy-start(bf16[4,256,256]{2,1,0:T(8,128)(2,1)} %constant.34.clone.rest_3_.rest_7_.rest_10_) | copy-start | bytes 1572868
  9.4 20.0 %collective-permute-start.2 = (bf16[2,160,1024]{2,1,0:T(8,128)(2,1)}, bf16[2,160,1024]{2,1,0:T(8,128)(2,1)S(1)}, u32[]{:S(2)}, u32[]{:S(2)}) collective-permute-start(bf16[2,160,1024]{2,1,0:T(8,128)(2,1)} %spectra.3.rest_0_.rest_1_), channel_id=1, source_target_pairs={{8,0},{12,4},{16,8},{20,12},{24,16},{28,20},{9,1},{13,5},{17,9},{2... | collective-permute-start | bytes 1966088 | tf_op jit(solution)/shard_map/ppermute | solution.py:391
  20.2 11.0 %collective-permute-start.1 = (s32[1,4]{1,0:T(1,128)S(1)}, s32[1,4]{1,0:T(1,128)S(1)}, u32[]{:S(2)}, u32[]{:S(2)}) collective-permute-start(s32[1,4]{1,0:T(1,128)S(1)} %copy-done.5), channel_id=1, source_target_pairs={{8,0},{12,4},{16,8},{20,12},{24,16},{28,20},{9,1},{13,5},{17,9},{2... | collective-permute-start | bytes 56 | tf_op jit(solution)/shard_map/ppermute | solution.py:393
  21.5 9.7 %collective-permute-start = (s32[1,4]{1,0:T(1,128)S(1)}, s32[1,4]{1,0:T(1,128)S(1)}, u32[]{:S(2)}, u32[]{:S(2)}) collective-permute-start(s32[1,4]{1,0:T(1,128)S(1)} %copy-done.5), channel_id=1, source_target_pairs={{4,0},{8,4},{12,8},{16,12},{20,16},{24,20},{28,24},{5,1},{9,5},{13... | collective-permute-start | bytes 56 | tf_op jit(solution)/shard_map/ppermute | solution.py:393
  22.8 15.7 %collective-permute-start.5 = (bf16[1,160,1024]{2,1,0:T(8,128)(2,1)}, bf16[1,160,1024]{2,1,0:T(8,128)(2,1)S(1)}, u32[]{:S(2)}, u32[]{:S(2)}) collective-permute-start(bf16[1,160,1024]{2,1,0:T(8,128)(2,1)} %get-tuple-element.17.rest_1_.rest_2_), channel_id=1, source_target_pairs={{8,0},{12,4},{16,8},{20,12},{24,16},{28,20},{9,1},{13,5},{17,9},{2... | collective-permute-start | bytes 983048 | tf_op jit(solution)/shard_map/ppermute | solution.py:391
  24.1 20.4 %collective-permute-start.7 = (bf16[1,160,1024]{2,1,0:T(8,128)(2,1)}, bf16[1,160,1024]{2,1,0:T(8,128)(2,1)S(1)}, u32[]{:S(2)}, u32[]{:S(2)}) collective-permute-start(bf16[1,160,1024]{2,1,0:T(8,128)(2,1)} %get-tuple-element.22.rest_2_.rest_3_), channel_id=1, source_target_pairs={{8,0},{12,4},{16,8},{20,12},{24,16},{28,20},{9,1},{13,5},{17,9},{2... | collective-permute-start | bytes 983048 | tf_op jit(solution)/shard_map/ppermute | solution.py:391
  29.5 17.9 %collective-permute-start.9 = (bf16[2,160,1024]{2,1,0:T(8,128)(2,1)S(1)}, bf16[2,160,1024]{2,1,0:T(8,128)(2,1)S(1)}, u32[]{:S(2)}, u32[]{:S(2)}) collective-permute-start(bf16[2,160,1024]{2,1,0:T(8,128)(2,1)S(1)} %broadcast_select_fusion), channel_id=1, source_target_pairs={{4,0},{0,4},{12,8},{8,12},{20,16},{16,20},{28,24},{24,28},{5,1},{1... | collective-permute-start | bytes 1966088 | tf_op jit(solution)/shard_map/ppermute | solution.py:405
  31.3 1.2 %collective-permute-start.3 = (s32[3]{0:T(128)S(1)}, s32[3]{0:T(128)S(1)}, u32[]{:S(2)}, u32[]{:S(2)}) collective-permute-start(s32[3]{0:T(128)S(1)} %fusion), channel_id=1, source_target_pairs={{0,1},{1,0},{2,3},{3,2},{4,5},{5,4},{6,7},{7,6},{8,9},{9,8},{10,11... | collective-permute-start | bytes 44 | tf_op jit(solution)/shard_map/ppermute | solution.py:403
  32.5 3.5 %collective-permute-start.4 = (s32[3]{0:T(128)S(1)}, s32[3]{0:T(128)S(1)}, u32[]{:S(2)}, u32[]{:S(2)}) collective-permute-start(s32[3]{0:T(128)S(1)} %add.22), channel_id=1, source_target_pairs={{0,2},{1,3},{2,0},{3,1},{4,6},{5,7},{6,4},{7,5},{8,10},{9,11},{10,... | collective-permute-start | bytes 44 | tf_op jit(solution)/shard_map/ppermute | solution.py:404
  38.5 21.0 %collective-permute-start.6 = (bf16[1,160,1024]{2,1,0:T(8,128)(2,1)S(1)}, bf16[1,160,1024]{2,1,0:T(8,128)(2,1)S(1)}, u32[]{:S(2)}, u32[]{:S(2)}) collective-permute-start(bf16[1,160,1024]{2,1,0:T(8,128)(2,1)S(1)} %broadcast_select_fusion.2), channel_id=1, source_target_pairs={{4,0},{0,4},{12,8},{8,12},{20,16},{16,20},{28,24},{24,28},{5,1},{1... | collective-permute-start | bytes 983048 | tf_op jit(solution)/shard_map/ppermute | solution.py:405
  44.6 14.9 %collective-permute-start.8 = (bf16[1,160,1024]{2,1,0:T(8,128)(2,1)S(1)}, bf16[1,160,1024]{2,1,0:T(8,128)(2,1)S(1)}, u32[]{:S(2)}, u32[]{:S(2)}) collective-permute-start(bf16[1,160,1024]{2,1,0:T(8,128)(2,1)S(1)} %broadcast_select_fusion.1), channel_id=1, source_target_pairs={{4,0},{0,4},{12,8},{8,12},{20,16},{16,20},{28,24},{24,28},{5,1},{1... | collective-permute-start | bytes 983048 | tf_op jit(solution)/shard_map/ppermute | solution.py:405
  47.3 12.1 %copy-start.1 = (bf16[1,160,1024]{2,1,0:T(8,128)(2,1)S(1)}, bf16[1,160,1024]{2,1,0:T(8,128)(2,1)}, u32[]{:S(2)}) copy-start(bf16[1,160,1024]{2,1,0:T(8,128)(2,1)} %get-tuple-element.17.rest_1_.rest_2_) | copy-start | bytes 983044
  47.4 12.1 %copy-start.2 = (bf16[1,160,1024]{2,1,0:T(8,128)(2,1)S(1)}, bf16[1,160,1024]{2,1,0:T(8,128)(2,1)}, u32[]{:S(2)}) copy-start(bf16[1,160,1024]{2,1,0:T(8,128)(2,1)} %get-tuple-element.22.rest_2_.rest_3_) | copy-start | bytes 983044
  68.1 1.7 %collective-permute-start.10 = (bf16[160,8,128]{2,1,0:T(8,128)(2,1)S(1)}, bf16[160,8,128]{2,1,0:T(8,128)(2,1)S(1)}, u32[]{:S(2)}, u32[]{:S(2)}) collective-permute-start(bf16[160,8,128]{2,1,0:T(8,128)(2,1)S(1)} %get-tuple-element.26), channel_id=1, source_target_pairs={{0,1},{1,0},{2,3},{3,2},{4,5},{5,4},{6,7},{7,6},{8,9},{9,8},{10,11... | collective-permute-start | bytes 983048 | tf_op jit(solution)/shard_map/ppermute | solution.py:414
  68.1 9.7 %collective-permute-start.11 = (bf16[160,8,128]{2,1,0:T(8,128)(2,1)S(1)}, bf16[160,8,128]{2,1,0:T(8,128)(2,1)S(1)}, u32[]{:S(2)}, u32[]{:S(2)}) collective-permute-start(bf16[160,8,128]{2,1,0:T(8,128)(2,1)S(1)} %get-tuple-element.28), channel_id=1, source_target_pairs={{0,1},{1,0},{2,3},{3,2},{4,5},{5,4},{6,7},{7,6},{8,9},{9,8},{10,11... | collective-permute-start | bytes 983048 | tf_op jit(solution)/shard_map/ppermute | solution.py:415
  69.8 9.8 %collective-permute-start.12 = (bf16[160,8,128]{2,1,0:T(8,128)(2,1)S(1)}, bf16[160,8,128]{2,1,0:T(8,128)(2,1)S(1)}, u32[]{:S(2)}, u32[]{:S(2)}) collective-permute-start(bf16[160,8,128]{2,1,0:T(8,128)(2,1)S(1)} %add_convert_fusion), channel_id=1, source_target_pairs={{0,2},{1,3},{2,0},{3,1},{4,6},{5,7},{6,4},{7,5},{8,10},{9,11},{10,... | collective-permute-start | bytes 983048 | tf_op jit(solution)/shard_map/ppermute | solution.py:417
